TPU v7x, 32 devices: a whole 2x2x4 slice. The times are simulated.
32 devices in a mesh: grp: 4 (over y, core), seq: 8 (over z, x).
Axes of the slice: x: 2, y: 2, z: 4, core: 2. Of those that a mesh axis runs over, the one named last changes fastest.
Arguments:
- queries: bfloat16 [32768, 1024], P(('grp', 'seq')), may hold values from -6 to 6
- key_rows: bfloat16 [32768, 1024], P(('grp', 'seq')), may hold values from -6 to 6
- value_rows: bfloat16 [32768, 1024], P(('grp', 'seq')), may hold values from -6 to 6
- norm_gain: float32 [1024], replicated, may hold values from 0.25 to 1.75
- cotangent: bfloat16 [32768, 1024], P(('grp', 'seq')), may hold values from -6 to 6
Outputs:
- normed_out: bfloat16 [32768, 1024], P(('grp', 'seq'))
- grad_queries: bfloat16 [32768, 1024], P(('grp', 'seq'))
- grad_keys: bfloat16 [32768, 1024], P(('grp', 'seq'))
- grad_values: bfloat16 [32768, 1024], P(('grp', 'seq'))
All inputs are finite; a program needn't handle non-finite values.
Results may differ from a plain program's by a relative error of at most 0.0058.
Values sent between devices are 32-bit elements; how exact they have to be, the bound alone decides.
No kernel may reach another device: no remote copies, remote signals or barrier semaphores. Data moves between devices by JAX's collectives and lax.ppermute only.
A program may use at most 128 MiB of HBM per device.

v0:
```python
import jax
import jax.numpy as jnp
from jax import lax
from jax.sharding import PartitionSpec as P

H = 8
HD = 128
BLOCK = 512


EPSILON = 1e-06


def lower_mask(length):
    indices = jnp.arange(length)
    return indices[:, None] >= indices[None, :]


def carried(own_total, reverse):
    devices = lax.axis_size(("grp", "seq"))
    flat = own_total.reshape(devices, own_total.size // devices)
    slices = lax.all_to_all(flat, ("grp", "seq"), split_axis=0, concat_axis=0, tiled=True)
    if reverse:
        inclusive = jnp.cumsum(slices[::-1], axis=0)[::-1]
    else:
        inclusive = jnp.cumsum(slices, axis=0)
    exclusive = inclusive - slices
    returned = lax.all_to_all(exclusive, ("grp", "seq"), split_axis=0, concat_axis=0, tiled=True)
    return returned.reshape(own_total.shape)


def body(queries, key_rows, value_rows, norm_gain, cotangent):
    tokens, features = queries.shape
    block_count = tokens // BLOCK
    block_shape = (block_count, BLOCK, H, HD)
    query_blocks = queries.reshape(block_shape)
    key_blocks = key_rows.reshape(block_shape)
    value_blocks = value_rows.reshape(block_shape)
    causal = lower_mask(BLOCK)[None, None]
    block_states = jnp.einsum(
        "bshd,bshe->bhde", key_blocks, value_blocks, preferred_element_type=jnp.float32
    )
    own_total = jnp.sum(block_states, axis=0)
    inside = jnp.cumsum(block_states, axis=0) - block_states
    scores = jnp.einsum(
        "bthd,bshd->bhts", query_blocks, key_blocks, preferred_element_type=jnp.float32
    )
    scores = jnp.where(causal, scores, 0.0).astype(jnp.bfloat16)
    local_part = jnp.einsum(
        "bhts,bshe->bthe", scores, value_blocks, preferred_element_type=jnp.float32
    )
    prior_state = (carried(own_total, False) + inside).astype(jnp.bfloat16)
    attended = local_part + jnp.einsum(
        "bthd,bhde->bthe", query_blocks, prior_state, preferred_element_type=jnp.float32
    )
    attended = attended.reshape(tokens, features)
    inverse = lax.rsqrt(jnp.mean(attended * attended, axis=1, keepdims=True) + EPSILON)
    unit_rows = attended * inverse
    gain_rows = norm_gain[None, :]
    normed_out = (unit_rows * gain_rows).astype(jnp.bfloat16)
    scaled = cotangent.astype(jnp.float32) * gain_rows
    grad_attended = inverse * (
        scaled - unit_rows * jnp.mean(scaled * unit_rows, axis=1, keepdims=True)
    )
    grad_blocks = grad_attended.astype(jnp.bfloat16).reshape(block_shape)
    grad_states = jnp.einsum(
        "bthd,bthe->bhde", query_blocks, grad_blocks, preferred_element_type=jnp.float32
    )
    grad_total = jnp.sum(grad_states, axis=0)
    later_inside = jnp.cumsum(grad_states[::-1], axis=0)[::-1] - grad_states
    grad_scores = jnp.einsum(
        "bthe,bshe->bhts", grad_blocks, value_blocks, preferred_element_type=jnp.float32
    )
    grad_scores = jnp.where(causal, grad_scores, 0.0).astype(jnp.bfloat16)
    local_q = jnp.einsum(
        "bhts,bshd->bthd", grad_scores, key_blocks, preferred_element_type=jnp.float32
    )
    local_k = jnp.einsum(
        "bhts,bthd->bshd", grad_scores, query_blocks, preferred_element_type=jnp.float32
    )
    local_v = jnp.einsum("bhts,bthe->bshe", scores, grad_blocks, preferred_element_type=jnp.float32)
    later_state = (carried(grad_total, True) + later_inside).astype(jnp.bfloat16)
    grad_q = local_q + jnp.einsum(
        "bthe,bhde->bthd", grad_blocks, prior_state, preferred_element_type=jnp.float32
    )
    grad_k = local_k + jnp.einsum(
        "bshe,bhde->bshd", value_blocks, later_state, preferred_element_type=jnp.float32
    )
    grad_v = local_v + jnp.einsum(
        "bshd,bhde->bshe", key_blocks, later_state, preferred_element_type=jnp.float32
    )
    return (
        normed_out,
        grad_q.astype(jnp.bfloat16).reshape(tokens, features),
        grad_k.astype(jnp.bfloat16).reshape(tokens, features),
        grad_v.astype(jnp.bfloat16).reshape(tokens, features),
    )


def solution(mesh):
    return jax.shard_map(
        body,
        mesh=mesh,
        in_specs=(
            P(("grp", "seq"), None),
            P(("grp", "seq"), None),
            P(("grp", "seq"), None),
            P(),
            P(("grp", "seq"), None),
        ),
        out_specs=(
            P(("grp", "seq"), None),
            P(("grp", "seq"), None),
            P(("grp", "seq"), None),
            P(("grp", "seq"), None),
        ),
        check_vma=False,
    )
```

profile of v0, /device:TPU:0, one launch (start us, length us, event | category | flops | bytes accessed | tf_op | source)
XLA Modules:
  0.0 159.8 jit_solution(1732613189303977116)
XLA Ops:
  0.6 2.4 %copy.120 = bf16[128,8,8,128]{3,2,1,0:T(8,128)(2,1)S(1)} copy(bf16[128,8,8,128]{3,1,2,0:T(8,128)(2,1)} %bitcast.105) | data formatting | bytes 4194304
  3.0 0.6 copy.121
  3.7 0.7 copy-done.7
  4.4 2.9 %fusion.22 = (f32[8,128,128]{2,1,0:T(8,128)}, f32[2,8,128,128]{3,2,1,0:T(8,128)}) fusion(bf16[2,512,8,128]{3,2,1,0:T(8,128)(2,1)S(1)} %bitcast.93, bf16[2,512,8,128]{3,2,1,0:T(8,128)(2,1)S(1)} %bitcast.97), kind=kOutput, calls=%fused_computation.46 | convolution fusion | flops 268566528 | bytes 5767168 | tf_op jit(solution)/shard_map/bshd,bshe->bhde/dot_general | solution.py:40
  7.3 7.3 %all-to-all-start = ((f32[32,1,4096]{2,1,0:T(1,128)}), f32[32,1,4096]{2,1,0:T(1,128)S(1)}, u32[]{:S(2)}, u32[]{:S(2)}) async-start(f32[32,1,4096]{2,1,0:T(1,128)} %bitcast.1), calls=%async_computation | async-start | bytes 1048576 | tf_op jit(solution)/shard_map/all_to_all | solution.py:22
  14.6 2.2 %copy.119 = bf16[128,8,8,128]{3,2,1,0:T(8,128)(2,1)S(1)} copy(bf16[128,8,8,128]{3,1,2,0:T(8,128)(2,1)} %bitcast.107) | data formatting | bytes 4194304
  17.0 13.9 %all-to-all-done = f32[32,1,4096]{2,1,0:T(1,128)S(1)} async-done(((f32[32,1,4096]{2,1,0:T(1,128)}), f32[32,1,4096]{2,1,0:T(1,128)S(1)}, u32[]{:S(2)}, u32[]{:S(2)}) %all-to-all-start) | async-done | bytes 524320 | tf_op jit(solution)/shard_map/all_to_all | solution.py:22
  30.9 1.2 reduce-window_subtract_fusion.1
  32.0 3.5 %all-to-all-start.1 = ((f32[32,1,4096]{2,1,0:T(1,128)}), f32[32,1,4096]{2,1,0:T(1,128)}, u32[]{:S(2)}, u32[]{:S(2)}) async-start(f32[32,1,4096]{2,1,0:T(1,128)} %reduce-window_subtract_fusion.1), calls=%async_computation.1 | async-start | bytes 1048576 | tf_op jit(solution)/shard_map/all_to_all | solution.py:28
  35.6 4.0 %select_convert_fusion.1 = bf16[2,8,512,512]{3,2,1,0:T(8,128)(2,1)S(1)} fusion(pred[512,512]{1,0:T(8,128)(4,1)S(1)} %iota_compare_fusion, bf16[2,512,8,128]{3,2,1,0:T(8,128)(2,1)} %bitcast.98, bf16[2,512,8,128]{3,2,1,0:T(8,128)(2,1)S(1)} %bitcast.89), kind=kOutput, calls=%fused_computation.1 | convolution fusion | flops 1082130432 | bytes 12845056 | tf_op jit(solution)/shard_map/bthd,bshd->bhts/dot_general | solution.py:45
  39.6 3.2 %copy-done = bf16[2,8,512,512]{3,2,1,0:T(8,128)(2,1)} copy-done((bf16[2,8,512,512]{3,2,1,0:T(8,128)(2,1)}, bf16[2,8,512,512]{3,2,1,0:T(8,128)(2,1)S(1)}, u32[]{:S(2)}) %copy-start) | copy-done | bytes 8388632
  42.8 6.5 %fusion.6 = f32[2,8,512,128]{2,3,1,0:T(8,128)} fusion(bf16[2,8,512,512]{3,2,1,0:T(8,128)(2,1)S(1)} %select_convert_fusion.1, bf16[2,512,8,128]{3,2,1,0:T(8,128)(2,1)} %bitcast.94), kind=kOutput, calls=%fused_computation.23 | convolution fusion | flops 1073741824 | bytes 14680064 | tf_op jit(solution)/shard_map/bhts,bshe->bthe/dot_general | solution.py:49
  49.3 2.3 %all-to-all-done.1 = f32[32,1,4096]{2,1,0:T(1,128)} async-done(((f32[32,1,4096]{2,1,0:T(1,128)}), f32[32,1,4096]{2,1,0:T(1,128)}, u32[]{:S(2)}, u32[]{:S(2)}) %all-to-all-start.1) | async-done | bytes 524320 | tf_op jit(solution)/shard_map/all_to_all | solution.py:28
  51.6 1.2 fusion.5
  52.8 5.3 %multiply_reduce_fusion.1 = (f32[2,512]{1,0:T(2,128)S(1)}, f32[2,512,8,128]{1,3,2,0:T(8,128)}) fusion(bf16[2,8,128,128]{3,2,1,0:T(8,128)(2,1)S(1)} %fusion.5, bf16[2,512,8,128]{3,2,1,0:T(8,128)(2,1)S(1)} %bitcast.90, f32[2,8,512,128]{2,3,1,0:T(8,128)} %fusion.6), kind=kOutput, calls=%fused_computation.13 | convolution fusion | flops 271580160 | bytes 11014144 | tf_op jit(solution)/shard_map/bthd,bhde->bthe/dot_general | solution.py:53
  58.2 5.4 %copy.91 = f32[2,512,8,128]{3,2,1,0:T(8,128)} copy(f32[2,512,8,128]{1,3,2,0:T(8,128)} %get-tuple-element.9) | data formatting | bytes 8388608 | tf_op jit(solution)/shard_map/add | solution.py:53
  63.6 3.5 %multiply_reduce_fusion = f32[1024]{0:T(1024)S(1)} fusion(bf16[1024,1024]{1,0:T(8,128)(2,1)S(1)} %copy-done.9, f32[128,8,8,128]{3,2,1,0:T(8,128)} %bitcast.87, f32[1024]{0:T(1024)S(1)} %copy-done.17, f32[1024]{0:T(1024)S(1)} %bitcast.111), kind=kLoop, calls=%fused_computation.10 | loop fusion | flops 5241856 | bytes 6303744 | tf_op jit(solution)/shard_map/reduce_sum | solution.py:63
  67.2 2.6 %fusion.2 = (bf16[128,8,8,128]{3,1,2,0:T(8,128)(2,1)S(1)}, bf16[1024,1024]{1,0:T(8,128)(2,1)}) fusion(f32[128,8,8,128]{3,2,1,0:T(8,128)S(1)} %bitcast.88, bf16[1024,1024]{1,0:T(8,128)(2,1)S(1)} %copy-done.9, f32[1024]{0:T(1024)S(1)} %broadcast_multiply_fusion, f32[1024]{0:T(1024)S(1)} %copy-done.17, f32[1024]{0:T(1024)S(1)} %bitcast.112), kind=kLoop, calls=%fused_computation.14 | loop fusion | flops 9437184 | bytes 10498048
  69.8 1.9 %copy.124 = bf16[128,8,8,128]{3,2,1,0:T(8,128)(2,1)} copy(bf16[128,8,8,128]{3,1,2,0:T(8,128)(2,1)S(1)} %get-tuple-element.4) | data formatting | bytes 4194304
  71.7 3.2 %copy.100 = bf16[2,512,8,128]{1,3,2,0:T(8,128)(2,1)S(1)} copy(bf16[2,512,8,128]{3,2,1,0:T(8,128)(2,1)} %bitcast.101) | data formatting | bytes 4194304 | tf_op jit(solution)/shard_map/reshape | solution.py:65
  74.9 3.4 %fusion.23 = (f32[8,128,128]{1,2,0:T(8,128)}, f32[2,8,128,128]{2,3,1,0:T(8,128)S(1)}) fusion(bf16[2,512,8,128]{1,3,2,0:T(8,128)(2,1)S(1)} %copy.100, bf16[2,512,8,128]{3,2,1,0:T(8,128)(2,1)} %bitcast.91), kind=kOutput, calls=%fused_computation.47 | convolution fusion | flops 268566528 | bytes 5767168 | tf_op jit(solution)/shard_map/bthd,bthe->bhde/dot_general | solution.py:66
  78.3 5.9 %select_convert_fusion = bf16[2,8,512,512]{3,2,1,0:T(8,128)(2,1)} fusion(pred[512,512]{1,0:T(8,128)(4,1)S(1)} %iota_compare_fusion, bf16[2,512,8,128]{1,3,2,0:T(8,128)(2,1)S(1)} %copy.100, bf16[2,512,8,128]{3,2,1,0:T(8,128)(2,1)S(1)} %bitcast.95), kind=kOutput, calls=%fused_computation | convolution fusion | flops 1082130432 | bytes 12845056 | tf_op jit(solution)/shard_map/bthe,bshe->bhts/dot_general | solution.py:71
  84.1 2.1 %copy.102 = f32[8,128,128]{2,1,0:T(8,128)} copy(f32[8,128,128]{1,2,0:T(8,128)} %get-tuple-element.10) | data formatting | bytes 1048576 | tf_op jit(solution)/shard_map/reduce_sum | solution.py:69
  86.2 3.4 %all-to-all-start.2 = ((f32[32,1,4096]{2,1,0:T(1,128)}), f32[32,1,4096]{2,1,0:T(1,128)}, u32[]{:S(2)}, u32[]{:S(2)}) async-start(f32[32,1,4096]{2,1,0:T(1,128)} %bitcast.109), calls=%async_computation.2 | async-start | bytes 1048576 | tf_op jit(solution)/shard_map/all_to_all | solution.py:22
  89.7 6.4 %fusion.14 = f32[2,8,512,128]{3,2,1,0:T(8,128)S(1)} fusion(bf16[2,8,512,512]{3,2,1,0:T(8,128)(2,1)} %select_convert_fusion, bf16[2,512,8,128]{3,2,1,0:T(8,128)(2,1)} %bitcast.99), kind=kOutput, calls=%fused_computation.31 | convolution fusion | flops 1073741824 | bytes 14680064 | tf_op jit(solution)/shard_map/bhts,bshd->bthd/dot_general | solution.py:75
  96.1 2.3 %fusion.1 = bf16[2,512,8,128]{3,1,2,0:T(8,128)(2,1)} fusion(f32[2,8,512,128]{3,2,1,0:T(8,128)S(1)} %fusion.14, bf16[2,8,128,128]{3,2,1,0:T(8,128)(2,1)S(1)} %copy-done.12, bf16[2,512,8,128]{1,3,2,0:T(8,128)(2,1)S(1)} %copy.100), kind=kOutput, calls=%fused_computation.6 | convolution fusion | flops 270532608 | bytes 8912896 | tf_op jit(solution)/shard_map/bthe,bhde->bthd/dot_general | solution.py:83
  98.4 1.1 rev.14
  99.4 2.9 %copy.97 = bf16[2,512,8,128]{3,2,1,0:T(8,128)(2,1)S(1)} copy(bf16[2,512,8,128]{3,1,2,0:T(8,128)(2,1)} %fusion.1) | data formatting | bytes 4194304 | tf_op jit(solution)/shard_map/convert_element_type | solution.py:94
  102.4 1.9 %copy.175 = bf16[128,8,8,128]{3,1,2,0:T(8,128)(2,1)} copy(bf16[128,8,8,128]{3,2,1,0:T(8,128)(2,1)S(1)} %bitcast.102) | data formatting | bytes 4194304
  104.3 6.6 %fusion.25 = f32[2,8,128,512]{3,2,1,0:T(8,128)} fusion(bf16[2,512,8,128]{1,3,2,0:T(8,128)(2,1)S(1)} %copy.100, bf16[2,8,512,512]{3,2,1,0:T(8,128)(2,1)} %copy-done), kind=kOutput, calls=%fused_computation.49 | convolution fusion | flops 1073741824 | bytes 14680064 | tf_op jit(solution)/shard_map/bhts,bthe->bshe/dot_general | solution.py:81
  110.9 1.3 copy.176
  112.3 0.6 rev.12
  112.8 0.5 reduce_window_sum.36
  113.3 0.6 rev.13
  113.9 1.4 subtract_bitcast_fusion
  115.2 1.3 copy.104
  116.6 6.1 %all-to-all-start.3 = ((f32[32,1,4096]{2,1,0:T(1,128)}), f32[32,1,4096]{2,1,0:T(1,128)}, u32[]{:S(2)}, u32[]{:S(2)}) async-start(f32[32,1,4096]{2,1,0:T(1,128)} %copy.104), calls=%async_computation.3 | async-start | bytes 1048576 | tf_op jit(solution)/shard_map/all_to_all | solution.py:28
  122.7 2.4 %fusion.24 = f32[2,8,128,128]{2,3,1,0:T(8,128)} fusion(f32[2,8,128,128]{2,3,1,0:T(8,128)} %rev.14), kind=kOutput, calls=%fused_computation.48 | output fusion | flops 262144 | bytes 2097152 | tf_op jit(solution)/shard_map/jit(cumsum)/reduce_window_sum | solution.py:70
  125.1 7.9 %fusion.18 = f32[2,8,512,128]{3,2,1,0:T(8,128)} fusion(bf16[2,8,512,512]{3,2,1,0:T(8,128)(2,1)} %select_convert_fusion, bf16[2,512,8,128]{3,2,1,0:T(8,128)(2,1)S(1)} %bitcast.92), kind=kOutput, calls=%fused_computation.35 | convolution fusion | flops 1073741824 | bytes 14680064 | tf_op jit(solution)/shard_map/bhts,bthd->bshd/dot_general | solution.py:78
  132.9 5.7 %all-to-all-done.3 = f32[32,1,4096]{2,1,0:T(1,128)} async-done(((f32[32,1,4096]{2,1,0:T(1,128)}), f32[32,1,4096]{2,1,0:T(1,128)}, u32[]{:S(2)}, u32[]{:S(2)}) %all-to-all-start.3) | async-done | bytes 524320 | tf_op jit(solution)/shard_map/all_to_all | solution.py:28
  138.7 2.2 %copy.105 = f32[8,128,128]{1,2,0:T(8,128)} copy(f32[8,128,128]{2,1,0:T(8,128)} %bitcast.10) | data formatting | bytes 1048576 | tf_op jit(solution)/shard_map/add | solution.py:82
  140.8 1.5 add_convert_fusion.1
  142.4 0.8 copy-done.13
  143.2 4.4 %fusion.3 = bf16[2,512,8,128]{1,3,2,0:T(8,128)(2,1)} fusion(f32[2,8,128,512]{3,2,1,0:T(8,128)} %fusion.25, bf16[2,8,128,128]{2,3,1,0:T(8,128)(2,1)S(1)} %add_convert_fusion.1, bf16[2,512,8,128]{3,2,1,0:T(8,128)(2,1)S(1)} %bitcast.100), kind=kOutput, calls=%fused_computation.18 | convolution fusion | flops 270532608 | bytes 8912896 | tf_op jit(solution)/shard_map/bshd,bhde->bshe/dot_general | solution.py:89
  147.5 4.4 %copy.112 = bf16[2,512,8,128]{3,2,1,0:T(8,128)(2,1)} copy(bf16[2,512,8,128]{1,3,2,0:T(8,128)(2,1)} %fusion.3) | data formatting | bytes 4194304 | tf_op jit(solution)/shard_map/convert_element_type | solution.py:96
  152.0 2.9 %fusion = bf16[2,512,8,128]{3,1,2,0:T(8,128)(2,1)S(1)} fusion(f32[2,8,512,128]{3,2,1,0:T(8,128)} %fusion.18, bf16[2,8,128,128]{2,3,1,0:T(8,128)(2,1)S(1)} %copy-done.14, bf16[2,512,8,128]{3,2,1,0:T(8,128)(2,1)S(1)} %bitcast.96), kind=kOutput, calls=%fused_computation.4 | convolution fusion | flops 270532608 | bytes 8912896 | tf_op jit(solution)/shard_map/bshe,bhde->bshd/dot_general | solution.py:86
  154.9 1.4 copy.109
  156.5 3.3 %copy_bitcast_fusion = (bf16[1024,1024]{1,0:T(8,128)(2,1)}, bf16[1024,1024]{1,0:T(8,128)(2,1)}) fusion(bf16[128,8,8,128]{3,2,1,0:T(8,128)(2,1)S(1)} %bitcast.103, bf16[128,8,8,128]{3,2,1,0:T(8,128)(2,1)S(1)} %bitcast.104), kind=kLoop, calls=%fused_computation.15 | loop fusion | bytes 8388608 | tf_op jit(solution)/shard_map/reshape | solution.py:96
  (38 shorter events, 0.4 us)
Async XLA Ops:
  0.6 2.4 %copy-start.16 = (bf16[1024,1024]{1,0:T(8,128)(2,1)S(1)}, bf16[1024,1024]{1,0:T(8,128)(2,1)}, u32[]{:S(2)}) copy-start(bf16[1024,1024]{1,0:T(8,128)(2,1)} %param.7) | copy-start | bytes 6291460
  3.0 1.4 copy-start.7
  3.7 3.7 %copy-start.4 = (bf16[128,8,8,128]{3,2,1,0:T(8,128)(2,1)}, bf16[128,8,8,128]{3,2,1,0:T(8,128)(2,1)S(1)}, u32[]{:S(2)}) copy-start(bf16[128,8,8,128]{3,2,1,0:T(8,128)(2,1)S(1)} %copy.121) | copy-start | bytes 6291460
  7.3 23.6 %all-to-all-start = ((f32[32,1,4096]{2,1,0:T(1,128)}), f32[32,1,4096]{2,1,0:T(1,128)S(1)}, u32[]{:S(2)}, u32[]{:S(2)}) async-start(f32[32,1,4096]{2,1,0:T(1,128)} %bitcast.1), calls=%async_computation | async-start | bytes 1048576 | tf_op jit(solution)/shard_map/all_to_all | solution.py:22
  16.9 35.9 %copy-start.2 = (bf16[128,8,8,128]{3,2,1,0:T(8,128)(2,1)}, bf16[128,8,8,128]{3,2,1,0:T(8,128)(2,1)S(1)}, u32[]{:S(2)}) copy-start(bf16[128,8,8,128]{3,2,1,0:T(8,128)(2,1)S(1)} %copy.119) | copy-start | bytes 6291460
  32.0 19.6 %all-to-all-start.1 = ((f32[32,1,4096]{2,1,0:T(1,128)}), f32[32,1,4096]{2,1,0:T(1,128)}, u32[]{:S(2)}, u32[]{:S(2)}) async-start(f32[32,1,4096]{2,1,0:T(1,128)} %reduce-window_subtract_fusion.1), calls=%async_computation.1 | async-start | bytes 1048576 | tf_op jit(solution)/shard_map/all_to_all | solution.py:28
  39.6 3.2 %copy-start = (bf16[2,8,512,512]{3,2,1,0:T(8,128)(2,1)}, bf16[2,8,512,512]{3,2,1,0:T(8,128)(2,1)S(1)}, u32[]{:S(2)}) copy-start(bf16[2,8,512,512]{3,2,1,0:T(8,128)(2,1)S(1)} %select_convert_fusion.1) | copy-start | bytes 25165828
  42.8 8.8 %copy-start.15 = (f32[2,8,128,128]{3,2,1,0:T(8,128)S(1)}, f32[2,8,128,128]{3,2,1,0:T(8,128)}, u32[]{:S(2)}) copy-start(f32[2,8,128,128]{3,2,1,0:T(8,128)} %get-tuple-element.7) | copy-start | bytes 3145732
  52.8 5.3 %copy-start.11 = (bf16[2,8,128,128]{3,2,1,0:T(8,128)(2,1)}, bf16[2,8,128,128]{3,2,1,0:T(8,128)(2,1)S(1)}, u32[]{:S(2)}) copy-start(bf16[2,8,128,128]{3,2,1,0:T(8,128)(2,1)S(1)} %fusion.5) | copy-start | bytes 1572868
  58.2 5.4 %copy-start.9 = (bf16[1024,1024]{1,0:T(8,128)(2,1)S(1)}, bf16[1024,1024]{1,0:T(8,128)(2,1)}, u32[]{:S(2)}) copy-start(bf16[1024,1024]{1,0:T(8,128)(2,1)} %param.9) | copy-start | bytes 6291460
  58.2 5.4 %copy-start.17 = (f32[1024]{0:T(1024)S(1)}, f32[1024]{0:T(1024)}, u32[]{:S(2)}) copy-start(f32[1024]{0:T(1024)} %param.8) | copy-start | bytes 12292
  63.6 3.6 %copy-start.1 = (f32[2,512,8,128]{3,2,1,0:T(8,128)S(1)}, f32[2,512,8,128]{3,2,1,0:T(8,128)}, u32[]{:S(2)}) copy-start(f32[2,512,8,128]{3,2,1,0:T(8,128)} %copy.91) | copy-start | bytes 12582916
  74.9 3.4 %copy-start.5 = (bf16[128,8,8,128]{3,2,1,0:T(8,128)(2,1)S(1)}, bf16[128,8,8,128]{3,2,1,0:T(8,128)(2,1)}, u32[]{:S(2)}) copy-start(bf16[128,8,8,128]{3,2,1,0:T(8,128)(2,1)} %copy-done.4) | copy-start | bytes 6291460
  86.2 24.7 %all-to-all-start.2 = ((f32[32,1,4096]{2,1,0:T(1,128)}), f32[32,1,4096]{2,1,0:T(1,128)}, u32[]{:S(2)}, u32[]{:S(2)}) async-start(f32[32,1,4096]{2,1,0:T(1,128)} %bitcast.109), calls=%async_computation.2 | async-start | bytes 1048576 | tf_op jit(solution)/shard_map/all_to_all | solution.py:22
  89.7 6.4 %copy-start.12 = (bf16[2,8,128,128]{3,2,1,0:T(8,128)(2,1)S(1)}, bf16[2,8,128,128]{3,2,1,0:T(8,128)(2,1)}, u32[]{:S(2)}) copy-start(bf16[2,8,128,128]{3,2,1,0:T(8,128)(2,1)} %copy-done.11) | copy-start | bytes 1572868
  115.2 9.8 %copy-start.3 = (bf16[128,8,8,128]{3,2,1,0:T(8,128)(2,1)S(1)}, bf16[128,8,8,128]{3,2,1,0:T(8,128)(2,1)}, u32[]{:S(2)}) copy-start(bf16[128,8,8,128]{3,2,1,0:T(8,128)(2,1)} %copy-done.2) | copy-start | bytes 6291460
  116.6 22.1 %all-to-all-start.3 = ((f32[32,1,4096]{2,1,0:T(1,128)}), f32[32,1,4096]{2,1,0:T(1,128)}, u32[]{:S(2)}, u32[]{:S(2)}) async-start(f32[32,1,4096]{2,1,0:T(1,128)} %copy.104), calls=%async_computation.3 | async-start | bytes 1048576 | tf_op jit(solution)/shard_map/all_to_all | solution.py:28
  138.7 4.5 %copy-start.8 = (bf16[128,8,8,128]{3,2,1,0:T(8,128)(2,1)S(1)}, bf16[128,8,8,128]{3,2,1,0:T(8,128)(2,1)}, u32[]{:S(2)}) copy-start(bf16[128,8,8,128]{3,2,1,0:T(8,128)(2,1)} %copy-done.7) | copy-start | bytes 6291460
  142.4 0.8 copy-start.13
  147.5 4.4 %copy-start.6 = (bf16[128,8,8,128]{3,2,1,0:T(8,128)(2,1)S(1)}, bf16[128,8,8,128]{3,2,1,0:T(8,128)(2,1)}, u32[]{:S(2)}) copy-start(bf16[128,8,8,128]{3,2,1,0:T(8,128)(2,1)} %copy-done.4) | copy-start | bytes 6291460
  147.5 4.4 %copy-start.14 = (bf16[2,8,128,128]{2,3,1,0:T(8,128)(2,1)S(1)}, bf16[2,8,128,128]{2,3,1,0:T(8,128)(2,1)}, u32[]{:S(2)}) copy-start(bf16[2,8,128,128]{2,3,1,0:T(8,128)(2,1)} %copy-done.13) | copy-start | bytes 1572868
  154.9 1.6 copy-start.10
where the time goes:
time: 161 us; the launch traced here: 160 us
  matrix products  58.4 us (36%)
  local copies, waits for them, and re-layouts  43.9 us (27%)
  waiting for transfers between devices  21.9 us (14%)
  starting transfers between devices  20.4 us (13%)
  other arithmetic  14.3 us (9%)
    unnamed x43, local copies, waits for them, and re-layouts  15.5 us
    all_to_all x2, waiting for transfers between devices, carried(): lax.all_to_all(flat, ('grp', 'seq'), split_axis=0, concat_axis=0, tiled=T...  13.9 us
    all_to_all x2, starting transfers between devices, carried(): lax.all_to_all(flat, ('grp', 'seq'), split_axis=0, concat_axis=0, tiled=T...  10.8 us
    all_to_all x2, starting transfers between devices, carried(): lax.all_to_all(exclusive, ('grp', 'seq'), split_axis=0, concat_axis=0, ti...  9.66 us
    all_to_all x2, waiting for transfers between devices, carried(): lax.all_to_all(exclusive, ('grp', 'seq'), split_axis=0, concat_axis=0, ti...  7.99 us
    dot_general x1, matrix products, body(): jnp.einsum('bhts,bthd->bshd', grad_scores, query_blocks, preferred_elemen...  7.87 us
    dot_general x1, matrix products, body(): jnp.einsum('bhts,bthe->bshe', scores, grad_blocks, preferred_element_type...  6.58 us
    dot_general x1, matrix products, body(): jnp.einsum('bhts,bshe->bthe', scores, value_blocks, preferred_element_typ...  6.49 us
  transfers between devices with their start and end apart: 4, of which 3 were waited for; matrix products, arithmetic and copies ran while one was open for 28% of the time, Pallas kernels for 0%

commit v1 on v0

v1 whole, which is shorter than its diff:
```python
import functools

import jax
import jax.numpy as jnp
from jax import lax
from jax.experimental import pallas as pl
from jax.experimental.pallas import tpu as pltpu
from jax.sharding import PartitionSpec as P

H = 8
HD = 128
BLOCK = 512
EPSILON = 1e-06
AXES = ("grp", "seq")
LANES = 2
QUAD = 4
SHARE = H // (LANES * QUAD)
TILE = 256
F32 = jnp.float32
BF16 = jnp.bfloat16


def mm(a, b, ca, cb):
    return lax.dot_general(a, b, (((ca,), (cb,)), ((), ())), preferred_element_type=F32)


def place_of(head, where):
    unit = head // SHARE
    lane = (unit // QUAD) ^ where[0]
    slot = (unit % QUAD) ^ where[1]
    return slot, lane, head % SHARE


def put_piece(pieces, head, where, value):
    slot, lane, share = place_of(head, where)
    for i, piece in enumerate(pieces):

        @pl.when(slot == i)
        def _():
            piece[lane, share] = value


def piece_shapes():
    return [jax.ShapeDtypeStruct((LANES, SHARE, HD, HD), F32)] * QUAD


def whole(shape):
    return pl.BlockSpec(shape, lambda *_: (0,) * len(shape))


def totals_kernel(where, k_ref, v_ref, *outs):
    pieces, inside = outs[:QUAD], outs[QUAD]
    head = pl.program_id(0)
    blocks = k_ref.shape[0] // BLOCK
    total = None
    for b in range(blocks):
        rows = pl.ds(b * BLOCK, BLOCK)
        state = mm(k_ref[rows, :], v_ref[rows, :], 0, 0)
        inside[b, 0] = jnp.zeros_like(state) if total is None else total
        total = state if total is None else total + state
    put_piece(pieces, head, where, total)


def totals(where, keys, values):
    tokens = keys.shape[0]
    blocks = tokens // BLOCK
    column = pl.BlockSpec((tokens, HD), lambda h, *_: (0, h))
    piece = (LANES, SHARE, HD, HD)
    return pl.pallas_call(
        totals_kernel,
        out_shape=piece_shapes() + [jax.ShapeDtypeStruct((blocks, H, HD, HD), F32)],
        grid_spec=pltpu.PrefetchScalarGridSpec(
            num_scalar_prefetch=1,
            grid=(H,),
            in_specs=[column, column],
            out_specs=[whole(piece)] * QUAD
            + [pl.BlockSpec((blocks, 1, HD, HD), lambda h, *_: (0, h, 0, 0))],
        ),
        cost_estimate=pl.CostEstimate(
            flops=2 * tokens * H * HD * HD, bytes_accessed=4 * tokens * H * HD, transcendentals=0
        ),
        name="totals",
    )(where, keys, values)


def triangle(upper=False):
    row = lax.broadcasted_iota(jnp.int32, (TILE, TILE), 0)
    col = lax.broadcasted_iota(jnp.int32, (TILE, TILE), 1)
    return row <= col if upper else row >= col


def local_kernel(q_ref, k_ref, v_ref, out_ref):
    mask = triangle()
    for i in range(BLOCK // TILE):
        rows = pl.ds(i * TILE, TILE)
        q = q_ref[rows, :]
        diag = jnp.where(mask, mm(q, k_ref[rows, :], 1, 1), 0.0).astype(BF16)
        acc = mm(diag, v_ref[rows, :], 1, 0)
        if i:
            past = pl.ds(0, i * TILE)
            acc += mm(mm(q, k_ref[past, :], 1, 1).astype(BF16), v_ref[past, :], 1, 0)
        out_ref[rows, :] = acc


def local_part(queries, keys, values):
    tokens = queries.shape[0]
    blk = pl.BlockSpec((BLOCK, HD), lambda h, b: (b, h))
    return pl.pallas_call(
        local_kernel,
        out_shape=jax.ShapeDtypeStruct(queries.shape, F32),
        grid=(H, tokens // BLOCK),
        in_specs=[blk] * 3,
        out_specs=blk,
        cost_estimate=pl.CostEstimate(
            flops=4 * tokens * BLOCK * H * HD, bytes_accessed=10 * tokens * H * HD, transcendentals=0
        ),
        name="local",
    )(queries, keys, values)


def middle_kernel(where, local_ref, q_ref, dy_ref, gain_ref, *refs):
    carried, inside = refs[:QUAD], refs[QUAD]
    out_ref, grad_ref, prior_ref = refs[QUAD + 1 : QUAD + 4]
    pieces, later_ref = refs[QUAD + 4 : 2 * QUAD + 4], refs[2 * QUAD + 4]
    att_ref, run_ref = refs[2 * QUAD + 5 :]
    step = pl.program_id(0)
    steps = pl.num_programs(0)
    per_block = BLOCK // q_ref.shape[0]
    block = steps // per_block - 1 - step // per_block

    @pl.when(step % per_block == 0)
    def _():
        for head in range(H):
            slot, lane, share = place_of(head, where)
            for i in range(QUAD):

                @pl.when(slot == i)
                def _():
                    prior_ref[0, head] = (carried[i][lane, share] + inside[0, head]).astype(BF16)

    @pl.when(step == 0)
    def _():
        run_ref[...] = jnp.zeros_like(run_ref)

    @pl.when(step % per_block == 0)
    def _():
        later_ref[0] = run_ref[...]

    square = None
    for head in range(H):
        cols = pl.ds(head * HD, HD)
        att = local_ref[:, cols] + mm(q_ref[:, cols], prior_ref[0, head], 1, 0)
        att_ref[:, cols] = att
        square = att * att if square is None else square + att * att
    features = H * HD
    inverse = lax.rsqrt(jnp.sum(square, axis=1, keepdims=True) / features + EPSILON)
    cross = None
    for head in range(H):
        cols = pl.ds(head * HD, HD)
        unit = att_ref[:, cols] * inverse
        gain = gain_ref[:, cols]
        out_ref[:, cols] = (unit * gain).astype(BF16)
        term = dy_ref[:, cols].astype(F32) * gain * unit
        cross = term if cross is None else cross + term
    mean = jnp.sum(cross, axis=1, keepdims=True) / features
    for head in range(H):
        cols = pl.ds(head * HD, HD)
        unit = att_ref[:, cols] * inverse
        scaled = dy_ref[:, cols].astype(F32) * gain_ref[:, cols]
        grad = (inverse * (scaled - unit * mean)).astype(BF16)
        grad_ref[:, cols] = grad
        run_ref[head] += mm(q_ref[:, cols], grad, 0, 0)

    @pl.when(step == steps - 1)
    def _():
        for head in range(H):
            put_piece(pieces, head, where, run_ref[head])


def middle(where, local, queries, cotangent, gain, carried, inside):
    tokens, features = queries.shape
    rows = TILE
    per_block = BLOCK // rows
    blocks = tokens // BLOCK
    steps = tokens // rows

    def row_of(i, *_):
        return ((blocks - 1 - i // per_block) * per_block + i % per_block, 0)

    def block_of(i, *_):
        return (blocks - 1 - i // per_block, 0, 0, 0)

    tile = pl.BlockSpec((rows, features), row_of)
    state = pl.BlockSpec((1, H, HD, HD), block_of)
    piece = (LANES, SHARE, HD, HD)
    return pl.pallas_call(
        middle_kernel,
        out_shape=[
            jax.ShapeDtypeStruct((tokens, features), BF16),
            jax.ShapeDtypeStruct((tokens, features), BF16),
            jax.ShapeDtypeStruct((blocks, H, HD, HD), BF16),
        ]
        + piece_shapes()
        + [jax.ShapeDtypeStruct((blocks, H, HD, HD), F32)],
        grid_spec=pltpu.PrefetchScalarGridSpec(
            num_scalar_prefetch=1,
            grid=(steps,),
            in_specs=[tile, tile, tile, whole((1, features))] + [whole(piece)] * QUAD + [state],
            out_specs=[tile, tile, state] + [whole(piece)] * QUAD + [state],
            scratch_shapes=[pltpu.VMEM((rows, features), F32), pltpu.VMEM((H, HD, HD), F32)],
        ),
        cost_estimate=pl.CostEstimate(
            flops=4 * tokens * features * HD, bytes_accessed=12 * tokens * features, transcendentals=0
        ),
        name="middle",
    )(where, local, queries, cotangent, gain, *carried, inside)


def back_kernel(q_ref, k_ref, v_ref, g_ref, prior_ref, gq_ref, lk_ref, lv_ref):
    mask = triangle()
    turned = triangle(True)
    tiles = BLOCK // TILE
    prior = prior_ref[0, 0]
    for i in range(tiles):
        rows = pl.ds(i * TILE, TILE)
        q, k, v, g = q_ref[rows, :], k_ref[rows, :], v_ref[rows, :], g_ref[rows, :]
        acc = mm(g, prior, 1, 1)
        acc += mm(jnp.where(mask, mm(g, v, 1, 1), 0.0).astype(BF16), k, 1, 0)
        if i:
            past = pl.ds(0, i * TILE)
            acc += mm(mm(g, v_ref[past, :], 1, 1).astype(BF16), k_ref[past, :], 1, 0)
        gq_ref[rows, :] = acc.astype(BF16)
        lk = mm(jnp.where(turned, mm(v, g, 1, 1), 0.0).astype(BF16), q, 1, 0)
        lv = mm(jnp.where(turned, mm(k, q, 1, 1), 0.0).astype(BF16), g, 1, 0)
        if i < tiles - 1:
            rest = pl.ds((i + 1) * TILE, BLOCK - (i + 1) * TILE)
            lk += mm(mm(v, g_ref[rest, :], 1, 1).astype(BF16), q_ref[rest, :], 1, 0)
            lv += mm(mm(k, q_ref[rest, :], 1, 1).astype(BF16), g_ref[rest, :], 1, 0)
        lk_ref[rows, :] = lk
        lv_ref[rows, :] = lv


def back_part(queries, keys, values, grads, prior):
    tokens = queries.shape[0]
    blk = pl.BlockSpec((BLOCK, HD), lambda h, b: (b, h))
    return pl.pallas_call(
        back_kernel,
        out_shape=[
            jax.ShapeDtypeStruct(queries.shape, BF16),
            jax.ShapeDtypeStruct(queries.shape, F32),
            jax.ShapeDtypeStruct(queries.shape, F32),
        ],
        grid=(H, tokens // BLOCK),
        in_specs=[blk] * 4 + [pl.BlockSpec((1, 1, HD, HD), lambda h, b: (b, h, 0, 0))],
        out_specs=[blk] * 3,
        cost_estimate=pl.CostEstimate(
            flops=12 * tokens * BLOCK * H * HD, bytes_accessed=18 * tokens * H * HD, transcendentals=0
        ),
        name="back",
    )(queries, keys, values, grads, prior)


def final_kernel(where, lk_ref, lv_ref, k_ref, v_ref, *refs):
    carried, later = refs[:QUAD], refs[QUAD]
    gk_ref, gv_ref, state_ref = refs[QUAD + 1 :]
    head = pl.program_id(0)
    slot, lane, share = place_of(head, where)
    for i in range(QUAD):

        @pl.when(slot == i)
        def _():
            state_ref[...] = carried[i][lane, share]

    for b in range(k_ref.shape[0] // BLOCK):
        rows = pl.ds(b * BLOCK, BLOCK)
        state = (state_ref[...] + later[b, 0]).astype(BF16)
        gk_ref[rows, :] = (lk_ref[rows, :] + mm(v_ref[rows, :], state, 1, 1)).astype(BF16)
        gv_ref[rows, :] = (lv_ref[rows, :] + mm(k_ref[rows, :], state, 1, 0)).astype(BF16)


def final_part(where, local_k, local_v, keys, values, carried, later):
    tokens, features = keys.shape
    blocks = tokens // BLOCK
    column = pl.BlockSpec((tokens, HD), lambda h, *_: (0, h))
    piece = (LANES, SHARE, HD, HD)
    return pl.pallas_call(
        final_kernel,
        out_shape=[jax.ShapeDtypeStruct((tokens, features), BF16)] * 2,
        grid_spec=pltpu.PrefetchScalarGridSpec(
            num_scalar_prefetch=1,
            grid=(H,),
            in_specs=[column] * 4
            + [whole(piece)] * QUAD
            + [pl.BlockSpec((blocks, 1, HD, HD), lambda h, *_: (0, h, 0, 0))],
            out_specs=[column] * 2,
            scratch_shapes=[pltpu.VMEM((HD, HD), F32)],
        ),
        cost_estimate=pl.CostEstimate(
            flops=4 * tokens * features * HD, bytes_accessed=16 * tokens * features, transcendentals=0
        ),
        name="final",
    )(where, local_k, local_v, keys, values, *carried, later)


def moved(value, move):
    groups, shards = lax.axis_size("grp"), lax.axis_size("seq")
    pairs = []
    for g in range(groups):
        for s in range(shards):
            to_g, to_s = move(g, s)
            pairs.append((g * shards + s, to_g * shards + to_s))
    return lax.ppermute(value, AXES, pairs)


def carry(pieces, reverse):
    grp, seq = lax.axis_index("grp"), lax.axis_index("seq")
    lane, quad = grp % LANES, seq % QUAD
    row, far = grp // LANES, seq // QUAD
    row_count = lax.axis_size("grp") // LANES
    far_count = lax.axis_size("seq") // QUAD
    order = (3, 1, 2)

    def before(a, b):
        return a > b if reverse else a < b

    def swap_quad(o):
        return lambda g, s: (g, s ^ o)

    def swap_lane(g, s):
        return g ^ 1, s

    def shift(dr, df):
        return lambda g, s: (
            (g // LANES + dr) % row_count * LANES + g % LANES,
            (s // QUAD + df) % far_count * QUAD + s % QUAD,
        )

    held = [pieces[0]] + [None] * (QUAD - 1)
    for o in order:
        held[o] = moved(pieces[o], swap_quad(o))
    quad_sum = held[0] + held[1] + held[2] + held[3]
    mine, other = quad_sum[0], moved(quad_sum[1], swap_lane)
    pair, both = jnp.stack([mine, other]), mine + other
    shifts = [(dr, df) for dr in range(row_count) for df in range(far_count) if dr or df]
    shifts.sort(key=lambda shift_by: -sum(shift_by))
    came = [moved(both if dr else pair, shift(dr, df)) for dr, df in shifts]
    takes = lane == (0 if reverse else 1)
    sum_mine = jnp.where(takes, other, 0.0)
    sum_other = jnp.where(takes, 0.0, mine)
    for (dr, df), value in zip(shifts, came):
        if dr:
            value = jnp.where(before((row - dr) % row_count, row), value, 0.0)
            sum_mine, sum_other = sum_mine + value, sum_other + value
        else:
            near = before((far - df) % far_count, far)
            sum_mine += jnp.where(near, value[0], 0.0) + jnp.where(takes, value[1], 0.0)
            sum_other += jnp.where(near, value[1], 0.0) + jnp.where(takes, 0.0, value[0])
    base = jnp.stack([sum_mine, moved(sum_other, swap_lane)])
    back = []
    for o in range(QUAD):
        value = base
        for i in range(QUAD):
            if i != o:
                value = value + jnp.where(before(quad ^ i, quad ^ o), held[i], 0.0)
        back.append(value)
    result = [back[0]] + [None] * (QUAD - 1)
    for o in order:
        result[o] = moved(back[o], swap_quad(o))
    return result


def body(queries, key_rows, value_rows, norm_gain, cotangent):
    grp, seq = lax.axis_index("grp"), lax.axis_index("seq")
    where = jnp.stack([grp % LANES, seq % QUAD]).astype(jnp.int32)
    *pieces, inside = totals(where, key_rows, value_rows)
    local = local_part(queries, key_rows, value_rows)
    prior = carry(pieces, False)
    normed, grads, prior_half, *rest = middle(
        where, local, queries, cotangent, norm_gain[None, :], prior, inside
    )
    grad_pieces, later = rest[:QUAD], rest[QUAD]
    grad_q, local_k, local_v = back_part(queries, key_rows, value_rows, grads, prior_half)
    after = carry(grad_pieces, True)
    grad_k, grad_v = final_part(where, local_k, local_v, key_rows, value_rows, after, later)
    return normed, grad_q, grad_k, grad_v


def solution(mesh):
    rows = P(AXES, None)
    return jax.shard_map(
        body,
        mesh=mesh,
        in_specs=(rows, rows, rows, P(), rows),
        out_specs=(rows, rows, rows, rows),
        check_vma=False,
    )
```

time: 161 us -> 139 us (0.86)
  Pallas kernels: 0 us -> 65.1 us
  matrix products: 58.4 us -> 0 us
  local copies, waits for them, and re-layouts: 43.9 us -> 1.43 us
  waiting for transfers between devices: 21.9 us -> 41.9 us
  other arithmetic: 14.3 us -> 4.14 us
  starting transfers between devices: 20.4 us -> 24.5 us
    pallas_call x0 -> x5, Pallas kernels: none -> 65.1 us  [the longest x1 21.8 us: back_part(): pl.pallas_call(back_kernel, out_shape=[jax.ShapeDtypeStruct(queries.shape...]
    dot_general x12 -> x0, matrix products: 58.4 us -> none  [the longest x1 7.87 us: body(): jnp.einsum('bhts,bthd->bshd', grad_scores, query_blocks, preferred_elemen...]
    ppermute x0 -> x22, waiting for transfers between devices: none -> 41.9 us  [moved(): return lax.ppermute(value, AXES, pairs)]
    ppermute x0 -> x22, starting transfers between devices: none -> 24.5 us  [moved(): return lax.ppermute(value, AXES, pairs)]
    all_to_all x4 -> x0, waiting for transfers between devices: 21.9 us -> none  [the longest x2 13.9 us: carried(): lax.all_to_all(flat, ('grp', 'seq'), split_axis=0, concat_axis=0, tiled=T...]
    all_to_all x4 -> x0, starting transfers between devices: 20.4 us -> none  [the longest x2 10.8 us: carried(): lax.all_to_all(flat, ('grp', 'seq'), split_axis=0, concat_axis=0, tiled=T...]
    unnamed x43 -> x16, local copies, waits for them, and re-layouts: 15.5 us -> 1.41 us
    convert_element_type x3 -> x0, local copies, waits for them, and re-layouts: 8.73 us -> none  [the longest x1 4.43 us: body(): grad_v.astype(jnp.bfloat16).reshape(tokens, features)]
  transfers between devices with their start and end apart: 4 -> 22, of which waited for: 3 -> 16; matrix products, arithmetic and copies ran while one was open for 28% -> 1% of each run, Pallas kernels for 0% -> 27%
where the time goes in v1:
time: 139 us; the launch traced here: 138 us
  Pallas kernels  65.1 us (47%)
  waiting for transfers between devices  41.9 us (30%)
  starting transfers between devices  24.5 us (18%)
  other arithmetic  4.14 us (3%)
  local copies, waits for them, and re-layouts  1.43 us (1%)
    ppermute x22, waiting for transfers between devices, moved(): return lax.ppermute(value, AXES, pairs)  41.9 us
    ppermute x22, starting transfers between devices, moved(): return lax.ppermute(value, AXES, pairs)  24.5 us
    pallas_call x1, Pallas kernels, back_part(): pl.pallas_call(back_kernel, out_shape=[jax.ShapeDtypeStruct(queries.shape...  21.8 us
    pallas_call x1, Pallas kernels, local_part(): pl.pallas_call(local_kernel, out_shape=jax.ShapeDtypeStruct(queries.shape...  14.8 us
    pallas_call x1, Pallas kernels, final_part(): pl.pallas_call(final_kernel, out_shape=[jax.ShapeDtypeStruct((tokens, fea...  10.4 us
    pallas_call x1, Pallas kernels, middle(): pl.pallas_call(middle_kernel, out_shape=[jax.ShapeDtypeStruct((tokens, fe...  10.4 us
    pallas_call x1, Pallas kernels, totals(): pl.pallas_call(totals_kernel, out_shape=piece_shapes() + [jax.ShapeDtypeS...  7.73 us
  transfers between devices with their start and end apart: 22, of which 16 were waited for; matrix products, arithmetic and copies ran while one was open for 1% of the time, Pallas kernels for 27%

profile of v1, /device:TPU:0, one launch (start us, length us, event | category | flops | bytes accessed | tf_op | source)
XLA Modules:
  0.0 137.9 jit_solution(11744720802407835527)
XLA Ops:
  0.7 0.6 pad_add_fusion.where
  1.3 7.7 %totals.1 = (f32[2,1,128,128]{3,2,1,0:T(8,128)}, f32[2,1,128,128]{3,2,1,0:T(8,128)}, f32[2,1,128,128]{3,2,1,0:T(8,128)}, f32[2,1,128,128]{3,2,1,0:T(8,128)}, f32[2,8,128,128]{3,2,1,0:T(8,128)}) custom-call(s32[2]{0:T(128)} %pad_add_fusion.where, bf16[1024,1024]{1,0:T(8,128)(2,1)} %k_ref.7, bf16[1024,1024]{1,0:T(8,128)(2,1)} %v_ref.7), custom_call_target="tpu_custom_call" | custom-call | flops 268435456 | bytes 4194304 | tf_op jit(solution)/shard_map/totals/pallas_call | solution.py:69
  9.0 3.0 %collective-permute-start = (f32[2,1,128,128]{3,2,1,0:T(8,128)}, f32[2,1,128,128]{3,2,1,0:T(8,128)S(1)}, u32[]{:S(2)}, u32[]{:S(2)}) collective-permute-start(f32[2,1,128,128]{3,2,1,0:T(8,128)} %get-tuple-element.23), channel_id=1, source_target_pairs={{0,1},{1,0},{2,3},{3,2},{4,5},{5,4},{6,7},{7,6},{8,9},{9,8},{10,11... | collective-permute-start | bytes 393224 | tf_op jit(solution)/shard_map/ppermute | solution.py:312
  12.0 1.6 %collective-permute-start.1 = (f32[2,1,128,128]{3,2,1,0:T(8,128)}, f32[2,1,128,128]{3,2,1,0:T(8,128)S(1)}, u32[]{:S(2)}, u32[]{:S(2)}) collective-permute-start(f32[2,1,128,128]{3,2,1,0:T(8,128)} %get-tuple-element.24), channel_id=1, source_target_pairs={{0,2},{1,3},{2,0},{3,1},{4,6},{5,7},{6,4},{7,5},{8,10},{9,11},{10,... | collective-permute-start | bytes 393224 | tf_op jit(solution)/shard_map/ppermute | solution.py:312
  13.6 2.1 %collective-permute-done = f32[2,1,128,128]{3,2,1,0:T(8,128)S(1)} collective-permute-done((f32[2,1,128,128]{3,2,1,0:T(8,128)}, f32[2,1,128,128]{3,2,1,0:T(8,128)S(1)}, u32[]{:S(2)}, u32[]{:S(2)}) %collective-permute-start) | collective-permute-done | bytes 131104 | tf_op jit(solution)/shard_map/ppermute | solution.py:312
  15.7 2.9 %collective-permute-done.1 = f32[2,1,128,128]{3,2,1,0:T(8,128)S(1)} collective-permute-done((f32[2,1,128,128]{3,2,1,0:T(8,128)}, f32[2,1,128,128]{3,2,1,0:T(8,128)S(1)}, u32[]{:S(2)}, u32[]{:S(2)}) %collective-permute-start.1) | collective-permute-done | bytes 131104 | tf_op jit(solution)/shard_map/ppermute | solution.py:312
  18.5 1.2 collective-permute-done.2
  19.8 0.9 add_add_fusion.1
  20.7 0.1 collective-permute-start.3
  20.8 1.2 collective-permute-done.3
  22.0 2.8 %collective-permute-start.5 = (f32[2,1,128,128]{3,2,1,0:T(8,128)S(1)}, f32[2,1,128,128]{3,2,1,0:T(8,128)S(1)}, u32[]{:S(2)}, u32[]{:S(2)}) collective-permute-start(f32[2,1,128,128]{3,2,1,0:T(8,128)S(1)} %pad_maximum_fusion), channel_id=1, source_target_pairs={{0,4},{1,5},{2,6},{3,7},{4,0},{5,1},{6,2},{7,3},{8,12},{9,13},{10,... | collective-permute-start | bytes 393224 | tf_op jit(solution)/shard_map/ppermute | solution.py:312
  24.9 1.6 %collective-permute-start.6 = (f32[1,128,128]{2,1,0:T(8,128)S(1)}, f32[1,128,128]{2,1,0:T(8,128)S(1)}, u32[]{:S(2)}, u32[]{:S(2)}) collective-permute-start(f32[1,128,128]{2,1,0:T(8,128)S(1)} %bitcast_add_fusion.5), channel_id=1, source_target_pairs={{0,16},{1,17},{2,18},{3,19},{4,20},{5,21},{6,22},{7,23},{8,24},{9,... | collective-permute-start | bytes 196616 | tf_op jit(solution)/shard_map/ppermute | solution.py:312
  26.5 0.1 collective-permute-start.4
  26.6 2.6 %collective-permute-done.6 = f32[1,128,128]{2,1,0:T(8,128)S(1)} collective-permute-done((f32[1,128,128]{2,1,0:T(8,128)S(1)}, f32[1,128,128]{2,1,0:T(8,128)S(1)}, u32[]{:S(2)}, u32[]{:S(2)}) %collective-permute-start.6) | collective-permute-done | bytes 65568 | tf_op jit(solution)/shard_map/ppermute | solution.py:312
  29.2 6.1 %collective-permute-done.4 = f32[1,128,128]{2,1,0:T(8,128)S(1)} collective-permute-done((f32[1,128,128]{2,1,0:T(8,128)S(1)}, f32[1,128,128]{2,1,0:T(8,128)S(1)}, u32[]{:S(2)}, u32[]{:S(2)}) %collective-permute-start.4) | collective-permute-done | bytes 65568 | tf_op jit(solution)/shard_map/ppermute | solution.py:312
  35.5 14.8 %local.1.local_ref = f32[1024,1024]{1,0:T(8,128)} custom-call(bf16[1024,1024]{1,0:T(8,128)(2,1)} %q_ref.5, bf16[1024,1024]{1,0:T(8,128)(2,1)} %k_ref.7, bf16[1024,1024]{1,0:T(8,128)(2,1)} %v_ref.7), custom_call_target="tpu_custom_call" | custom-call | flops 2147483648 | bytes 10485760 | tf_op jit(solution)/shard_map/local/pallas_call | solution.py:108
  50.3 0.1 select_add_fusion.4
  50.4 0.7 collective-permute-start.10
  51.1 2.3 %collective-permute-start.9 = (f32[2,1,128,128]{3,2,1,0:T(8,128)S(1)}, f32[2,1,128,128]{3,2,1,0:T(8,128)S(1)}, u32[]{:S(2)}, u32[]{:S(2)}) collective-permute-start(f32[2,1,128,128]{3,2,1,0:T(8,128)S(1)} %get-tuple-element.44), channel_id=1, source_target_pairs={{0,2},{1,3},{2,0},{3,1},{4,6},{5,7},{6,4},{7,5},{8,10},{9,11},{10,... | collective-permute-start | bytes 393224 | tf_op jit(solution)/shard_map/ppermute | solution.py:312
  53.4 0.6 collective-permute-start.8
  53.9 0.7 select_add_fusion.7.refs_0_
  54.6 3.1 %collective-permute-done.10.refs_3_ = f32[2,1,128,128]{3,2,1,0:T(8,128)S(1)} collective-permute-done((f32[2,1,128,128]{3,2,1,0:T(8,128)S(1)}, f32[2,1,128,128]{3,2,1,0:T(8,128)S(1)}, u32[]{:S(2)}, u32[]{:S(2)}) %collective-permute-start.10) | collective-permute-done | bytes 131104 | tf_op jit(solution)/shard_map/ppermute | solution.py:312
  57.7 2.4 %collective-permute-done.9.refs_2_ = f32[2,1,128,128]{3,2,1,0:T(8,128)S(1)} collective-permute-done((f32[2,1,128,128]{3,2,1,0:T(8,128)S(1)}, f32[2,1,128,128]{3,2,1,0:T(8,128)S(1)}, u32[]{:S(2)}, u32[]{:S(2)}) %collective-permute-start.9) | collective-permute-done | bytes 131104 | tf_op jit(solution)/shard_map/ppermute | solution.py:312
  60.1 0.6 copy-done.3
  60.7 0.1 copy-done.5
  60.8 10.4 %middle.1 = (bf16[1024,1024]{1,0:T(8,128)(2,1)}, bf16[1024,1024]{1,0:T(8,128)(2,1)}, bf16[2,8,128,128]{3,2,1,0:T(8,128)(2,1)}, f32[2,1,128,128]{3,2,1,0:T(8,128)...) custom-call(s32[2]{0:T(128)} %pad_add_fusion.where, ...), custom_call_target="tpu_custom_call" | custom-call | flops 536870912 | bytes 12582912 | tf_op jit(solution)/shard_map/middle/pallas_call | solution.py:196
  71.1 1.4 %collective-permute-start.11 = (f32[2,1,128,128]{3,2,1,0:T(8,128)}, f32[2,1,128,128]{3,2,1,0:T(8,128)S(1)}, u32[]{:S(2)}, u32[]{:S(2)}) collective-permute-start(f32[2,1,128,128]{3,2,1,0:T(8,128)} %get-tuple-element.34), channel_id=1, source_target_pairs={{0,1},{1,0},{2,3},{3,2},{4,5},{5,4},{6,7},{7,6},{8,9},{9,8},{10,11... | collective-permute-start | bytes 393224 | tf_op jit(solution)/shard_map/ppermute | solution.py:312
  72.5 2.1 %collective-permute-start.13 = (f32[2,1,128,128]{3,2,1,0:T(8,128)}, f32[2,1,128,128]{3,2,1,0:T(8,128)S(1)}, u32[]{:S(2)}, u32[]{:S(2)}) collective-permute-start(f32[2,1,128,128]{3,2,1,0:T(8,128)} %get-tuple-element.36), channel_id=1, source_target_pairs={{0,3},{1,2},{2,1},{3,0},{4,7},{5,6},{6,5},{7,4},{8,11},{9,10},{10,... | collective-permute-start | bytes 393224 | tf_op jit(solution)/shard_map/ppermute | solution.py:312
  74.7 2.2 %collective-permute-done.11 = f32[2,1,128,128]{3,2,1,0:T(8,128)S(1)} collective-permute-done((f32[2,1,128,128]{3,2,1,0:T(8,128)}, f32[2,1,128,128]{3,2,1,0:T(8,128)S(1)}, u32[]{:S(2)}, u32[]{:S(2)}) %collective-permute-start.11) | collective-permute-done | bytes 131104 | tf_op jit(solution)/shard_map/ppermute | solution.py:312
  76.9 2.2 %collective-permute-done.12 = f32[2,1,128,128]{3,2,1,0:T(8,128)S(1)} collective-permute-done((f32[2,1,128,128]{3,2,1,0:T(8,128)}, f32[2,1,128,128]{3,2,1,0:T(8,128)S(1)}, u32[]{:S(2)}, u32[]{:S(2)}) %collective-permute-start.12) | collective-permute-done | bytes 131104 | tf_op jit(solution)/shard_map/ppermute | solution.py:312
  79.1 1.6 %collective-permute-done.13 = f32[2,1,128,128]{3,2,1,0:T(8,128)S(1)} collective-permute-done((f32[2,1,128,128]{3,2,1,0:T(8,128)}, f32[2,1,128,128]{3,2,1,0:T(8,128)S(1)}, u32[]{:S(2)}, u32[]{:S(2)}) %collective-permute-start.13) | collective-permute-done | bytes 131104 | tf_op jit(solution)/shard_map/ppermute | solution.py:312
  80.7 0.9 add_add_fusion
  81.7 1.2 collective-permute-done.14
  83.0 2.4 %collective-permute-start.16 = (f32[2,1,128,128]{3,2,1,0:T(8,128)S(1)}, f32[2,1,128,128]{3,2,1,0:T(8,128)S(1)}, u32[]{:S(2)}, u32[]{:S(2)}) collective-permute-start(f32[2,1,128,128]{3,2,1,0:T(8,128)S(1)} %pad_maximum_fusion.2), channel_id=1, source_target_pairs={{0,4},{1,5},{2,6},{3,7},{4,0},{5,1},{6,2},{7,3},{8,12},{9,13},{10,... | collective-permute-start | bytes 393224 | tf_op jit(solution)/shard_map/ppermute | solution.py:312
  85.4 0.6 collective-permute-start.17
  86.0 1.5 %collective-permute-start.15 = (f32[1,128,128]{2,1,0:T(8,128)S(1)}, f32[1,128,128]{2,1,0:T(8,128)S(1)}, u32[]{:S(2)}, u32[]{:S(2)}) collective-permute-start(f32[1,128,128]{2,1,0:T(8,128)S(1)} %bitcast_add_fusion.2), channel_id=1, source_target_pairs={{0,20},{1,21},{2,22},{3,23},{4,16},{5,17},{6,18},{7,19},{8,28},{9,... | collective-permute-start | bytes 196616 | tf_op jit(solution)/shard_map/ppermute | solution.py:312
  87.5 2.2 %collective-permute-done.17 = f32[1,128,128]{2,1,0:T(8,128)S(1)} collective-permute-done((f32[1,128,128]{2,1,0:T(8,128)S(1)}, f32[1,128,128]{2,1,0:T(8,128)S(1)}, u32[]{:S(2)}, u32[]{:S(2)}) %collective-permute-start.17) | collective-permute-done | bytes 65568 | tf_op jit(solution)/shard_map/ppermute | solution.py:312
  89.7 5.3 %collective-permute-done.15 = f32[1,128,128]{2,1,0:T(8,128)S(1)} collective-permute-done((f32[1,128,128]{2,1,0:T(8,128)S(1)}, f32[1,128,128]{2,1,0:T(8,128)S(1)}, u32[]{:S(2)}, u32[]{:S(2)}) %collective-permute-start.15) | collective-permute-done | bytes 65568 | tf_op jit(solution)/shard_map/ppermute | solution.py:312
  95.2 21.8 %back.1 = (bf16[1024,1024]{1,0:T(8,128)(2,1)}, f32[1024,1024]{1,0:T(8,128)}, f32[1024,1024]{1,0:T(8,128)}) custom-call(bf16[1024,1024]{1,0:T(8,128)(2,1)} %q_ref.5, bf16[1024,1024]{1,0:T(8,128)(2,1)} %k_ref.7, bf16[1024,1024]{1,0:T(8,128)(2,1)} %v_ref.7, bf16[1024,1024]{1,0:T(8,128)(2,1)} %get-tuple-element.28.g_ref, ...), custom_call_target="tpu_custom_call" | custom-call | flops 6442450944 | bytes 18874368 | tf_op jit(solution)/shard_map/back/pallas_call | solution.py:246
  117.0 0.1 select_add_fusion
  117.1 1.5 %collective-permute-start.21 = (f32[2,1,128,128]{3,2,1,0:T(8,128)S(1)}, f32[2,1,128,128]{3,2,1,0:T(8,128)S(1)}, u32[]{:S(2)}, u32[]{:S(2)}) collective-permute-start(f32[2,1,128,128]{3,2,1,0:T(8,128)S(1)} %get-tuple-element.40), channel_id=1, source_target_pairs={{0,3},{1,2},{2,1},{3,0},{4,7},{5,6},{6,5},{7,4},{8,11},{9,10},{10,... | collective-permute-start | bytes 393224 | tf_op jit(solution)/shard_map/ppermute | solution.py:312
  118.6 1.6 %collective-permute-start.20 = (f32[2,1,128,128]{3,2,1,0:T(8,128)S(1)}, f32[2,1,128,128]{3,2,1,0:T(8,128)S(1)}, u32[]{:S(2)}, u32[]{:S(2)}) collective-permute-start(f32[2,1,128,128]{3,2,1,0:T(8,128)S(1)} %get-tuple-element.41), channel_id=1, source_target_pairs={{0,2},{1,3},{2,0},{3,1},{4,6},{5,7},{6,4},{7,5},{8,10},{9,11},{10,... | collective-permute-start | bytes 393224 | tf_op jit(solution)/shard_map/ppermute | solution.py:312
  120.1 0.5 collective-permute-start.19
  120.6 0.7 select_add_fusion.3.refs_0_
  121.3 3.1 %collective-permute-done.21.refs_3_ = f32[2,1,128,128]{3,2,1,0:T(8,128)S(1)} collective-permute-done((f32[2,1,128,128]{3,2,1,0:T(8,128)S(1)}, f32[2,1,128,128]{3,2,1,0:T(8,128)S(1)}, u32[]{:S(2)}, u32[]{:S(2)}) %collective-permute-start.21) | collective-permute-done | bytes 131104 | tf_op jit(solution)/shard_map/ppermute | solution.py:312
  124.4 2.4 %collective-permute-done.20.refs_2_ = f32[2,1,128,128]{3,2,1,0:T(8,128)S(1)} collective-permute-done((f32[2,1,128,128]{3,2,1,0:T(8,128)S(1)}, f32[2,1,128,128]{3,2,1,0:T(8,128)S(1)}, u32[]{:S(2)}, u32[]{:S(2)}) %collective-permute-start.20) | collective-permute-done | bytes 131104 | tf_op jit(solution)/shard_map/ppermute | solution.py:312
  126.8 0.6 copy-done.6
  127.5 10.4 %final.1 = (bf16[1024,1024]{1,0:T(8,128)(2,1)}, bf16[1024,1024]{1,0:T(8,128)(2,1)}) custom-call(s32[2]{0:T(128)} %pad_add_fusion.where, f32[1024,1024]{1,0:T(8,128)} %get-tuple-element.31.lk_ref, f32[1024,1024]{1,0:T(8,128)} %get-tuple-element.32.lv_ref, bf16[1024,1024]{1,0:T(8,128)(2,1)} %k_ref.7, bf16[1024,1024]{1,0:T(8,128)(2,1)} %v_ref.7, ...), custom_call_target="tpu_custom_call" | custom-call | flops 536870912 | bytes 16777216 | tf_op jit(solution)/shard_map/final/pallas_call | solution.py:286
  (32 shorter events, 0.4 us)
Async XLA Ops:
  9.0 6.7 %collective-permute-start = (f32[2,1,128,128]{3,2,1,0:T(8,128)}, f32[2,1,128,128]{3,2,1,0:T(8,128)S(1)}, u32[]{:S(2)}, u32[]{:S(2)}) collective-permute-start(f32[2,1,128,128]{3,2,1,0:T(8,128)} %get-tuple-element.23), channel_id=1, source_target_pairs={{0,1},{1,0},{2,3},{3,2},{4,5},{5,4},{6,7},{7,6},{8,9},{9,8},{10,11... | collective-permute-start | bytes 393224 | tf_op jit(solution)/shard_map/ppermute | solution.py:312
  12.0 6.6 %collective-permute-start.1 = (f32[2,1,128,128]{3,2,1,0:T(8,128)}, f32[2,1,128,128]{3,2,1,0:T(8,128)S(1)}, u32[]{:S(2)}, u32[]{:S(2)}) collective-permute-start(f32[2,1,128,128]{3,2,1,0:T(8,128)} %get-tuple-element.24), channel_id=1, source_target_pairs={{0,2},{1,3},{2,0},{3,1},{4,6},{5,7},{6,4},{7,5},{8,10},{9,11},{10,... | collective-permute-start | bytes 393224 | tf_op jit(solution)/shard_map/ppermute | solution.py:312
  13.5 6.2 %collective-permute-start.2 = (f32[2,1,128,128]{3,2,1,0:T(8,128)}, f32[2,1,128,128]{3,2,1,0:T(8,128)S(1)}, u32[]{:S(2)}, u32[]{:S(2)}) collective-permute-start(f32[2,1,128,128]{3,2,1,0:T(8,128)} %get-tuple-element.25), channel_id=1, source_target_pairs={{0,3},{1,2},{2,1},{3,0},{4,7},{5,6},{6,5},{7,4},{8,11},{9,10},{10,... | collective-permute-start | bytes 393224 | tf_op jit(solution)/shard_map/ppermute | solution.py:312
  20.7 1.3 collective-permute-start.3
  22.0 13.3 %collective-permute-start.5 = (f32[2,1,128,128]{3,2,1,0:T(8,128)S(1)}, f32[2,1,128,128]{3,2,1,0:T(8,128)S(1)}, u32[]{:S(2)}, u32[]{:S(2)}) collective-permute-start(f32[2,1,128,128]{3,2,1,0:T(8,128)S(1)} %pad_maximum_fusion), channel_id=1, source_target_pairs={{0,4},{1,5},{2,6},{3,7},{4,0},{5,1},{6,2},{7,3},{8,12},{9,13},{10,... | collective-permute-start | bytes 393224 | tf_op jit(solution)/shard_map/ppermute | solution.py:312
  24.9 4.3 %collective-permute-start.6 = (f32[1,128,128]{2,1,0:T(8,128)S(1)}, f32[1,128,128]{2,1,0:T(8,128)S(1)}, u32[]{:S(2)}, u32[]{:S(2)}) collective-permute-start(f32[1,128,128]{2,1,0:T(8,128)S(1)} %bitcast_add_fusion.5), channel_id=1, source_target_pairs={{0,16},{1,17},{2,18},{3,19},{4,20},{5,21},{6,22},{7,23},{8,24},{9,... | collective-permute-start | bytes 196616 | tf_op jit(solution)/shard_map/ppermute | solution.py:312
  26.5 8.8 %collective-permute-start.4 = (f32[1,128,128]{2,1,0:T(8,128)S(1)}, f32[1,128,128]{2,1,0:T(8,128)S(1)}, u32[]{:S(2)}, u32[]{:S(2)}) collective-permute-start(f32[1,128,128]{2,1,0:T(8,128)S(1)} %bitcast_add_fusion.5), channel_id=1, source_target_pairs={{0,20},{1,21},{2,22},{3,23},{4,16},{5,17},{6,18},{7,19},{8,28},{9,... | collective-permute-start | bytes 196616 | tf_op jit(solution)/shard_map/ppermute | solution.py:312
  35.4 14.9 %copy-start = (f32[2,1,128,128]{3,2,1,0:T(8,128)S(1)}, f32[2,1,128,128]{3,2,1,0:T(8,128)}, u32[]{:S(2)}) copy-start(f32[2,1,128,128]{3,2,1,0:T(8,128)} %get-tuple-element.22) | copy-start | bytes 393220
  35.4 14.9 %collective-permute-start.7 = (f32[1,128,128]{2,1,0:T(8,128)S(1)}, f32[1,128,128]{2,1,0:T(8,128)S(1)}, u32[]{:S(2)}, u32[]{:S(2)}) collective-permute-start(f32[1,128,128]{2,1,0:T(8,128)S(1)} %get-tuple-element.49), channel_id=1, source_target_pairs={{0,8},{1,9},{2,10},{3,11},{4,12},{5,13},{6,14},{7,15},{8,0},{9,1},... | collective-permute-start | bytes 196616 | tf_op jit(solution)/shard_map/ppermute | solution.py:312
  50.4 7.3 %collective-permute-start.10 = (f32[2,1,128,128]{3,2,1,0:T(8,128)S(1)}, f32[2,1,128,128]{3,2,1,0:T(8,128)S(1)}, u32[]{:S(2)}, u32[]{:S(2)}) collective-permute-start(f32[2,1,128,128]{3,2,1,0:T(8,128)S(1)} %get-tuple-element.43), channel_id=1, source_target_pairs={{0,3},{1,2},{2,1},{3,0},{4,7},{5,6},{6,5},{7,4},{8,11},{9,10},{10,... | collective-permute-start | bytes 393224 | tf_op jit(solution)/shard_map/ppermute | solution.py:312
  51.1 9.0 %collective-permute-start.9 = (f32[2,1,128,128]{3,2,1,0:T(8,128)S(1)}, f32[2,1,128,128]{3,2,1,0:T(8,128)S(1)}, u32[]{:S(2)}, u32[]{:S(2)}) collective-permute-start(f32[2,1,128,128]{3,2,1,0:T(8,128)S(1)} %get-tuple-element.44), channel_id=1, source_target_pairs={{0,2},{1,3},{2,0},{3,1},{4,6},{5,7},{6,4},{7,5},{8,10},{9,11},{10,... | collective-permute-start | bytes 393224 | tf_op jit(solution)/shard_map/ppermute | solution.py:312
  53.4 6.7 %collective-permute-start.8 = (f32[2,1,128,128]{3,2,1,0:T(8,128)S(1)}, f32[2,1,128,128]{3,2,1,0:T(8,128)S(1)}, u32[]{:S(2)}, u32[]{:S(2)}) collective-permute-start(f32[2,1,128,128]{3,2,1,0:T(8,128)S(1)} %get-tuple-element.45), channel_id=1, source_target_pairs={{0,1},{1,0},{2,3},{3,2},{4,5},{5,4},{6,7},{7,6},{8,9},{9,8},{10,11... | collective-permute-start | bytes 393224 | tf_op jit(solution)/shard_map/ppermute | solution.py:312
  57.7 2.4 %copy-start.2 = (f32[2,1,128,128]{3,2,1,0:T(8,128)}, f32[2,1,128,128]{3,2,1,0:T(8,128)S(1)}, u32[]{:S(2)}) copy-start(f32[2,1,128,128]{3,2,1,0:T(8,128)S(1)} %collective-permute-done.10.refs_3_) | copy-start | bytes 393220
  60.0 0.7 copy-start.3
  60.1 0.7 copy-start.5
  71.1 5.7 %collective-permute-start.11 = (f32[2,1,128,128]{3,2,1,0:T(8,128)}, f32[2,1,128,128]{3,2,1,0:T(8,128)S(1)}, u32[]{:S(2)}, u32[]{:S(2)}) collective-permute-start(f32[2,1,128,128]{3,2,1,0:T(8,128)} %get-tuple-element.34), channel_id=1, source_target_pairs={{0,1},{1,0},{2,3},{3,2},{4,5},{5,4},{6,7},{7,6},{8,9},{9,8},{10,11... | collective-permute-start | bytes 393224 | tf_op jit(solution)/shard_map/ppermute | solution.py:312
  72.5 6.6 %collective-permute-start.12 = (f32[2,1,128,128]{3,2,1,0:T(8,128)}, f32[2,1,128,128]{3,2,1,0:T(8,128)S(1)}, u32[]{:S(2)}, u32[]{:S(2)}) collective-permute-start(f32[2,1,128,128]{3,2,1,0:T(8,128)} %get-tuple-element.35), channel_id=1, source_target_pairs={{0,2},{1,3},{2,0},{3,1},{4,6},{5,7},{6,4},{7,5},{8,10},{9,11},{10,... | collective-permute-start | bytes 393224 | tf_op jit(solution)/shard_map/ppermute | solution.py:312
  72.5 8.1 %collective-permute-start.13 = (f32[2,1,128,128]{3,2,1,0:T(8,128)}, f32[2,1,128,128]{3,2,1,0:T(8,128)S(1)}, u32[]{:S(2)}, u32[]{:S(2)}) collective-permute-start(f32[2,1,128,128]{3,2,1,0:T(8,128)} %get-tuple-element.36), channel_id=1, source_target_pairs={{0,3},{1,2},{2,1},{3,0},{4,7},{5,6},{6,5},{7,4},{8,11},{9,10},{10,... | collective-permute-start | bytes 393224 | tf_op jit(solution)/shard_map/ppermute | solution.py:312
  81.6 1.3 collective-permute-start.14
  83.0 12.0 %collective-permute-start.16 = (f32[2,1,128,128]{3,2,1,0:T(8,128)S(1)}, f32[2,1,128,128]{3,2,1,0:T(8,128)S(1)}, u32[]{:S(2)}, u32[]{:S(2)}) collective-permute-start(f32[2,1,128,128]{3,2,1,0:T(8,128)S(1)} %pad_maximum_fusion.2), channel_id=1, source_target_pairs={{0,4},{1,5},{2,6},{3,7},{4,0},{5,1},{6,2},{7,3},{8,12},{9,13},{10,... | collective-permute-start | bytes 393224 | tf_op jit(solution)/shard_map/ppermute | solution.py:312
  85.4 4.3 %collective-permute-start.17 = (f32[1,128,128]{2,1,0:T(8,128)S(1)}, f32[1,128,128]{2,1,0:T(8,128)S(1)}, u32[]{:S(2)}, u32[]{:S(2)}) collective-permute-start(f32[1,128,128]{2,1,0:T(8,128)S(1)} %bitcast_add_fusion.2), channel_id=1, source_target_pairs={{0,16},{1,17},{2,18},{3,19},{4,20},{5,21},{6,22},{7,23},{8,24},{9,... | collective-permute-start | bytes 196616 | tf_op jit(solution)/shard_map/ppermute | solution.py:312
  86.0 9.0 %collective-permute-start.15 = (f32[1,128,128]{2,1,0:T(8,128)S(1)}, f32[1,128,128]{2,1,0:T(8,128)S(1)}, u32[]{:S(2)}, u32[]{:S(2)}) collective-permute-start(f32[1,128,128]{2,1,0:T(8,128)S(1)} %bitcast_add_fusion.2), channel_id=1, source_target_pairs={{0,20},{1,21},{2,22},{3,23},{4,16},{5,17},{6,18},{7,19},{8,28},{9,... | collective-permute-start | bytes 196616 | tf_op jit(solution)/shard_map/ppermute | solution.py:312
  95.1 21.9 %collective-permute-start.18 = (f32[1,128,128]{2,1,0:T(8,128)S(1)}, f32[1,128,128]{2,1,0:T(8,128)S(1)}, u32[]{:S(2)}, u32[]{:S(2)}) collective-permute-start(f32[1,128,128]{2,1,0:T(8,128)S(1)} %get-tuple-element.47), channel_id=1, source_target_pairs={{0,8},{1,9},{2,10},{3,11},{4,12},{5,13},{6,14},{7,15},{8,0},{9,1},... | collective-permute-start | bytes 196616 | tf_op jit(solution)/shard_map/ppermute | solution.py:312
  95.1 21.8 %copy-start.1 = (f32[2,1,128,128]{3,2,1,0:T(8,128)S(1)}, f32[2,1,128,128]{3,2,1,0:T(8,128)}, u32[]{:S(2)}) copy-start(f32[2,1,128,128]{3,2,1,0:T(8,128)} %get-tuple-element.33) | copy-start | bytes 393220
  117.1 7.3 %collective-permute-start.21 = (f32[2,1,128,128]{3,2,1,0:T(8,128)S(1)}, f32[2,1,128,128]{3,2,1,0:T(8,128)S(1)}, u32[]{:S(2)}, u32[]{:S(2)}) collective-permute-start(f32[2,1,128,128]{3,2,1,0:T(8,128)S(1)} %get-tuple-element.40), channel_id=1, source_target_pairs={{0,3},{1,2},{2,1},{3,0},{4,7},{5,6},{6,5},{7,4},{8,11},{9,10},{10,... | collective-permute-start | bytes 393224 | tf_op jit(solution)/shard_map/ppermute | solution.py:312
  118.6 8.3 %collective-permute-start.20 = (f32[2,1,128,128]{3,2,1,0:T(8,128)S(1)}, f32[2,1,128,128]{3,2,1,0:T(8,128)S(1)}, u32[]{:S(2)}, u32[]{:S(2)}) collective-permute-start(f32[2,1,128,128]{3,2,1,0:T(8,128)S(1)} %get-tuple-element.41), channel_id=1, source_target_pairs={{0,2},{1,3},{2,0},{3,1},{4,6},{5,7},{6,4},{7,5},{8,10},{9,11},{10,... | collective-permute-start | bytes 393224 | tf_op jit(solution)/shard_map/ppermute | solution.py:312
  120.1 6.7 %collective-permute-start.19 = (f32[2,1,128,128]{3,2,1,0:T(8,128)S(1)}, f32[2,1,128,128]{3,2,1,0:T(8,128)S(1)}, u32[]{:S(2)}, u32[]{:S(2)}) collective-permute-start(f32[2,1,128,128]{3,2,1,0:T(8,128)S(1)} %get-tuple-element.42), channel_id=1, source_target_pairs={{0,1},{1,0},{2,3},{3,2},{4,5},{5,4},{6,7},{7,6},{8,9},{9,8},{10,11... | collective-permute-start | bytes 393224 | tf_op jit(solution)/shard_map/ppermute | solution.py:312
  124.4 2.4 %copy-start.4 = (f32[2,1,128,128]{3,2,1,0:T(8,128)}, f32[2,1,128,128]{3,2,1,0:T(8,128)S(1)}, u32[]{:S(2)}) copy-start(f32[2,1,128,128]{3,2,1,0:T(8,128)S(1)} %collective-permute-done.21.refs_3_) | copy-start | bytes 393220
  126.8 0.7 copy-start.6
  126.8 0.7 copy-start.7

commit v2 on v0

v2 whole, which is shorter than its diff:
```python
import functools

import jax
import jax.numpy as jnp
from jax import lax
from jax.experimental import pallas as pl
from jax.experimental.pallas import tpu as pltpu
from jax.sharding import PartitionSpec as P


H = 8
HD = 128
BLOCK = 512
EPSILON = 1e-06
AXES = ("grp", "seq")
LANES = 2
QUAD = 4
SHARE = H // (LANES * QUAD)
TILE = 256
CUT = 512
SLAB = 256
UNROLL_TOTALS = 4
UNROLL_LOCAL = 4
UNROLL_BACK = 4
UNROLL_FINAL = 4
DEPTH = 2
F32 = jnp.float32
BF16 = jnp.bfloat16


def mm(a, b, ca, cb):
    return lax.dot_general(a, b, (((ca,), (cb,)), ((), ())), preferred_element_type=F32)


def place_of(head, where):
    unit = head // SHARE
    lane = (unit // QUAD) ^ where[0]
    slot = (unit % QUAD) ^ where[1]
    return slot, lane, head % SHARE


def put_piece(pieces, head, where, value):
    slot, lane, share = place_of(head, where)
    for i, piece in enumerate(pieces):

        @pl.when(slot == i)
        def _():
            piece[lane, share] = value


def vmem(*shape, dtype=F32):
    return pltpu.VMEM(shape, dtype)


def near(value):
    return pltpu.with_memory_space_constraint(value, pltpu.VMEM)


def far(value):
    return pltpu.with_memory_space_constraint(value, pltpu.HBM)


def piece_shapes():
    return [vmem(LANES, SHARE, HD, HD)] * QUAD


def call(kernel, out_shape, args, flops, scratch=(), grant=8, far_in=(), far_out=()):
    any_space = pl.BlockSpec(memory_space=pltpu.HBM)
    near_space = pl.BlockSpec(memory_space=pltpu.VMEM)
    in_specs = [pl.BlockSpec(memory_space=pltpu.SMEM)]
    in_specs += [any_space if i in far_in else near_space for i in range(len(args) - 1)]
    out_specs = [any_space if i in far_out else near_space for i in range(len(out_shape))]
    args = [args[0]] + [far(a) if i in far_in else near(a) for i, a in enumerate(args[1:])]
    return pl.pallas_call(
        kernel,
        out_shape=out_shape,
        in_specs=in_specs,
        out_specs=out_specs,
        scratch_shapes=scratch,
        compiler_params=pltpu.CompilerParams(vmem_limit_bytes=grant << 20),
        cost_estimate=pl.CostEstimate(flops=flops, bytes_accessed=flops // 100, transcendentals=0),
    )(*args)


def head_cols(head):
    return pl.ds(pl.multiple_of(head * HD, HD), HD)


def over_heads(step, unroll):
    def several(i, _):
        for j in range(unroll):
            step(i * unroll + j)
        return 0

    lax.fori_loop(0, H // unroll, several, 0)


def totals_kernel(where, k_far, v_far, *refs):
    pieces, (inside, k_ref, v_ref, run, sems) = refs[:QUAD], refs[QUAD:]
    blocks = k_ref.shape[0] // BLOCK
    copies = []
    for b in range(blocks):
        rows = pl.ds(b * BLOCK, BLOCK)
        for j, (source, target) in enumerate(((k_far, k_ref), (v_far, v_ref))):
            copies.append(pltpu.make_async_copy(source.at[rows, :], target.at[rows, :], sems.at[b, j]))
    for copy in copies[: 2 * DEPTH]:
        copy.start()
    for b in range(blocks):
        for j in range(2):
            copies[2 * b + j].wait()
            if b + DEPTH < blocks:
                copies[2 * (b + DEPTH) + j].start()
        rows = pl.ds(b * BLOCK, BLOCK)
        for head in range(H):
            cols = pl.ds(head * HD, HD)
            state = mm(k_ref[rows, cols], v_ref[rows, cols], 0, 0)
            inside[b, head] = run[head] if b else jnp.zeros_like(state)
            state = run[head] + state if b else state
            if b < blocks - 1:
                run[head] = state
            else:
                put_piece(pieces, head, where, state)


def totals(where, keys, values):
    tokens, features = keys.shape
    blocks = tokens // BLOCK
    return call(
        totals_kernel,
        piece_shapes()
        + [vmem(blocks, H, HD, HD)]
        + [vmem(tokens, features, dtype=BF16)] * 2,
        [where, keys, values],
        2 * tokens * features * HD,
        scratch=[vmem(H, HD, HD), pltpu.SemaphoreType.DMA((blocks, 2))],
        far_in=(0, 1),
    )


def triangle(size, upper=False):
    row = lax.broadcasted_iota(jnp.int32, (size, size), 0)
    col = lax.broadcasted_iota(jnp.int32, (size, size), 1)
    return row <= col if upper else row >= col


def local_kernel(where, q_ref, k_ref, v_ref, out_ref):
    mask = triangle(CUT)

    def step(unit):
        block, cols = unit // H, head_cols(unit % H)
        for i in range(BLOCK // CUT):
            rows = pl.ds(pl.multiple_of(block * BLOCK + i * CUT, CUT), CUT)
            q = q_ref[rows, cols]
            diag = jnp.where(mask, mm(q, k_ref[rows, cols], 1, 1), 0.0).astype(BF16)
            acc = mm(diag, v_ref[rows, cols], 1, 0)
            if i:
                past = pl.ds(pl.multiple_of(block * BLOCK, CUT), i * CUT)
                acc += mm(mm(q, k_ref[past, cols], 1, 1).astype(BF16), v_ref[past, cols], 1, 0)
            out_ref[rows, cols] = acc

    def several(i, _):
        for j in range(UNROLL_LOCAL):
            step(i * UNROLL_LOCAL + j)
        return 0

    lax.fori_loop(0, q_ref.shape[0] // BLOCK * H // UNROLL_LOCAL, several, 0)


def local_part(where, queries, keys, values):
    tokens, features = queries.shape
    return call(
        local_kernel,
        [vmem(tokens, features)],
        [where, queries, keys, values],
        4 * tokens * BLOCK * features,
    )[0]


def middle_kernel(where, local_ref, q_ref, dy_ref, gain_ref, *refs):
    carried, inside = refs[:QUAD], refs[QUAD]
    out_ref, grad_ref, prior_ref = refs[QUAD + 1 : QUAD + 4]
    pieces, later_ref = refs[QUAD + 4 : 2 * QUAD + 4], refs[2 * QUAD + 4]
    att_ref, run_ref = refs[2 * QUAD + 5 :]
    blocks = q_ref.shape[0] // BLOCK
    features = H * HD
    for head in range(H):
        slot, lane, share = place_of(head, where)
        for i in range(QUAD):

            @pl.when(slot == i)
            def _():
                for b in range(blocks):
                    prior_ref[b, head] = (carried[i][lane, share] + inside[b, head]).astype(BF16)

    run_ref[...] = jnp.zeros_like(run_ref)

    def tile_step(block, i):
        rows = pl.ds(pl.multiple_of(block * BLOCK + i * SLAB, SLAB), SLAB)
        square = None
        for head in range(H):
            cols = pl.ds(head * HD, HD)
            att = local_ref[rows, cols] + mm(q_ref[rows, cols], prior_ref[block, head], 1, 0)
            att_ref[:, cols] = att
            square = att * att if square is None else square + att * att
        inverse = lax.rsqrt(jnp.sum(square, axis=1, keepdims=True) / features + EPSILON)
        cross = None
        for head in range(H):
            cols = pl.ds(head * HD, HD)
            unit = att_ref[:, cols] * inverse
            gain = gain_ref[:, cols]
            out_ref[rows, cols] = (unit * gain).astype(BF16)
            term = dy_ref[rows, cols].astype(F32) * gain * unit
            cross = term if cross is None else cross + term
        mean = jnp.sum(cross, axis=1, keepdims=True) / features
        for head in range(H):
            cols = pl.ds(head * HD, HD)
            unit = att_ref[:, cols] * inverse
            scaled = dy_ref[rows, cols].astype(F32) * gain_ref[:, cols]
            grad_ref[rows, cols] = (inverse * (scaled - unit * mean)).astype(BF16)

    for block in reversed(range(blocks)):
        rows = pl.ds(block * BLOCK, BLOCK)
        lax.fori_loop(0, BLOCK // SLAB, lambda i, _: tile_step(block, i) or 0, 0)
        later_ref[block] = run_ref[...]

        def add(head):
            cols = head_cols(head)
            run_ref[head] += mm(q_ref[rows, cols], grad_ref[rows, cols], 0, 0)

        over_heads(add, UNROLL_TOTALS)
    for head in range(H):
        put_piece(pieces, head, where, run_ref[head])


def middle(where, local, queries, cotangent, gain, carried, inside):
    tokens, features = queries.shape
    blocks = tokens // BLOCK
    return call(
        middle_kernel,
        [vmem(tokens, features, dtype=BF16)] * 2
        + [vmem(blocks, H, HD, HD, dtype=BF16)]
        + piece_shapes()
        + [vmem(blocks, H, HD, HD)],
        [where, local, queries, cotangent, gain, *carried, inside],
        4 * tokens * features * HD,
        scratch=[vmem(SLAB, features), vmem(H, HD, HD)],
    )


def over_units(count, step):
    def several(i, _):
        for j in range(UNROLL_BACK):
            unit = i * UNROLL_BACK + j
            step(unit // H, unit % H)
        return 0

    lax.fori_loop(0, count // UNROLL_BACK, several, 0)


def block_part(block, first, count):
    return pl.ds(pl.multiple_of(block * BLOCK + first * CUT, CUT), count * CUT)


def query_kernel(where, g_ref, v_ref, k_ref, prior_ref, out_ref):
    mask = triangle(CUT)

    def step(block, head):
        cols = head_cols(head)
        for i in range(BLOCK // CUT):
            rows = block_part(block, i, 1)
            g = g_ref[rows, cols]
            acc = mm(g, prior_ref[block, head], 1, 1)
            scores = jnp.where(mask, mm(g, v_ref[rows, cols], 1, 1), 0.0).astype(BF16)
            acc += mm(scores, k_ref[rows, cols], 1, 0)
            if i:
                past = block_part(block, 0, i)
                scores = mm(g, v_ref[past, cols], 1, 1).astype(BF16)
                acc += mm(scores, k_ref[past, cols], 1, 0)
            out_ref[rows, cols] = acc.astype(BF16)

    over_units(g_ref.shape[0] // BLOCK * H, step)


def query_part(where, grads, values, keys, prior):
    tokens, features = grads.shape
    return call(
        query_kernel,
        [vmem(tokens, features, dtype=BF16)],
        [where, grads, values, keys, prior],
        4 * tokens * BLOCK * features,
    )[0]


def turned_kernel(where, a_ref, b_ref, c_ref, ready_ref, out_ref, far_ref, sem):
    copy = pltpu.make_async_copy(ready_ref, far_ref, sem)
    copy.start()
    mask, tiles = triangle(CUT, True), BLOCK // CUT

    def step(block, head):
        cols = head_cols(head)
        for i in range(tiles):
            rows = block_part(block, i, 1)
            a = a_ref[rows, cols]
            scores = jnp.where(mask, mm(a, b_ref[rows, cols], 1, 1), 0.0).astype(BF16)
            acc = mm(scores, c_ref[rows, cols], 1, 0)
            if i < tiles - 1:
                rest = block_part(block, i + 1, tiles - 1 - i)
                scores = mm(a, b_ref[rest, cols], 1, 1).astype(BF16)
                acc += mm(scores, c_ref[rest, cols], 1, 0)
            out_ref[rows, cols] = acc

    over_units(a_ref.shape[0] // BLOCK * H, step)
    copy.wait()


def turned_part(where, a, b, c, ready):
    tokens, features = a.shape
    return call(
        turned_kernel,
        [vmem(tokens, features), jax.ShapeDtypeStruct(ready.shape, ready.dtype)],
        [where, a, b, c, ready],
        4 * tokens * BLOCK * features,
        scratch=[pltpu.SemaphoreType.DMA(())],
        far_out=(1,),
    )


def final_kernel(where, lk_ref, lv_ref, k_ref, v_ref, *refs):
    carried, later = refs[:QUAD], refs[QUAD]
    gk_far, gv_far, gk_ref, gv_ref, state_ref, sems = refs[QUAD + 1 :]
    blocks = k_ref.shape[0] // BLOCK
    for head in range(H):
        slot, lane, share = place_of(head, where)
        for i in range(QUAD):

            @pl.when(slot == i)
            def _():
                for b in range(blocks):
                    state_ref[b, head] = (carried[i][lane, share] + later[b, head]).astype(BF16)

    copies = []
    for i in range(k_ref.shape[0] // TILE):
        rows = pl.ds(i * TILE, TILE)
        block = i // (BLOCK // TILE)

        def one(head):
            cols = head_cols(head)
            state = state_ref[block, head]
            gk_ref[rows, cols] = (lk_ref[rows, cols] + mm(v_ref[rows, cols], state, 1, 1)).astype(BF16)
            gv_ref[rows, cols] = (lv_ref[rows, cols] + mm(k_ref[rows, cols], state, 1, 0)).astype(BF16)

        over_heads(one, UNROLL_FINAL)
        for j, (source, target) in enumerate(((gk_ref, gk_far), (gv_ref, gv_far))):
            copy = pltpu.make_async_copy(source.at[rows, :], target.at[rows, :], sems.at[i, j])
            copy.start()
            copies.append(copy)
    for copy in copies:
        copy.wait()


def final_part(where, local_k, local_v, keys, values, carried, later):
    tokens, features = keys.shape
    blocks = tokens // BLOCK
    return call(
        final_kernel,
        [jax.ShapeDtypeStruct((tokens, features), BF16)] * 2,
        [where, local_k, local_v, keys, values, *carried, later],
        4 * tokens * features * HD,
        scratch=[
            vmem(tokens, features, dtype=BF16),
            vmem(tokens, features, dtype=BF16),
            vmem(blocks, H, HD, HD, dtype=BF16),
            pltpu.SemaphoreType.DMA((tokens // TILE, 2)),
        ],
        far_out=(0, 1),
        grant=12,
    )


def moved(value, move):
    groups, shards = lax.axis_size("grp"), lax.axis_size("seq")
    pairs = []
    for g in range(groups):
        for s in range(shards):
            to_g, to_s = move(g, s)
            pairs.append((g * shards + s, to_g * shards + to_s))
    return lax.ppermute(value, AXES, pairs)


def sum_kernel(where, *refs):
    held, (mine_ref, rest_ref) = refs[:QUAD], refs[QUAD:]
    for lane, out in enumerate((mine_ref, rest_ref)):
        out[...] = (held[0][lane] + held[1][lane]) + (held[2][lane] + held[3][lane])


def pair_kernel(where, mine_ref, other_ref, pair_ref, both_ref):
    mine, other = mine_ref[...], other_ref[...]
    pair_ref[0], pair_ref[1] = mine, other
    both_ref[...] = mine + other


def before(a, b, reverse):
    return a > b if reverse else a < b


def base_kernel(shifts, counts, reverse, where, pair_ref, *refs):
    came, (mine_ref, other_ref) = refs[: len(shifts)], refs[len(shifts) :]
    lane, row, far = where[0], where[2], where[3]
    takes = lane == (0 if reverse else 1)
    mine, other = pair_ref[0], pair_ref[1]
    sum_mine, sum_other = jnp.where(takes, other, 0.0), jnp.where(takes, 0.0, mine)
    for (dr, df), value in zip(shifts, came):
        if dr:
            source = lax.rem(row - dr + counts[0], counts[0])
            add = jnp.where(before(source, row, reverse), value[...], 0.0)
            sum_mine, sum_other = sum_mine + add, sum_other + add
        else:
            near_by = before(lax.rem(far - df + counts[1], counts[1]), far, reverse)
            mine, other = value[0], value[1]
            sum_mine += jnp.where(near_by, mine, 0.0) + jnp.where(takes, other, 0.0)
            sum_other += jnp.where(near_by, other, 0.0) + jnp.where(takes, 0.0, mine)
    mine_ref[...], other_ref[...] = sum_mine, sum_other


def back_sum_kernel(reverse, where, mine_ref, other_ref, *refs):
    held, back = refs[:QUAD], refs[QUAD:]
    quad = where[1]
    for lane, base in enumerate((mine_ref, other_ref)):
        for o in range(QUAD):
            value = base[...]
            for i in range(QUAD):
                if i != o:
                    near_by = before(quad ^ i, quad ^ o, reverse)
                    value += jnp.where(near_by, held[i][lane], 0.0)
            back[o][lane] = value


def carry(where, pieces, reverse):
    counts = lax.axis_size("grp") // LANES, lax.axis_size("seq") // QUAD
    order = (3, 1, 2)
    one, two = vmem(SHARE, HD, HD), vmem(LANES, SHARE, HD, HD)

    def swap_quad(o):
        return lambda g, s: (g, s ^ o)

    def swap_lane(g, s):
        return g ^ 1, s

    def shift(dr, df):
        return lambda g, s: (
            (g // LANES + dr) % counts[0] * LANES + g % LANES,
            (s // QUAD + df) % counts[1] * QUAD + s % QUAD,
        )

    held = [pieces[0]] + [None] * (QUAD - 1)
    for o in order:
        held[o] = moved(pieces[o], swap_quad(o))
    mine, rest = call(sum_kernel, [one, one], [where, *held], 1000, grant=2)
    other = moved(rest, swap_lane)
    pair, both = call(pair_kernel, [two, one], [where, mine, other], 1000, grant=2)
    shifts = [(dr, df) for dr in range(counts[0]) for df in range(counts[1]) if dr or df]
    shifts.sort(key=lambda shift_by: -sum(shift_by))
    came = []
    for dr, df in shifts:
        came.append(moved(both if dr else pair, shift(dr, df)))
    kernel = functools.partial(base_kernel, shifts, counts, reverse)
    sum_mine, sum_other = call(kernel, [one, one], [where, pair, *came], 1000, grant=2)
    other = moved(sum_other, swap_lane)
    kernel = functools.partial(back_sum_kernel, reverse)
    back = call(kernel, [two] * QUAD, [where, sum_mine, other, *held], 1000, grant=2)
    result = [back[0]] + [None] * (QUAD - 1)
    for o in order:
        result[o] = moved(back[o], swap_quad(o))
    return result


def body(queries, key_rows, value_rows, norm_gain, cotangent):
    grp, seq = lax.axis_index("grp"), lax.axis_index("seq")
    parts = [grp % LANES, seq % QUAD, grp // LANES, seq // QUAD]
    where = jnp.stack(parts).astype(jnp.int32)
    *pieces, inside, keys, values = totals(where, key_rows, value_rows)
    queries = near(queries)
    local = local_part(where, queries, keys, values)
    prior = carry(where, pieces, False)
    normed, grads, prior_half, *rest = middle(
        where, local, queries, cotangent, norm_gain[None, :], prior, inside
    )
    grad_pieces, later = rest[:QUAD], rest[QUAD]
    after = carry(where, grad_pieces, True)
    local_v, normed = turned_part(where, keys, queries, grads, normed)
    grad_q = query_part(where, grads, values, keys, prior_half)
    local_k, grad_q = turned_part(where, values, grads, queries, grad_q)
    grad_k, grad_v = final_part(where, local_k, local_v, keys, values, after, later)
    return normed, grad_q, grad_k, grad_v


def solution(mesh):
    rows = P(AXES, None)
    return jax.shard_map(
        body,
        mesh=mesh,
        in_specs=(rows, rows, rows, P(), rows),
        out_specs=(rows, rows, rows, rows),
        check_vma=False,
    )
```

time: 161 us -> 97.6 us (0.61)
  matrix products: 58.4 us -> 0 us
  Pallas kernels: 0 us -> 45.3 us
  local copies, waits for them, and re-layouts: 43.9 us -> 0.01 us
  other arithmetic: 14.3 us -> 0.08 us
  waiting for transfers between devices: 21.9 us -> 26.5 us
  starting transfers between devices: 20.4 us -> 24.5 us
    dot_general x12 -> x0, matrix products: 58.4 us -> none  [the longest x1 7.87 us: body(): jnp.einsum('bhts,bthd->bshd', grad_scores, query_blocks, preferred_elemen...]
    pallas_call x0 -> x15, Pallas kernels: none -> 45.3 us  [call(): pl.pallas_call(kernel, out_shape=out_shape, in_specs=in_specs, out_specs=...]
    ppermute x0 -> x22, waiting for transfers between devices: none -> 26.5 us  [moved(): return lax.ppermute(value, AXES, pairs)]
    ppermute x0 -> x22, starting transfers between devices: none -> 24.5 us  [moved(): return lax.ppermute(value, AXES, pairs)]
    all_to_all x4 -> x0, waiting for transfers between devices: 21.9 us -> none  [the longest x2 13.9 us: carried(): lax.all_to_all(flat, ('grp', 'seq'), split_axis=0, concat_axis=0, tiled=T...]
    all_to_all x4 -> x0, starting transfers between devices: 20.4 us -> none  [the longest x2 10.8 us: carried(): lax.all_to_all(flat, ('grp', 'seq'), split_axis=0, concat_axis=0, tiled=T...]
    unnamed x43 -> x6, local copies, waits for them, and re-layouts: 15.5 us -> 0.01 us
    convert_element_type x3 -> x0, local copies, waits for them, and re-layouts: 8.73 us -> none  [the longest x1 4.43 us: body(): grad_v.astype(jnp.bfloat16).reshape(tokens, features)]
  transfers between devices with their start and end apart: 4 -> 22, of which waited for: 3 -> 14; matrix products, arithmetic and copies ran while one was open for 28% -> 0% of each run, Pallas kernels for 0% -> 25%
where the time goes in v2:
time: 97.6 us; the launch traced here: 97.4 us
  Pallas kernels  45.3 us (46%)
  waiting for transfers between devices  26.5 us (27%)
  starting transfers between devices  24.5 us (25%)
  between operations  1.04 us (1%)
    pallas_call x15, Pallas kernels, call(): pl.pallas_call(kernel, out_shape=out_shape, in_specs=in_specs, out_specs=...  45.3 us
    ppermute x22, waiting for transfers between devices, moved(): return lax.ppermute(value, AXES, pairs)  26.5 us
    ppermute x22, starting transfers between devices, moved(): return lax.ppermute(value, AXES, pairs)  24.5 us
  transfers between devices with their start and end apart: 22, of which 14 were waited for; matrix products, arithmetic and copies ran while one was open for 0% of the time, Pallas kernels for 25%

profile of v2, /device:TPU:0, one launch (start us, length us, event | category | flops | bytes accessed | tf_op | source)
XLA Modules:
  0.0 97.4 jit_solution(16673429203088976838)
XLA Ops:
  0.7 0.1 pad_add_fusion.where
  0.7 5.1 %shard_map.84 = (f32[2,1,128,128]{3,2,1,0:T(8,128)S(1)}, f32[2,1,128,128]{3,2,1,0:T(8,128)S(1)}, f32[2,1,128,128]{3,2,1,0:T(8,128)S(1)}, f32[2,1,128,128]{3,2,1,...) custom-call(s32[4]{0:T(128)S(1)} %pad_add_fusion.where, ...), custom_call_target="tpu_custom_call" | custom-call | flops 268435456 | bytes 2684354 | tf_op jit(solution)/shard_map/pallas_call | solution.py:74
  5.8 3.0 %collective-permute-start = (f32[2,1,128,128]{3,2,1,0:T(8,128)S(1)}, f32[2,1,128,128]{3,2,1,0:T(8,128)S(1)}, u32[]{:S(2)}, u32[]{:S(2)}) collective-permute-start(f32[2,1,128,128]{3,2,1,0:T(8,128)S(1)} %get-tuple-element.48), channel_id=1, source_target_pairs={{0,1},{1,0},{2,3},{3,2},{4,5},{5,4},{6,7},{7,6},{8,9},{9,8},{10,11... | collective-permute-start | bytes 393224 | tf_op jit(solution)/shard_map/ppermute | solution.py:387
  8.9 1.6 %collective-permute-start.1 = (f32[2,1,128,128]{3,2,1,0:T(8,128)S(1)}, f32[2,1,128,128]{3,2,1,0:T(8,128)S(1)}, u32[]{:S(2)}, u32[]{:S(2)}) collective-permute-start(f32[2,1,128,128]{3,2,1,0:T(8,128)S(1)} %get-tuple-element.49), channel_id=1, source_target_pairs={{0,2},{1,3},{2,0},{3,1},{4,6},{5,7},{6,4},{7,5},{8,10},{9,11},{10,... | collective-permute-start | bytes 393224 | tf_op jit(solution)/shard_map/ppermute | solution.py:387
  10.4 1.9 %collective-permute-done.refs_1_ = f32[2,1,128,128]{3,2,1,0:T(8,128)S(1)} collective-permute-done((f32[2,1,128,128]{3,2,1,0:T(8,128)S(1)}, f32[2,1,128,128]{3,2,1,0:T(8,128)S(1)}, u32[]{:S(2)}, u32[]{:S(2)}) %collective-permute-start) | collective-permute-done | bytes 131104 | tf_op jit(solution)/shard_map/ppermute | solution.py:387
  12.4 2.9 %collective-permute-done.1.refs_2_ = f32[2,1,128,128]{3,2,1,0:T(8,128)S(1)} collective-permute-done((f32[2,1,128,128]{3,2,1,0:T(8,128)S(1)}, f32[2,1,128,128]{3,2,1,0:T(8,128)S(1)}, u32[]{:S(2)}, u32[]{:S(2)}) %collective-permute-start.1) | collective-permute-done | bytes 131104 | tf_op jit(solution)/shard_map/ppermute | solution.py:387
  15.2 1.2 %collective-permute-done.2.refs_3_ = f32[2,1,128,128]{3,2,1,0:T(8,128)S(1)} collective-permute-done((f32[2,1,128,128]{3,2,1,0:T(8,128)S(1)}, f32[2,1,128,128]{3,2,1,0:T(8,128)S(1)}, u32[]{:S(2)}, u32[]{:S(2)}) %collective-permute-start.2) | collective-permute-done | bytes 131104 | tf_op jit(solution)/shard_map/ppermute | solution.py:387
  16.4 0.6 shard_map.86
  17.1 1.2 %collective-permute-done.3.other_ref = f32[1,128,128]{2,1,0:T(8,128)S(1)} collective-permute-done((f32[1,128,128]{2,1,0:T(8,128)S(1)}, f32[1,128,128]{2,1,0:T(8,128)S(1)}, u32[]{:S(2)}, u32[]{:S(2)}) %collective-permute-start.3) | collective-permute-done | bytes 65568 | tf_op jit(solution)/shard_map/ppermute | solution.py:387
  18.3 0.6 shard_map.87
  18.9 2.8 %collective-permute-start.5 = (f32[2,1,128,128]{3,2,1,0:T(8,128)S(1)}, f32[2,1,128,128]{3,2,1,0:T(8,128)S(1)}, u32[]{:S(2)}, u32[]{:S(2)}) collective-permute-start(f32[2,1,128,128]{3,2,1,0:T(8,128)S(1)} %get-tuple-element.53.pair_ref), channel_id=1, source_target_pairs={{0,4},{1,5},{2,6},{3,7},{4,0},{5,1},{6,2},{7,3},{8,12},{9,13},{10,... | collective-permute-start | bytes 393224 | tf_op jit(solution)/shard_map/ppermute | solution.py:387
  21.7 1.5 %collective-permute-start.6 = (f32[1,128,128]{2,1,0:T(8,128)S(1)}, f32[1,128,128]{2,1,0:T(8,128)S(1)}, u32[]{:S(2)}, u32[]{:S(2)}) collective-permute-start(f32[1,128,128]{2,1,0:T(8,128)S(1)} %get-tuple-element.54), channel_id=1, source_target_pairs={{0,16},{1,17},{2,18},{3,19},{4,20},{5,21},{6,22},{7,23},{8,24},{9,... | collective-permute-start | bytes 196616 | tf_op jit(solution)/shard_map/ppermute | solution.py:387
  23.2 0.1 collective-permute-start.4
  23.3 2.6 %collective-permute-done.6.refs_2_ = f32[1,128,128]{2,1,0:T(8,128)S(1)} collective-permute-done((f32[1,128,128]{2,1,0:T(8,128)S(1)}, f32[1,128,128]{2,1,0:T(8,128)S(1)}, u32[]{:S(2)}, u32[]{:S(2)}) %collective-permute-start.6) | collective-permute-done | bytes 65568 | tf_op jit(solution)/shard_map/ppermute | solution.py:387
  26.0 6.2 %collective-permute-done.4.refs_0_ = f32[1,128,128]{2,1,0:T(8,128)S(1)} collective-permute-done((f32[1,128,128]{2,1,0:T(8,128)S(1)}, f32[1,128,128]{2,1,0:T(8,128)S(1)}, u32[]{:S(2)}, u32[]{:S(2)}) %collective-permute-start.4) | collective-permute-done | bytes 65568 | tf_op jit(solution)/shard_map/ppermute | solution.py:387
  32.2 0.6 shard_map.88
  32.8 0.1 collective-permute-start.7
  32.8 1.2 %collective-permute-done.7.other_ref = f32[1,128,128]{2,1,0:T(8,128)S(1)} collective-permute-done((f32[1,128,128]{2,1,0:T(8,128)S(1)}, f32[1,128,128]{2,1,0:T(8,128)S(1)}, u32[]{:S(2)}, u32[]{:S(2)}) %collective-permute-start.7) | collective-permute-done | bytes 65568 | tf_op jit(solution)/shard_map/ppermute | solution.py:387
  34.1 0.7 shard_map.89
  34.7 1.5 %collective-permute-start.8 = (f32[2,1,128,128]{3,2,1,0:T(8,128)S(1)}, f32[2,1,128,128]{3,2,1,0:T(8,128)S(1)}, u32[]{:S(2)}, u32[]{:S(2)}) collective-permute-start(f32[2,1,128,128]{3,2,1,0:T(8,128)S(1)} %get-tuple-element.58), channel_id=1, source_target_pairs={{0,1},{1,0},{2,3},{3,2},{4,5},{5,4},{6,7},{7,6},{8,9},{9,8},{10,11... | collective-permute-start | bytes 393224 | tf_op jit(solution)/shard_map/ppermute | solution.py:387
  36.3 2.0 %collective-permute-start.10 = (f32[2,1,128,128]{3,2,1,0:T(8,128)S(1)}, f32[2,1,128,128]{3,2,1,0:T(8,128)S(1)}, u32[]{:S(2)}, u32[]{:S(2)}) collective-permute-start(f32[2,1,128,128]{3,2,1,0:T(8,128)S(1)} %get-tuple-element.60), channel_id=1, source_target_pairs={{0,3},{1,2},{2,1},{3,0},{4,7},{5,6},{6,5},{7,4},{8,11},{9,10},{10,... | collective-permute-start | bytes 393224 | tf_op jit(solution)/shard_map/ppermute | solution.py:387
  38.3 6.1 %shard_map.85.local_ref = f32[1024,1024]{1,0:T(8,128)S(1)} custom-call(s32[4]{0:T(128)S(1)} %pad_add_fusion.where, bf16[1024,1024]{1,0:T(8,128)(2,1)S(1)} %copy-done, bf16[1024,1024]{1,0:T(8,128)(2,1)S(1)} %get-tuple-element.45.k_ref.a_ref, bf16[1024,1024]{1,0:T(8,128)(2,1)S(1)} %get-tuple-element.46.v_ref.a_ref), custom_call_target="tpu_custom_call" | custom-call | flops 2147483648 | bytes 21474836 | tf_op jit(solution)/shard_map/pallas_call | solution.py:74
  44.4 6.6 %shard_map.90 = (bf16[1024,1024]{1,0:T(8,128)(2,1)S(1)}, bf16[1024,1024]{1,0:T(8,128)(2,1)S(1)}, bf16[2,8,128,128]{3,2,1,0:T(8,128)(2,1)S(1)}, f32[2,1,128,128]{...) custom-call(s32[4]{0:T(128)S(1)} %pad_add_fusion.where, ...), custom_call_target="tpu_custom_call" | custom-call | flops 536870912 | bytes 5368709 | tf_op jit(solution)/shard_map/pallas_call | solution.py:74
  51.0 1.5 %collective-permute-start.11 = (f32[2,1,128,128]{3,2,1,0:T(8,128)S(1)}, f32[2,1,128,128]{3,2,1,0:T(8,128)S(1)}, u32[]{:S(2)}, u32[]{:S(2)}) collective-permute-start(f32[2,1,128,128]{3,2,1,0:T(8,128)S(1)} %get-tuple-element.70), channel_id=1, source_target_pairs={{0,1},{1,0},{2,3},{3,2},{4,5},{5,4},{6,7},{7,6},{8,9},{9,8},{10,11... | collective-permute-start | bytes 393224 | tf_op jit(solution)/shard_map/ppermute | solution.py:387
  52.6 0.2 collective-permute-start.12
  52.8 1.8 %collective-permute-start.13 = (f32[2,1,128,128]{3,2,1,0:T(8,128)S(1)}, f32[2,1,128,128]{3,2,1,0:T(8,128)S(1)}, u32[]{:S(2)}, u32[]{:S(2)}) collective-permute-start(f32[2,1,128,128]{3,2,1,0:T(8,128)S(1)} %get-tuple-element.72), channel_id=1, source_target_pairs={{0,3},{1,2},{2,1},{3,0},{4,7},{5,6},{6,5},{7,4},{8,11},{9,10},{10,... | collective-permute-start | bytes 393224 | tf_op jit(solution)/shard_map/ppermute | solution.py:387
  54.6 2.5 %collective-permute-done.11.refs_1_ = f32[2,1,128,128]{3,2,1,0:T(8,128)S(1)} collective-permute-done((f32[2,1,128,128]{3,2,1,0:T(8,128)S(1)}, f32[2,1,128,128]{3,2,1,0:T(8,128)S(1)}, u32[]{:S(2)}, u32[]{:S(2)}) %collective-permute-start.11) | collective-permute-done | bytes 131104 | tf_op jit(solution)/shard_map/ppermute | solution.py:387
  57.1 1.4 %collective-permute-done.12.refs_2_ = f32[2,1,128,128]{3,2,1,0:T(8,128)S(1)} collective-permute-done((f32[2,1,128,128]{3,2,1,0:T(8,128)S(1)}, f32[2,1,128,128]{3,2,1,0:T(8,128)S(1)}, u32[]{:S(2)}, u32[]{:S(2)}) %collective-permute-start.12) | collective-permute-done | bytes 131104 | tf_op jit(solution)/shard_map/ppermute | solution.py:387
  58.4 1.4 %collective-permute-done.13.refs_3_ = f32[2,1,128,128]{3,2,1,0:T(8,128)S(1)} collective-permute-done((f32[2,1,128,128]{3,2,1,0:T(8,128)S(1)}, f32[2,1,128,128]{3,2,1,0:T(8,128)S(1)}, u32[]{:S(2)}, u32[]{:S(2)}) %collective-permute-start.13) | collective-permute-done | bytes 131104 | tf_op jit(solution)/shard_map/ppermute | solution.py:387
  59.8 0.6 shard_map.94
  60.4 0.1 collective-permute-start.14
  60.5 1.2 %collective-permute-done.14.other_ref = f32[1,128,128]{2,1,0:T(8,128)S(1)} collective-permute-done((f32[1,128,128]{2,1,0:T(8,128)S(1)}, f32[1,128,128]{2,1,0:T(8,128)S(1)}, u32[]{:S(2)}, u32[]{:S(2)}) %collective-permute-start.14) | collective-permute-done | bytes 65568 | tf_op jit(solution)/shard_map/ppermute | solution.py:387
  61.7 0.6 shard_map.95
  62.3 0.5 collective-permute-start.17
  62.8 3.8 %collective-permute-start.15 = (f32[1,128,128]{2,1,0:T(8,128)S(1)}, f32[1,128,128]{2,1,0:T(8,128)S(1)}, u32[]{:S(2)}, u32[]{:S(2)}) collective-permute-start(f32[1,128,128]{2,1,0:T(8,128)S(1)} %get-tuple-element.76), channel_id=1, source_target_pairs={{0,20},{1,21},{2,22},{3,23},{4,16},{5,17},{6,18},{7,19},{8,28},{9,... | collective-permute-start | bytes 196616 | tf_op jit(solution)/shard_map/ppermute | solution.py:387
  66.6 0.1 collective-permute-start.16
  66.7 6.4 %shard_map.92.ready_ref = bf16[1024,1024]{1,0:T(8,128)(2,1)S(1)} custom-call(s32[4]{0:T(128)S(1)} %pad_add_fusion.where, bf16[1024,1024]{1,0:T(8,128)(2,1)S(1)} %get-tuple-element.62.c_ref.g_ref.b_ref, bf16[1024,1024]{1,0:T(8,128)(2,1)S(1)} %get-tuple-element.46.v_ref.a_ref, bf16[1024,1024]{1,0:T(8,128)(2,1)S(1)} %get-tuple-element.45.k_ref.a_ref, ...), custom_call_target="tpu_custom_call" | custom-call | flops 2147483648 | bytes 21474836 | tf_op jit(solution)/shard_map/pallas_call | solution.py:74
  73.2 0.3 collective-permute-done.15.refs_0_
  73.4 2.2 %collective-permute-done.16.refs_1_ = f32[2,1,128,128]{3,2,1,0:T(8,128)S(1)} collective-permute-done((f32[2,1,128,128]{3,2,1,0:T(8,128)S(1)}, f32[2,1,128,128]{3,2,1,0:T(8,128)S(1)}, u32[]{:S(2)}, u32[]{:S(2)}) %collective-permute-start.16) | collective-permute-done | bytes 131104 | tf_op jit(solution)/shard_map/ppermute | solution.py:387
  75.6 0.6 shard_map.96
  76.3 6.1 %shard_map.93 = (f32[1024,1024]{1,0:T(8,128)S(1)}, bf16[1024,1024]{1,0:T(8,128)(2,1)}) custom-call(s32[4]{0:T(128)S(1)} %pad_add_fusion.where, bf16[1024,1024]{1,0:T(8,128)(2,1)S(1)} %get-tuple-element.46.v_ref.a_ref, bf16[1024,1024]{1,0:T(8,128)(2,1)S(1)} %get-tuple-element.62.c_ref.g_ref.b_ref, bf16[1024,1024]{1,0:T(8,128)(2,1)S(1)} %copy-done, ...), custom_call_target="tpu_custom_call" | custom-call | flops 2147483648 | bytes 21474836 | tf_op jit(solution)/shard_map/pallas_call | solution.py:74
  82.4 0.7 shard_map.97
  83.0 1.4 %collective-permute-start.19 = (f32[2,1,128,128]{3,2,1,0:T(8,128)S(1)}, f32[2,1,128,128]{3,2,1,0:T(8,128)S(1)}, u32[]{:S(2)}, u32[]{:S(2)}) collective-permute-start(f32[2,1,128,128]{3,2,1,0:T(8,128)S(1)} %get-tuple-element.80), channel_id=1, source_target_pairs={{0,1},{1,0},{2,3},{3,2},{4,5},{5,4},{6,7},{7,6},{8,9},{9,8},{10,11... | collective-permute-start | bytes 393224 | tf_op jit(solution)/shard_map/ppermute | solution.py:387
  84.5 0.6 collective-permute-start.20
  85.0 1.6 %collective-permute-start.21 = (f32[2,1,128,128]{3,2,1,0:T(8,128)S(1)}, f32[2,1,128,128]{3,2,1,0:T(8,128)S(1)}, u32[]{:S(2)}, u32[]{:S(2)}) collective-permute-start(f32[2,1,128,128]{3,2,1,0:T(8,128)S(1)} %get-tuple-element.82), channel_id=1, source_target_pairs={{0,3},{1,2},{2,1},{3,0},{4,7},{5,6},{6,5},{7,4},{8,11},{9,10},{10,... | collective-permute-start | bytes 393224 | tf_op jit(solution)/shard_map/ppermute | solution.py:387
  86.6 6.1 %shard_map.91 = (f32[1024,1024]{1,0:T(8,128)S(1)}, bf16[1024,1024]{1,0:T(8,128)(2,1)}) custom-call(s32[4]{0:T(128)S(1)} %pad_add_fusion.where, bf16[1024,1024]{1,0:T(8,128)(2,1)S(1)} %get-tuple-element.45.k_ref.a_ref, bf16[1024,1024]{1,0:T(8,128)(2,1)S(1)} %copy-done, bf16[1024,1024]{1,0:T(8,128)(2,1)S(1)} %get-tuple-element.62.c_ref.g_ref.b_ref, ...), custom_call_target="tpu_custom_call" | custom-call | flops 2147483648 | bytes 21474836 | tf_op jit(solution)/shard_map/pallas_call | solution.py:74
  92.7 0.3 collective-permute-done.21.refs_3_
  93.0 4.3 %shard_map.98 = (bf16[1024,1024]{1,0:T(8,128)(2,1)}, bf16[1024,1024]{1,0:T(8,128)(2,1)}) custom-call(s32[4]{0:T(128)S(1)} %pad_add_fusion.where, f32[1024,1024]{1,0:T(8,128)S(1)} %get-tuple-element.67.lk_ref, f32[1024,1024]{1,0:T(8,128)S(1)} %get-tuple-element.68.lv_ref, bf16[1024,1024]{1,0:T(8,128)(2,1)S(1)} %get-tuple-element.45.k_ref.a_ref, ...), custom_call_target="tpu_custom_call" | custom-call | flops 536870912 | bytes 5368709 | tf_op jit(solution)/shard_map/pallas_call | solution.py:74
  (18 shorter events, 0.2 us)
Async XLA Ops:
  0.7 37.6 %copy-start = (bf16[1024,1024]{1,0:T(8,128)(2,1)S(1)}, bf16[1024,1024]{1,0:T(8,128)(2,1)}, u32[]{:S(2)}) copy-start(bf16[1024,1024]{1,0:T(8,128)(2,1)} %c_ref.1) | copy-start | bytes 6291460
  5.8 6.5 %collective-permute-start = (f32[2,1,128,128]{3,2,1,0:T(8,128)S(1)}, f32[2,1,128,128]{3,2,1,0:T(8,128)S(1)}, u32[]{:S(2)}, u32[]{:S(2)}) collective-permute-start(f32[2,1,128,128]{3,2,1,0:T(8,128)S(1)} %get-tuple-element.48), channel_id=1, source_target_pairs={{0,1},{1,0},{2,3},{3,2},{4,5},{5,4},{6,7},{7,6},{8,9},{9,8},{10,11... | collective-permute-start | bytes 393224 | tf_op jit(solution)/shard_map/ppermute | solution.py:387
  8.9 6.4 %collective-permute-start.1 = (f32[2,1,128,128]{3,2,1,0:T(8,128)S(1)}, f32[2,1,128,128]{3,2,1,0:T(8,128)S(1)}, u32[]{:S(2)}, u32[]{:S(2)}) collective-permute-start(f32[2,1,128,128]{3,2,1,0:T(8,128)S(1)} %get-tuple-element.49), channel_id=1, source_target_pairs={{0,2},{1,3},{2,0},{3,1},{4,6},{5,7},{6,4},{7,5},{8,10},{9,11},{10,... | collective-permute-start | bytes 393224 | tf_op jit(solution)/shard_map/ppermute | solution.py:387
  10.4 6.0 %collective-permute-start.2 = (f32[2,1,128,128]{3,2,1,0:T(8,128)S(1)}, f32[2,1,128,128]{3,2,1,0:T(8,128)S(1)}, u32[]{:S(2)}, u32[]{:S(2)}) collective-permute-start(f32[2,1,128,128]{3,2,1,0:T(8,128)S(1)} %get-tuple-element.50), channel_id=1, source_target_pairs={{0,3},{1,2},{2,1},{3,0},{4,7},{5,6},{6,5},{7,4},{8,11},{9,10},{10,... | collective-permute-start | bytes 393224 | tf_op jit(solution)/shard_map/ppermute | solution.py:387
  17.0 1.3 %collective-permute-start.3 = (f32[1,128,128]{2,1,0:T(8,128)S(1)}, f32[1,128,128]{2,1,0:T(8,128)S(1)}, u32[]{:S(2)}, u32[]{:S(2)}) collective-permute-start(f32[1,128,128]{2,1,0:T(8,128)S(1)} %get-tuple-element.52), channel_id=1, source_target_pairs={{0,8},{1,9},{2,10},{3,11},{4,12},{5,13},{6,14},{7,15},{8,0},{9,1},... | collective-permute-start | bytes 196616 | tf_op jit(solution)/shard_map/ppermute | solution.py:387
  18.9 13.3 %collective-permute-start.5 = (f32[2,1,128,128]{3,2,1,0:T(8,128)S(1)}, f32[2,1,128,128]{3,2,1,0:T(8,128)S(1)}, u32[]{:S(2)}, u32[]{:S(2)}) collective-permute-start(f32[2,1,128,128]{3,2,1,0:T(8,128)S(1)} %get-tuple-element.53.pair_ref), channel_id=1, source_target_pairs={{0,4},{1,5},{2,6},{3,7},{4,0},{5,1},{6,2},{7,3},{8,12},{9,13},{10,... | collective-permute-start | bytes 393224 | tf_op jit(solution)/shard_map/ppermute | solution.py:387
  21.7 4.3 %collective-permute-start.6 = (f32[1,128,128]{2,1,0:T(8,128)S(1)}, f32[1,128,128]{2,1,0:T(8,128)S(1)}, u32[]{:S(2)}, u32[]{:S(2)}) collective-permute-start(f32[1,128,128]{2,1,0:T(8,128)S(1)} %get-tuple-element.54), channel_id=1, source_target_pairs={{0,16},{1,17},{2,18},{3,19},{4,20},{5,21},{6,22},{7,23},{8,24},{9,... | collective-permute-start | bytes 196616 | tf_op jit(solution)/shard_map/ppermute | solution.py:387
  23.2 8.9 %collective-permute-start.4 = (f32[1,128,128]{2,1,0:T(8,128)S(1)}, f32[1,128,128]{2,1,0:T(8,128)S(1)}, u32[]{:S(2)}, u32[]{:S(2)}) collective-permute-start(f32[1,128,128]{2,1,0:T(8,128)S(1)} %get-tuple-element.54), channel_id=1, source_target_pairs={{0,20},{1,21},{2,22},{3,23},{4,16},{5,17},{6,18},{7,19},{8,28},{9,... | collective-permute-start | bytes 196616 | tf_op jit(solution)/shard_map/ppermute | solution.py:387
  32.8 1.3 %collective-permute-start.7 = (f32[1,128,128]{2,1,0:T(8,128)S(1)}, f32[1,128,128]{2,1,0:T(8,128)S(1)}, u32[]{:S(2)}, u32[]{:S(2)}) collective-permute-start(f32[1,128,128]{2,1,0:T(8,128)S(1)} %get-tuple-element.56), channel_id=1, source_target_pairs={{0,8},{1,9},{2,10},{3,11},{4,12},{5,13},{6,14},{7,15},{8,0},{9,1},... | collective-permute-start | bytes 196616 | tf_op jit(solution)/shard_map/ppermute | solution.py:387
  34.7 9.6 %collective-permute-start.8 = (f32[2,1,128,128]{3,2,1,0:T(8,128)S(1)}, f32[2,1,128,128]{3,2,1,0:T(8,128)S(1)}, u32[]{:S(2)}, u32[]{:S(2)}) collective-permute-start(f32[2,1,128,128]{3,2,1,0:T(8,128)S(1)} %get-tuple-element.58), channel_id=1, source_target_pairs={{0,1},{1,0},{2,3},{3,2},{4,5},{5,4},{6,7},{7,6},{8,9},{9,8},{10,11... | collective-permute-start | bytes 393224 | tf_op jit(solution)/shard_map/ppermute | solution.py:387
  36.3 8.1 %collective-permute-start.9 = (f32[2,1,128,128]{3,2,1,0:T(8,128)S(1)}, f32[2,1,128,128]{3,2,1,0:T(8,128)S(1)}, u32[]{:S(2)}, u32[]{:S(2)}) collective-permute-start(f32[2,1,128,128]{3,2,1,0:T(8,128)S(1)} %get-tuple-element.59), channel_id=1, source_target_pairs={{0,2},{1,3},{2,0},{3,1},{4,6},{5,7},{6,4},{7,5},{8,10},{9,11},{10,... | collective-permute-start | bytes 393224 | tf_op jit(solution)/shard_map/ppermute | solution.py:387
  36.3 8.1 %collective-permute-start.10 = (f32[2,1,128,128]{3,2,1,0:T(8,128)S(1)}, f32[2,1,128,128]{3,2,1,0:T(8,128)S(1)}, u32[]{:S(2)}, u32[]{:S(2)}) collective-permute-start(f32[2,1,128,128]{3,2,1,0:T(8,128)S(1)} %get-tuple-element.60), channel_id=1, source_target_pairs={{0,3},{1,2},{2,1},{3,0},{4,7},{5,6},{6,5},{7,4},{8,11},{9,10},{10,... | collective-permute-start | bytes 393224 | tf_op jit(solution)/shard_map/ppermute | solution.py:387
  38.3 6.1 %copy-start.1 = (bf16[1024,1024]{1,0:T(8,128)(2,1)S(1)}, bf16[1024,1024]{1,0:T(8,128)(2,1)}, u32[]{:S(2)}) copy-start(bf16[1024,1024]{1,0:T(8,128)(2,1)} %dy_ref.1) | copy-start | bytes 6291460
  38.3 6.1 %copy-start.2 = (f32[1024]{0:T(1024)S(1)}, f32[1024]{0:T(1024)}, u32[]{:S(2)}) copy-start(f32[1024]{0:T(1024)} %param.8) | copy-start | bytes 12292
  51.0 6.0 %collective-permute-start.11 = (f32[2,1,128,128]{3,2,1,0:T(8,128)S(1)}, f32[2,1,128,128]{3,2,1,0:T(8,128)S(1)}, u32[]{:S(2)}, u32[]{:S(2)}) collective-permute-start(f32[2,1,128,128]{3,2,1,0:T(8,128)S(1)} %get-tuple-element.70), channel_id=1, source_target_pairs={{0,1},{1,0},{2,3},{3,2},{4,5},{5,4},{6,7},{7,6},{8,9},{9,8},{10,11... | collective-permute-start | bytes 393224 | tf_op jit(solution)/shard_map/ppermute | solution.py:387
  52.6 5.8 %collective-permute-start.12 = (f32[2,1,128,128]{3,2,1,0:T(8,128)S(1)}, f32[2,1,128,128]{3,2,1,0:T(8,128)S(1)}, u32[]{:S(2)}, u32[]{:S(2)}) collective-permute-start(f32[2,1,128,128]{3,2,1,0:T(8,128)S(1)} %get-tuple-element.71), channel_id=1, source_target_pairs={{0,2},{1,3},{2,0},{3,1},{4,6},{5,7},{6,4},{7,5},{8,10},{9,11},{10,... | collective-permute-start | bytes 393224 | tf_op jit(solution)/shard_map/ppermute | solution.py:387
  52.8 7.0 %collective-permute-start.13 = (f32[2,1,128,128]{3,2,1,0:T(8,128)S(1)}, f32[2,1,128,128]{3,2,1,0:T(8,128)S(1)}, u32[]{:S(2)}, u32[]{:S(2)}) collective-permute-start(f32[2,1,128,128]{3,2,1,0:T(8,128)S(1)} %get-tuple-element.72), channel_id=1, source_target_pairs={{0,3},{1,2},{2,1},{3,0},{4,7},{5,6},{6,5},{7,4},{8,11},{9,10},{10,... | collective-permute-start | bytes 393224 | tf_op jit(solution)/shard_map/ppermute | solution.py:387
  60.4 1.3 %collective-permute-start.14 = (f32[1,128,128]{2,1,0:T(8,128)S(1)}, f32[1,128,128]{2,1,0:T(8,128)S(1)}, u32[]{:S(2)}, u32[]{:S(2)}) collective-permute-start(f32[1,128,128]{2,1,0:T(8,128)S(1)} %get-tuple-element.74), channel_id=1, source_target_pairs={{0,8},{1,9},{2,10},{3,11},{4,12},{5,13},{6,14},{7,15},{8,0},{9,1},... | collective-permute-start | bytes 196616 | tf_op jit(solution)/shard_map/ppermute | solution.py:387
  62.3 10.9 %collective-permute-start.17 = (f32[1,128,128]{2,1,0:T(8,128)S(1)}, f32[1,128,128]{2,1,0:T(8,128)S(1)}, u32[]{:S(2)}, u32[]{:S(2)}) collective-permute-start(f32[1,128,128]{2,1,0:T(8,128)S(1)} %get-tuple-element.76), channel_id=1, source_target_pairs={{0,16},{1,17},{2,18},{3,19},{4,20},{5,21},{6,22},{7,23},{8,24},{9,... | collective-permute-start | bytes 196616 | tf_op jit(solution)/shard_map/ppermute | solution.py:387
  62.8 10.6 %collective-permute-start.15 = (f32[1,128,128]{2,1,0:T(8,128)S(1)}, f32[1,128,128]{2,1,0:T(8,128)S(1)}, u32[]{:S(2)}, u32[]{:S(2)}) collective-permute-start(f32[1,128,128]{2,1,0:T(8,128)S(1)} %get-tuple-element.76), channel_id=1, source_target_pairs={{0,20},{1,21},{2,22},{3,23},{4,16},{5,17},{6,18},{7,19},{8,28},{9,... | collective-permute-start | bytes 196616 | tf_op jit(solution)/shard_map/ppermute | solution.py:387
  66.6 9.0 %collective-permute-start.16 = (f32[2,1,128,128]{3,2,1,0:T(8,128)S(1)}, f32[2,1,128,128]{3,2,1,0:T(8,128)S(1)}, u32[]{:S(2)}, u32[]{:S(2)}) collective-permute-start(f32[2,1,128,128]{3,2,1,0:T(8,128)S(1)} %get-tuple-element.75.pair_ref), channel_id=1, source_target_pairs={{0,4},{1,5},{2,6},{3,7},{4,0},{5,1},{6,2},{7,3},{8,12},{9,13},{10,... | collective-permute-start | bytes 393224 | tf_op jit(solution)/shard_map/ppermute | solution.py:387
  76.2 6.2 %collective-permute-start.18 = (f32[1,128,128]{2,1,0:T(8,128)S(1)}, f32[1,128,128]{2,1,0:T(8,128)S(1)}, u32[]{:S(2)}, u32[]{:S(2)}) collective-permute-start(f32[1,128,128]{2,1,0:T(8,128)S(1)} %get-tuple-element.78), channel_id=1, source_target_pairs={{0,8},{1,9},{2,10},{3,11},{4,12},{5,13},{6,14},{7,15},{8,0},{9,1},... | collective-permute-start | bytes 196616 | tf_op jit(solution)/shard_map/ppermute | solution.py:387
  83.0 9.6 %collective-permute-start.19 = (f32[2,1,128,128]{3,2,1,0:T(8,128)S(1)}, f32[2,1,128,128]{3,2,1,0:T(8,128)S(1)}, u32[]{:S(2)}, u32[]{:S(2)}) collective-permute-start(f32[2,1,128,128]{3,2,1,0:T(8,128)S(1)} %get-tuple-element.80), channel_id=1, source_target_pairs={{0,1},{1,0},{2,3},{3,2},{4,5},{5,4},{6,7},{7,6},{8,9},{9,8},{10,11... | collective-permute-start | bytes 393224 | tf_op jit(solution)/shard_map/ppermute | solution.py:387
  84.5 8.2 %collective-permute-start.20 = (f32[2,1,128,128]{3,2,1,0:T(8,128)S(1)}, f32[2,1,128,128]{3,2,1,0:T(8,128)S(1)}, u32[]{:S(2)}, u32[]{:S(2)}) collective-permute-start(f32[2,1,128,128]{3,2,1,0:T(8,128)S(1)} %get-tuple-element.81), channel_id=1, source_target_pairs={{0,2},{1,3},{2,0},{3,1},{4,6},{5,7},{6,4},{7,5},{8,10},{9,11},{10,... | collective-permute-start | bytes 393224 | tf_op jit(solution)/shard_map/ppermute | solution.py:387
  85.0 8.0 %collective-permute-start.21 = (f32[2,1,128,128]{3,2,1,0:T(8,128)S(1)}, f32[2,1,128,128]{3,2,1,0:T(8,128)S(1)}, u32[]{:S(2)}, u32[]{:S(2)}) collective-permute-start(f32[2,1,128,128]{3,2,1,0:T(8,128)S(1)} %get-tuple-element.82), channel_id=1, source_target_pairs={{0,3},{1,2},{2,1},{3,0},{4,7},{5,6},{6,5},{7,4},{8,11},{9,10},{10,... | collective-permute-start | bytes 393224 | tf_op jit(solution)/shard_map/ppermute | solution.py:387

commit v3 on v2

v3 whole, which is shorter than its diff:
```python
import functools

import jax
import jax.numpy as jnp
from jax import lax
from jax.experimental import pallas as pl
from jax.experimental.pallas import tpu as pltpu
from jax.sharding import PartitionSpec as P


H = 8
HD = 128
BLOCK = 512
EPSILON = 1e-06
AXES = ("grp", "seq")
LANES = 2
QUAD = 4
SHARE = H // (LANES * QUAD)
TILE = 256
CUT = 256
SLAB = 256
ORDER = (3, 1, 2, 0)
EARLY = (0, 3)
UNROLL = 4
PAIR = 2
UNROLL_FINAL = 4
DEPTH = 2
F32 = jnp.float32
BF16 = jnp.bfloat16


def mm(a, b, ca, cb):
    return lax.dot_general(a, b, (((ca,), (cb,)), ((), ())), preferred_element_type=F32)


def vmem(*shape, dtype=F32):
    return pltpu.VMEM(shape, dtype)


def near(value):
    return pltpu.with_memory_space_constraint(value, pltpu.VMEM)


def far(value):
    return pltpu.with_memory_space_constraint(value, pltpu.HBM)


def call(kernel, out_shape, args, flops, scratch=(), grant=8, far_in=(), far_out=(), aliases=None):
    any_space = pl.BlockSpec(memory_space=pltpu.HBM)
    near_space = pl.BlockSpec(memory_space=pltpu.VMEM)
    in_specs = [pl.BlockSpec(memory_space=pltpu.SMEM)]
    in_specs += [any_space if i in far_in else near_space for i in range(len(args) - 1)]
    out_specs = [any_space if i in far_out else near_space for i in range(len(out_shape))]
    args = [args[0]] + [far(a) if i in far_in else near(a) for i, a in enumerate(args[1:])]
    return pl.pallas_call(
        kernel,
        out_shape=out_shape,
        in_specs=in_specs,
        out_specs=out_specs,
        scratch_shapes=scratch,
        input_output_aliases=aliases or {},
        compiler_params=pltpu.CompilerParams(vmem_limit_bytes=grant << 20),
        cost_estimate=pl.CostEstimate(flops=flops, bytes_accessed=flops // 100, transcendentals=0),
    )(*args)


def head_cols(head):
    return pl.ds(pl.multiple_of(head * HD, HD), HD)


def over_heads(step, unroll):
    def several(i, _):
        for j in range(unroll):
            step(i * unroll + j)
        return 0

    lax.fori_loop(0, H // unroll, several, 0)


def heads_of(slot, where):
    for lane in range(LANES):
        for share in range(SHARE):
            unit = (where[0] ^ lane) * QUAD + (where[1] ^ slot)
            yield lane, share, unit * SHARE + share


def slot_block(slot, reverse, where, block, blocks, a_ref, b_ref, piece_ref, inside_ref):
    rows = pl.ds(block * BLOCK, BLOCK)
    for lane, share, head in heads_of(slot, where):
        cols = head_cols(head)
        state = mm(a_ref[rows, cols], b_ref[rows, cols], 0, 0)
        if block == (blocks - 1 if reverse else 0):
            inside_ref[block, lane, share] = jnp.zeros_like(state)
            piece_ref[lane, share] = state
        else:
            run = piece_ref[lane, share]
            inside_ref[block, lane, share] = run
            piece_ref[lane, share] = run + state


def slot_kernel(slots, reverse, where, a_ref, b_ref, *outs):
    blocks = a_ref.shape[0] // BLOCK
    for i, slot in enumerate(slots):
        for block in reversed(range(blocks)) if reverse else range(blocks):
            slot_block(slot, reverse, where, block, blocks, a_ref, b_ref, *outs[2 * i : 2 * i + 2])


def slot_shapes(blocks):
    return [vmem(LANES, SHARE, HD, HD), vmem(blocks, LANES, SHARE, HD, HD)]


def slot_totals(slots, reverse, where, a, b):
    tokens, features = a.shape
    outs = call(
        functools.partial(slot_kernel, slots, reverse),
        slot_shapes(tokens // BLOCK) * len(slots),
        [where, a, b],
        2 * tokens * features // QUAD * len(slots) * HD,
    )
    return {slot: outs[2 * i : 2 * i + 2] for i, slot in enumerate(slots)}


def load_kernel(slot, where, k_far, v_far, piece_ref, inside_ref, k_ref, v_ref, sems):
    blocks = k_ref.shape[0] // BLOCK
    copies = []
    for block in range(blocks):
        rows = pl.ds(block * BLOCK, BLOCK)
        for j, (source, target) in enumerate(((k_far, k_ref), (v_far, v_ref))):
            copy = pltpu.make_async_copy(source.at[rows, :], target.at[rows, :], sems.at[block, j])
            copies.append(copy)
    for copy in copies[: 2 * DEPTH]:
        copy.start()
    for block in range(blocks):
        for j in range(2):
            copies[2 * block + j].wait()
            if block + DEPTH < blocks:
                copies[2 * (block + DEPTH) + j].start()
        slot_block(slot, False, where, block, blocks, k_ref, v_ref, piece_ref, inside_ref)


def load_totals(slot, where, keys, values):
    tokens, features = keys.shape
    blocks = tokens // BLOCK
    return call(
        functools.partial(load_kernel, slot),
        slot_shapes(blocks) + [vmem(tokens, features, dtype=BF16)] * 2,
        [where, keys, values],
        2 * tokens * features * HD,
        scratch=[pltpu.SemaphoreType.DMA((blocks, 2))],
        far_in=(0, 1),
    )


def triangle(size, upper=False):
    row = lax.broadcasted_iota(jnp.int32, (size, size), 0)
    col = lax.broadcasted_iota(jnp.int32, (size, size), 1)
    return row <= col if upper else row >= col


def over_units(count, step):
    def several(i, _):
        for j in range(UNROLL):
            unit = i * UNROLL + j
            step(unit // H, unit % H)
        return 0

    lax.fori_loop(0, count // UNROLL, several, 0)


def block_part(block, first, count):
    return pl.ds(pl.multiple_of(block * BLOCK + first * CUT, CUT), count * CUT)


def attend(block, cols, a_ref, b_ref, c_ref, mask, turned):
    tiles = BLOCK // CUT
    sums = [None] * tiles
    for j in range(tiles):
        first, count = (0, j + 1) if turned else (j, tiles - j)
        rows, here = block_part(block, first, count), block_part(block, j, 1)
        scores = mm(a_ref[rows, cols], b_ref[here, cols], 1, 1)
        at = (j - first) * CUT
        parts = [jnp.where(mask, scores[at : at + CUT], 0.0)]
        if at:
            parts.insert(0, scores[:at])
        if at + CUT < count * CUT:
            parts.append(scores[at + CUT :])
        scores = jnp.concatenate([part.astype(BF16) for part in parts], axis=0)
        product = mm(scores, c_ref[here, cols], 1, 0)
        for i in range(count):
            value = product[i * CUT : (i + 1) * CUT]
            sums[first + i] = value if sums[first + i] is None else sums[first + i] + value
    return sums


def local_kernel(where, q_ref, k_ref, v_ref, out_ref):
    mask = triangle(CUT)

    def step(block, head):
        cols = head_cols(head)
        sums = attend(block, cols, q_ref, k_ref, v_ref, mask, False)
        for i, value in enumerate(sums):
            out_ref[block_part(block, i, 1), cols] = value

    over_units(q_ref.shape[0] // BLOCK * H, step)


def local_part(where, queries, keys, values):
    tokens, features = queries.shape
    return call(
        local_kernel,
        [vmem(tokens, features)],
        [where, queries, keys, values],
        4 * tokens * BLOCK * features,
    )[0]


def scores_kernel(where, k_ref, q_ref, out_ref):
    mask = triangle(CUT, True)

    def step(block, head):
        cols = head_cols(head)
        for j in range(BLOCK // CUT):
            rows, here = block_part(block, 0, j + 1), block_part(block, j, 1)
            scores = mm(k_ref[rows, cols], q_ref[here, cols], 1, 1)
            to = pl.ds(j * CUT, CUT)
            out_ref[block, head, to, to] = jnp.where(mask, scores[j * CUT :], 0.0).astype(BF16)
            if j:
                out_ref[block, head, pl.ds(0, j * CUT), to] = scores[: j * CUT].astype(BF16)

    over_units(k_ref.shape[0] // BLOCK * H, step)


def turned_scores(where, keys, queries):
    tokens, features = keys.shape
    return call(
        scores_kernel,
        [vmem(tokens // BLOCK, H, BLOCK, BLOCK, dtype=BF16)],
        [where, keys, queries],
        2 * tokens * BLOCK * features,
    )[0]


def value_kernel(where, scores_ref, g_ref, ready_ref, out_ref, far_ref, sem):
    copy = pltpu.make_async_copy(ready_ref, far_ref, sem)
    copy.start()

    def step(block, head):
        cols = head_cols(head)
        tiles = BLOCK // CUT
        sums = [None] * tiles
        for j in range(tiles):
            rows = pl.ds(0, (j + 1) * CUT)
            scores = scores_ref[block, head, rows, pl.ds(j * CUT, CUT)]
            product = mm(scores, g_ref[block_part(block, j, 1), cols], 1, 0)
            for i in range(j + 1):
                value = product[i * CUT : (i + 1) * CUT]
                sums[i] = value if sums[i] is None else sums[i] + value
        for i, value in enumerate(sums):
            out_ref[block_part(block, i, 1), cols] = value

    over_units(g_ref.shape[0] // BLOCK * H, step)
    copy.wait()


def value_part(where, scores, grads, ready):
    tokens, features = grads.shape
    return call(
        value_kernel,
        [vmem(tokens, features), jax.ShapeDtypeStruct(ready.shape, ready.dtype)],
        [where, scores, grads, ready],
        2 * tokens * BLOCK * features,
        scratch=[pltpu.SemaphoreType.DMA(())],
        far_out=(1,),
    )


def attended_kernel(slot, first, where, carried_ref, inside_ref, local_ref, q_ref, dy_ref, gain_ref, *refs):
    if first:
        att_ref, square_ref, cross_ref, prior_ref = refs
    else:
        old_square, old_cross, att_ref, square_ref, cross_ref, prior_ref = refs
    blocks = q_ref.shape[0] // BLOCK
    for block in range(blocks):
        rows = pl.ds(block * BLOCK, BLOCK)
        square = None if first else old_square[rows, :]
        cross = None if first else old_cross[rows, :]
        for lane, share, head in heads_of(slot, where):
            cols = head_cols(head)
            prior = (carried_ref[lane, share] + inside_ref[block, lane, share]).astype(BF16)
            prior_ref[block, lane, share] = prior
            att = local_ref[rows, cols] + mm(q_ref[rows, cols], prior, 1, 0)
            att_ref[rows, cols] = att
            term = dy_ref[rows, cols].astype(F32) * gain_ref[:, cols] * att
            square = att * att if square is None else square + att * att
            cross = term if cross is None else cross + term
        square_ref[rows, :] = square
        cross_ref[rows, :] = cross


def attended_slot(slot, where, carried, inside, local, queries, cotangent, gain, sums):
    tokens, features = queries.shape
    blocks = tokens // BLOCK
    first = not sums
    return call(
        functools.partial(attended_kernel, slot, first),
        [vmem(tokens, features), vmem(tokens, HD), vmem(tokens, HD)]
        + [vmem(blocks, LANES, SHARE, HD, HD, dtype=BF16)],
        [where, carried, inside, local, queries, cotangent, gain, *sums],
        2 * tokens * features // QUAD * HD,
        aliases={3: 0},
    )


def norm_kernel(slots, where, *refs):
    count = len(slots)
    carried, inside = refs[:count], refs[count : 2 * count]
    local_ref, q_ref, dy_ref, gain_ref, old_square, old_cross = refs[2 * count : 2 * count + 6]
    outs = refs[2 * count + 6 :]
    att_ref, out_ref, grad_ref = outs[:3]
    priors, (piece_ref, later_ref, square_ref, cross_ref) = outs[3 : 3 + count], outs[3 + count :]
    blocks = q_ref.shape[0] // BLOCK
    features = H * HD
    for block in reversed(range(blocks)):
        rows = pl.ds(block * BLOCK, BLOCK)
        square, cross = old_square[rows, :], old_cross[rows, :]
        for i, slot in enumerate(slots):
            for lane, share, head in heads_of(slot, where):
                cols = head_cols(head)
                prior = (carried[i][lane, share] + inside[i][block, lane, share]).astype(BF16)
                priors[i][block, lane, share] = prior
                att = local_ref[rows, cols] + mm(q_ref[rows, cols], prior, 1, 0)
                att_ref[rows, cols] = att
                square += att * att
                cross += dy_ref[rows, cols].astype(F32) * gain_ref[:, cols] * att
        square_ref[...], cross_ref[...] = square, cross

        def step(i, _):
            here = pl.ds(pl.multiple_of(i * SLAB, SLAB), SLAB)
            rows = pl.ds(pl.multiple_of(block * BLOCK + i * SLAB, SLAB), SLAB)
            square = jnp.sum(square_ref[here, :], axis=1, keepdims=True) / features
            inverse = lax.rsqrt(square + EPSILON)
            mean = inverse * (jnp.sum(cross_ref[here, :], axis=1, keepdims=True) / features)
            for head in range(H):
                cols = pl.ds(head * HD, HD)
                unit = att_ref[rows, cols] * inverse
                gain = gain_ref[:, cols]
                out_ref[rows, cols] = (unit * gain).astype(BF16)
                scaled = dy_ref[rows, cols].astype(F32) * gain
                grad_ref[rows, cols] = (inverse * (scaled - unit * mean)).astype(BF16)
            return 0

        lax.fori_loop(0, BLOCK // SLAB, step, 0)
        slot_block(ORDER[0], True, where, block, blocks, q_ref, grad_ref, piece_ref, later_ref)


def norm(slots, where, carried, inside, attended, queries, cotangent, gain, sums):
    tokens, features = attended.shape
    blocks = tokens // BLOCK
    half = vmem(tokens, features, dtype=BF16)
    prior = vmem(blocks, LANES, SHARE, HD, HD, dtype=BF16)
    carried, inside = [carried[o] for o in slots], [inside[o] for o in slots]
    _, normed, grads, *outs = call(
        functools.partial(norm_kernel, slots),
        [vmem(tokens, features), half, half] + [prior] * len(slots) + slot_shapes(blocks),
        [where, *carried, *inside, attended, queries, cotangent, gain, *sums],
        20 * tokens * features,
        scratch=[vmem(BLOCK, HD)] * 2,
        aliases={1 + 2 * len(slots): 0},
    )
    return normed, grads, outs[: len(slots)], outs[len(slots) :]


def query_kernel(where, g_ref, v_ref, k_ref, *refs):
    priors, (out_ref, prior_ref) = refs[:QUAD], refs[QUAD:]
    mask = triangle(CUT)
    prior_ref[...] = jnp.zeros_like(prior_ref)
    for slot in range(QUAD):
        for lane, share, head in heads_of(slot, where):
            cols = head_cols(head % PAIR)
            for block in range(prior_ref.shape[0]):
                prior_ref[block, head // PAIR, cols, cols] = priors[slot][block, lane, share]

    def step(block, pair):
        wide = pl.ds(pl.multiple_of(pair * PAIR * HD, PAIR * HD), PAIR * HD)
        rows = block_part(block, 0, BLOCK // CUT)
        far_part = mm(g_ref[rows, wide], prior_ref[block, pair], 1, 1)
        for j in range(PAIR):
            cols = head_cols(pair * PAIR + j)
            sums = attend(block, cols, g_ref, v_ref, k_ref, mask, False)
            for i, value in enumerate(sums):
                value += far_part[i * CUT : (i + 1) * CUT, j * HD : (j + 1) * HD]
                out_ref[block_part(block, i, 1), cols] = value.astype(BF16)

    def several(i, _):
        for j in range(UNROLL // PAIR):
            unit = i * (UNROLL // PAIR) + j
            step(unit // (H // PAIR), unit % (H // PAIR))
        return 0

    lax.fori_loop(0, g_ref.shape[0] // BLOCK * H // UNROLL, several, 0)


def query_part(where, grads, values, keys, priors):
    tokens, features = grads.shape
    return call(
        query_kernel,
        [vmem(tokens, features, dtype=BF16)],
        [where, grads, values, keys, *priors],
        4 * tokens * BLOCK * features,
        scratch=[vmem(tokens // BLOCK, H // PAIR, PAIR * HD, PAIR * HD, dtype=BF16)],
    )[0]


def turned_kernel(where, a_ref, b_ref, c_ref, ready_ref, out_ref, far_ref, sem):
    copy = pltpu.make_async_copy(ready_ref, far_ref, sem)
    copy.start()
    mask = triangle(CUT, True)

    def step(block, head):
        cols = head_cols(head)
        sums = attend(block, cols, a_ref, b_ref, c_ref, mask, True)
        for i, value in enumerate(sums):
            out_ref[block_part(block, i, 1), cols] = value

    over_units(a_ref.shape[0] // BLOCK * H, step)
    copy.wait()


def turned_part(where, a, b, c, ready):
    tokens, features = a.shape
    return call(
        turned_kernel,
        [vmem(tokens, features), jax.ShapeDtypeStruct(ready.shape, ready.dtype)],
        [where, a, b, c, ready],
        4 * tokens * BLOCK * features,
        scratch=[pltpu.SemaphoreType.DMA(())],
        far_out=(1,),
    )


def final_kernel(where, lk_ref, lv_ref, k_ref, v_ref, *refs):
    carried, later = refs[:QUAD], refs[QUAD : 2 * QUAD]
    gk_far, gv_far, gk_ref, gv_ref, state_ref, sems = refs[2 * QUAD :]
    for slot in range(QUAD):
        for lane, share, head in heads_of(slot, where):
            for b in range(k_ref.shape[0] // BLOCK):
                state = carried[slot][lane, share] + later[slot][b, lane, share]
                state_ref[b, head] = state.astype(BF16)

    copies = []
    for i in range(k_ref.shape[0] // TILE):
        rows = pl.ds(i * TILE, TILE)
        block = i // (BLOCK // TILE)

        def one(head):
            cols = head_cols(head)
            state = state_ref[block, head]
            gk_ref[rows, cols] = (lk_ref[rows, cols] + mm(v_ref[rows, cols], state, 1, 1)).astype(BF16)
            gv_ref[rows, cols] = (lv_ref[rows, cols] + mm(k_ref[rows, cols], state, 1, 0)).astype(BF16)

        over_heads(one, UNROLL_FINAL)
        for j, (source, target) in enumerate(((gk_ref, gk_far), (gv_ref, gv_far))):
            copy = pltpu.make_async_copy(source.at[rows, :], target.at[rows, :], sems.at[i, j])
            copy.start()
            copies.append(copy)
    for copy in copies:
        copy.wait()


def final_part(where, local_k, local_v, keys, values, carried, later):
    tokens, features = keys.shape
    blocks = tokens // BLOCK
    return call(
        final_kernel,
        [jax.ShapeDtypeStruct((tokens, features), BF16)] * 2,
        [where, local_k, local_v, keys, values, *carried, *later],
        4 * tokens * features * HD,
        scratch=[
            vmem(tokens, features, dtype=BF16),
            vmem(tokens, features, dtype=BF16),
            vmem(blocks, H, HD, HD, dtype=BF16),
            pltpu.SemaphoreType.DMA((tokens // TILE, 2)),
        ],
        far_out=(0, 1),
        grant=12,
    )


def moved(value, move):
    groups, shards = lax.axis_size("grp"), lax.axis_size("seq")
    pairs = []
    for g in range(groups):
        for s in range(shards):
            to_g, to_s = move(g, s)
            pairs.append((g * shards + s, to_g * shards + to_s))
    return lax.ppermute(value, AXES, pairs)


def sum_kernel(where, *refs):
    held, (mine_ref, rest_ref) = refs[:QUAD], refs[QUAD:]
    for lane, out in enumerate((mine_ref, rest_ref)):
        out[...] = (held[0][lane] + held[1][lane]) + (held[2][lane] + held[3][lane])


def both_kernel(where, mine_ref, other_ref, both_ref):
    both_ref[...] = mine_ref[...] + other_ref[...]


def before(a, b, reverse):
    return a > b if reverse else a < b


def base_kernel(near_shifts, far_shifts, counts, reverse, where, mine_ref, other_ref, *refs):
    refs = list(refs)
    lane, row, far_row = where[0], where[2], where[3]
    takes = lane == (0 if reverse else 1)
    sum_mine = jnp.where(takes, other_ref[...], 0.0)
    sum_other = jnp.where(takes, 0.0, mine_ref[...])
    near_mine = [refs.pop(0) for _ in near_shifts]
    near_other = [refs.pop(0) for _ in near_shifts]
    for df, mine, other in zip(near_shifts, near_mine, near_other):
        near_by = before(lax.rem(far_row - df + counts[1], counts[1]), far_row, reverse)
        mine, other = mine[...], other[...]
        sum_mine += jnp.where(near_by, mine, 0.0) + jnp.where(takes, other, 0.0)
        sum_other += jnp.where(near_by, other, 0.0) + jnp.where(takes, 0.0, mine)
    for dr, _ in far_shifts:
        source = lax.rem(row - dr + counts[0], counts[0])
        add = jnp.where(before(source, row, reverse), refs.pop(0)[...], 0.0)
        sum_mine, sum_other = sum_mine + add, sum_other + add
    refs[0][...], refs[1][...] = sum_mine, sum_other


def back_sum_kernel(reverse, where, mine_ref, other_ref, *refs):
    held, back = refs[:QUAD], refs[QUAD:]
    quad = where[1]
    for lane, base in enumerate((mine_ref, other_ref)):
        for o in range(QUAD):
            value = base[...]
            for i in range(QUAD):
                if i != o:
                    near_by = before(quad ^ i, quad ^ o, reverse)
                    value += jnp.where(near_by, held[i][lane], 0.0)
            back[o][lane] = value


def far_shifts_of(counts):
    shifts = [(dr, df) for dr in range(1, counts[0]) for df in range(counts[1])]
    return sorted(shifts, key=lambda shift: -sum(shift))


def carry(where, first, rest, reverse):
    counts = lax.axis_size("grp") // LANES, lax.axis_size("seq") // QUAD
    one, two = vmem(SHARE, HD, HD), vmem(LANES, SHARE, HD, HD)

    def swap_quad(o):
        return lambda g, s: (g, s ^ o)

    def swap_lane(g, s):
        return g ^ 1, s

    def shift(dr, df):
        return lambda g, s: (
            (g // LANES + dr) % counts[0] * LANES + g % LANES,
            (s // QUAD + df) % counts[1] * QUAD + s % QUAD,
        )

    held, inside = [None] * QUAD, [None] * QUAD
    held[ORDER[0]], inside[ORDER[0]] = first
    held[ORDER[0]] = moved(held[ORDER[0]], swap_quad(ORDER[0]))
    rest = slot_totals(ORDER[1:], reverse, where, *rest)
    for o in ORDER[1:]:
        held[o], inside[o] = rest[o]
        if o:
            held[o] = moved(held[o], swap_quad(o))
    mine, rest = call(sum_kernel, [one, one], [where, *held], 1000, grant=2)
    near_shifts, far_shifts = range(1, counts[1]), far_shifts_of(counts)
    came_mine, came_other, came_both = [], [], []
    for df in near_shifts:
        came_mine.append(moved(mine, shift(0, df)))
    other = moved(rest, swap_lane)
    for df in near_shifts:
        came_other.append(moved(other, shift(0, df)))
    both = call(both_kernel, [one], [where, mine, other], 1000, grant=2)[0]
    for dr, df in far_shifts:
        came_both.append(moved(both, shift(dr, df)))
    kernel = functools.partial(base_kernel, near_shifts, far_shifts, counts, reverse)
    args = [where, mine, other, *came_mine, *came_other, *came_both]
    sum_mine, sum_other = call(kernel, [one, one], args, 1000, grant=2)
    other = moved(sum_other, swap_lane)
    kernel = functools.partial(back_sum_kernel, reverse)
    back = call(kernel, [two] * QUAD, [where, sum_mine, other, *held], 1000, grant=2)
    result = [back[0]] + [None] * (QUAD - 1)
    for o in ORDER[:-1]:
        result[o] = moved(back[o], swap_quad(o))
    return result, inside


def body(queries, key_rows, value_rows, norm_gain, cotangent):
    grp, seq = lax.axis_index("grp"), lax.axis_index("seq")
    parts = [grp % LANES, seq % QUAD, grp // LANES, seq // QUAD]
    where = jnp.stack(parts).astype(jnp.int32)
    gain = norm_gain[None, :]
    *first, keys, values = load_totals(ORDER[0], where, key_rows, value_rows)
    queries, cotangent = near(queries), near(cotangent)
    carried, inside = carry(where, first, (keys, values), False)
    attended = local_part(where, queries, keys, values)
    scores = turned_scores(where, keys, queries)
    priors, sums = [None] * QUAD, []
    for o in EARLY:
        attended, *sums, priors[o] = attended_slot(
            o, where, carried[o], inside[o], attended, queries, cotangent, gain, sums
        )
    late = [o for o in ORDER if o not in EARLY]
    normed, grads, late_priors, first = norm(
        late, where, carried, inside, attended, queries, cotangent, gain, sums
    )
    for o, prior in zip(late, late_priors):
        priors[o] = prior
    carried, later = carry(where, first, (queries, grads), True)
    local_v, normed = value_part(where, scores, grads, normed)
    grad_q = query_part(where, grads, values, keys, priors)
    local_k, grad_q = turned_part(where, values, grads, queries, grad_q)
    grad_k, grad_v = final_part(where, local_k, local_v, keys, values, carried, later)
    return normed, grad_q, grad_k, grad_v


def solution(mesh):
    rows = P(AXES, None)
    return jax.shard_map(
        body,
        mesh=mesh,
        in_specs=(rows, rows, rows, P(), rows),
        out_specs=(rows, rows, rows, rows),
        check_vma=False,
    )
```

time: 97.6 us -> 96.2 us (0.986)
  waiting for transfers between devices: 26.5 us -> 20.1 us
  starting transfers between devices: 24.5 us -> 30.1 us
    ppermute x22 -> x24, waiting for transfers between devices: 26.5 us -> 20.1 us  [moved(): return lax.ppermute(value, AXES, pairs)]
    ppermute x22 -> x24, starting transfers between devices: 24.5 us -> 30.1 us  [moved(): return lax.ppermute(value, AXES, pairs)]
    pallas_call x15 -> x20, Pallas kernels: 45.3 us -> 44.7 us  [call(): pl.pallas_call(kernel, out_shape=out_shape, in_specs=in_specs, out_specs=...]
  transfers between devices with their start and end apart: 22 -> 24, of which waited for: 14 -> 11; matrix products, arithmetic and copies ran while one was open for 0% -> 0% of each run, Pallas kernels for 25% -> 27%
where the time goes in v3:
time: 96.2 us; the launch traced here: 96 us
  Pallas kernels  44.7 us (46%)
  starting transfers between devices  30.1 us (31%)
  waiting for transfers between devices  20.1 us (21%)
  between operations  1.1 us (1%)
    pallas_call x20, Pallas kernels, call(): pl.pallas_call(kernel, out_shape=out_shape, in_specs=in_specs, out_specs=...  44.7 us
    ppermute x24, starting transfers between devices, moved(): return lax.ppermute(value, AXES, pairs)  30.1 us
    ppermute x24, waiting for transfers between devices, moved(): return lax.ppermute(value, AXES, pairs)  20.1 us
  transfers between devices with their start and end apart: 24, of which 11 were waited for; matrix products, arithmetic and copies ran while one was open for 0% of the time, Pallas kernels for 27%

profile of v3, /device:TPU:0, one launch (start us, length us, event | category | flops | bytes accessed | tf_op | source)
XLA Modules:
  0.0 96.0 jit_solution(255201292983885268)
XLA Ops:
  0.7 3.1 %shard_map.84 = (f32[2,1,128,128]{3,2,1,0:T(8,128)S(1)}, f32[2,2,1,128,128]{4,3,2,1,0:T(8,128)S(1)}, bf16[1024,1024]{1,0:T(8,128)(2,1)S(1)}, bf16[1024,1024]{1,0:T(8,128)(2,1)S(1)}) custom-call(s32[4]{0:T(128)S(1)} %pad_add_fusion.where, bf16[1024,1024]{1,0:T(8,128)(2,1)} %k_far.1, bf16[1024,1024]{1,0:T(8,128)(2,1)} %v_far.1), custom_call_target="tpu_custom_call" | custom-call | flops 268435456 | bytes 2684354 | tf_op jit(solution)/shard_map/pallas_call | solution.py:55
  3.8 1.8 %shard_map.86 = (f32[2,1,128,128]{3,2,1,0:T(8,128)S(1)}, f32[2,2,1,128,128]{4,3,2,1,0:T(8,128)S(1)}, f32[2,1,128,128]{3,2,1,0:T(8,128)S(1)}, f32[2,2,1,128,128]{...) custom-call(s32[4]{0:T(128)S(1)} %pad_add_fusion.where, ...), custom_call_target="tpu_custom_call" | custom-call | flops 201326592 | bytes 2013265 | tf_op jit(solution)/shard_map/pallas_call | solution.py:55
  5.6 3.0 %collective-permute-start = (f32[2,1,128,128]{3,2,1,0:T(8,128)S(1)}, f32[2,1,128,128]{3,2,1,0:T(8,128)S(1)}, u32[]{:S(2)}, u32[]{:S(2)}) collective-permute-start(f32[2,1,128,128]{3,2,1,0:T(8,128)S(1)} %get-tuple-element.59), channel_id=1, source_target_pairs={{0,1},{1,0},{2,3},{3,2},{4,5},{5,4},{6,7},{7,6},{8,9},{9,8},{10,11... | collective-permute-start | bytes 393224 | tf_op jit(solution)/shard_map/ppermute | solution.py:496
  8.6 1.6 %collective-permute-start.1 = (f32[2,1,128,128]{3,2,1,0:T(8,128)S(1)}, f32[2,1,128,128]{3,2,1,0:T(8,128)S(1)}, u32[]{:S(2)}, u32[]{:S(2)}) collective-permute-start(f32[2,1,128,128]{3,2,1,0:T(8,128)S(1)} %get-tuple-element.60), channel_id=1, source_target_pairs={{0,2},{1,3},{2,0},{3,1},{4,6},{5,7},{6,4},{7,5},{8,10},{9,11},{10,... | collective-permute-start | bytes 393224 | tf_op jit(solution)/shard_map/ppermute | solution.py:496
  10.2 1.9 %collective-permute-done.refs_1_ = f32[2,1,128,128]{3,2,1,0:T(8,128)S(1)} collective-permute-done((f32[2,1,128,128]{3,2,1,0:T(8,128)S(1)}, f32[2,1,128,128]{3,2,1,0:T(8,128)S(1)}, u32[]{:S(2)}, u32[]{:S(2)}) %collective-permute-start) | collective-permute-done | bytes 131104 | tf_op jit(solution)/shard_map/ppermute | solution.py:496
  12.1 2.9 %collective-permute-done.1.refs_2_ = f32[2,1,128,128]{3,2,1,0:T(8,128)S(1)} collective-permute-done((f32[2,1,128,128]{3,2,1,0:T(8,128)S(1)}, f32[2,1,128,128]{3,2,1,0:T(8,128)S(1)}, u32[]{:S(2)}, u32[]{:S(2)}) %collective-permute-start.1) | collective-permute-done | bytes 131104 | tf_op jit(solution)/shard_map/ppermute | solution.py:496
  15.0 1.2 %collective-permute-done.2.refs_3_ = f32[2,1,128,128]{3,2,1,0:T(8,128)S(1)} collective-permute-done((f32[2,1,128,128]{3,2,1,0:T(8,128)S(1)}, f32[2,1,128,128]{3,2,1,0:T(8,128)S(1)}, u32[]{:S(2)}, u32[]{:S(2)}) %collective-permute-start.2) | collective-permute-done | bytes 131104 | tf_op jit(solution)/shard_map/ppermute | solution.py:496
  16.2 0.6 shard_map.87
  16.8 2.8 %collective-permute-start.4 = (f32[1,128,128]{2,1,0:T(8,128)S(1)}, f32[1,128,128]{2,1,0:T(8,128)S(1)}, u32[]{:S(2)}, u32[]{:S(2)}) collective-permute-start(f32[1,128,128]{2,1,0:T(8,128)S(1)} %get-tuple-element.62.mine_ref), channel_id=1, source_target_pairs={{0,4},{1,5},{2,6},{3,7},{4,0},{5,1},{6,2},{7,3},{8,12},{9,13},{10,... | collective-permute-start | bytes 196616 | tf_op jit(solution)/shard_map/ppermute | solution.py:496
  19.7 1.2 %collective-permute-start.5 = (f32[1,128,128]{2,1,0:T(8,128)S(1)}, f32[1,128,128]{2,1,0:T(8,128)S(1)}, u32[]{:S(2)}, u32[]{:S(2)}) collective-permute-start(f32[1,128,128]{2,1,0:T(8,128)S(1)} %collective-permute-done.3.other_ref), channel_id=1, source_target_pairs={{0,4},{1,5},{2,6},{3,7},{4,0},{5,1},{6,2},{7,3},{8,12},{9,13},{10,... | collective-permute-start | bytes 196616 | tf_op jit(solution)/shard_map/ppermute | solution.py:496
  20.9 0.5 shard_map.88
  21.4 2.8 %collective-permute-start.6 = (f32[1,128,128]{2,1,0:T(8,128)S(1)}, f32[1,128,128]{2,1,0:T(8,128)S(1)}, u32[]{:S(2)}, u32[]{:S(2)}) collective-permute-start(f32[1,128,128]{2,1,0:T(8,128)S(1)} %shard_map.88), channel_id=1, source_target_pairs={{0,20},{1,21},{2,22},{3,23},{4,16},{5,17},{6,18},{7,19},{8,28},{9,... | collective-permute-start | bytes 196616 | tf_op jit(solution)/shard_map/ppermute | solution.py:496
  24.2 0.5 collective-permute-start.7
  24.7 3.0 %collective-permute-done.5.refs_1_ = f32[1,128,128]{2,1,0:T(8,128)S(1)} collective-permute-done((f32[1,128,128]{2,1,0:T(8,128)S(1)}, f32[1,128,128]{2,1,0:T(8,128)S(1)}, u32[]{:S(2)}, u32[]{:S(2)}) %collective-permute-start.5) | collective-permute-done | bytes 65568 | tf_op jit(solution)/shard_map/ppermute | solution.py:496
  27.7 2.7 %collective-permute-done.6.refs_2_ = f32[1,128,128]{2,1,0:T(8,128)S(1)} collective-permute-done((f32[1,128,128]{2,1,0:T(8,128)S(1)}, f32[1,128,128]{2,1,0:T(8,128)S(1)}, u32[]{:S(2)}, u32[]{:S(2)}) %collective-permute-start.6) | collective-permute-done | bytes 65568 | tf_op jit(solution)/shard_map/ppermute | solution.py:496
  30.4 0.6 shard_map.89
  31.1 1.2 %collective-permute-done.8.other_ref = f32[1,128,128]{2,1,0:T(8,128)S(1)} collective-permute-done((f32[1,128,128]{2,1,0:T(8,128)S(1)}, f32[1,128,128]{2,1,0:T(8,128)S(1)}, u32[]{:S(2)}, u32[]{:S(2)}) %collective-permute-start.8) | collective-permute-done | bytes 65568 | tf_op jit(solution)/shard_map/ppermute | solution.py:496
  32.3 0.7 shard_map.90
  33.0 1.5 %collective-permute-start.9 = (f32[2,1,128,128]{3,2,1,0:T(8,128)S(1)}, f32[2,1,128,128]{3,2,1,0:T(8,128)S(1)}, u32[]{:S(2)}, u32[]{:S(2)}) collective-permute-start(f32[2,1,128,128]{3,2,1,0:T(8,128)S(1)} %get-tuple-element.66), channel_id=1, source_target_pairs={{0,1},{1,0},{2,3},{3,2},{4,5},{5,4},{6,7},{7,6},{8,9},{9,8},{10,11... | collective-permute-start | bytes 393224 | tf_op jit(solution)/shard_map/ppermute | solution.py:496
  34.5 2.0 %collective-permute-start.11 = (f32[2,1,128,128]{3,2,1,0:T(8,128)S(1)}, f32[2,1,128,128]{3,2,1,0:T(8,128)S(1)}, u32[]{:S(2)}, u32[]{:S(2)}) collective-permute-start(f32[2,1,128,128]{3,2,1,0:T(8,128)S(1)} %get-tuple-element.70), channel_id=1, source_target_pairs={{0,3},{1,2},{2,1},{3,0},{4,7},{5,6},{6,5},{7,4},{8,11},{9,10},{10,... | collective-permute-start | bytes 393224 | tf_op jit(solution)/shard_map/ppermute | solution.py:496
  36.5 5.1 %shard_map.91.local_ref = f32[1024,1024]{1,0:T(8,128)S(1)} custom-call(s32[4]{0:T(128)S(1)} %pad_add_fusion.where, bf16[1024,1024]{1,0:T(8,128)(2,1)S(1)} %copy-done, bf16[1024,1024]{1,0:T(8,128)(2,1)S(1)} %get-tuple-element.56.k_ref.a_ref, bf16[1024,1024]{1,0:T(8,128)(2,1)S(1)} %get-tuple-element.57.b_ref.v_ref.a_ref), custom_call_target="tpu_custom_call" | custom-call | flops 2147483648 | bytes 21474836 | tf_op jit(solution)/shard_map/pallas_call | solution.py:55
  41.7 1.4 %shard_map.92 = (f32[1024,1024]{1,0:T(8,128)S(1)}, f32[1024,128]{1,0:T(8,128)S(1)}, f32[1024,128]{1,0:T(8,128)S(1)}, bf16[2,2,1,128,128]{4,3,2,1,0:T(8,128)(2,1)S(1)}) custom-call(s32[4]{0:T(128)S(1)} %pad_add_fusion.where, f32[2,1,128,128]{3,2,1,0:T(8,128)S(1)} %get-tuple-element.72.carried_ref, ...), custom_call_target="tpu_custom_call", output_to_operand_aliasing={{0}: (3, {})} | custom-call | flops 67108864 | bytes 671088 | tf_op jit(solution)/shard_map/pallas_call | solution.py:55
  43.1 1.4 %shard_map.93 = (f32[1024,1024]{1,0:T(8,128)S(1)}, f32[1024,128]{1,0:T(8,128)S(1)}, f32[1024,128]{1,0:T(8,128)S(1)}, bf16[2,2,1,128,128]{4,3,2,1,0:T(8,128)(2,1)S(1)}) custom-call(s32[4]{0:T(128)S(1)} %pad_add_fusion.where, f32[2,1,128,128]{3,2,1,0:T(8,128)S(1)} %collective-permute-done.11.carried_ref, ...), custom_call_target="tpu_custom_call", output_to_operand_aliasing={{0}: (3, {})} | custom-call | flops 67108864 | bytes 671088 | tf_op jit(solution)/shard_map/pallas_call | solution.py:55
  44.5 4.1 %shard_map.94 = (f32[1024,1024]{1,0:T(8,128)S(1)}, bf16[1024,1024]{1,0:T(8,128)(2,1)S(1)}, bf16[1024,1024]{1,0:T(8,128)(2,1)S(1)}, bf16[2,2,1,128,128]{4,3,2,1,0...) custom-call(s32[4]{0:T(128)S(1)} %pad_add_fusion.where, ...), custom_call_target="tpu_custom_call", output_to_operand_aliasing={{0}: (5, {})} | custom-call | flops 20971520 | bytes 209715 | tf_op jit(solution)/shard_map/pallas_call | solution.py:55
  48.6 1.7 %shard_map.98 = (f32[2,1,128,128]{3,2,1,0:T(8,128)S(1)}, f32[2,2,1,128,128]{4,3,2,1,0:T(8,128)S(1)}, f32[2,1,128,128]{3,2,1,0:T(8,128)S(1)}, f32[2,2,1,128,128]{...) custom-call(s32[4]{0:T(128)S(1)} %pad_add_fusion.where, ...), custom_call_target="tpu_custom_call" | custom-call | flops 201326592 | bytes 2013265 | tf_op jit(solution)/shard_map/pallas_call | solution.py:55
  50.4 1.5 %collective-permute-start.12 = (f32[2,1,128,128]{3,2,1,0:T(8,128)S(1)}, f32[2,1,128,128]{3,2,1,0:T(8,128)S(1)}, u32[]{:S(2)}, u32[]{:S(2)}) collective-permute-start(f32[2,1,128,128]{3,2,1,0:T(8,128)S(1)} %get-tuple-element.91), channel_id=1, source_target_pairs={{0,1},{1,0},{2,3},{3,2},{4,5},{5,4},{6,7},{7,6},{8,9},{9,8},{10,11... | collective-permute-start | bytes 393224 | tf_op jit(solution)/shard_map/ppermute | solution.py:496
  51.9 2.0 %collective-permute-start.14 = (f32[2,1,128,128]{3,2,1,0:T(8,128)S(1)}, f32[2,1,128,128]{3,2,1,0:T(8,128)S(1)}, u32[]{:S(2)}, u32[]{:S(2)}) collective-permute-start(f32[2,1,128,128]{3,2,1,0:T(8,128)S(1)} %get-tuple-element.93), channel_id=1, source_target_pairs={{0,3},{1,2},{2,1},{3,0},{4,7},{5,6},{6,5},{7,4},{8,11},{9,10},{10,... | collective-permute-start | bytes 393224 | tf_op jit(solution)/shard_map/ppermute | solution.py:496
  53.9 2.5 %collective-permute-done.12.refs_1_ = f32[2,1,128,128]{3,2,1,0:T(8,128)S(1)} collective-permute-done((f32[2,1,128,128]{3,2,1,0:T(8,128)S(1)}, f32[2,1,128,128]{3,2,1,0:T(8,128)S(1)}, u32[]{:S(2)}, u32[]{:S(2)}) %collective-permute-start.12) | collective-permute-done | bytes 131104 | tf_op jit(solution)/shard_map/ppermute | solution.py:496
  56.4 1.4 %collective-permute-done.13.refs_2_ = f32[2,1,128,128]{3,2,1,0:T(8,128)S(1)} collective-permute-done((f32[2,1,128,128]{3,2,1,0:T(8,128)S(1)}, f32[2,1,128,128]{3,2,1,0:T(8,128)S(1)}, u32[]{:S(2)}, u32[]{:S(2)}) %collective-permute-start.13) | collective-permute-done | bytes 131104 | tf_op jit(solution)/shard_map/ppermute | solution.py:496
  57.8 1.4 %collective-permute-done.14.refs_3_ = f32[2,1,128,128]{3,2,1,0:T(8,128)S(1)} collective-permute-done((f32[2,1,128,128]{3,2,1,0:T(8,128)S(1)}, f32[2,1,128,128]{3,2,1,0:T(8,128)S(1)}, u32[]{:S(2)}, u32[]{:S(2)}) %collective-permute-start.14) | collective-permute-done | bytes 131104 | tf_op jit(solution)/shard_map/ppermute | solution.py:496
  59.2 0.6 shard_map.99
  59.8 2.8 %collective-permute-start.16 = (f32[1,128,128]{2,1,0:T(8,128)S(1)}, f32[1,128,128]{2,1,0:T(8,128)S(1)}, u32[]{:S(2)}, u32[]{:S(2)}) collective-permute-start(f32[1,128,128]{2,1,0:T(8,128)S(1)} %get-tuple-element.94.mine_ref), channel_id=1, source_target_pairs={{0,4},{1,5},{2,6},{3,7},{4,0},{5,1},{6,2},{7,3},{8,12},{9,13},{10,... | collective-permute-start | bytes 196616 | tf_op jit(solution)/shard_map/ppermute | solution.py:496
  62.6 0.5 shard_map.100
  63.1 1.2 %collective-permute-start.18 = (f32[1,128,128]{2,1,0:T(8,128)S(1)}, f32[1,128,128]{2,1,0:T(8,128)S(1)}, u32[]{:S(2)}, u32[]{:S(2)}) collective-permute-start(f32[1,128,128]{2,1,0:T(8,128)S(1)} %shard_map.100), channel_id=1, source_target_pairs={{0,20},{1,21},{2,22},{3,23},{4,16},{5,17},{6,18},{7,19},{8,28},{9,... | collective-permute-start | bytes 196616 | tf_op jit(solution)/shard_map/ppermute | solution.py:496
  64.3 1.5 %collective-permute-start.19 = (f32[1,128,128]{2,1,0:T(8,128)S(1)}, f32[1,128,128]{2,1,0:T(8,128)S(1)}, u32[]{:S(2)}, u32[]{:S(2)}) collective-permute-start(f32[1,128,128]{2,1,0:T(8,128)S(1)} %shard_map.100), channel_id=1, source_target_pairs={{0,16},{1,17},{2,18},{3,19},{4,20},{5,21},{6,22},{7,23},{8,24},{9,... | collective-permute-start | bytes 196616 | tf_op jit(solution)/shard_map/ppermute | solution.py:496
  65.8 1.8 %collective-permute-start.17 = (f32[1,128,128]{2,1,0:T(8,128)S(1)}, f32[1,128,128]{2,1,0:T(8,128)S(1)}, u32[]{:S(2)}, u32[]{:S(2)}) collective-permute-start(f32[1,128,128]{2,1,0:T(8,128)S(1)} %collective-permute-done.15.other_ref), channel_id=1, source_target_pairs={{0,4},{1,5},{2,6},{3,7},{4,0},{5,1},{6,2},{7,3},{8,12},{9,13},{10,... | collective-permute-start | bytes 196616 | tf_op jit(solution)/shard_map/ppermute | solution.py:496
  67.6 3.2 %shard_map.85.scores_ref = bf16[2,8,512,512]{3,2,1,0:T(8,128)(2,1)S(1)} custom-call(s32[4]{0:T(128)S(1)} %pad_add_fusion.where, bf16[1024,1024]{1,0:T(8,128)(2,1)S(1)} %get-tuple-element.56.k_ref.a_ref, bf16[1024,1024]{1,0:T(8,128)(2,1)S(1)} %copy-done), custom_call_target="tpu_custom_call" | custom-call | flops 1073741824 | bytes 10737418 | tf_op jit(solution)/shard_map/pallas_call | solution.py:55
  70.8 1.7 %collective-permute-done.17.refs_1_ = f32[1,128,128]{2,1,0:T(8,128)S(1)} collective-permute-done((f32[1,128,128]{2,1,0:T(8,128)S(1)}, f32[1,128,128]{2,1,0:T(8,128)S(1)}, u32[]{:S(2)}, u32[]{:S(2)}) %collective-permute-start.17) | collective-permute-done | bytes 65568 | tf_op jit(solution)/shard_map/ppermute | solution.py:496
  72.5 0.2 collective-permute-done.18.refs_2_
  72.7 0.6 shard_map.101
  73.4 6.2 %shard_map.96.ready_ref = bf16[1024,1024]{1,0:T(8,128)(2,1)S(1)} custom-call(s32[4]{0:T(128)S(1)} %pad_add_fusion.where, bf16[1024,1024]{1,0:T(8,128)(2,1)S(1)} %get-tuple-element.80.g_ref.b_ref, bf16[1024,1024]{1,0:T(8,128)(2,1)S(1)} %get-tuple-element.57.b_ref.v_ref.a_ref, bf16[1024,1024]{1,0:T(8,128)(2,1)S(1)} %get-tuple-element.56.k_ref.a_ref, ...), custom_call_target="tpu_custom_call" | custom-call | flops 2147483648 | bytes 21474836 | tf_op jit(solution)/shard_map/pallas_call | solution.py:55
  79.6 0.7 shard_map.102
  80.3 1.1 %collective-permute-start.21 = (f32[2,1,128,128]{3,2,1,0:T(8,128)S(1)}, f32[2,1,128,128]{3,2,1,0:T(8,128)S(1)}, u32[]{:S(2)}, u32[]{:S(2)}) collective-permute-start(f32[2,1,128,128]{3,2,1,0:T(8,128)S(1)} %get-tuple-element.99), channel_id=1, source_target_pairs={{0,1},{1,0},{2,3},{3,2},{4,5},{5,4},{6,7},{7,6},{8,9},{9,8},{10,11... | collective-permute-start | bytes 393224 | tf_op jit(solution)/shard_map/ppermute | solution.py:496
  81.3 0.5 collective-permute-start.22
  81.8 2.0 %collective-permute-start.23 = (f32[2,1,128,128]{3,2,1,0:T(8,128)S(1)}, f32[2,1,128,128]{3,2,1,0:T(8,128)S(1)}, u32[]{:S(2)}, u32[]{:S(2)}) collective-permute-start(f32[2,1,128,128]{3,2,1,0:T(8,128)S(1)} %get-tuple-element.101), channel_id=1, source_target_pairs={{0,3},{1,2},{2,1},{3,0},{4,7},{5,6},{6,5},{7,4},{8,11},{9,10},{10,... | collective-permute-start | bytes 393224 | tf_op jit(solution)/shard_map/ppermute | solution.py:496
  83.8 5.0 %shard_map.97 = (f32[1024,1024]{1,0:T(8,128)S(1)}, bf16[1024,1024]{1,0:T(8,128)(2,1)}) custom-call(s32[4]{0:T(128)S(1)} %pad_add_fusion.where, bf16[1024,1024]{1,0:T(8,128)(2,1)S(1)} %get-tuple-element.57.b_ref.v_ref.a_ref, bf16[1024,1024]{1,0:T(8,128)(2,1)S(1)} %get-tuple-element.80.g_ref.b_ref, bf16[1024,1024]{1,0:T(8,128)(2,1)S(1)} %copy-done, ...), custom_call_target="tpu_custom_call" | custom-call | flops 2147483648 | bytes 21474836 | tf_op jit(solution)/shard_map/pallas_call | solution.py:55
  88.8 2.9 %shard_map.95 = (f32[1024,1024]{1,0:T(8,128)S(1)}, bf16[1024,1024]{1,0:T(8,128)(2,1)}) custom-call(s32[4]{0:T(128)S(1)} %pad_add_fusion.where, bf16[2,8,512,512]{3,2,1,0:T(8,128)(2,1)S(1)} %shard_map.85.scores_ref, bf16[1024,1024]{1,0:T(8,128)(2,1)S(1)} %get-tuple-element.80.g_ref.b_ref, bf16[1024,1024]{1,0:T(8,128)(2,1)S(1)} %get-tuple-element.81.ready_ref), custom_call_target="tpu_custom_call" | custom-call | flops 1073741824 | bytes 10737418 | tf_op jit(solution)/shard_map/pallas_call | solution.py:55
  91.8 4.1 %shard_map.103 = (bf16[1024,1024]{1,0:T(8,128)(2,1)}, bf16[1024,1024]{1,0:T(8,128)(2,1)}) custom-call(s32[4]{0:T(128)S(1)} %pad_add_fusion.where, f32[1024,1024]{1,0:T(8,128)S(1)} %get-tuple-element.88.lk_ref, f32[1024,1024]{1,0:T(8,128)S(1)} %get-tuple-element.89.lv_ref, bf16[1024,1024]{1,0:T(8,128)(2,1)S(1)} %get-tuple-element.56.k_ref.a_ref, ...), custom_call_target="tpu_custom_call" | custom-call | flops 536870912 | bytes 5368709 | tf_op jit(solution)/shard_map/pallas_call | solution.py:55
  (27 shorter events, 0.4 us)
Async XLA Ops:
  3.8 32.7 %copy-start = (bf16[1024,1024]{1,0:T(8,128)(2,1)S(1)}, bf16[1024,1024]{1,0:T(8,128)(2,1)}, u32[]{:S(2)}) copy-start(bf16[1024,1024]{1,0:T(8,128)(2,1)} %a_ref.1) | copy-start | bytes 6291460
  5.6 6.5 %collective-permute-start = (f32[2,1,128,128]{3,2,1,0:T(8,128)S(1)}, f32[2,1,128,128]{3,2,1,0:T(8,128)S(1)}, u32[]{:S(2)}, u32[]{:S(2)}) collective-permute-start(f32[2,1,128,128]{3,2,1,0:T(8,128)S(1)} %get-tuple-element.59), channel_id=1, source_target_pairs={{0,1},{1,0},{2,3},{3,2},{4,5},{5,4},{6,7},{7,6},{8,9},{9,8},{10,11... | collective-permute-start | bytes 393224 | tf_op jit(solution)/shard_map/ppermute | solution.py:496
  8.6 6.4 %collective-permute-start.1 = (f32[2,1,128,128]{3,2,1,0:T(8,128)S(1)}, f32[2,1,128,128]{3,2,1,0:T(8,128)S(1)}, u32[]{:S(2)}, u32[]{:S(2)}) collective-permute-start(f32[2,1,128,128]{3,2,1,0:T(8,128)S(1)} %get-tuple-element.60), channel_id=1, source_target_pairs={{0,2},{1,3},{2,0},{3,1},{4,6},{5,7},{6,4},{7,5},{8,10},{9,11},{10,... | collective-permute-start | bytes 393224 | tf_op jit(solution)/shard_map/ppermute | solution.py:496
  10.2 6.0 %collective-permute-start.2 = (f32[2,1,128,128]{3,2,1,0:T(8,128)S(1)}, f32[2,1,128,128]{3,2,1,0:T(8,128)S(1)}, u32[]{:S(2)}, u32[]{:S(2)}) collective-permute-start(f32[2,1,128,128]{3,2,1,0:T(8,128)S(1)} %get-tuple-element.61), channel_id=1, source_target_pairs={{0,3},{1,2},{2,1},{3,0},{4,7},{5,6},{6,5},{7,4},{8,11},{9,10},{10,... | collective-permute-start | bytes 393224 | tf_op jit(solution)/shard_map/ppermute | solution.py:496
  16.8 2.9 %collective-permute-start.3 = (f32[1,128,128]{2,1,0:T(8,128)S(1)}, f32[1,128,128]{2,1,0:T(8,128)S(1)}, u32[]{:S(2)}, u32[]{:S(2)}) collective-permute-start(f32[1,128,128]{2,1,0:T(8,128)S(1)} %get-tuple-element.63), channel_id=1, source_target_pairs={{0,8},{1,9},{2,10},{3,11},{4,12},{5,13},{6,14},{7,15},{8,0},{9,1},... | collective-permute-start | bytes 196616 | tf_op jit(solution)/shard_map/ppermute | solution.py:496
  16.8 7.9 %collective-permute-start.4 = (f32[1,128,128]{2,1,0:T(8,128)S(1)}, f32[1,128,128]{2,1,0:T(8,128)S(1)}, u32[]{:S(2)}, u32[]{:S(2)}) collective-permute-start(f32[1,128,128]{2,1,0:T(8,128)S(1)} %get-tuple-element.62.mine_ref), channel_id=1, source_target_pairs={{0,4},{1,5},{2,6},{3,7},{4,0},{5,1},{6,2},{7,3},{8,12},{9,13},{10,... | collective-permute-start | bytes 196616 | tf_op jit(solution)/shard_map/ppermute | solution.py:496
  19.7 8.0 %collective-permute-start.5 = (f32[1,128,128]{2,1,0:T(8,128)S(1)}, f32[1,128,128]{2,1,0:T(8,128)S(1)}, u32[]{:S(2)}, u32[]{:S(2)}) collective-permute-start(f32[1,128,128]{2,1,0:T(8,128)S(1)} %collective-permute-done.3.other_ref), channel_id=1, source_target_pairs={{0,4},{1,5},{2,6},{3,7},{4,0},{5,1},{6,2},{7,3},{8,12},{9,13},{10,... | collective-permute-start | bytes 196616 | tf_op jit(solution)/shard_map/ppermute | solution.py:496
  21.4 9.0 %collective-permute-start.6 = (f32[1,128,128]{2,1,0:T(8,128)S(1)}, f32[1,128,128]{2,1,0:T(8,128)S(1)}, u32[]{:S(2)}, u32[]{:S(2)}) collective-permute-start(f32[1,128,128]{2,1,0:T(8,128)S(1)} %shard_map.88), channel_id=1, source_target_pairs={{0,20},{1,21},{2,22},{3,23},{4,16},{5,17},{6,18},{7,19},{8,28},{9,... | collective-permute-start | bytes 196616 | tf_op jit(solution)/shard_map/ppermute | solution.py:496
  24.2 6.2 %collective-permute-start.7 = (f32[1,128,128]{2,1,0:T(8,128)S(1)}, f32[1,128,128]{2,1,0:T(8,128)S(1)}, u32[]{:S(2)}, u32[]{:S(2)}) collective-permute-start(f32[1,128,128]{2,1,0:T(8,128)S(1)} %shard_map.88), channel_id=1, source_target_pairs={{0,16},{1,17},{2,18},{3,19},{4,20},{5,21},{6,22},{7,23},{8,24},{9,... | collective-permute-start | bytes 196616 | tf_op jit(solution)/shard_map/ppermute | solution.py:496
  31.0 1.3 %collective-permute-start.8 = (f32[1,128,128]{2,1,0:T(8,128)S(1)}, f32[1,128,128]{2,1,0:T(8,128)S(1)}, u32[]{:S(2)}, u32[]{:S(2)}) collective-permute-start(f32[1,128,128]{2,1,0:T(8,128)S(1)} %get-tuple-element.65), channel_id=1, source_target_pairs={{0,8},{1,9},{2,10},{3,11},{4,12},{5,13},{6,14},{7,15},{8,0},{9,1},... | collective-permute-start | bytes 196616 | tf_op jit(solution)/shard_map/ppermute | solution.py:496
  33.0 11.5 %collective-permute-start.9 = (f32[2,1,128,128]{3,2,1,0:T(8,128)S(1)}, f32[2,1,128,128]{3,2,1,0:T(8,128)S(1)}, u32[]{:S(2)}, u32[]{:S(2)}) collective-permute-start(f32[2,1,128,128]{3,2,1,0:T(8,128)S(1)} %get-tuple-element.66), channel_id=1, source_target_pairs={{0,1},{1,0},{2,3},{3,2},{4,5},{5,4},{6,7},{7,6},{8,9},{9,8},{10,11... | collective-permute-start | bytes 393224 | tf_op jit(solution)/shard_map/ppermute | solution.py:496
  34.5 10.0 %collective-permute-start.10 = (f32[2,1,128,128]{3,2,1,0:T(8,128)S(1)}, f32[2,1,128,128]{3,2,1,0:T(8,128)S(1)}, u32[]{:S(2)}, u32[]{:S(2)}) collective-permute-start(f32[2,1,128,128]{3,2,1,0:T(8,128)S(1)} %get-tuple-element.67), channel_id=1, source_target_pairs={{0,2},{1,3},{2,0},{3,1},{4,6},{5,7},{6,4},{7,5},{8,10},{9,11},{10,... | collective-permute-start | bytes 393224 | tf_op jit(solution)/shard_map/ppermute | solution.py:496
  34.5 7.2 %copy-start.1 = (bf16[1024,1024]{1,0:T(8,128)(2,1)S(1)}, bf16[1024,1024]{1,0:T(8,128)(2,1)}, u32[]{:S(2)}) copy-start(bf16[1024,1024]{1,0:T(8,128)(2,1)} %refs_6_.1) | copy-start | bytes 6291460
  34.5 7.2 %copy-start.2 = (f32[1024]{0:T(1024)S(1)}, f32[1024]{0:T(1024)}, u32[]{:S(2)}) copy-start(f32[1024]{0:T(1024)} %param.8) | copy-start | bytes 12292
  34.5 8.5 %collective-permute-start.11 = (f32[2,1,128,128]{3,2,1,0:T(8,128)S(1)}, f32[2,1,128,128]{3,2,1,0:T(8,128)S(1)}, u32[]{:S(2)}, u32[]{:S(2)}) collective-permute-start(f32[2,1,128,128]{3,2,1,0:T(8,128)S(1)} %get-tuple-element.70), channel_id=1, source_target_pairs={{0,3},{1,2},{2,1},{3,0},{4,7},{5,6},{6,5},{7,4},{8,11},{9,10},{10,... | collective-permute-start | bytes 393224 | tf_op jit(solution)/shard_map/ppermute | solution.py:496
  50.4 6.0 %collective-permute-start.12 = (f32[2,1,128,128]{3,2,1,0:T(8,128)S(1)}, f32[2,1,128,128]{3,2,1,0:T(8,128)S(1)}, u32[]{:S(2)}, u32[]{:S(2)}) collective-permute-start(f32[2,1,128,128]{3,2,1,0:T(8,128)S(1)} %get-tuple-element.91), channel_id=1, source_target_pairs={{0,1},{1,0},{2,3},{3,2},{4,5},{5,4},{6,7},{7,6},{8,9},{9,8},{10,11... | collective-permute-start | bytes 393224 | tf_op jit(solution)/shard_map/ppermute | solution.py:496
  51.9 5.9 %collective-permute-start.13 = (f32[2,1,128,128]{3,2,1,0:T(8,128)S(1)}, f32[2,1,128,128]{3,2,1,0:T(8,128)S(1)}, u32[]{:S(2)}, u32[]{:S(2)}) collective-permute-start(f32[2,1,128,128]{3,2,1,0:T(8,128)S(1)} %get-tuple-element.92), channel_id=1, source_target_pairs={{0,2},{1,3},{2,0},{3,1},{4,6},{5,7},{6,4},{7,5},{8,10},{9,11},{10,... | collective-permute-start | bytes 393224 | tf_op jit(solution)/shard_map/ppermute | solution.py:496
  51.9 7.2 %collective-permute-start.14 = (f32[2,1,128,128]{3,2,1,0:T(8,128)S(1)}, f32[2,1,128,128]{3,2,1,0:T(8,128)S(1)}, u32[]{:S(2)}, u32[]{:S(2)}) collective-permute-start(f32[2,1,128,128]{3,2,1,0:T(8,128)S(1)} %get-tuple-element.93), channel_id=1, source_target_pairs={{0,3},{1,2},{2,1},{3,0},{4,7},{5,6},{6,5},{7,4},{8,11},{9,10},{10,... | collective-permute-start | bytes 393224 | tf_op jit(solution)/shard_map/ppermute | solution.py:496
  59.7 2.9 %collective-permute-start.15 = (f32[1,128,128]{2,1,0:T(8,128)S(1)}, f32[1,128,128]{2,1,0:T(8,128)S(1)}, u32[]{:S(2)}, u32[]{:S(2)}) collective-permute-start(f32[1,128,128]{2,1,0:T(8,128)S(1)} %get-tuple-element.95), channel_id=1, source_target_pairs={{0,8},{1,9},{2,10},{3,11},{4,12},{5,13},{6,14},{7,15},{8,0},{9,1},... | collective-permute-start | bytes 196616 | tf_op jit(solution)/shard_map/ppermute | solution.py:496
  59.8 11.0 %collective-permute-start.16 = (f32[1,128,128]{2,1,0:T(8,128)S(1)}, f32[1,128,128]{2,1,0:T(8,128)S(1)}, u32[]{:S(2)}, u32[]{:S(2)}) collective-permute-start(f32[1,128,128]{2,1,0:T(8,128)S(1)} %get-tuple-element.94.mine_ref), channel_id=1, source_target_pairs={{0,4},{1,5},{2,6},{3,7},{4,0},{5,1},{6,2},{7,3},{8,12},{9,13},{10,... | collective-permute-start | bytes 196616 | tf_op jit(solution)/shard_map/ppermute | solution.py:496
  63.1 9.6 %collective-permute-start.18 = (f32[1,128,128]{2,1,0:T(8,128)S(1)}, f32[1,128,128]{2,1,0:T(8,128)S(1)}, u32[]{:S(2)}, u32[]{:S(2)}) collective-permute-start(f32[1,128,128]{2,1,0:T(8,128)S(1)} %shard_map.100), channel_id=1, source_target_pairs={{0,20},{1,21},{2,22},{3,23},{4,16},{5,17},{6,18},{7,19},{8,28},{9,... | collective-permute-start | bytes 196616 | tf_op jit(solution)/shard_map/ppermute | solution.py:496
  64.3 8.4 %collective-permute-start.19 = (f32[1,128,128]{2,1,0:T(8,128)S(1)}, f32[1,128,128]{2,1,0:T(8,128)S(1)}, u32[]{:S(2)}, u32[]{:S(2)}) collective-permute-start(f32[1,128,128]{2,1,0:T(8,128)S(1)} %shard_map.100), channel_id=1, source_target_pairs={{0,16},{1,17},{2,18},{3,19},{4,20},{5,21},{6,22},{7,23},{8,24},{9,... | collective-permute-start | bytes 196616 | tf_op jit(solution)/shard_map/ppermute | solution.py:496
  65.8 6.6 %collective-permute-start.17 = (f32[1,128,128]{2,1,0:T(8,128)S(1)}, f32[1,128,128]{2,1,0:T(8,128)S(1)}, u32[]{:S(2)}, u32[]{:S(2)}) collective-permute-start(f32[1,128,128]{2,1,0:T(8,128)S(1)} %collective-permute-done.15.other_ref), channel_id=1, source_target_pairs={{0,4},{1,5},{2,6},{3,7},{4,0},{5,1},{6,2},{7,3},{8,12},{9,13},{10,... | collective-permute-start | bytes 196616 | tf_op jit(solution)/shard_map/ppermute | solution.py:496
  73.3 6.3 %collective-permute-start.20 = (f32[1,128,128]{2,1,0:T(8,128)S(1)}, f32[1,128,128]{2,1,0:T(8,128)S(1)}, u32[]{:S(2)}, u32[]{:S(2)}) collective-permute-start(f32[1,128,128]{2,1,0:T(8,128)S(1)} %get-tuple-element.97), channel_id=1, source_target_pairs={{0,8},{1,9},{2,10},{3,11},{4,12},{5,13},{6,14},{7,15},{8,0},{9,1},... | collective-permute-start | bytes 196616 | tf_op jit(solution)/shard_map/ppermute | solution.py:496
  80.3 11.5 %collective-permute-start.21 = (f32[2,1,128,128]{3,2,1,0:T(8,128)S(1)}, f32[2,1,128,128]{3,2,1,0:T(8,128)S(1)}, u32[]{:S(2)}, u32[]{:S(2)}) collective-permute-start(f32[2,1,128,128]{3,2,1,0:T(8,128)S(1)} %get-tuple-element.99), channel_id=1, source_target_pairs={{0,1},{1,0},{2,3},{3,2},{4,5},{5,4},{6,7},{7,6},{8,9},{9,8},{10,11... | collective-permute-start | bytes 393224 | tf_op jit(solution)/shard_map/ppermute | solution.py:496
  81.3 10.4 %collective-permute-start.22 = (f32[2,1,128,128]{3,2,1,0:T(8,128)S(1)}, f32[2,1,128,128]{3,2,1,0:T(8,128)S(1)}, u32[]{:S(2)}, u32[]{:S(2)}) collective-permute-start(f32[2,1,128,128]{3,2,1,0:T(8,128)S(1)} %get-tuple-element.100), channel_id=1, source_target_pairs={{0,2},{1,3},{2,0},{3,1},{4,6},{5,7},{6,4},{7,5},{8,10},{9,11},{10,... | collective-permute-start | bytes 393224 | tf_op jit(solution)/shard_map/ppermute | solution.py:496
  81.8 10.0 %collective-permute-start.23 = (f32[2,1,128,128]{3,2,1,0:T(8,128)S(1)}, f32[2,1,128,128]{3,2,1,0:T(8,128)S(1)}, u32[]{:S(2)}, u32[]{:S(2)}) collective-permute-start(f32[2,1,128,128]{3,2,1,0:T(8,128)S(1)} %get-tuple-element.101), channel_id=1, source_target_pairs={{0,3},{1,2},{2,1},{3,0},{4,7},{5,6},{6,5},{7,4},{8,11},{9,10},{10,... | collective-permute-start | bytes 393224 | tf_op jit(solution)/shard_map/ppermute | solution.py:496

commit v4 on v3

--- a/solution.py
+++ b/solution.py
@@ -45,23 +45,24 @@
     return pltpu.with_memory_space_constraint(value, pltpu.HBM)
 
 
+def place():
+    grp, seq = lax.axis_index("grp"), lax.axis_index("seq")
+    return lax.rem(grp, LANES), lax.rem(seq, QUAD), lax.div(grp, LANES), lax.div(seq, QUAD)
+
+
 def call(kernel, out_shape, args, flops, scratch=(), grant=8, far_in=(), far_out=(), aliases=None):
     any_space = pl.BlockSpec(memory_space=pltpu.HBM)
     near_space = pl.BlockSpec(memory_space=pltpu.VMEM)
-    in_specs = [pl.BlockSpec(memory_space=pltpu.SMEM)]
-    in_specs += [any_space if i in far_in else near_space for i in range(len(args) - 1)]
-    out_specs = [any_space if i in far_out else near_space for i in range(len(out_shape))]
-    args = [args[0]] + [far(a) if i in far_in else near(a) for i, a in enumerate(args[1:])]
     return pl.pallas_call(
-        kernel,
+        lambda *refs: kernel(place(), *refs),
         out_shape=out_shape,
-        in_specs=in_specs,
-        out_specs=out_specs,
+        in_specs=[any_space if i in far_in else near_space for i in range(len(args))],
+        out_specs=[any_space if i in far_out else near_space for i in range(len(out_shape))],
         scratch_shapes=scratch,
         input_output_aliases=aliases or {},
         compiler_params=pltpu.CompilerParams(vmem_limit_bytes=grant << 20),
         cost_estimate=pl.CostEstimate(flops=flops, bytes_accessed=flops // 100, transcendentals=0),
-    )(*args)
+    )(*[far(a) if i in far_in else near(a) for i, a in enumerate(args)])
 
 
 def head_cols(head):
@@ -109,12 +110,12 @@
     return [vmem(LANES, SHARE, HD, HD), vmem(blocks, LANES, SHARE, HD, HD)]
 
 
-def slot_totals(slots, reverse, where, a, b):
+def slot_totals(slots, reverse, a, b):
     tokens, features = a.shape
     outs = call(
         functools.partial(slot_kernel, slots, reverse),
         slot_shapes(tokens // BLOCK) * len(slots),
-        [where, a, b],
+        [a, b],
         2 * tokens * features // QUAD * len(slots) * HD,
     )
     return {slot: outs[2 * i : 2 * i + 2] for i, slot in enumerate(slots)}
@@ -138,13 +139,13 @@
         slot_block(slot, False, where, block, blocks, k_ref, v_ref, piece_ref, inside_ref)
 
 
-def load_totals(slot, where, keys, values):
+def load_totals(slot, keys, values):
     tokens, features = keys.shape
     blocks = tokens // BLOCK
     return call(
         functools.partial(load_kernel, slot),
         slot_shapes(blocks) + [vmem(tokens, features, dtype=BF16)] * 2,
-        [where, keys, values],
+        [keys, values],
         2 * tokens * features * HD,
         scratch=[pltpu.SemaphoreType.DMA((blocks, 2))],
         far_in=(0, 1),
@@ -204,12 +205,12 @@
     over_units(q_ref.shape[0] // BLOCK * H, step)
 
 
-def local_part(where, queries, keys, values):
+def local_part(queries, keys, values):
     tokens, features = queries.shape
     return call(
         local_kernel,
         [vmem(tokens, features)],
-        [where, queries, keys, values],
+        [queries, keys, values],
         4 * tokens * BLOCK * features,
     )[0]
 
@@ -230,12 +231,12 @@
     over_units(k_ref.shape[0] // BLOCK * H, step)
 
 
-def turned_scores(where, keys, queries):
+def turned_scores(keys, queries):
     tokens, features = keys.shape
     return call(
         scores_kernel,
         [vmem(tokens // BLOCK, H, BLOCK, BLOCK, dtype=BF16)],
-        [where, keys, queries],
+        [keys, queries],
         2 * tokens * BLOCK * features,
     )[0]
 
@@ -262,12 +263,12 @@
     copy.wait()
 
 
-def value_part(where, scores, grads, ready):
+def value_part(scores, grads, ready):
     tokens, features = grads.shape
     return call(
         value_kernel,
         [vmem(tokens, features), jax.ShapeDtypeStruct(ready.shape, ready.dtype)],
-        [where, scores, grads, ready],
+        [scores, grads, ready],
         2 * tokens * BLOCK * features,
         scratch=[pltpu.SemaphoreType.DMA(())],
         far_out=(1,),
@@ -297,7 +298,7 @@
         cross_ref[rows, :] = cross
 
 
-def attended_slot(slot, where, carried, inside, local, queries, cotangent, gain, sums):
+def attended_slot(slot, carried, inside, local, queries, cotangent, gain, sums):
     tokens, features = queries.shape
     blocks = tokens // BLOCK
     first = not sums
@@ -305,9 +306,9 @@
         functools.partial(attended_kernel, slot, first),
         [vmem(tokens, features), vmem(tokens, HD), vmem(tokens, HD)]
         + [vmem(blocks, LANES, SHARE, HD, HD, dtype=BF16)],
-        [where, carried, inside, local, queries, cotangent, gain, *sums],
+        [carried, inside, local, queries, cotangent, gain, *sums],
         2 * tokens * features // QUAD * HD,
-        aliases={3: 0},
+        aliases={2: 0},
     )
 
 
@@ -353,7 +354,7 @@
         slot_block(ORDER[0], True, where, block, blocks, q_ref, grad_ref, piece_ref, later_ref)
 
 
-def norm(slots, where, carried, inside, attended, queries, cotangent, gain, sums):
+def norm(slots, carried, inside, attended, queries, cotangent, gain, sums):
     tokens, features = attended.shape
     blocks = tokens // BLOCK
     half = vmem(tokens, features, dtype=BF16)
@@ -362,10 +363,10 @@
     _, normed, grads, *outs = call(
         functools.partial(norm_kernel, slots),
         [vmem(tokens, features), half, half] + [prior] * len(slots) + slot_shapes(blocks),
-        [where, *carried, *inside, attended, queries, cotangent, gain, *sums],
+        [*carried, *inside, attended, queries, cotangent, gain, *sums],
         20 * tokens * features,
         scratch=[vmem(BLOCK, HD)] * 2,
-        aliases={1 + 2 * len(slots): 0},
+        aliases={2 * len(slots): 0},
     )
     return normed, grads, outs[: len(slots)], outs[len(slots) :]
 
@@ -400,12 +401,12 @@
     lax.fori_loop(0, g_ref.shape[0] // BLOCK * H // UNROLL, several, 0)
 
 
-def query_part(where, grads, values, keys, priors):
+def query_part(grads, values, keys, priors):
     tokens, features = grads.shape
     return call(
         query_kernel,
         [vmem(tokens, features, dtype=BF16)],
-        [where, grads, values, keys, *priors],
+        [grads, values, keys, *priors],
         4 * tokens * BLOCK * features,
         scratch=[vmem(tokens // BLOCK, H // PAIR, PAIR * HD, PAIR * HD, dtype=BF16)],
     )[0]
@@ -426,12 +427,12 @@
     copy.wait()
 
 
-def turned_part(where, a, b, c, ready):
+def turned_part(a, b, c, ready):
     tokens, features = a.shape
     return call(
         turned_kernel,
         [vmem(tokens, features), jax.ShapeDtypeStruct(ready.shape, ready.dtype)],
-        [where, a, b, c, ready],
+        [a, b, c, ready],
         4 * tokens * BLOCK * features,
         scratch=[pltpu.SemaphoreType.DMA(())],
         far_out=(1,),
@@ -467,13 +468,13 @@
         copy.wait()
 
 
-def final_part(where, local_k, local_v, keys, values, carried, later):
+def final_part(local_k, local_v, keys, values, carried, later):
     tokens, features = keys.shape
     blocks = tokens // BLOCK
     return call(
         final_kernel,
         [jax.ShapeDtypeStruct((tokens, features), BF16)] * 2,
-        [where, local_k, local_v, keys, values, *carried, *later],
+        [local_k, local_v, keys, values, *carried, *later],
         4 * tokens * features * HD,
         scratch=[
             vmem(tokens, features, dtype=BF16),
@@ -548,7 +549,7 @@
     return sorted(shifts, key=lambda shift: -sum(shift))
 
 
-def carry(where, first, rest, reverse):
+def carry(first, rest, reverse):
     counts = lax.axis_size("grp") // LANES, lax.axis_size("seq") // QUAD
     one, two = vmem(SHARE, HD, HD), vmem(LANES, SHARE, HD, HD)
 
@@ -567,12 +568,12 @@
     held, inside = [None] * QUAD, [None] * QUAD
     held[ORDER[0]], inside[ORDER[0]] = first
     held[ORDER[0]] = moved(held[ORDER[0]], swap_quad(ORDER[0]))
-    rest = slot_totals(ORDER[1:], reverse, where, *rest)
+    rest = slot_totals(ORDER[1:], reverse, *rest)
     for o in ORDER[1:]:
         held[o], inside[o] = rest[o]
         if o:
             held[o] = moved(held[o], swap_quad(o))
-    mine, rest = call(sum_kernel, [one, one], [where, *held], 1000, grant=2)
+    mine, rest = call(sum_kernel, [one, one], [*held], 1000, grant=2)
     near_shifts, far_shifts = range(1, counts[1]), far_shifts_of(counts)
     came_mine, came_other, came_both = [], [], []
     for df in near_shifts:
@@ -580,15 +581,15 @@
     other = moved(rest, swap_lane)
     for df in near_shifts:
         came_other.append(moved(other, shift(0, df)))
-    both = call(both_kernel, [one], [where, mine, other], 1000, grant=2)[0]
+    both = call(both_kernel, [one], [mine, other], 1000, grant=2)[0]
     for dr, df in far_shifts:
         came_both.append(moved(both, shift(dr, df)))
     kernel = functools.partial(base_kernel, near_shifts, far_shifts, counts, reverse)
-    args = [where, mine, other, *came_mine, *came_other, *came_both]
+    args = [mine, other, *came_mine, *came_other, *came_both]
     sum_mine, sum_other = call(kernel, [one, one], args, 1000, grant=2)
     other = moved(sum_other, swap_lane)
     kernel = functools.partial(back_sum_kernel, reverse)
-    back = call(kernel, [two] * QUAD, [where, sum_mine, other, *held], 1000, grant=2)
+    back = call(kernel, [two] * QUAD, [sum_mine, other, *held], 1000, grant=2)
     result = [back[0]] + [None] * (QUAD - 1)
     for o in ORDER[:-1]:
         result[o] = moved(back[o], swap_quad(o))
@@ -596,31 +597,28 @@
 
 
 def body(queries, key_rows, value_rows, norm_gain, cotangent):
-    grp, seq = lax.axis_index("grp"), lax.axis_index("seq")
-    parts = [grp % LANES, seq % QUAD, grp // LANES, seq // QUAD]
-    where = jnp.stack(parts).astype(jnp.int32)
     gain = norm_gain[None, :]
-    *first, keys, values = load_totals(ORDER[0], where, key_rows, value_rows)
+    *first, keys, values = load_totals(ORDER[0], key_rows, value_rows)
     queries, cotangent = near(queries), near(cotangent)
-    carried, inside = carry(where, first, (keys, values), False)
-    attended = local_part(where, queries, keys, values)
-    scores = turned_scores(where, keys, queries)
+    carried, inside = carry(first, (keys, values), False)
+    attended = local_part(queries, keys, values)
+    scores = turned_scores(keys, queries)
     priors, sums = [None] * QUAD, []
     for o in EARLY:
         attended, *sums, priors[o] = attended_slot(
-            o, where, carried[o], inside[o], attended, queries, cotangent, gain, sums
+            o, carried[o], inside[o], attended, queries, cotangent, gain, sums
         )
     late = [o for o in ORDER if o not in EARLY]
     normed, grads, late_priors, first = norm(
-        late, where, carried, inside, attended, queries, cotangent, gain, sums
+        late, carried, inside, attended, queries, cotangent, gain, sums
     )
     for o, prior in zip(late, late_priors):
         priors[o] = prior
-    carried, later = carry(where, first, (queries, grads), True)
-    local_v, normed = value_part(where, scores, grads, normed)
-    grad_q = query_part(where, grads, values, keys, priors)
-    local_k, grad_q = turned_part(where, values, grads, queries, grad_q)
-    grad_k, grad_v = final_part(where, local_k, local_v, keys, values, carried, later)
+    carried, later = carry(first, (queries, grads), True)
+    local_v, normed = value_part(scores, grads, normed)
+    grad_q = query_part(grads, values, keys, priors)
+    local_k, grad_q = turned_part(values, grads, queries, grad_q)
+    grad_k, grad_v = final_part(local_k, local_v, keys, values, carried, later)
     return normed, grad_q, grad_k, grad_v
 
 

time: 96.2 us -> 87.2 us (0.906)
  Pallas kernels: 44.7 us -> 33.9 us
  waiting for transfers between devices: 20.1 us -> 21.6 us
    pallas_call x20, Pallas kernels: 44.7 us -> 33.9 us  [call(): pl.pallas_call(lambda *refs: kernel(place(), *refs), out_shape=out_shape,...]
    ppermute x24, waiting for transfers between devices: 20.1 us -> 21.6 us  [moved(): return lax.ppermute(value, AXES, pairs)]
  transfers between devices with their start and end apart: 24 -> 24, of which waited for: 11 -> 11; matrix products, arithmetic and copies ran while one was open for 0% -> 0% of each run, Pallas kernels for 27% -> 25%
where the time goes in v4:
time: 87.2 us; the launch traced here: 87.1 us
  Pallas kernels  33.9 us (39%)
  starting transfers between devices  30.5 us (35%)
  waiting for transfers between devices  21.6 us (25%)
  between operations  1.04 us (1%)
    pallas_call x20, Pallas kernels, call(): pl.pallas_call(lambda *refs: kernel(place(), *refs), out_shape=out_shape,...  33.9 us
    ppermute x24, starting transfers between devices, moved(): return lax.ppermute(value, AXES, pairs)  30.5 us
    ppermute x24, waiting for transfers between devices, moved(): return lax.ppermute(value, AXES, pairs)  21.6 us
  transfers between devices with their start and end apart: 24, of which 11 were waited for; matrix products, arithmetic and copies ran while one was open for 0% of the time, Pallas kernels for 25%

profile of v4, /device:TPU:0, one launch (start us, length us, event | category | flops | bytes accessed | tf_op | source)
XLA Modules:
  0.0 87.1 jit_solution(14014215396764229797)
XLA Ops:
  0.6 2.5 %shard_map.84 = (f32[2,1,128,128]{3,2,1,0:T(8,128)S(1)}, f32[2,2,1,128,128]{4,3,2,1,0:T(8,128)S(1)}, bf16[1024,1024]{1,0:T(8,128)(2,1)S(1)}, bf16[1024,1024]{1,0:T(8,128)(2,1)S(1)}) custom-call(bf16[1024,1024]{1,0:T(8,128)(2,1)} %refs_0_.3, bf16[1024,1024]{1,0:T(8,128)(2,1)} %refs_1_.2), custom_call_target="tpu_custom_call" | custom-call | flops 268435456 | bytes 2684354 | tf_op jit(solution)/shard_map/pallas_call | solution.py:56
  3.2 0.0 copy-start
  3.2 1.2 %shard_map.86 = (f32[2,1,128,128]{3,2,1,0:T(8,128)S(1)}, f32[2,2,1,128,128]{4,3,2,1,0:T(8,128)S(1)}, f32[2,1,128,128]{3,2,1,0:T(8,128)S(1)}, f32[2,2,1,128,128]{...) custom-call(bf16[1024,1024]{1,0:T(8,128)(2,1)S(1)} %get-tuple-element.56.refs_0_.refs_1_.refs_2_,, ...), custom_call_target="tpu_custom_call" | custom-call | flops 201326592 | bytes 2013265 | tf_op jit(solution)/shard_map/pallas_call | solution.py:56
  4.4 3.0 %collective-permute-start = (f32[2,1,128,128]{3,2,1,0:T(8,128)S(1)}, f32[2,1,128,128]{3,2,1,0:T(8,128)S(1)}, u32[]{:S(2)}, u32[]{:S(2)}) collective-permute-start(f32[2,1,128,128]{3,2,1,0:T(8,128)S(1)} %get-tuple-element.59), channel_id=1, source_target_pairs={{0,1},{1,0},{2,3},{3,2},{4,5},{5,4},{6,7},{7,6},{8,9},{9,8},{10,11... | collective-permute-start | bytes 393224 | tf_op jit(solution)/shard_map/ppermute | solution.py:497
  7.4 1.6 %collective-permute-start.1 = (f32[2,1,128,128]{3,2,1,0:T(8,128)S(1)}, f32[2,1,128,128]{3,2,1,0:T(8,128)S(1)}, u32[]{:S(2)}, u32[]{:S(2)}) collective-permute-start(f32[2,1,128,128]{3,2,1,0:T(8,128)S(1)} %get-tuple-element.60), channel_id=1, source_target_pairs={{0,2},{1,3},{2,0},{3,1},{4,6},{5,7},{6,4},{7,5},{8,10},{9,11},{10,... | collective-permute-start | bytes 393224 | tf_op jit(solution)/shard_map/ppermute | solution.py:497
  9.0 1.9 %collective-permute-done.refs_1_.refs_3_ = f32[2,1,128,128]{3,2,1,0:T(8,128)S(1)} collective-permute-done((f32[2,1,128,128]{3,2,1,0:T(8,128)S(1)}, f32[2,1,128,128]{3,2,1,0:T(8,128)S(1)}, u32[]{:S(2)}, u32[]{:S(2)}) %collective-permute-start) | collective-permute-done | bytes 131104 | tf_op jit(solution)/shard_map/ppermute | solution.py:497
  10.9 2.9 %collective-permute-done.1.refs_2_.refs_4_ = f32[2,1,128,128]{3,2,1,0:T(8,128)S(1)} collective-permute-done((f32[2,1,128,128]{3,2,1,0:T(8,128)S(1)}, f32[2,1,128,128]{3,2,1,0:T(8,128)S(1)}, u32[]{:S(2)}, u32[]{:S(2)}) %collective-permute-start.1) | collective-permute-done | bytes 131104 | tf_op jit(solution)/shard_map/ppermute | solution.py:497
  13.8 1.2 %collective-permute-done.2.refs_3_.refs_5_ = f32[2,1,128,128]{3,2,1,0:T(8,128)S(1)} collective-permute-done((f32[2,1,128,128]{3,2,1,0:T(8,128)S(1)}, f32[2,1,128,128]{3,2,1,0:T(8,128)S(1)}, u32[]{:S(2)}, u32[]{:S(2)}) %collective-permute-start.2) | collective-permute-done | bytes 131104 | tf_op jit(solution)/shard_map/ppermute | solution.py:497
  15.0 0.1 collective-permute-start.3
  15.1 2.8 %collective-permute-start.4 = (f32[1,128,128]{2,1,0:T(8,128)S(1)}, f32[1,128,128]{2,1,0:T(8,128)S(1)}, u32[]{:S(2)}, u32[]{:S(2)}) collective-permute-start(f32[1,128,128]{2,1,0:T(8,128)S(1)} %get-tuple-element.62.refs_0_), channel_id=1, source_target_pairs={{0,4},{1,5},{2,6},{3,7},{4,0},{5,1},{6,2},{7,3},{8,12},{9,13},{10,... | collective-permute-start | bytes 196616 | tf_op jit(solution)/shard_map/ppermute | solution.py:497
  18.0 1.2 %collective-permute-start.5 = (f32[1,128,128]{2,1,0:T(8,128)S(1)}, f32[1,128,128]{2,1,0:T(8,128)S(1)}, u32[]{:S(2)}, u32[]{:S(2)}) collective-permute-start(f32[1,128,128]{2,1,0:T(8,128)S(1)} %collective-permute-done.3.refs_1_), channel_id=1, source_target_pairs={{0,4},{1,5},{2,6},{3,7},{4,0},{5,1},{6,2},{7,3},{8,12},{9,13},{10,... | collective-permute-start | bytes 196616 | tf_op jit(solution)/shard_map/ppermute | solution.py:497
  19.1 2.8 %collective-permute-start.6 = (f32[1,128,128]{2,1,0:T(8,128)S(1)}, f32[1,128,128]{2,1,0:T(8,128)S(1)}, u32[]{:S(2)}, u32[]{:S(2)}) collective-permute-start(f32[1,128,128]{2,1,0:T(8,128)S(1)} %shard_map.88), channel_id=1, source_target_pairs={{0,20},{1,21},{2,22},{3,23},{4,16},{5,17},{6,18},{7,19},{8,28},{9,... | collective-permute-start | bytes 196616 | tf_op jit(solution)/shard_map/ppermute | solution.py:497
  21.9 0.5 collective-permute-start.7
  22.4 4.2 %collective-permute-done.5.refs_3_ = f32[1,128,128]{2,1,0:T(8,128)S(1)} collective-permute-done((f32[1,128,128]{2,1,0:T(8,128)S(1)}, f32[1,128,128]{2,1,0:T(8,128)S(1)}, u32[]{:S(2)}, u32[]{:S(2)}) %collective-permute-start.5) | collective-permute-done | bytes 65568 | tf_op jit(solution)/shard_map/ppermute | solution.py:497
  26.6 2.0 %collective-permute-done.6.refs_4_ = f32[1,128,128]{2,1,0:T(8,128)S(1)} collective-permute-done((f32[1,128,128]{2,1,0:T(8,128)S(1)}, f32[1,128,128]{2,1,0:T(8,128)S(1)}, u32[]{:S(2)}, u32[]{:S(2)}) %collective-permute-start.6) | collective-permute-done | bytes 65568 | tf_op jit(solution)/shard_map/ppermute | solution.py:497
  28.7 0.1 collective-permute-start.8
  28.8 1.2 %collective-permute-done.8.refs_1_ = f32[1,128,128]{2,1,0:T(8,128)S(1)} collective-permute-done((f32[1,128,128]{2,1,0:T(8,128)S(1)}, f32[1,128,128]{2,1,0:T(8,128)S(1)}, u32[]{:S(2)}, u32[]{:S(2)}) %collective-permute-start.8) | collective-permute-done | bytes 65568 | tf_op jit(solution)/shard_map/ppermute | solution.py:497
  30.1 0.1 shard_map.90
  30.2 1.5 %collective-permute-start.9 = (f32[2,1,128,128]{3,2,1,0:T(8,128)S(1)}, f32[2,1,128,128]{3,2,1,0:T(8,128)S(1)}, u32[]{:S(2)}, u32[]{:S(2)}) collective-permute-start(f32[2,1,128,128]{3,2,1,0:T(8,128)S(1)} %get-tuple-element.66), channel_id=1, source_target_pairs={{0,1},{1,0},{2,3},{3,2},{4,5},{5,4},{6,7},{7,6},{8,9},{9,8},{10,11... | collective-permute-start | bytes 393224 | tf_op jit(solution)/shard_map/ppermute | solution.py:497
  31.7 2.0 %collective-permute-start.11 = (f32[2,1,128,128]{3,2,1,0:T(8,128)S(1)}, f32[2,1,128,128]{3,2,1,0:T(8,128)S(1)}, u32[]{:S(2)}, u32[]{:S(2)}) collective-permute-start(f32[2,1,128,128]{3,2,1,0:T(8,128)S(1)} %get-tuple-element.70), channel_id=1, source_target_pairs={{0,3},{1,2},{2,1},{3,0},{4,7},{5,6},{6,5},{7,4},{8,11},{9,10},{10,... | collective-permute-start | bytes 393224 | tf_op jit(solution)/shard_map/ppermute | solution.py:497
  33.7 4.6 %shard_map.91.refs_2_ = f32[1024,1024]{1,0:T(8,128)S(1)} custom-call(bf16[1024,1024]{1,0:T(8,128)(2,1)S(1)} %copy-done, bf16[1024,1024]{1,0:T(8,128)(2,1)S(1)} %get-tuple-element.56.refs_0_.refs_1_.refs_2_, bf16[1024,1024]{1,0:T(8,128)(2,1)S(1)} %get-tuple-element.57.refs_1_.refs_2_.refs_0_.refs_3_), custom_call_target="tpu_custom_call" | custom-call | flops 2147483648 | bytes 21474836 | tf_op jit(solution)/shard_map/pallas_call | solution.py:56
  38.4 0.8 shard_map.92
  39.2 0.6 collective-permute-done.11.refs_0_
  39.8 0.8 shard_map.93
  40.7 3.6 %shard_map.94 = (f32[1024,1024]{1,0:T(8,128)S(1)}, bf16[1024,1024]{1,0:T(8,128)(2,1)S(1)}, bf16[1024,1024]{1,0:T(8,128)(2,1)S(1)}, bf16[2,2,1,128,128]{4,3,2,1,0...) custom-call(f32[2,1,128,128]{3,2,1,0:T(8,128)S(1)} %collective-permu, ...), custom_call_target="tpu_custom_call", output_to_operand_aliasing={{0}: (4, {})} | custom-call | flops 20971520 | bytes 209715 | tf_op jit(solution)/shard_map/pallas_call | solution.py:56
  44.2 1.2 %shard_map.98 = (f32[2,1,128,128]{3,2,1,0:T(8,128)S(1)}, f32[2,2,1,128,128]{4,3,2,1,0:T(8,128)S(1)}, f32[2,1,128,128]{3,2,1,0:T(8,128)S(1)}, f32[2,2,1,128,128]{...) custom-call(bf16[1024,1024]{1,0:T(8,128)(2,1)S(1)} %copy-done, ...), custom_call_target="tpu_custom_call" | custom-call | flops 201326592 | bytes 2013265 | tf_op jit(solution)/shard_map/pallas_call | solution.py:56
  45.5 1.5 %collective-permute-start.12 = (f32[2,1,128,128]{3,2,1,0:T(8,128)S(1)}, f32[2,1,128,128]{3,2,1,0:T(8,128)S(1)}, u32[]{:S(2)}, u32[]{:S(2)}) collective-permute-start(f32[2,1,128,128]{3,2,1,0:T(8,128)S(1)} %get-tuple-element.91), channel_id=1, source_target_pairs={{0,1},{1,0},{2,3},{3,2},{4,5},{5,4},{6,7},{7,6},{8,9},{9,8},{10,11... | collective-permute-start | bytes 393224 | tf_op jit(solution)/shard_map/ppermute | solution.py:497
  47.0 0.3 collective-permute-start.13
  47.3 1.7 %collective-permute-start.14 = (f32[2,1,128,128]{3,2,1,0:T(8,128)S(1)}, f32[2,1,128,128]{3,2,1,0:T(8,128)S(1)}, u32[]{:S(2)}, u32[]{:S(2)}) collective-permute-start(f32[2,1,128,128]{3,2,1,0:T(8,128)S(1)} %get-tuple-element.93), channel_id=1, source_target_pairs={{0,3},{1,2},{2,1},{3,0},{4,7},{5,6},{6,5},{7,4},{8,11},{9,10},{10,... | collective-permute-start | bytes 393224 | tf_op jit(solution)/shard_map/ppermute | solution.py:497
  49.0 2.9 %collective-permute-done.12.refs_1_.refs_3_ = f32[2,1,128,128]{3,2,1,0:T(8,128)S(1)} collective-permute-done((f32[2,1,128,128]{3,2,1,0:T(8,128)S(1)}, f32[2,1,128,128]{3,2,1,0:T(8,128)S(1)}, u32[]{:S(2)}, u32[]{:S(2)}) %collective-permute-start.12) | collective-permute-done | bytes 131104 | tf_op jit(solution)/shard_map/ppermute | solution.py:497
  51.9 0.6 collective-permute-done.13.refs_2_.refs_4_
  52.5 1.4 %collective-permute-done.14.refs_3_.refs_5_ = f32[2,1,128,128]{3,2,1,0:T(8,128)S(1)} collective-permute-done((f32[2,1,128,128]{3,2,1,0:T(8,128)S(1)}, f32[2,1,128,128]{3,2,1,0:T(8,128)S(1)}, u32[]{:S(2)}, u32[]{:S(2)}) %collective-permute-start.14) | collective-permute-done | bytes 131104 | tf_op jit(solution)/shard_map/ppermute | solution.py:497
  54.0 0.1 collective-permute-start.15
  54.0 3.2 %collective-permute-start.16 = (f32[1,128,128]{2,1,0:T(8,128)S(1)}, f32[1,128,128]{2,1,0:T(8,128)S(1)}, u32[]{:S(2)}, u32[]{:S(2)}) collective-permute-start(f32[1,128,128]{2,1,0:T(8,128)S(1)} %get-tuple-element.94.refs_0_), channel_id=1, source_target_pairs={{0,4},{1,5},{2,6},{3,7},{4,0},{5,1},{6,2},{7,3},{8,12},{9,13},{10,... | collective-permute-start | bytes 196616 | tf_op jit(solution)/shard_map/ppermute | solution.py:497
  57.3 1.2 %collective-permute-start.18 = (f32[1,128,128]{2,1,0:T(8,128)S(1)}, f32[1,128,128]{2,1,0:T(8,128)S(1)}, u32[]{:S(2)}, u32[]{:S(2)}) collective-permute-start(f32[1,128,128]{2,1,0:T(8,128)S(1)} %shard_map.100), channel_id=1, source_target_pairs={{0,20},{1,21},{2,22},{3,23},{4,16},{5,17},{6,18},{7,19},{8,28},{9,... | collective-permute-start | bytes 196616 | tf_op jit(solution)/shard_map/ppermute | solution.py:497
  58.4 1.5 %collective-permute-start.19 = (f32[1,128,128]{2,1,0:T(8,128)S(1)}, f32[1,128,128]{2,1,0:T(8,128)S(1)}, u32[]{:S(2)}, u32[]{:S(2)}) collective-permute-start(f32[1,128,128]{2,1,0:T(8,128)S(1)} %shard_map.100), channel_id=1, source_target_pairs={{0,16},{1,17},{2,18},{3,19},{4,20},{5,21},{6,22},{7,23},{8,24},{9,... | collective-permute-start | bytes 196616 | tf_op jit(solution)/shard_map/ppermute | solution.py:497
  60.0 1.8 %collective-permute-start.17 = (f32[1,128,128]{2,1,0:T(8,128)S(1)}, f32[1,128,128]{2,1,0:T(8,128)S(1)}, u32[]{:S(2)}, u32[]{:S(2)}) collective-permute-start(f32[1,128,128]{2,1,0:T(8,128)S(1)} %collective-permute-done.15.refs_1_), channel_id=1, source_target_pairs={{0,4},{1,5},{2,6},{3,7},{4,0},{5,1},{6,2},{7,3},{8,12},{9,13},{10,... | collective-permute-start | bytes 196616 | tf_op jit(solution)/shard_map/ppermute | solution.py:497
  61.7 2.6 %shard_map.85.refs_0_ = bf16[2,8,512,512]{3,2,1,0:T(8,128)(2,1)S(1)} custom-call(bf16[1024,1024]{1,0:T(8,128)(2,1)S(1)} %get-tuple-element.56.refs_0_.refs_1_.refs_2_, bf16[1024,1024]{1,0:T(8,128)(2,1)S(1)} %copy-done), custom_call_target="tpu_custom_call" | custom-call | flops 1073741824 | bytes 10737418 | tf_op jit(solution)/shard_map/pallas_call | solution.py:56
  64.4 2.6 %collective-permute-done.17.refs_3_ = f32[1,128,128]{2,1,0:T(8,128)S(1)} collective-permute-done((f32[1,128,128]{2,1,0:T(8,128)S(1)}, f32[1,128,128]{2,1,0:T(8,128)S(1)}, u32[]{:S(2)}, u32[]{:S(2)}) %collective-permute-start.17) | collective-permute-done | bytes 65568 | tf_op jit(solution)/shard_map/ppermute | solution.py:497
  67.0 0.1 collective-permute-start.20
  67.1 5.7 %shard_map.96.refs_3_ = bf16[1024,1024]{1,0:T(8,128)(2,1)S(1)} custom-call(bf16[1024,1024]{1,0:T(8,128)(2,1)S(1)} %get-tuple-element.80.refs_1_.refs_0_, bf16[1024,1024]{1,0:T(8,128)(2,1)S(1)} %get-tuple-element.57.refs_1_.refs_2_.refs_0_.refs_3_, bf16[1024,1024]{1,0:T(8,128)(2,1)S(1)} %get-tuple-element.56.refs_0_.refs_1_.refs_2_, ...), custom_call_target="tpu_custom_call" | custom-call | flops 2147483648 | bytes 21474836 | tf_op jit(solution)/shard_map/pallas_call | solution.py:56
  72.8 0.1 shard_map.102
  72.9 1.0 %collective-permute-start.21 = (f32[2,1,128,128]{3,2,1,0:T(8,128)S(1)}, f32[2,1,128,128]{3,2,1,0:T(8,128)S(1)}, u32[]{:S(2)}, u32[]{:S(2)}) collective-permute-start(f32[2,1,128,128]{3,2,1,0:T(8,128)S(1)} %get-tuple-element.99), channel_id=1, source_target_pairs={{0,1},{1,0},{2,3},{3,2},{4,5},{5,4},{6,7},{7,6},{8,9},{9,8},{10,11... | collective-permute-start | bytes 393224 | tf_op jit(solution)/shard_map/ppermute | solution.py:497
  74.0 0.7 collective-permute-start.22
  74.7 1.8 %collective-permute-start.23 = (f32[2,1,128,128]{3,2,1,0:T(8,128)S(1)}, f32[2,1,128,128]{3,2,1,0:T(8,128)S(1)}, u32[]{:S(2)}, u32[]{:S(2)}) collective-permute-start(f32[2,1,128,128]{3,2,1,0:T(8,128)S(1)} %get-tuple-element.101), channel_id=1, source_target_pairs={{0,3},{1,2},{2,1},{3,0},{4,7},{5,6},{6,5},{7,4},{8,11},{9,10},{10,... | collective-permute-start | bytes 393224 | tf_op jit(solution)/shard_map/ppermute | solution.py:497
  76.5 4.4 %shard_map.97 = (f32[1024,1024]{1,0:T(8,128)S(1)}, bf16[1024,1024]{1,0:T(8,128)(2,1)}) custom-call(bf16[1024,1024]{1,0:T(8,128)(2,1)S(1)} %get-tuple-element.57.refs_1_.refs_2_.refs_0_.refs_3_, bf16[1024,1024]{1,0:T(8,128)(2,1)S(1)} %get-tuple-element.80.refs_1_.refs_0_, bf16[1024,1024]{1,0:T(8,128)(2,1)S(1)} %copy-done, ...), custom_call_target="tpu_custom_call" | custom-call | flops 2147483648 | bytes 21474836 | tf_op jit(solution)/shard_map/pallas_call | solution.py:56
  80.9 2.4 %shard_map.95 = (f32[1024,1024]{1,0:T(8,128)S(1)}, bf16[1024,1024]{1,0:T(8,128)(2,1)}) custom-call(bf16[2,8,512,512]{3,2,1,0:T(8,128)(2,1)S(1)} %shard_map.85.refs_0_, bf16[1024,1024]{1,0:T(8,128)(2,1)S(1)} %get-tuple-element.80.refs_1_.refs_0_, bf16[1024,1024]{1,0:T(8,128)(2,1)S(1)} %get-tuple-element.81.refs_2_), custom_call_target="tpu_custom_call" | custom-call | flops 1073741824 | bytes 10737418 | tf_op jit(solution)/shard_map/pallas_call | solution.py:56
  83.4 3.6 %shard_map.103 = (bf16[1024,1024]{1,0:T(8,128)(2,1)}, bf16[1024,1024]{1,0:T(8,128)(2,1)}) custom-call(f32[1024,1024]{1,0:T(8,128)S(1)} %get-tuple-element.88.refs_0_, f32[1024,1024]{1,0:T(8,128)S(1)} %get-tuple-element.89.refs_1_, bf16[1024,1024]{1,0:T(8,128)(2,1)S(1)} %get-tuple-element.56.refs_0_.refs_1_.refs_2_, ...), custom_call_target="tpu_custom_call" | custom-call | flops 536870912 | bytes 5368709 | tf_op jit(solution)/shard_map/pallas_call | solution.py:56
  (26 shorter events, 0.2 us)
Async XLA Ops:
  3.2 30.6 %copy-start = (bf16[1024,1024]{1,0:T(8,128)(2,1)S(1)}, bf16[1024,1024]{1,0:T(8,128)(2,1)}, u32[]{:S(2)}) copy-start(bf16[1024,1024]{1,0:T(8,128)(2,1)} %refs_0_.5) | copy-start | bytes 6291460
  4.4 6.5 %collective-permute-start = (f32[2,1,128,128]{3,2,1,0:T(8,128)S(1)}, f32[2,1,128,128]{3,2,1,0:T(8,128)S(1)}, u32[]{:S(2)}, u32[]{:S(2)}) collective-permute-start(f32[2,1,128,128]{3,2,1,0:T(8,128)S(1)} %get-tuple-element.59), channel_id=1, source_target_pairs={{0,1},{1,0},{2,3},{3,2},{4,5},{5,4},{6,7},{7,6},{8,9},{9,8},{10,11... | collective-permute-start | bytes 393224 | tf_op jit(solution)/shard_map/ppermute | solution.py:497
  7.4 6.4 %collective-permute-start.1 = (f32[2,1,128,128]{3,2,1,0:T(8,128)S(1)}, f32[2,1,128,128]{3,2,1,0:T(8,128)S(1)}, u32[]{:S(2)}, u32[]{:S(2)}) collective-permute-start(f32[2,1,128,128]{3,2,1,0:T(8,128)S(1)} %get-tuple-element.60), channel_id=1, source_target_pairs={{0,2},{1,3},{2,0},{3,1},{4,6},{5,7},{6,4},{7,5},{8,10},{9,11},{10,... | collective-permute-start | bytes 393224 | tf_op jit(solution)/shard_map/ppermute | solution.py:497
  9.0 6.0 %collective-permute-start.2 = (f32[2,1,128,128]{3,2,1,0:T(8,128)S(1)}, f32[2,1,128,128]{3,2,1,0:T(8,128)S(1)}, u32[]{:S(2)}, u32[]{:S(2)}) collective-permute-start(f32[2,1,128,128]{3,2,1,0:T(8,128)S(1)} %get-tuple-element.61), channel_id=1, source_target_pairs={{0,3},{1,2},{2,1},{3,0},{4,7},{5,6},{6,5},{7,4},{8,11},{9,10},{10,... | collective-permute-start | bytes 393224 | tf_op jit(solution)/shard_map/ppermute | solution.py:497
  15.0 2.9 %collective-permute-start.3 = (f32[1,128,128]{2,1,0:T(8,128)S(1)}, f32[1,128,128]{2,1,0:T(8,128)S(1)}, u32[]{:S(2)}, u32[]{:S(2)}) collective-permute-start(f32[1,128,128]{2,1,0:T(8,128)S(1)} %get-tuple-element.63), channel_id=1, source_target_pairs={{0,8},{1,9},{2,10},{3,11},{4,12},{5,13},{6,14},{7,15},{8,0},{9,1},... | collective-permute-start | bytes 196616 | tf_op jit(solution)/shard_map/ppermute | solution.py:497
  15.1 7.3 %collective-permute-start.4 = (f32[1,128,128]{2,1,0:T(8,128)S(1)}, f32[1,128,128]{2,1,0:T(8,128)S(1)}, u32[]{:S(2)}, u32[]{:S(2)}) collective-permute-start(f32[1,128,128]{2,1,0:T(8,128)S(1)} %get-tuple-element.62.refs_0_), channel_id=1, source_target_pairs={{0,4},{1,5},{2,6},{3,7},{4,0},{5,1},{6,2},{7,3},{8,12},{9,13},{10,... | collective-permute-start | bytes 196616 | tf_op jit(solution)/shard_map/ppermute | solution.py:497
  18.0 8.7 %collective-permute-start.5 = (f32[1,128,128]{2,1,0:T(8,128)S(1)}, f32[1,128,128]{2,1,0:T(8,128)S(1)}, u32[]{:S(2)}, u32[]{:S(2)}) collective-permute-start(f32[1,128,128]{2,1,0:T(8,128)S(1)} %collective-permute-done.3.refs_1_), channel_id=1, source_target_pairs={{0,4},{1,5},{2,6},{3,7},{4,0},{5,1},{6,2},{7,3},{8,12},{9,13},{10,... | collective-permute-start | bytes 196616 | tf_op jit(solution)/shard_map/ppermute | solution.py:497
  19.1 9.5 %collective-permute-start.6 = (f32[1,128,128]{2,1,0:T(8,128)S(1)}, f32[1,128,128]{2,1,0:T(8,128)S(1)}, u32[]{:S(2)}, u32[]{:S(2)}) collective-permute-start(f32[1,128,128]{2,1,0:T(8,128)S(1)} %shard_map.88), channel_id=1, source_target_pairs={{0,20},{1,21},{2,22},{3,23},{4,16},{5,17},{6,18},{7,19},{8,28},{9,... | collective-permute-start | bytes 196616 | tf_op jit(solution)/shard_map/ppermute | solution.py:497
  21.9 6.8 %collective-permute-start.7 = (f32[1,128,128]{2,1,0:T(8,128)S(1)}, f32[1,128,128]{2,1,0:T(8,128)S(1)}, u32[]{:S(2)}, u32[]{:S(2)}) collective-permute-start(f32[1,128,128]{2,1,0:T(8,128)S(1)} %shard_map.88), channel_id=1, source_target_pairs={{0,16},{1,17},{2,18},{3,19},{4,20},{5,21},{6,22},{7,23},{8,24},{9,... | collective-permute-start | bytes 196616 | tf_op jit(solution)/shard_map/ppermute | solution.py:497
  28.7 1.3 %collective-permute-start.8 = (f32[1,128,128]{2,1,0:T(8,128)S(1)}, f32[1,128,128]{2,1,0:T(8,128)S(1)}, u32[]{:S(2)}, u32[]{:S(2)}) collective-permute-start(f32[1,128,128]{2,1,0:T(8,128)S(1)} %get-tuple-element.65), channel_id=1, source_target_pairs={{0,8},{1,9},{2,10},{3,11},{4,12},{5,13},{6,14},{7,15},{8,0},{9,1},... | collective-permute-start | bytes 196616 | tf_op jit(solution)/shard_map/ppermute | solution.py:497
  30.2 10.5 %collective-permute-start.9 = (f32[2,1,128,128]{3,2,1,0:T(8,128)S(1)}, f32[2,1,128,128]{3,2,1,0:T(8,128)S(1)}, u32[]{:S(2)}, u32[]{:S(2)}) collective-permute-start(f32[2,1,128,128]{3,2,1,0:T(8,128)S(1)} %get-tuple-element.66), channel_id=1, source_target_pairs={{0,1},{1,0},{2,3},{3,2},{4,5},{5,4},{6,7},{7,6},{8,9},{9,8},{10,11... | collective-permute-start | bytes 393224 | tf_op jit(solution)/shard_map/ppermute | solution.py:497
  31.7 8.9 %collective-permute-start.10 = (f32[2,1,128,128]{3,2,1,0:T(8,128)S(1)}, f32[2,1,128,128]{3,2,1,0:T(8,128)S(1)}, u32[]{:S(2)}, u32[]{:S(2)}) collective-permute-start(f32[2,1,128,128]{3,2,1,0:T(8,128)S(1)} %get-tuple-element.67), channel_id=1, source_target_pairs={{0,2},{1,3},{2,0},{3,1},{4,6},{5,7},{6,4},{7,5},{8,10},{9,11},{10,... | collective-permute-start | bytes 393224 | tf_op jit(solution)/shard_map/ppermute | solution.py:497
  31.7 6.6 %copy-start.1 = (bf16[1024,1024]{1,0:T(8,128)(2,1)S(1)}, bf16[1024,1024]{1,0:T(8,128)(2,1)}, u32[]{:S(2)}) copy-start(bf16[1024,1024]{1,0:T(8,128)(2,1)} %refs_6_.1) | copy-start | bytes 6291460
  31.7 6.6 %copy-start.2 = (f32[1024]{0:T(1024)S(1)}, f32[1024]{0:T(1024)}, u32[]{:S(2)}) copy-start(f32[1024]{0:T(1024)} %param.8) | copy-start | bytes 12292
  31.7 8.1 %collective-permute-start.11 = (f32[2,1,128,128]{3,2,1,0:T(8,128)S(1)}, f32[2,1,128,128]{3,2,1,0:T(8,128)S(1)}, u32[]{:S(2)}, u32[]{:S(2)}) collective-permute-start(f32[2,1,128,128]{3,2,1,0:T(8,128)S(1)} %get-tuple-element.70), channel_id=1, source_target_pairs={{0,3},{1,2},{2,1},{3,0},{4,7},{5,6},{6,5},{7,4},{8,11},{9,10},{10,... | collective-permute-start | bytes 393224 | tf_op jit(solution)/shard_map/ppermute | solution.py:497
  45.5 6.4 %collective-permute-start.12 = (f32[2,1,128,128]{3,2,1,0:T(8,128)S(1)}, f32[2,1,128,128]{3,2,1,0:T(8,128)S(1)}, u32[]{:S(2)}, u32[]{:S(2)}) collective-permute-start(f32[2,1,128,128]{3,2,1,0:T(8,128)S(1)} %get-tuple-element.91), channel_id=1, source_target_pairs={{0,1},{1,0},{2,3},{3,2},{4,5},{5,4},{6,7},{7,6},{8,9},{9,8},{10,11... | collective-permute-start | bytes 393224 | tf_op jit(solution)/shard_map/ppermute | solution.py:497
  47.0 5.5 %collective-permute-start.13 = (f32[2,1,128,128]{3,2,1,0:T(8,128)S(1)}, f32[2,1,128,128]{3,2,1,0:T(8,128)S(1)}, u32[]{:S(2)}, u32[]{:S(2)}) collective-permute-start(f32[2,1,128,128]{3,2,1,0:T(8,128)S(1)} %get-tuple-element.92), channel_id=1, source_target_pairs={{0,2},{1,3},{2,0},{3,1},{4,6},{5,7},{6,4},{7,5},{8,10},{9,11},{10,... | collective-permute-start | bytes 393224 | tf_op jit(solution)/shard_map/ppermute | solution.py:497
  47.3 6.6 %collective-permute-start.14 = (f32[2,1,128,128]{3,2,1,0:T(8,128)S(1)}, f32[2,1,128,128]{3,2,1,0:T(8,128)S(1)}, u32[]{:S(2)}, u32[]{:S(2)}) collective-permute-start(f32[2,1,128,128]{3,2,1,0:T(8,128)S(1)} %get-tuple-element.93), channel_id=1, source_target_pairs={{0,3},{1,2},{2,1},{3,0},{4,7},{5,6},{6,5},{7,4},{8,11},{9,10},{10,... | collective-permute-start | bytes 393224 | tf_op jit(solution)/shard_map/ppermute | solution.py:497
  54.0 3.3 %collective-permute-start.15 = (f32[1,128,128]{2,1,0:T(8,128)S(1)}, f32[1,128,128]{2,1,0:T(8,128)S(1)}, u32[]{:S(2)}, u32[]{:S(2)}) collective-permute-start(f32[1,128,128]{2,1,0:T(8,128)S(1)} %get-tuple-element.95), channel_id=1, source_target_pairs={{0,8},{1,9},{2,10},{3,11},{4,12},{5,13},{6,14},{7,15},{8,0},{9,1},... | collective-permute-start | bytes 196616 | tf_op jit(solution)/shard_map/ppermute | solution.py:497
  54.0 10.3 %collective-permute-start.16 = (f32[1,128,128]{2,1,0:T(8,128)S(1)}, f32[1,128,128]{2,1,0:T(8,128)S(1)}, u32[]{:S(2)}, u32[]{:S(2)}) collective-permute-start(f32[1,128,128]{2,1,0:T(8,128)S(1)} %get-tuple-element.94.refs_0_), channel_id=1, source_target_pairs={{0,4},{1,5},{2,6},{3,7},{4,0},{5,1},{6,2},{7,3},{8,12},{9,13},{10,... | collective-permute-start | bytes 196616 | tf_op jit(solution)/shard_map/ppermute | solution.py:497
  57.3 9.7 %collective-permute-start.18 = (f32[1,128,128]{2,1,0:T(8,128)S(1)}, f32[1,128,128]{2,1,0:T(8,128)S(1)}, u32[]{:S(2)}, u32[]{:S(2)}) collective-permute-start(f32[1,128,128]{2,1,0:T(8,128)S(1)} %shard_map.100), channel_id=1, source_target_pairs={{0,20},{1,21},{2,22},{3,23},{4,16},{5,17},{6,18},{7,19},{8,28},{9,... | collective-permute-start | bytes 196616 | tf_op jit(solution)/shard_map/ppermute | solution.py:497
  58.4 8.5 %collective-permute-start.19 = (f32[1,128,128]{2,1,0:T(8,128)S(1)}, f32[1,128,128]{2,1,0:T(8,128)S(1)}, u32[]{:S(2)}, u32[]{:S(2)}) collective-permute-start(f32[1,128,128]{2,1,0:T(8,128)S(1)} %shard_map.100), channel_id=1, source_target_pairs={{0,16},{1,17},{2,18},{3,19},{4,20},{5,21},{6,22},{7,23},{8,24},{9,... | collective-permute-start | bytes 196616 | tf_op jit(solution)/shard_map/ppermute | solution.py:497
  60.0 7.0 %collective-permute-start.17 = (f32[1,128,128]{2,1,0:T(8,128)S(1)}, f32[1,128,128]{2,1,0:T(8,128)S(1)}, u32[]{:S(2)}, u32[]{:S(2)}) collective-permute-start(f32[1,128,128]{2,1,0:T(8,128)S(1)} %collective-permute-done.15.refs_1_), channel_id=1, source_target_pairs={{0,4},{1,5},{2,6},{3,7},{4,0},{5,1},{6,2},{7,3},{8,12},{9,13},{10,... | collective-permute-start | bytes 196616 | tf_op jit(solution)/shard_map/ppermute | solution.py:497
  67.0 5.8 %collective-permute-start.20 = (f32[1,128,128]{2,1,0:T(8,128)S(1)}, f32[1,128,128]{2,1,0:T(8,128)S(1)}, u32[]{:S(2)}, u32[]{:S(2)}) collective-permute-start(f32[1,128,128]{2,1,0:T(8,128)S(1)} %get-tuple-element.97), channel_id=1, source_target_pairs={{0,8},{1,9},{2,10},{3,11},{4,12},{5,13},{6,14},{7,15},{8,0},{9,1},... | collective-permute-start | bytes 196616 | tf_op jit(solution)/shard_map/ppermute | solution.py:497
  72.9 10.4 %collective-permute-start.21 = (f32[2,1,128,128]{3,2,1,0:T(8,128)S(1)}, f32[2,1,128,128]{3,2,1,0:T(8,128)S(1)}, u32[]{:S(2)}, u32[]{:S(2)}) collective-permute-start(f32[2,1,128,128]{3,2,1,0:T(8,128)S(1)} %get-tuple-element.99), channel_id=1, source_target_pairs={{0,1},{1,0},{2,3},{3,2},{4,5},{5,4},{6,7},{7,6},{8,9},{9,8},{10,11... | collective-permute-start | bytes 393224 | tf_op jit(solution)/shard_map/ppermute | solution.py:497
  74.0 9.4 %collective-permute-start.22 = (f32[2,1,128,128]{3,2,1,0:T(8,128)S(1)}, f32[2,1,128,128]{3,2,1,0:T(8,128)S(1)}, u32[]{:S(2)}, u32[]{:S(2)}) collective-permute-start(f32[2,1,128,128]{3,2,1,0:T(8,128)S(1)} %get-tuple-element.100), channel_id=1, source_target_pairs={{0,2},{1,3},{2,0},{3,1},{4,6},{5,7},{6,4},{7,5},{8,10},{9,11},{10,... | collective-permute-start | bytes 393224 | tf_op jit(solution)/shard_map/ppermute | solution.py:497
  74.7 8.7 %collective-permute-start.23 = (f32[2,1,128,128]{3,2,1,0:T(8,128)S(1)}, f32[2,1,128,128]{3,2,1,0:T(8,128)S(1)}, u32[]{:S(2)}, u32[]{:S(2)}) collective-permute-start(f32[2,1,128,128]{3,2,1,0:T(8,128)S(1)} %get-tuple-element.101), channel_id=1, source_target_pairs={{0,3},{1,2},{2,1},{3,0},{4,7},{5,6},{6,5},{7,4},{8,11},{9,10},{10,... | collective-permute-start | bytes 393224 | tf_op jit(solution)/shard_map/ppermute | solution.py:497

commit v5 on v4

--- a/solution.py
+++ b/solution.py
@@ -16,15 +16,12 @@
 LANES = 2
 QUAD = 4
 SHARE = H // (LANES * QUAD)
-TILE = 256
 CUT = 256
 SLAB = 256
 ORDER = (3, 1, 2, 0)
 EARLY = (0, 3)
 UNROLL = 4
 PAIR = 2
-UNROLL_FINAL = 4
-DEPTH = 2
 F32 = jnp.float32
 BF16 = jnp.bfloat16
 
@@ -69,15 +66,6 @@
     return pl.ds(pl.multiple_of(head * HD, HD), HD)
 
 
-def over_heads(step, unroll):
-    def several(i, _):
-        for j in range(unroll):
-            step(i * unroll + j)
-        return 0
-
-    lax.fori_loop(0, H // unroll, several, 0)
-
-
 def heads_of(slot, where):
     for lane in range(LANES):
         for share in range(SHARE):
@@ -121,33 +109,34 @@
     return {slot: outs[2 * i : 2 * i + 2] for i, slot in enumerate(slots)}
 
 
-def load_kernel(slot, where, k_far, v_far, piece_ref, inside_ref, k_ref, v_ref, sems):
-    blocks = k_ref.shape[0] // BLOCK
+def first_kernel(slot, where, k_far, v_far, piece_ref, inside_ref, k_ref, v_ref, sems):
     copies = []
-    for block in range(blocks):
-        rows = pl.ds(block * BLOCK, BLOCK)
+    for at, (_, _, head) in enumerate(heads_of(slot, where)):
         for j, (source, target) in enumerate(((k_far, k_ref), (v_far, v_ref))):
-            copy = pltpu.make_async_copy(source.at[rows, :], target.at[rows, :], sems.at[block, j])
+            copy = pltpu.make_async_copy(source.at[:, head_cols(head)], target.at[at], sems.at[at, j])
+            copy.start()
             copies.append(copy)
-    for copy in copies[: 2 * DEPTH]:
-        copy.start()
-    for block in range(blocks):
-        for j in range(2):
-            copies[2 * block + j].wait()
-            if block + DEPTH < blocks:
-                copies[2 * (block + DEPTH) + j].start()
-        slot_block(slot, False, where, block, blocks, k_ref, v_ref, piece_ref, inside_ref)
-
-
-def load_totals(slot, keys, values):
-    tokens, features = keys.shape
-    blocks = tokens // BLOCK
-    return call(
-        functools.partial(load_kernel, slot),
-        slot_shapes(blocks) + [vmem(tokens, features, dtype=BF16)] * 2,
+    for at, (lane, share, _) in enumerate(heads_of(slot, where)):
+        copies[2 * at].wait()
+        copies[2 * at + 1].wait()
+        run = None
+        for block in range(inside_ref.shape[0]):
+            rows = pl.ds(block * BLOCK, BLOCK)
+            state = mm(k_ref[at, rows, :], v_ref[at, rows, :], 0, 0)
+            inside_ref[block, lane, share] = jnp.zeros_like(state) if run is None else run
+            run = state if run is None else run + state
+        piece_ref[lane, share] = run
+
+
+def first_totals(slot, keys, values):
+    tokens, _ = keys.shape
+    heads = LANES * SHARE
+    return call(
+        functools.partial(first_kernel, slot),
+        slot_shapes(tokens // BLOCK),
         [keys, values],
-        2 * tokens * features * HD,
-        scratch=[pltpu.SemaphoreType.DMA((blocks, 2))],
+        2 * tokens * heads * HD * HD,
+        scratch=[vmem(heads, tokens, HD, dtype=BF16)] * 2 + [pltpu.SemaphoreType.DMA((heads, 2))],
         far_in=(0, 1),
     )
 
@@ -439,51 +428,44 @@
     )
 
 
-def final_kernel(where, lk_ref, lv_ref, k_ref, v_ref, *refs):
-    carried, later = refs[:QUAD], refs[QUAD : 2 * QUAD]
-    gk_far, gv_far, gk_ref, gv_ref, state_ref, sems = refs[2 * QUAD :]
-    for slot in range(QUAD):
+def final_kernel(slots, where, lk_ref, lv_ref, k_ref, v_ref, *refs):
+    count = len(slots)
+    carried, later = refs[:count], refs[count : 2 * count]
+    gk_far, gv_far, gk_ref, gv_ref, sems = refs[-5:]
+    copies = []
+    for i, slot in enumerate(slots):
         for lane, share, head in heads_of(slot, where):
-            for b in range(k_ref.shape[0] // BLOCK):
-                state = carried[slot][lane, share] + later[slot][b, lane, share]
-                state_ref[b, head] = state.astype(BF16)
-
-    copies = []
-    for i in range(k_ref.shape[0] // TILE):
-        rows = pl.ds(i * TILE, TILE)
-        block = i // (BLOCK // TILE)
-
-        def one(head):
-            cols = head_cols(head)
-            state = state_ref[block, head]
-            gk_ref[rows, cols] = (lk_ref[rows, cols] + mm(v_ref[rows, cols], state, 1, 1)).astype(BF16)
-            gv_ref[rows, cols] = (lv_ref[rows, cols] + mm(k_ref[rows, cols], state, 1, 0)).astype(BF16)
-
-        over_heads(one, UNROLL_FINAL)
-        for j, (source, target) in enumerate(((gk_ref, gk_far), (gv_ref, gv_far))):
-            copy = pltpu.make_async_copy(source.at[rows, :], target.at[rows, :], sems.at[i, j])
-            copy.start()
-            copies.append(copy)
+            cols, at = head_cols(head), len(copies) // 2
+            for block in range(k_ref.shape[0] // BLOCK):
+                rows = pl.ds(block * BLOCK, BLOCK)
+                state = (carried[i][lane, share] + later[i][block, lane, share]).astype(BF16)
+                grad_k = lk_ref[rows, cols] + mm(v_ref[rows, cols], state, 1, 1)
+                grad_v = lv_ref[rows, cols] + mm(k_ref[rows, cols], state, 1, 0)
+                gk_ref[at, rows, :], gv_ref[at, rows, :] = grad_k.astype(BF16), grad_v.astype(BF16)
+            for j, (source, target) in enumerate(((gk_ref, gk_far), (gv_ref, gv_far))):
+                copy = pltpu.make_async_copy(source.at[at], target.at[:, cols], sems.at[at, j])
+                copy.start()
+                copies.append(copy)
     for copy in copies:
         copy.wait()
 
 
-def final_part(local_k, local_v, keys, values, carried, later):
+def final_part(slots, local_k, local_v, keys, values, carried, later, made=()):
     tokens, features = keys.shape
-    blocks = tokens // BLOCK
-    return call(
-        final_kernel,
+    heads = len(slots) * LANES * SHARE
+    args = [local_k, local_v, keys, values]
+    args += [carried[o] for o in slots] + [later[o] for o in slots]
+    places = range(len(args), len(args) + len(made))
+    return call(
+        functools.partial(final_kernel, slots),
         [jax.ShapeDtypeStruct((tokens, features), BF16)] * 2,
-        [local_k, local_v, keys, values, *carried, *later],
-        4 * tokens * features * HD,
-        scratch=[
-            vmem(tokens, features, dtype=BF16),
-            vmem(tokens, features, dtype=BF16),
-            vmem(blocks, H, HD, HD, dtype=BF16),
-            pltpu.SemaphoreType.DMA((tokens // TILE, 2)),
-        ],
+        [*args, *made],
+        4 * tokens * heads * HD * HD,
+        scratch=[vmem(heads, tokens, HD, dtype=BF16)] * 2 + [pltpu.SemaphoreType.DMA((heads, 2))],
+        far_in=places,
         far_out=(0, 1),
         grant=12,
+        aliases={place: i for i, place in enumerate(places)},
     )
 
 
@@ -598,8 +580,8 @@
 
 def body(queries, key_rows, value_rows, norm_gain, cotangent):
     gain = norm_gain[None, :]
-    *first, keys, values = load_totals(ORDER[0], key_rows, value_rows)
-    queries, cotangent = near(queries), near(cotangent)
+    first = first_totals(ORDER[0], key_rows, value_rows)
+    keys, values, queries, cotangent = (near(a) for a in (key_rows, value_rows, queries, cotangent))
     carried, inside = carry(first, (keys, values), False)
     attended = local_part(queries, keys, values)
     scores = turned_scores(keys, queries)
@@ -618,7 +600,9 @@
     local_v, normed = value_part(scores, grads, normed)
     grad_q = query_part(grads, values, keys, priors)
     local_k, grad_q = turned_part(values, grads, queries, grad_q)
-    grad_k, grad_v = final_part(local_k, local_v, keys, values, carried, later)
+    args = local_k, local_v, keys, values, carried, later
+    made = final_part((0,), *args)
+    grad_k, grad_v = final_part(ORDER[:-1], *args, made)
     return normed, grad_q, grad_k, grad_v
 
 

time: 87.2 us -> 89.6 us (1.028)
  local copies, waits for them, and re-layouts: 0.01 us -> 3.2 us
  starting transfers between devices: 30.5 us -> 29.4 us
    unnamed x6 -> x14, local copies, waits for them, and re-layouts: 0.01 us -> 3.2 us
    ppermute x24, starting transfers between devices: 30.5 us -> 29.4 us  [moved(): return lax.ppermute(value, AXES, pairs)]
    pallas_call x20 -> x21, Pallas kernels: 33.9 us -> 33.8 us  [call(): pl.pallas_call(lambda *refs: kernel(place(), *refs), out_shape=out_shape,...]
  transfers between devices with their start and end apart: 24 -> 24, of which waited for: 11 -> 11; matrix products, arithmetic and copies ran while one was open for 0% -> 0% of each run, Pallas kernels for 25% -> 28%
where the time goes in v5:
time: 89.6 us; the launch traced here: 89.4 us
  Pallas kernels  33.8 us (38%)
  starting transfers between devices  29.4 us (33%)
  waiting for transfers between devices  22 us (25%)
  local copies, waits for them, and re-layouts  3.2 us (4%)
  between operations  1.07 us (1%)
    pallas_call x21, Pallas kernels, call(): pl.pallas_call(lambda *refs: kernel(place(), *refs), out_shape=out_shape,...  33.8 us
    ppermute x24, starting transfers between devices, moved(): return lax.ppermute(value, AXES, pairs)  29.4 us
    ppermute x24, waiting for transfers between devices, moved(): return lax.ppermute(value, AXES, pairs)  22 us
    unnamed x14, local copies, waits for them, and re-layouts  3.2 us
  transfers between devices with their start and end apart: 24, of which 11 were waited for; matrix products, arithmetic and copies ran while one was open for 0% of the time, Pallas kernels for 28%

profile of v5, /device:TPU:0, one launch (start us, length us, event | category | flops | bytes accessed | tf_op | source)
XLA Modules:
  0.0 89.4 jit_solution(5935602808141933904)
XLA Ops:
  0.6 1.6 %copy-done = bf16[1024,1024]{1,0:T(8,128)(2,1)S(1)} copy-done((bf16[1024,1024]{1,0:T(8,128)(2,1)S(1)}, bf16[1024,1024]{1,0:T(8,128)(2,1)}, u32[]{:S(2)}) %copy-start) | copy-done | bytes 2097176
  2.2 1.6 %copy-done.2 = bf16[1024,1024]{1,0:T(8,128)(2,1)S(1)} copy-done((bf16[1024,1024]{1,0:T(8,128)(2,1)S(1)}, bf16[1024,1024]{1,0:T(8,128)(2,1)}, u32[]{:S(2)}) %copy-start.2) | copy-done | bytes 2097176
  3.8 1.2 %shard_map.85 = (f32[2,1,128,128]{3,2,1,0:T(8,128)S(1)}, f32[2,2,1,128,128]{4,3,2,1,0:T(8,128)S(1)}, f32[2,1,128,128]{3,2,1,0:T(8,128)S(1)}, f32[2,2,1,128,128]{...) custom-call(bf16[1024,1024]{1,0:T(8,128)(2,1)S(1)} %copy-done, ...), custom_call_target="tpu_custom_call" | custom-call | flops 201326592 | bytes 2013265 | tf_op jit(solution)/shard_map/pallas_call | solution.py:53
  5.0 3.0 %collective-permute-start = (f32[2,1,128,128]{3,2,1,0:T(8,128)S(1)}, f32[2,1,128,128]{3,2,1,0:T(8,128)S(1)}, u32[]{:S(2)}, u32[]{:S(2)}) collective-permute-start(f32[2,1,128,128]{3,2,1,0:T(8,128)S(1)} %get-tuple-element.57), channel_id=1, source_target_pairs={{0,1},{1,0},{2,3},{3,2},{4,5},{5,4},{6,7},{7,6},{8,9},{9,8},{10,11... | collective-permute-start | bytes 393224 | tf_op jit(solution)/shard_map/ppermute | solution.py:479
  8.1 1.6 %collective-permute-start.1 = (f32[2,1,128,128]{3,2,1,0:T(8,128)S(1)}, f32[2,1,128,128]{3,2,1,0:T(8,128)S(1)}, u32[]{:S(2)}, u32[]{:S(2)}) collective-permute-start(f32[2,1,128,128]{3,2,1,0:T(8,128)S(1)} %get-tuple-element.58), channel_id=1, source_target_pairs={{0,2},{1,3},{2,0},{3,1},{4,6},{5,7},{6,4},{7,5},{8,10},{9,11},{10,... | collective-permute-start | bytes 393224 | tf_op jit(solution)/shard_map/ppermute | solution.py:479
  9.6 1.6 %shard_map.86 = (f32[2,1,128,128]{3,2,1,0:T(8,128)S(1)}, f32[2,2,1,128,128]{4,3,2,1,0:T(8,128)S(1)}) custom-call(bf16[1024,1024]{1,0:T(8,128)(2,1)} %refs_2_.9, bf16[1024,1024]{1,0:T(8,128)(2,1)} %refs_3_.7), custom_call_target="tpu_custom_call" | custom-call | flops 67108864 | bytes 671088 | tf_op jit(solution)/shard_map/pallas_call | solution.py:53
  11.3 0.2 collective-permute-start.2
  11.5 0.1 collective-permute-done.refs_1_.refs_3_
  11.6 1.6 %collective-permute-done.1.refs_2_.refs_4_ = f32[2,1,128,128]{3,2,1,0:T(8,128)S(1)} collective-permute-done((f32[2,1,128,128]{3,2,1,0:T(8,128)S(1)}, f32[2,1,128,128]{3,2,1,0:T(8,128)S(1)}, u32[]{:S(2)}, u32[]{:S(2)}) %collective-permute-start.1) | collective-permute-done | bytes 131104 | tf_op jit(solution)/shard_map/ppermute | solution.py:479
  13.1 4.1 %collective-permute-done.2.refs_3_.refs_5_ = f32[2,1,128,128]{3,2,1,0:T(8,128)S(1)} collective-permute-done((f32[2,1,128,128]{3,2,1,0:T(8,128)S(1)}, f32[2,1,128,128]{3,2,1,0:T(8,128)S(1)}, u32[]{:S(2)}, u32[]{:S(2)}) %collective-permute-start.2) | collective-permute-done | bytes 131104 | tf_op jit(solution)/shard_map/ppermute | solution.py:479
  17.2 0.1 collective-permute-start.3
  17.3 2.7 %collective-permute-start.4 = (f32[1,128,128]{2,1,0:T(8,128)S(1)}, f32[1,128,128]{2,1,0:T(8,128)S(1)}, u32[]{:S(2)}, u32[]{:S(2)}) collective-permute-start(f32[1,128,128]{2,1,0:T(8,128)S(1)} %get-tuple-element.60.refs_0_), channel_id=1, source_target_pairs={{0,4},{1,5},{2,6},{3,7},{4,0},{5,1},{6,2},{7,3},{8,12},{9,13},{10,... | collective-permute-start | bytes 196616 | tf_op jit(solution)/shard_map/ppermute | solution.py:479
  20.0 1.2 %collective-permute-start.5 = (f32[1,128,128]{2,1,0:T(8,128)S(1)}, f32[1,128,128]{2,1,0:T(8,128)S(1)}, u32[]{:S(2)}, u32[]{:S(2)}) collective-permute-start(f32[1,128,128]{2,1,0:T(8,128)S(1)} %collective-permute-done.3.refs_1_), channel_id=1, source_target_pairs={{0,4},{1,5},{2,6},{3,7},{4,0},{5,1},{6,2},{7,3},{8,12},{9,13},{10,... | collective-permute-start | bytes 196616 | tf_op jit(solution)/shard_map/ppermute | solution.py:479
  21.2 2.8 %collective-permute-start.6 = (f32[1,128,128]{2,1,0:T(8,128)S(1)}, f32[1,128,128]{2,1,0:T(8,128)S(1)}, u32[]{:S(2)}, u32[]{:S(2)}) collective-permute-start(f32[1,128,128]{2,1,0:T(8,128)S(1)} %shard_map.88), channel_id=1, source_target_pairs={{0,20},{1,21},{2,22},{3,23},{4,16},{5,17},{6,18},{7,19},{8,28},{9,... | collective-permute-start | bytes 196616 | tf_op jit(solution)/shard_map/ppermute | solution.py:479
  23.9 0.5 collective-permute-start.7
  24.4 2.0 %collective-permute-done.4.refs_2_ = f32[1,128,128]{2,1,0:T(8,128)S(1)} collective-permute-done((f32[1,128,128]{2,1,0:T(8,128)S(1)}, f32[1,128,128]{2,1,0:T(8,128)S(1)}, u32[]{:S(2)}, u32[]{:S(2)}) %collective-permute-start.4) | collective-permute-done | bytes 65568 | tf_op jit(solution)/shard_map/ppermute | solution.py:479
  26.4 2.1 %collective-permute-done.5.refs_3_ = f32[1,128,128]{2,1,0:T(8,128)S(1)} collective-permute-done((f32[1,128,128]{2,1,0:T(8,128)S(1)}, f32[1,128,128]{2,1,0:T(8,128)S(1)}, u32[]{:S(2)}, u32[]{:S(2)}) %collective-permute-start.5) | collective-permute-done | bytes 65568 | tf_op jit(solution)/shard_map/ppermute | solution.py:479
  28.5 2.2 %collective-permute-done.6.refs_4_ = f32[1,128,128]{2,1,0:T(8,128)S(1)} collective-permute-done((f32[1,128,128]{2,1,0:T(8,128)S(1)}, f32[1,128,128]{2,1,0:T(8,128)S(1)}, u32[]{:S(2)}, u32[]{:S(2)}) %collective-permute-start.6) | collective-permute-done | bytes 65568 | tf_op jit(solution)/shard_map/ppermute | solution.py:479
  30.8 1.2 %collective-permute-done.8.refs_1_ = f32[1,128,128]{2,1,0:T(8,128)S(1)} collective-permute-done((f32[1,128,128]{2,1,0:T(8,128)S(1)}, f32[1,128,128]{2,1,0:T(8,128)S(1)}, u32[]{:S(2)}, u32[]{:S(2)}) %collective-permute-start.8) | collective-permute-done | bytes 65568 | tf_op jit(solution)/shard_map/ppermute | solution.py:479
  32.1 0.1 shard_map.90
  32.2 0.6 collective-permute-start.9
  32.8 3.0 %collective-permute-start.11 = (f32[2,1,128,128]{3,2,1,0:T(8,128)S(1)}, f32[2,1,128,128]{3,2,1,0:T(8,128)S(1)}, u32[]{:S(2)}, u32[]{:S(2)}) collective-permute-start(f32[2,1,128,128]{3,2,1,0:T(8,128)S(1)} %get-tuple-element.68), channel_id=1, source_target_pairs={{0,3},{1,2},{2,1},{3,0},{4,7},{5,6},{6,5},{7,4},{8,11},{9,10},{10,... | collective-permute-start | bytes 393224 | tf_op jit(solution)/shard_map/ppermute | solution.py:479
  35.8 4.6 %shard_map.91.refs_2_ = f32[1024,1024]{1,0:T(8,128)S(1)} custom-call(bf16[1024,1024]{1,0:T(8,128)(2,1)S(1)} %copy-done.4, bf16[1024,1024]{1,0:T(8,128)(2,1)S(1)} %copy-done.1, bf16[1024,1024]{1,0:T(8,128)(2,1)S(1)} %copy-done.3), custom_call_target="tpu_custom_call" | custom-call | flops 2147483648 | bytes 21474836 | tf_op jit(solution)/shard_map/pallas_call | solution.py:53
  40.4 0.8 shard_map.92
  41.2 0.6 collective-permute-done.11.refs_0_
  41.8 0.8 shard_map.93
  42.7 3.6 %shard_map.94 = (f32[1024,1024]{1,0:T(8,128)S(1)}, bf16[1024,1024]{1,0:T(8,128)(2,1)S(1)}, bf16[1024,1024]{1,0:T(8,128)(2,1)S(1)}, bf16[2,2,1,128,128]{4,3,2,1,0...) custom-call(f32[2,1,128,128]{3,2,1,0:T(8,128)S(1)} %collective-permu, ...), custom_call_target="tpu_custom_call", output_to_operand_aliasing={{0}: (4, {})} | custom-call | flops 20971520 | bytes 209715 | tf_op jit(solution)/shard_map/pallas_call | solution.py:53
  46.3 1.2 %shard_map.98 = (f32[2,1,128,128]{3,2,1,0:T(8,128)S(1)}, f32[2,2,1,128,128]{4,3,2,1,0:T(8,128)S(1)}, f32[2,1,128,128]{3,2,1,0:T(8,128)S(1)}, f32[2,2,1,128,128]{...) custom-call(bf16[1024,1024]{1,0:T(8,128)(2,1)S(1)} %copy-done.4, ...), custom_call_target="tpu_custom_call" | custom-call | flops 201326592 | bytes 2013265 | tf_op jit(solution)/shard_map/pallas_call | solution.py:53
  47.5 0.6 collective-permute-start.12
  48.1 0.3 collective-permute-start.13
  48.4 2.7 %collective-permute-start.14 = (f32[2,1,128,128]{3,2,1,0:T(8,128)S(1)}, f32[2,1,128,128]{3,2,1,0:T(8,128)S(1)}, u32[]{:S(2)}, u32[]{:S(2)}) collective-permute-start(f32[2,1,128,128]{3,2,1,0:T(8,128)S(1)} %get-tuple-element.91), channel_id=1, source_target_pairs={{0,3},{1,2},{2,1},{3,0},{4,7},{5,6},{6,5},{7,4},{8,11},{9,10},{10,... | collective-permute-start | bytes 393224 | tf_op jit(solution)/shard_map/ppermute | solution.py:479
  51.1 2.9 %collective-permute-done.12.refs_1_.refs_3_ = f32[2,1,128,128]{3,2,1,0:T(8,128)S(1)} collective-permute-done((f32[2,1,128,128]{3,2,1,0:T(8,128)S(1)}, f32[2,1,128,128]{3,2,1,0:T(8,128)S(1)}, u32[]{:S(2)}, u32[]{:S(2)}) %collective-permute-start.12) | collective-permute-done | bytes 131104 | tf_op jit(solution)/shard_map/ppermute | solution.py:479
  54.0 2.0 %collective-permute-done.14.refs_3_.refs_5_ = f32[2,1,128,128]{3,2,1,0:T(8,128)S(1)} collective-permute-done((f32[2,1,128,128]{3,2,1,0:T(8,128)S(1)}, f32[2,1,128,128]{3,2,1,0:T(8,128)S(1)}, u32[]{:S(2)}, u32[]{:S(2)}) %collective-permute-start.14) | collective-permute-done | bytes 131104 | tf_op jit(solution)/shard_map/ppermute | solution.py:479
  56.1 2.1 %collective-permute-start.16 = (f32[1,128,128]{2,1,0:T(8,128)S(1)}, f32[1,128,128]{2,1,0:T(8,128)S(1)}, u32[]{:S(2)}, u32[]{:S(2)}) collective-permute-start(f32[1,128,128]{2,1,0:T(8,128)S(1)} %get-tuple-element.92.refs_0_), channel_id=1, source_target_pairs={{0,4},{1,5},{2,6},{3,7},{4,0},{5,1},{6,2},{7,3},{8,12},{9,13},{10,... | collective-permute-start | bytes 196616 | tf_op jit(solution)/shard_map/ppermute | solution.py:479
  58.2 1.2 %collective-permute-start.18 = (f32[1,128,128]{2,1,0:T(8,128)S(1)}, f32[1,128,128]{2,1,0:T(8,128)S(1)}, u32[]{:S(2)}, u32[]{:S(2)}) collective-permute-start(f32[1,128,128]{2,1,0:T(8,128)S(1)} %shard_map.100), channel_id=1, source_target_pairs={{0,20},{1,21},{2,22},{3,23},{4,16},{5,17},{6,18},{7,19},{8,28},{9,... | collective-permute-start | bytes 196616 | tf_op jit(solution)/shard_map/ppermute | solution.py:479
  59.4 1.5 %collective-permute-start.19 = (f32[1,128,128]{2,1,0:T(8,128)S(1)}, f32[1,128,128]{2,1,0:T(8,128)S(1)}, u32[]{:S(2)}, u32[]{:S(2)}) collective-permute-start(f32[1,128,128]{2,1,0:T(8,128)S(1)} %shard_map.100), channel_id=1, source_target_pairs={{0,16},{1,17},{2,18},{3,19},{4,20},{5,21},{6,22},{7,23},{8,24},{9,... | collective-permute-start | bytes 196616 | tf_op jit(solution)/shard_map/ppermute | solution.py:479
  60.9 1.8 %collective-permute-start.17 = (f32[1,128,128]{2,1,0:T(8,128)S(1)}, f32[1,128,128]{2,1,0:T(8,128)S(1)}, u32[]{:S(2)}, u32[]{:S(2)}) collective-permute-start(f32[1,128,128]{2,1,0:T(8,128)S(1)} %collective-permute-done.15.refs_1_), channel_id=1, source_target_pairs={{0,4},{1,5},{2,6},{3,7},{4,0},{5,1},{6,2},{7,3},{8,12},{9,13},{10,... | collective-permute-start | bytes 196616 | tf_op jit(solution)/shard_map/ppermute | solution.py:479
  62.7 2.6 %shard_map.84.refs_0_ = bf16[2,8,512,512]{3,2,1,0:T(8,128)(2,1)S(1)} custom-call(bf16[1024,1024]{1,0:T(8,128)(2,1)S(1)} %copy-done.1, bf16[1024,1024]{1,0:T(8,128)(2,1)S(1)} %copy-done.4), custom_call_target="tpu_custom_call" | custom-call | flops 1073741824 | bytes 10737418 | tf_op jit(solution)/shard_map/pallas_call | solution.py:53
  65.3 3.2 %collective-permute-done.17.refs_3_ = f32[1,128,128]{2,1,0:T(8,128)S(1)} collective-permute-done((f32[1,128,128]{2,1,0:T(8,128)S(1)}, f32[1,128,128]{2,1,0:T(8,128)S(1)}, u32[]{:S(2)}, u32[]{:S(2)}) %collective-permute-start.17) | collective-permute-done | bytes 65568 | tf_op jit(solution)/shard_map/ppermute | solution.py:479
  68.7 5.7 %shard_map.96.refs_3_ = bf16[1024,1024]{1,0:T(8,128)(2,1)S(1)} custom-call(bf16[1024,1024]{1,0:T(8,128)(2,1)S(1)} %get-tuple-element.78.refs_1_.refs_0_, bf16[1024,1024]{1,0:T(8,128)(2,1)S(1)} %copy-done.3, bf16[1024,1024]{1,0:T(8,128)(2,1)S(1)} %copy-done.1, bf16[2,2,1,128,128]{4,3,2,1,0:T(8,128)(2,1)S(1)} %get-tuple-element.81.refs_3_, ...), custom_call_target="tpu_custom_call" | custom-call | flops 2147483648 | bytes 21474836 | tf_op jit(solution)/shard_map/pallas_call | solution.py:53
  74.4 0.1 shard_map.102
  74.5 0.4 collective-permute-start.21
  74.9 1.0 %collective-permute-start.22 = (f32[2,1,128,128]{3,2,1,0:T(8,128)S(1)}, f32[2,1,128,128]{3,2,1,0:T(8,128)S(1)}, u32[]{:S(2)}, u32[]{:S(2)}) collective-permute-start(f32[2,1,128,128]{3,2,1,0:T(8,128)S(1)} %get-tuple-element.97), channel_id=1, source_target_pairs={{0,1},{1,0},{2,3},{3,2},{4,5},{5,4},{6,7},{7,6},{8,9},{9,8},{10,11... | collective-permute-start | bytes 393224 | tf_op jit(solution)/shard_map/ppermute | solution.py:479
  75.9 2.1 %collective-permute-start.23 = (f32[2,1,128,128]{3,2,1,0:T(8,128)S(1)}, f32[2,1,128,128]{3,2,1,0:T(8,128)S(1)}, u32[]{:S(2)}, u32[]{:S(2)}) collective-permute-start(f32[2,1,128,128]{3,2,1,0:T(8,128)S(1)} %get-tuple-element.98), channel_id=1, source_target_pairs={{0,2},{1,3},{2,0},{3,1},{4,6},{5,7},{6,4},{7,5},{8,10},{9,11},{10,... | collective-permute-start | bytes 393224 | tf_op jit(solution)/shard_map/ppermute | solution.py:479
  78.1 4.4 %shard_map.97 = (f32[1024,1024]{1,0:T(8,128)S(1)}, bf16[1024,1024]{1,0:T(8,128)(2,1)}) custom-call(bf16[1024,1024]{1,0:T(8,128)(2,1)S(1)} %copy-done.3, bf16[1024,1024]{1,0:T(8,128)(2,1)S(1)} %get-tuple-element.78.refs_1_.refs_0_, bf16[1024,1024]{1,0:T(8,128)(2,1)S(1)} %copy-done.4, bf16[1024,1024]{1,0:T(8,128)(2,1)S(1)} %shard_map.96.refs_3_), custom_call_target="tpu_custom_call" | custom-call | flops 2147483648 | bytes 21474836 | tf_op jit(solution)/shard_map/pallas_call | solution.py:53
  82.5 2.6 %shard_map.95 = (f32[1024,1024]{1,0:T(8,128)S(1)}, bf16[1024,1024]{1,0:T(8,128)(2,1)}) custom-call(bf16[2,8,512,512]{3,2,1,0:T(8,128)(2,1)S(1)} %shard_map.84.refs_0_, bf16[1024,1024]{1,0:T(8,128)(2,1)S(1)} %get-tuple-element.78.refs_1_.refs_0_, bf16[1024,1024]{1,0:T(8,128)(2,1)S(1)} %get-tuple-element.79.refs_2_), custom_call_target="tpu_custom_call" | custom-call | flops 1073741824 | bytes 10737418 | tf_op jit(solution)/shard_map/pallas_call | solution.py:53
  85.1 1.4 %shard_map.103 = (bf16[1024,1024]{1,0:T(8,128)(2,1)}, bf16[1024,1024]{1,0:T(8,128)(2,1)}) custom-call(f32[1024,1024]{1,0:T(8,128)S(1)} %get-tuple-element.86.refs_0_, f32[1024,1024]{1,0:T(8,128)S(1)} %get-tuple-element.87.refs_1_, bf16[1024,1024]{1,0:T(8,128)(2,1)S(1)} %copy-done.1, bf16[1024,1024]{1,0:T(8,128)(2,1)S(1)} %copy-done.3, ...), custom_call_target="tpu_custom_call" | custom-call | flops 134217728 | bytes 1342177 | tf_op jit(solution)/shard_map/pallas_call | solution.py:53
  86.6 2.6 %shard_map.104 = (bf16[1024,1024]{1,0:T(8,128)(2,1)}, bf16[1024,1024]{1,0:T(8,128)(2,1)}) custom-call(f32[1024,1024]{1,0:T(8,128)S(1)} %get-tuple-element.86.refs_0_, f32[1024,1024]{1,0:T(8,128)S(1)} %get-tuple-element.87.refs_1_, bf16[1024,1024]{1,0:T(8,128)(2,1)S(1)} %copy-done.1, ...), custom_call_target="tpu_custom_call", output_to_operand_aliasing={{0}: (10, {}), {1}: (11, {})} | custom-call | flops 402653184 | bytes 4026531 | tf_op jit(solution)/shard_map/pallas_call | solution.py:53
  (35 shorter events, 0.4 us)
Async XLA Ops:
  0.6 1.6 %copy-start = (bf16[1024,1024]{1,0:T(8,128)(2,1)S(1)}, bf16[1024,1024]{1,0:T(8,128)(2,1)}, u32[]{:S(2)}) copy-start(bf16[1024,1024]{1,0:T(8,128)(2,1)} %refs_2_.9) | copy-start | bytes 6291460
  2.2 1.6 %copy-start.2 = (bf16[1024,1024]{1,0:T(8,128)(2,1)S(1)}, bf16[1024,1024]{1,0:T(8,128)(2,1)}, u32[]{:S(2)}) copy-start(bf16[1024,1024]{1,0:T(8,128)(2,1)} %refs_3_.7) | copy-start | bytes 6291460
  3.8 31.9 %copy-start.4 = (bf16[1024,1024]{1,0:T(8,128)(2,1)S(1)}, bf16[1024,1024]{1,0:T(8,128)(2,1)}, u32[]{:S(2)}) copy-start(bf16[1024,1024]{1,0:T(8,128)(2,1)} %refs_0_.11) | copy-start | bytes 6291460
  5.0 6.5 %collective-permute-start = (f32[2,1,128,128]{3,2,1,0:T(8,128)S(1)}, f32[2,1,128,128]{3,2,1,0:T(8,128)S(1)}, u32[]{:S(2)}, u32[]{:S(2)}) collective-permute-start(f32[2,1,128,128]{3,2,1,0:T(8,128)S(1)} %get-tuple-element.57), channel_id=1, source_target_pairs={{0,1},{1,0},{2,3},{3,2},{4,5},{5,4},{6,7},{7,6},{8,9},{9,8},{10,11... | collective-permute-start | bytes 393224 | tf_op jit(solution)/shard_map/ppermute | solution.py:479
  8.1 27.7 %copy-start.1 = (bf16[1024,1024]{1,0:T(8,128)(2,1)S(1)}, bf16[1024,1024]{1,0:T(8,128)(2,1)}, u32[]{:S(2)}) copy-start(bf16[1024,1024]{1,0:T(8,128)(2,1)} %refs_2_.9) | copy-start | bytes 6291460
  8.1 27.7 %copy-start.3 = (bf16[1024,1024]{1,0:T(8,128)(2,1)S(1)}, bf16[1024,1024]{1,0:T(8,128)(2,1)}, u32[]{:S(2)}) copy-start(bf16[1024,1024]{1,0:T(8,128)(2,1)} %refs_3_.7) | copy-start | bytes 6291460
  8.1 5.1 %collective-permute-start.1 = (f32[2,1,128,128]{3,2,1,0:T(8,128)S(1)}, f32[2,1,128,128]{3,2,1,0:T(8,128)S(1)}, u32[]{:S(2)}, u32[]{:S(2)}) collective-permute-start(f32[2,1,128,128]{3,2,1,0:T(8,128)S(1)} %get-tuple-element.58), channel_id=1, source_target_pairs={{0,2},{1,3},{2,0},{3,1},{4,6},{5,7},{6,4},{7,5},{8,10},{9,11},{10,... | collective-permute-start | bytes 393224 | tf_op jit(solution)/shard_map/ppermute | solution.py:479
  11.3 5.9 %collective-permute-start.2 = (f32[2,1,128,128]{3,2,1,0:T(8,128)S(1)}, f32[2,1,128,128]{3,2,1,0:T(8,128)S(1)}, u32[]{:S(2)}, u32[]{:S(2)}) collective-permute-start(f32[2,1,128,128]{3,2,1,0:T(8,128)S(1)} %get-tuple-element.59), channel_id=1, source_target_pairs={{0,3},{1,2},{2,1},{3,0},{4,7},{5,6},{6,5},{7,4},{8,11},{9,10},{10,... | collective-permute-start | bytes 393224 | tf_op jit(solution)/shard_map/ppermute | solution.py:479
  17.2 2.7 %collective-permute-start.3 = (f32[1,128,128]{2,1,0:T(8,128)S(1)}, f32[1,128,128]{2,1,0:T(8,128)S(1)}, u32[]{:S(2)}, u32[]{:S(2)}) collective-permute-start(f32[1,128,128]{2,1,0:T(8,128)S(1)} %get-tuple-element.61), channel_id=1, source_target_pairs={{0,8},{1,9},{2,10},{3,11},{4,12},{5,13},{6,14},{7,15},{8,0},{9,1},... | collective-permute-start | bytes 196616 | tf_op jit(solution)/shard_map/ppermute | solution.py:479
  17.3 9.1 %collective-permute-start.4 = (f32[1,128,128]{2,1,0:T(8,128)S(1)}, f32[1,128,128]{2,1,0:T(8,128)S(1)}, u32[]{:S(2)}, u32[]{:S(2)}) collective-permute-start(f32[1,128,128]{2,1,0:T(8,128)S(1)} %get-tuple-element.60.refs_0_), channel_id=1, source_target_pairs={{0,4},{1,5},{2,6},{3,7},{4,0},{5,1},{6,2},{7,3},{8,12},{9,13},{10,... | collective-permute-start | bytes 196616 | tf_op jit(solution)/shard_map/ppermute | solution.py:479
  20.0 8.6 %collective-permute-start.5 = (f32[1,128,128]{2,1,0:T(8,128)S(1)}, f32[1,128,128]{2,1,0:T(8,128)S(1)}, u32[]{:S(2)}, u32[]{:S(2)}) collective-permute-start(f32[1,128,128]{2,1,0:T(8,128)S(1)} %collective-permute-done.3.refs_1_), channel_id=1, source_target_pairs={{0,4},{1,5},{2,6},{3,7},{4,0},{5,1},{6,2},{7,3},{8,12},{9,13},{10,... | collective-permute-start | bytes 196616 | tf_op jit(solution)/shard_map/ppermute | solution.py:479
  21.2 9.5 %collective-permute-start.6 = (f32[1,128,128]{2,1,0:T(8,128)S(1)}, f32[1,128,128]{2,1,0:T(8,128)S(1)}, u32[]{:S(2)}, u32[]{:S(2)}) collective-permute-start(f32[1,128,128]{2,1,0:T(8,128)S(1)} %shard_map.88), channel_id=1, source_target_pairs={{0,20},{1,21},{2,22},{3,23},{4,16},{5,17},{6,18},{7,19},{8,28},{9,... | collective-permute-start | bytes 196616 | tf_op jit(solution)/shard_map/ppermute | solution.py:479
  23.9 6.8 %collective-permute-start.7 = (f32[1,128,128]{2,1,0:T(8,128)S(1)}, f32[1,128,128]{2,1,0:T(8,128)S(1)}, u32[]{:S(2)}, u32[]{:S(2)}) collective-permute-start(f32[1,128,128]{2,1,0:T(8,128)S(1)} %shard_map.88), channel_id=1, source_target_pairs={{0,16},{1,17},{2,18},{3,19},{4,20},{5,21},{6,22},{7,23},{8,24},{9,... | collective-permute-start | bytes 196616 | tf_op jit(solution)/shard_map/ppermute | solution.py:479
  30.8 1.3 %collective-permute-start.8 = (f32[1,128,128]{2,1,0:T(8,128)S(1)}, f32[1,128,128]{2,1,0:T(8,128)S(1)}, u32[]{:S(2)}, u32[]{:S(2)}) collective-permute-start(f32[1,128,128]{2,1,0:T(8,128)S(1)} %get-tuple-element.63), channel_id=1, source_target_pairs={{0,8},{1,9},{2,10},{3,11},{4,12},{5,13},{6,14},{7,15},{8,0},{9,1},... | collective-permute-start | bytes 196616 | tf_op jit(solution)/shard_map/ppermute | solution.py:479
  32.2 10.5 %collective-permute-start.9 = (f32[2,1,128,128]{3,2,1,0:T(8,128)S(1)}, f32[2,1,128,128]{3,2,1,0:T(8,128)S(1)}, u32[]{:S(2)}, u32[]{:S(2)}) collective-permute-start(f32[2,1,128,128]{3,2,1,0:T(8,128)S(1)} %get-tuple-element.64), channel_id=1, source_target_pairs={{0,1},{1,0},{2,3},{3,2},{4,5},{5,4},{6,7},{7,6},{8,9},{9,8},{10,11... | collective-permute-start | bytes 393224 | tf_op jit(solution)/shard_map/ppermute | solution.py:479
  32.8 9.9 %collective-permute-start.10 = (f32[2,1,128,128]{3,2,1,0:T(8,128)S(1)}, f32[2,1,128,128]{3,2,1,0:T(8,128)S(1)}, u32[]{:S(2)}, u32[]{:S(2)}) collective-permute-start(f32[2,1,128,128]{3,2,1,0:T(8,128)S(1)} %get-tuple-element.65), channel_id=1, source_target_pairs={{0,2},{1,3},{2,0},{3,1},{4,6},{5,7},{6,4},{7,5},{8,10},{9,11},{10,... | collective-permute-start | bytes 393224 | tf_op jit(solution)/shard_map/ppermute | solution.py:479
  32.8 7.6 %copy-start.5 = (bf16[1024,1024]{1,0:T(8,128)(2,1)S(1)}, bf16[1024,1024]{1,0:T(8,128)(2,1)}, u32[]{:S(2)}) copy-start(bf16[1024,1024]{1,0:T(8,128)(2,1)} %refs_6_.1) | copy-start | bytes 6291460
  32.8 7.6 %copy-start.6 = (f32[1024]{0:T(1024)S(1)}, f32[1024]{0:T(1024)}, u32[]{:S(2)}) copy-start(f32[1024]{0:T(1024)} %param.8) | copy-start | bytes 12292
  32.8 9.0 %collective-permute-start.11 = (f32[2,1,128,128]{3,2,1,0:T(8,128)S(1)}, f32[2,1,128,128]{3,2,1,0:T(8,128)S(1)}, u32[]{:S(2)}, u32[]{:S(2)}) collective-permute-start(f32[2,1,128,128]{3,2,1,0:T(8,128)S(1)} %get-tuple-element.68), channel_id=1, source_target_pairs={{0,3},{1,2},{2,1},{3,0},{4,7},{5,6},{6,5},{7,4},{8,11},{9,10},{10,... | collective-permute-start | bytes 393224 | tf_op jit(solution)/shard_map/ppermute | solution.py:479
  47.5 6.4 %collective-permute-start.12 = (f32[2,1,128,128]{3,2,1,0:T(8,128)S(1)}, f32[2,1,128,128]{3,2,1,0:T(8,128)S(1)}, u32[]{:S(2)}, u32[]{:S(2)}) collective-permute-start(f32[2,1,128,128]{3,2,1,0:T(8,128)S(1)} %get-tuple-element.89), channel_id=1, source_target_pairs={{0,1},{1,0},{2,3},{3,2},{4,5},{5,4},{6,7},{7,6},{8,9},{9,8},{10,11... | collective-permute-start | bytes 393224 | tf_op jit(solution)/shard_map/ppermute | solution.py:479
  48.1 5.8 %collective-permute-start.13 = (f32[2,1,128,128]{3,2,1,0:T(8,128)S(1)}, f32[2,1,128,128]{3,2,1,0:T(8,128)S(1)}, u32[]{:S(2)}, u32[]{:S(2)}) collective-permute-start(f32[2,1,128,128]{3,2,1,0:T(8,128)S(1)} %get-tuple-element.90), channel_id=1, source_target_pairs={{0,2},{1,3},{2,0},{3,1},{4,6},{5,7},{6,4},{7,5},{8,10},{9,11},{10,... | collective-permute-start | bytes 393224 | tf_op jit(solution)/shard_map/ppermute | solution.py:479
  48.4 7.6 %collective-permute-start.14 = (f32[2,1,128,128]{3,2,1,0:T(8,128)S(1)}, f32[2,1,128,128]{3,2,1,0:T(8,128)S(1)}, u32[]{:S(2)}, u32[]{:S(2)}) collective-permute-start(f32[2,1,128,128]{3,2,1,0:T(8,128)S(1)} %get-tuple-element.91), channel_id=1, source_target_pairs={{0,3},{1,2},{2,1},{3,0},{4,7},{5,6},{6,5},{7,4},{8,11},{9,10},{10,... | collective-permute-start | bytes 393224 | tf_op jit(solution)/shard_map/ppermute | solution.py:479
  56.0 2.2 %collective-permute-start.15 = (f32[1,128,128]{2,1,0:T(8,128)S(1)}, f32[1,128,128]{2,1,0:T(8,128)S(1)}, u32[]{:S(2)}, u32[]{:S(2)}) collective-permute-start(f32[1,128,128]{2,1,0:T(8,128)S(1)} %get-tuple-element.93), channel_id=1, source_target_pairs={{0,8},{1,9},{2,10},{3,11},{4,12},{5,13},{6,14},{7,15},{8,0},{9,1},... | collective-permute-start | bytes 196616 | tf_op jit(solution)/shard_map/ppermute | solution.py:479
  56.1 9.2 %collective-permute-start.16 = (f32[1,128,128]{2,1,0:T(8,128)S(1)}, f32[1,128,128]{2,1,0:T(8,128)S(1)}, u32[]{:S(2)}, u32[]{:S(2)}) collective-permute-start(f32[1,128,128]{2,1,0:T(8,128)S(1)} %get-tuple-element.92.refs_0_), channel_id=1, source_target_pairs={{0,4},{1,5},{2,6},{3,7},{4,0},{5,1},{6,2},{7,3},{8,12},{9,13},{10,... | collective-permute-start | bytes 196616 | tf_op jit(solution)/shard_map/ppermute | solution.py:479
  58.2 10.3 %collective-permute-start.18 = (f32[1,128,128]{2,1,0:T(8,128)S(1)}, f32[1,128,128]{2,1,0:T(8,128)S(1)}, u32[]{:S(2)}, u32[]{:S(2)}) collective-permute-start(f32[1,128,128]{2,1,0:T(8,128)S(1)} %shard_map.100), channel_id=1, source_target_pairs={{0,20},{1,21},{2,22},{3,23},{4,16},{5,17},{6,18},{7,19},{8,28},{9,... | collective-permute-start | bytes 196616 | tf_op jit(solution)/shard_map/ppermute | solution.py:479
  59.4 9.1 %collective-permute-start.19 = (f32[1,128,128]{2,1,0:T(8,128)S(1)}, f32[1,128,128]{2,1,0:T(8,128)S(1)}, u32[]{:S(2)}, u32[]{:S(2)}) collective-permute-start(f32[1,128,128]{2,1,0:T(8,128)S(1)} %shard_map.100), channel_id=1, source_target_pairs={{0,16},{1,17},{2,18},{3,19},{4,20},{5,21},{6,22},{7,23},{8,24},{9,... | collective-permute-start | bytes 196616 | tf_op jit(solution)/shard_map/ppermute | solution.py:479
  60.9 7.6 %collective-permute-start.17 = (f32[1,128,128]{2,1,0:T(8,128)S(1)}, f32[1,128,128]{2,1,0:T(8,128)S(1)}, u32[]{:S(2)}, u32[]{:S(2)}) collective-permute-start(f32[1,128,128]{2,1,0:T(8,128)S(1)} %collective-permute-done.15.refs_1_), channel_id=1, source_target_pairs={{0,4},{1,5},{2,6},{3,7},{4,0},{5,1},{6,2},{7,3},{8,12},{9,13},{10,... | collective-permute-start | bytes 196616 | tf_op jit(solution)/shard_map/ppermute | solution.py:479
  68.6 5.8 %collective-permute-start.20 = (f32[1,128,128]{2,1,0:T(8,128)S(1)}, f32[1,128,128]{2,1,0:T(8,128)S(1)}, u32[]{:S(2)}, u32[]{:S(2)}) collective-permute-start(f32[1,128,128]{2,1,0:T(8,128)S(1)} %get-tuple-element.95), channel_id=1, source_target_pairs={{0,8},{1,9},{2,10},{3,11},{4,12},{5,13},{6,14},{7,15},{8,0},{9,1},... | collective-permute-start | bytes 196616 | tf_op jit(solution)/shard_map/ppermute | solution.py:479
  74.5 12.1 %collective-permute-start.21 = (f32[2,1,128,128]{3,2,1,0:T(8,128)S(1)}, f32[2,1,128,128]{3,2,1,0:T(8,128)S(1)}, u32[]{:S(2)}, u32[]{:S(2)}) collective-permute-start(f32[2,1,128,128]{3,2,1,0:T(8,128)S(1)} %get-tuple-element.96), channel_id=1, source_target_pairs={{0,3},{1,2},{2,1},{3,0},{4,7},{5,6},{6,5},{7,4},{8,11},{9,10},{10,... | collective-permute-start | bytes 393224 | tf_op jit(solution)/shard_map/ppermute | solution.py:479
  74.9 11.7 %collective-permute-start.22 = (f32[2,1,128,128]{3,2,1,0:T(8,128)S(1)}, f32[2,1,128,128]{3,2,1,0:T(8,128)S(1)}, u32[]{:S(2)}, u32[]{:S(2)}) collective-permute-start(f32[2,1,128,128]{3,2,1,0:T(8,128)S(1)} %get-tuple-element.97), channel_id=1, source_target_pairs={{0,1},{1,0},{2,3},{3,2},{4,5},{5,4},{6,7},{7,6},{8,9},{9,8},{10,11... | collective-permute-start | bytes 393224 | tf_op jit(solution)/shard_map/ppermute | solution.py:479
  75.9 10.7 %collective-permute-start.23 = (f32[2,1,128,128]{3,2,1,0:T(8,128)S(1)}, f32[2,1,128,128]{3,2,1,0:T(8,128)S(1)}, u32[]{:S(2)}, u32[]{:S(2)}) collective-permute-start(f32[2,1,128,128]{3,2,1,0:T(8,128)S(1)} %get-tuple-element.98), channel_id=1, source_target_pairs={{0,2},{1,3},{2,0},{3,1},{4,6},{5,7},{6,4},{7,5},{8,10},{9,11},{10,... | collective-permute-start | bytes 393224 | tf_op jit(solution)/shard_map/ppermute | solution.py:479

commit v6 on v5

--- a/solution.py
+++ b/solution.py
@@ -17,10 +17,10 @@
 QUAD = 4
 SHARE = H // (LANES * QUAD)
 CUT = 256
-SLAB = 256
+SLAB = 512
 ORDER = (3, 1, 2, 0)
 EARLY = (0, 3)
-UNROLL = 4
+UNROLL = 8
 PAIR = 2
 F32 = jnp.float32
 BF16 = jnp.bfloat16
@@ -330,13 +330,15 @@
             square = jnp.sum(square_ref[here, :], axis=1, keepdims=True) / features
             inverse = lax.rsqrt(square + EPSILON)
             mean = inverse * (jnp.sum(cross_ref[here, :], axis=1, keepdims=True) / features)
+            weight = inverse * inverse * mean
+            inverse, weight = (jnp.broadcast_to(x, (SLAB, HD)) for x in (inverse, weight))
             for head in range(H):
                 cols = pl.ds(head * HD, HD)
-                unit = att_ref[rows, cols] * inverse
-                gain = gain_ref[:, cols]
-                out_ref[rows, cols] = (unit * gain).astype(BF16)
+                att = att_ref[rows, cols]
+                gain = gain_ref[:, cols] * inverse
+                out_ref[rows, cols] = (att * gain).astype(BF16)
                 scaled = dy_ref[rows, cols].astype(F32) * gain
-                grad_ref[rows, cols] = (inverse * (scaled - unit * mean)).astype(BF16)
+                grad_ref[rows, cols] = (scaled - att * weight).astype(BF16)
             return 0
 
         lax.fori_loop(0, BLOCK // SLAB, step, 0)
@@ -550,7 +552,8 @@
     held, inside = [None] * QUAD, [None] * QUAD
     held[ORDER[0]], inside[ORDER[0]] = first
     held[ORDER[0]] = moved(held[ORDER[0]], swap_quad(ORDER[0]))
-    rest = slot_totals(ORDER[1:], reverse, *rest)
+    sent = slot_totals(ORDER[1:-1], reverse, *rest)
+    rest = {**sent, **slot_totals(ORDER[-1:], reverse, *rest)}
     for o in ORDER[1:]:
         held[o], inside[o] = rest[o]
         if o:

time: 89.6 us -> 87.5 us (0.977)
  Pallas kernels: 33.8 us -> 31.7 us
    pallas_call x21 -> x23, Pallas kernels: 33.8 us -> 31.7 us  [call(): pl.pallas_call(lambda *refs: kernel(place(), *refs), out_shape=out_shape,...]
  transfers between devices with their start and end apart: 24 -> 24, of which waited for: 11 -> 10; matrix products, arithmetic and copies ran while one was open for 0% -> 0% of each run, Pallas kernels for 28% -> 27%
where the time goes in v6:
time: 87.5 us; the launch traced here: 87.3 us
  Pallas kernels  31.7 us (36%)
  starting transfers between devices  29.4 us (34%)
  waiting for transfers between devices  21.9 us (25%)
  local copies, waits for them, and re-layouts  3.2 us (4%)
  between operations  1.1 us (1%)
    pallas_call x23, Pallas kernels, call(): pl.pallas_call(lambda *refs: kernel(place(), *refs), out_shape=out_shape,...  31.7 us
    ppermute x24, starting transfers between devices, moved(): return lax.ppermute(value, AXES, pairs)  29.4 us
    ppermute x24, waiting for transfers between devices, moved(): return lax.ppermute(value, AXES, pairs)  21.9 us
    unnamed x14, local copies, waits for them, and re-layouts  3.2 us
  transfers between devices with their start and end apart: 24, of which 10 were waited for; matrix products, arithmetic and copies ran while one was open for 0% of the time, Pallas kernels for 27%

profile of v6, /device:TPU:0, one launch (start us, length us, event | category | flops | bytes accessed | tf_op | source)
XLA Modules:
  0.0 87.3 jit_solution(519855826914494504)
XLA Ops:
  0.6 1.6 %copy-done = bf16[1024,1024]{1,0:T(8,128)(2,1)S(1)} copy-done((bf16[1024,1024]{1,0:T(8,128)(2,1)S(1)}, bf16[1024,1024]{1,0:T(8,128)(2,1)}, u32[]{:S(2)}) %copy-start) | copy-done | bytes 2097176
  2.2 1.6 %copy-done.2 = bf16[1024,1024]{1,0:T(8,128)(2,1)S(1)} copy-done((bf16[1024,1024]{1,0:T(8,128)(2,1)S(1)}, bf16[1024,1024]{1,0:T(8,128)(2,1)}, u32[]{:S(2)}) %copy-start.2) | copy-done | bytes 2097176
  3.8 0.8 shard_map.86
  4.7 3.0 %collective-permute-start = (f32[2,1,128,128]{3,2,1,0:T(8,128)S(1)}, f32[2,1,128,128]{3,2,1,0:T(8,128)S(1)}, u32[]{:S(2)}, u32[]{:S(2)}) collective-permute-start(f32[2,1,128,128]{3,2,1,0:T(8,128)S(1)} %get-tuple-element.57), channel_id=1, source_target_pairs={{0,1},{1,0},{2,3},{3,2},{4,5},{5,4},{6,7},{7,6},{8,9},{9,8},{10,11... | collective-permute-start | bytes 393224 | tf_op jit(solution)/shard_map/ppermute | solution.py:481
  7.7 1.6 %collective-permute-start.1 = (f32[2,1,128,128]{3,2,1,0:T(8,128)S(1)}, f32[2,1,128,128]{3,2,1,0:T(8,128)S(1)}, u32[]{:S(2)}, u32[]{:S(2)}) collective-permute-start(f32[2,1,128,128]{3,2,1,0:T(8,128)S(1)} %get-tuple-element.58), channel_id=1, source_target_pairs={{0,2},{1,3},{2,0},{3,1},{4,6},{5,7},{6,4},{7,5},{8,10},{9,11},{10,... | collective-permute-start | bytes 393224 | tf_op jit(solution)/shard_map/ppermute | solution.py:481
  9.3 1.6 %shard_map.87 = (f32[2,1,128,128]{3,2,1,0:T(8,128)S(1)}, f32[2,2,1,128,128]{4,3,2,1,0:T(8,128)S(1)}) custom-call(bf16[1024,1024]{1,0:T(8,128)(2,1)} %refs_2_.9, bf16[1024,1024]{1,0:T(8,128)(2,1)} %refs_3_.7), custom_call_target="tpu_custom_call" | custom-call | flops 67108864 | bytes 671088 | tf_op jit(solution)/shard_map/pallas_call | solution.py:53
  10.9 0.2 collective-permute-start.2
  11.1 0.5 shard_map.85
  11.6 1.1 %collective-permute-done.1.refs_2_.refs_4_ = f32[2,1,128,128]{3,2,1,0:T(8,128)S(1)} collective-permute-done((f32[2,1,128,128]{3,2,1,0:T(8,128)S(1)}, f32[2,1,128,128]{3,2,1,0:T(8,128)S(1)}, u32[]{:S(2)}, u32[]{:S(2)}) %collective-permute-start.1) | collective-permute-done | bytes 131104 | tf_op jit(solution)/shard_map/ppermute | solution.py:481
  12.7 4.1 %collective-permute-done.2.refs_3_.refs_5_ = f32[2,1,128,128]{3,2,1,0:T(8,128)S(1)} collective-permute-done((f32[2,1,128,128]{3,2,1,0:T(8,128)S(1)}, f32[2,1,128,128]{3,2,1,0:T(8,128)S(1)}, u32[]{:S(2)}, u32[]{:S(2)}) %collective-permute-start.2) | collective-permute-done | bytes 131104 | tf_op jit(solution)/shard_map/ppermute | solution.py:481
  17.0 2.7 %collective-permute-start.4 = (f32[1,128,128]{2,1,0:T(8,128)S(1)}, f32[1,128,128]{2,1,0:T(8,128)S(1)}, u32[]{:S(2)}, u32[]{:S(2)}) collective-permute-start(f32[1,128,128]{2,1,0:T(8,128)S(1)} %get-tuple-element.60.refs_0_), channel_id=1, source_target_pairs={{0,4},{1,5},{2,6},{3,7},{4,0},{5,1},{6,2},{7,3},{8,12},{9,13},{10,... | collective-permute-start | bytes 196616 | tf_op jit(solution)/shard_map/ppermute | solution.py:481
  19.6 1.2 %collective-permute-start.5 = (f32[1,128,128]{2,1,0:T(8,128)S(1)}, f32[1,128,128]{2,1,0:T(8,128)S(1)}, u32[]{:S(2)}, u32[]{:S(2)}) collective-permute-start(f32[1,128,128]{2,1,0:T(8,128)S(1)} %collective-permute-done.3.refs_1_), channel_id=1, source_target_pairs={{0,4},{1,5},{2,6},{3,7},{4,0},{5,1},{6,2},{7,3},{8,12},{9,13},{10,... | collective-permute-start | bytes 196616 | tf_op jit(solution)/shard_map/ppermute | solution.py:481
  20.8 2.8 %collective-permute-start.6 = (f32[1,128,128]{2,1,0:T(8,128)S(1)}, f32[1,128,128]{2,1,0:T(8,128)S(1)}, u32[]{:S(2)}, u32[]{:S(2)}) collective-permute-start(f32[1,128,128]{2,1,0:T(8,128)S(1)} %shard_map.89), channel_id=1, source_target_pairs={{0,20},{1,21},{2,22},{3,23},{4,16},{5,17},{6,18},{7,19},{8,28},{9,... | collective-permute-start | bytes 196616 | tf_op jit(solution)/shard_map/ppermute | solution.py:481
  23.6 0.5 collective-permute-start.7
  24.1 2.0 %collective-permute-done.4.refs_2_ = f32[1,128,128]{2,1,0:T(8,128)S(1)} collective-permute-done((f32[1,128,128]{2,1,0:T(8,128)S(1)}, f32[1,128,128]{2,1,0:T(8,128)S(1)}, u32[]{:S(2)}, u32[]{:S(2)}) %collective-permute-start.4) | collective-permute-done | bytes 65568 | tf_op jit(solution)/shard_map/ppermute | solution.py:481
  26.1 2.1 %collective-permute-done.5.refs_3_ = f32[1,128,128]{2,1,0:T(8,128)S(1)} collective-permute-done((f32[1,128,128]{2,1,0:T(8,128)S(1)}, f32[1,128,128]{2,1,0:T(8,128)S(1)}, u32[]{:S(2)}, u32[]{:S(2)}) %collective-permute-start.5) | collective-permute-done | bytes 65568 | tf_op jit(solution)/shard_map/ppermute | solution.py:481
  28.2 2.2 %collective-permute-done.6.refs_4_ = f32[1,128,128]{2,1,0:T(8,128)S(1)} collective-permute-done((f32[1,128,128]{2,1,0:T(8,128)S(1)}, f32[1,128,128]{2,1,0:T(8,128)S(1)}, u32[]{:S(2)}, u32[]{:S(2)}) %collective-permute-start.6) | collective-permute-done | bytes 65568 | tf_op jit(solution)/shard_map/ppermute | solution.py:481
  30.5 1.2 %collective-permute-done.8.refs_1_ = f32[1,128,128]{2,1,0:T(8,128)S(1)} collective-permute-done((f32[1,128,128]{2,1,0:T(8,128)S(1)}, f32[1,128,128]{2,1,0:T(8,128)S(1)}, u32[]{:S(2)}, u32[]{:S(2)}) %collective-permute-start.8) | collective-permute-done | bytes 65568 | tf_op jit(solution)/shard_map/ppermute | solution.py:481
  31.7 0.1 shard_map.91
  31.8 0.6 collective-permute-start.9
  32.4 3.0 %collective-permute-start.11 = (f32[2,1,128,128]{3,2,1,0:T(8,128)S(1)}, f32[2,1,128,128]{3,2,1,0:T(8,128)S(1)}, u32[]{:S(2)}, u32[]{:S(2)}) collective-permute-start(f32[2,1,128,128]{3,2,1,0:T(8,128)S(1)} %get-tuple-element.68), channel_id=1, source_target_pairs={{0,3},{1,2},{2,1},{3,0},{4,7},{5,6},{6,5},{7,4},{8,11},{9,10},{10,... | collective-permute-start | bytes 393224 | tf_op jit(solution)/shard_map/ppermute | solution.py:481
  35.4 4.0 %shard_map.92.refs_2_ = f32[1024,1024]{1,0:T(8,128)S(1)} custom-call(bf16[1024,1024]{1,0:T(8,128)(2,1)S(1)} %copy-done.4, bf16[1024,1024]{1,0:T(8,128)(2,1)S(1)} %copy-done.1, bf16[1024,1024]{1,0:T(8,128)(2,1)S(1)} %copy-done.3), custom_call_target="tpu_custom_call" | custom-call | flops 2147483648 | bytes 21474836 | tf_op jit(solution)/shard_map/pallas_call | solution.py:53
  39.5 0.8 shard_map.93
  40.3 1.2 %collective-permute-done.11.refs_0_ = f32[2,1,128,128]{3,2,1,0:T(8,128)S(1)} collective-permute-done((f32[2,1,128,128]{3,2,1,0:T(8,128)S(1)}, f32[2,1,128,128]{3,2,1,0:T(8,128)S(1)}, u32[]{:S(2)}, u32[]{:S(2)}) %collective-permute-start.11) | collective-permute-done | bytes 131104 | tf_op jit(solution)/shard_map/ppermute | solution.py:481
  41.5 0.8 shard_map.94
  42.3 3.2 %shard_map.95 = (f32[1024,1024]{1,0:T(8,128)S(1)}, bf16[1024,1024]{1,0:T(8,128)(2,1)S(1)}, bf16[1024,1024]{1,0:T(8,128)(2,1)S(1)}, bf16[2,2,1,128,128]{4,3,2,1,0...) custom-call(f32[2,1,128,128]{3,2,1,0:T(8,128)S(1)} %collective-permu, ...), custom_call_target="tpu_custom_call", output_to_operand_aliasing={{0}: (4, {})} | custom-call | flops 20971520 | bytes 209715 | tf_op jit(solution)/shard_map/pallas_call | solution.py:53
  45.6 0.9 shard_map.100
  46.4 0.6 collective-permute-start.12
  47.0 0.3 collective-permute-start.13
  47.3 2.7 %collective-permute-start.14 = (f32[2,1,128,128]{3,2,1,0:T(8,128)S(1)}, f32[2,1,128,128]{3,2,1,0:T(8,128)S(1)}, u32[]{:S(2)}, u32[]{:S(2)}) collective-permute-start(f32[2,1,128,128]{3,2,1,0:T(8,128)S(1)} %get-tuple-element.91), channel_id=1, source_target_pairs={{0,3},{1,2},{2,1},{3,0},{4,7},{5,6},{6,5},{7,4},{8,11},{9,10},{10,... | collective-permute-start | bytes 393224 | tf_op jit(solution)/shard_map/ppermute | solution.py:481
  50.0 0.5 shard_map.99
  50.5 2.4 %collective-permute-done.12.refs_1_.refs_3_ = f32[2,1,128,128]{3,2,1,0:T(8,128)S(1)} collective-permute-done((f32[2,1,128,128]{3,2,1,0:T(8,128)S(1)}, f32[2,1,128,128]{3,2,1,0:T(8,128)S(1)}, u32[]{:S(2)}, u32[]{:S(2)}) %collective-permute-start.12) | collective-permute-done | bytes 131104 | tf_op jit(solution)/shard_map/ppermute | solution.py:481
  52.9 2.0 %collective-permute-done.14.refs_3_.refs_5_ = f32[2,1,128,128]{3,2,1,0:T(8,128)S(1)} collective-permute-done((f32[2,1,128,128]{3,2,1,0:T(8,128)S(1)}, f32[2,1,128,128]{3,2,1,0:T(8,128)S(1)}, u32[]{:S(2)}, u32[]{:S(2)}) %collective-permute-start.14) | collective-permute-done | bytes 131104 | tf_op jit(solution)/shard_map/ppermute | solution.py:481
  55.0 2.1 %collective-permute-start.16 = (f32[1,128,128]{2,1,0:T(8,128)S(1)}, f32[1,128,128]{2,1,0:T(8,128)S(1)}, u32[]{:S(2)}, u32[]{:S(2)}) collective-permute-start(f32[1,128,128]{2,1,0:T(8,128)S(1)} %get-tuple-element.92.refs_0_), channel_id=1, source_target_pairs={{0,4},{1,5},{2,6},{3,7},{4,0},{5,1},{6,2},{7,3},{8,12},{9,13},{10,... | collective-permute-start | bytes 196616 | tf_op jit(solution)/shard_map/ppermute | solution.py:481
  57.1 1.2 %collective-permute-start.18 = (f32[1,128,128]{2,1,0:T(8,128)S(1)}, f32[1,128,128]{2,1,0:T(8,128)S(1)}, u32[]{:S(2)}, u32[]{:S(2)}) collective-permute-start(f32[1,128,128]{2,1,0:T(8,128)S(1)} %shard_map.102), channel_id=1, source_target_pairs={{0,20},{1,21},{2,22},{3,23},{4,16},{5,17},{6,18},{7,19},{8,28},{9,... | collective-permute-start | bytes 196616 | tf_op jit(solution)/shard_map/ppermute | solution.py:481
  58.3 1.5 %collective-permute-start.19 = (f32[1,128,128]{2,1,0:T(8,128)S(1)}, f32[1,128,128]{2,1,0:T(8,128)S(1)}, u32[]{:S(2)}, u32[]{:S(2)}) collective-permute-start(f32[1,128,128]{2,1,0:T(8,128)S(1)} %shard_map.102), channel_id=1, source_target_pairs={{0,16},{1,17},{2,18},{3,19},{4,20},{5,21},{6,22},{7,23},{8,24},{9,... | collective-permute-start | bytes 196616 | tf_op jit(solution)/shard_map/ppermute | solution.py:481
  59.8 1.8 %collective-permute-start.17 = (f32[1,128,128]{2,1,0:T(8,128)S(1)}, f32[1,128,128]{2,1,0:T(8,128)S(1)}, u32[]{:S(2)}, u32[]{:S(2)}) collective-permute-start(f32[1,128,128]{2,1,0:T(8,128)S(1)} %collective-permute-done.15.refs_1_), channel_id=1, source_target_pairs={{0,4},{1,5},{2,6},{3,7},{4,0},{5,1},{6,2},{7,3},{8,12},{9,13},{10,... | collective-permute-start | bytes 196616 | tf_op jit(solution)/shard_map/ppermute | solution.py:481
  61.5 2.3 %shard_map.84.refs_0_ = bf16[2,8,512,512]{3,2,1,0:T(8,128)(2,1)S(1)} custom-call(bf16[1024,1024]{1,0:T(8,128)(2,1)S(1)} %copy-done.1, bf16[1024,1024]{1,0:T(8,128)(2,1)S(1)} %copy-done.4), custom_call_target="tpu_custom_call" | custom-call | flops 1073741824 | bytes 10737418 | tf_op jit(solution)/shard_map/pallas_call | solution.py:53
  63.8 3.6 %collective-permute-done.17.refs_3_ = f32[1,128,128]{2,1,0:T(8,128)S(1)} collective-permute-done((f32[1,128,128]{2,1,0:T(8,128)S(1)}, f32[1,128,128]{2,1,0:T(8,128)S(1)}, u32[]{:S(2)}, u32[]{:S(2)}) %collective-permute-start.17) | collective-permute-done | bytes 65568 | tf_op jit(solution)/shard_map/ppermute | solution.py:481
  67.6 5.5 %shard_map.97.refs_3_ = bf16[1024,1024]{1,0:T(8,128)(2,1)S(1)} custom-call(bf16[1024,1024]{1,0:T(8,128)(2,1)S(1)} %get-tuple-element.78.refs_1_.refs_0_, bf16[1024,1024]{1,0:T(8,128)(2,1)S(1)} %copy-done.3, bf16[1024,1024]{1,0:T(8,128)(2,1)S(1)} %copy-done.1, bf16[2,2,1,128,128]{4,3,2,1,0:T(8,128)(2,1)S(1)} %get-tuple-element.81.refs_3_, ...), custom_call_target="tpu_custom_call" | custom-call | flops 2147483648 | bytes 21474836 | tf_op jit(solution)/shard_map/pallas_call | solution.py:53
  73.1 0.1 shard_map.104
  73.3 0.4 collective-permute-start.21
  73.6 1.0 %collective-permute-start.22 = (f32[2,1,128,128]{3,2,1,0:T(8,128)S(1)}, f32[2,1,128,128]{3,2,1,0:T(8,128)S(1)}, u32[]{:S(2)}, u32[]{:S(2)}) collective-permute-start(f32[2,1,128,128]{3,2,1,0:T(8,128)S(1)} %get-tuple-element.97), channel_id=1, source_target_pairs={{0,1},{1,0},{2,3},{3,2},{4,5},{5,4},{6,7},{7,6},{8,9},{9,8},{10,11... | collective-permute-start | bytes 393224 | tf_op jit(solution)/shard_map/ppermute | solution.py:481
  74.6 2.2 %collective-permute-start.23 = (f32[2,1,128,128]{3,2,1,0:T(8,128)S(1)}, f32[2,1,128,128]{3,2,1,0:T(8,128)S(1)}, u32[]{:S(2)}, u32[]{:S(2)}) collective-permute-start(f32[2,1,128,128]{3,2,1,0:T(8,128)S(1)} %get-tuple-element.98), channel_id=1, source_target_pairs={{0,2},{1,3},{2,0},{3,1},{4,6},{5,7},{6,4},{7,5},{8,10},{9,11},{10,... | collective-permute-start | bytes 393224 | tf_op jit(solution)/shard_map/ppermute | solution.py:481
  76.8 4.0 %shard_map.98 = (f32[1024,1024]{1,0:T(8,128)S(1)}, bf16[1024,1024]{1,0:T(8,128)(2,1)}) custom-call(bf16[1024,1024]{1,0:T(8,128)(2,1)S(1)} %copy-done.3, bf16[1024,1024]{1,0:T(8,128)(2,1)S(1)} %get-tuple-element.78.refs_1_.refs_0_, bf16[1024,1024]{1,0:T(8,128)(2,1)S(1)} %copy-done.4, bf16[1024,1024]{1,0:T(8,128)(2,1)S(1)} %shard_map.97.refs_3_), custom_call_target="tpu_custom_call" | custom-call | flops 2147483648 | bytes 21474836 | tf_op jit(solution)/shard_map/pallas_call | solution.py:53
  80.9 2.1 %shard_map.96 = (f32[1024,1024]{1,0:T(8,128)S(1)}, bf16[1024,1024]{1,0:T(8,128)(2,1)}) custom-call(bf16[2,8,512,512]{3,2,1,0:T(8,128)(2,1)S(1)} %shard_map.84.refs_0_, bf16[1024,1024]{1,0:T(8,128)(2,1)S(1)} %get-tuple-element.78.refs_1_.refs_0_, bf16[1024,1024]{1,0:T(8,128)(2,1)S(1)} %get-tuple-element.79.refs_2_), custom_call_target="tpu_custom_call" | custom-call | flops 1073741824 | bytes 10737418 | tf_op jit(solution)/shard_map/pallas_call | solution.py:53
  83.0 1.4 %shard_map.105 = (bf16[1024,1024]{1,0:T(8,128)(2,1)}, bf16[1024,1024]{1,0:T(8,128)(2,1)}) custom-call(f32[1024,1024]{1,0:T(8,128)S(1)} %get-tuple-element.86.refs_0_, f32[1024,1024]{1,0:T(8,128)S(1)} %get-tuple-element.87.refs_1_, bf16[1024,1024]{1,0:T(8,128)(2,1)S(1)} %copy-done.1, bf16[1024,1024]{1,0:T(8,128)(2,1)S(1)} %copy-done.3, ...), custom_call_target="tpu_custom_call" | custom-call | flops 134217728 | bytes 1342177 | tf_op jit(solution)/shard_map/pallas_call | solution.py:53
  84.5 2.7 %shard_map.106 = (bf16[1024,1024]{1,0:T(8,128)(2,1)}, bf16[1024,1024]{1,0:T(8,128)(2,1)}) custom-call(f32[1024,1024]{1,0:T(8,128)S(1)} %get-tuple-element.86.refs_0_, f32[1024,1024]{1,0:T(8,128)S(1)} %get-tuple-element.87.refs_1_, bf16[1024,1024]{1,0:T(8,128)(2,1)S(1)} %copy-done.1, ...), custom_call_target="tpu_custom_call", output_to_operand_aliasing={{0}: (10, {}), {1}: (11, {})} | custom-call | flops 402653184 | bytes 4026531 | tf_op jit(solution)/shard_map/pallas_call | solution.py:53
  (37 shorter events, 0.5 us)
Async XLA Ops:
  0.6 1.6 %copy-start = (bf16[1024,1024]{1,0:T(8,128)(2,1)S(1)}, bf16[1024,1024]{1,0:T(8,128)(2,1)}, u32[]{:S(2)}) copy-start(bf16[1024,1024]{1,0:T(8,128)(2,1)} %refs_2_.9) | copy-start | bytes 6291460
  2.2 1.6 %copy-start.2 = (bf16[1024,1024]{1,0:T(8,128)(2,1)S(1)}, bf16[1024,1024]{1,0:T(8,128)(2,1)}, u32[]{:S(2)}) copy-start(bf16[1024,1024]{1,0:T(8,128)(2,1)} %refs_3_.7) | copy-start | bytes 6291460
  4.7 7.0 %collective-permute-start = (f32[2,1,128,128]{3,2,1,0:T(8,128)S(1)}, f32[2,1,128,128]{3,2,1,0:T(8,128)S(1)}, u32[]{:S(2)}, u32[]{:S(2)}) collective-permute-start(f32[2,1,128,128]{3,2,1,0:T(8,128)S(1)} %get-tuple-element.57), channel_id=1, source_target_pairs={{0,1},{1,0},{2,3},{3,2},{4,5},{5,4},{6,7},{7,6},{8,9},{9,8},{10,11... | collective-permute-start | bytes 393224 | tf_op jit(solution)/shard_map/ppermute | solution.py:481
  7.7 3.4 %copy-start.1 = (bf16[1024,1024]{1,0:T(8,128)(2,1)S(1)}, bf16[1024,1024]{1,0:T(8,128)(2,1)}, u32[]{:S(2)}) copy-start(bf16[1024,1024]{1,0:T(8,128)(2,1)} %refs_2_.9) | copy-start | bytes 6291460
  7.7 3.4 %copy-start.3 = (bf16[1024,1024]{1,0:T(8,128)(2,1)S(1)}, bf16[1024,1024]{1,0:T(8,128)(2,1)}, u32[]{:S(2)}) copy-start(bf16[1024,1024]{1,0:T(8,128)(2,1)} %refs_3_.7) | copy-start | bytes 6291460
  7.7 5.0 %collective-permute-start.1 = (f32[2,1,128,128]{3,2,1,0:T(8,128)S(1)}, f32[2,1,128,128]{3,2,1,0:T(8,128)S(1)}, u32[]{:S(2)}, u32[]{:S(2)}) collective-permute-start(f32[2,1,128,128]{3,2,1,0:T(8,128)S(1)} %get-tuple-element.58), channel_id=1, source_target_pairs={{0,2},{1,3},{2,0},{3,1},{4,6},{5,7},{6,4},{7,5},{8,10},{9,11},{10,... | collective-permute-start | bytes 393224 | tf_op jit(solution)/shard_map/ppermute | solution.py:481
  10.9 24.5 %copy-start.4 = (bf16[1024,1024]{1,0:T(8,128)(2,1)S(1)}, bf16[1024,1024]{1,0:T(8,128)(2,1)}, u32[]{:S(2)}) copy-start(bf16[1024,1024]{1,0:T(8,128)(2,1)} %refs_0_.15) | copy-start | bytes 6291460
  10.9 5.9 %collective-permute-start.2 = (f32[2,1,128,128]{3,2,1,0:T(8,128)S(1)}, f32[2,1,128,128]{3,2,1,0:T(8,128)S(1)}, u32[]{:S(2)}, u32[]{:S(2)}) collective-permute-start(f32[2,1,128,128]{3,2,1,0:T(8,128)S(1)} %get-tuple-element.59), channel_id=1, source_target_pairs={{0,3},{1,2},{2,1},{3,0},{4,7},{5,6},{6,5},{7,4},{8,11},{9,10},{10,... | collective-permute-start | bytes 393224 | tf_op jit(solution)/shard_map/ppermute | solution.py:481
  16.9 2.7 %collective-permute-start.3 = (f32[1,128,128]{2,1,0:T(8,128)S(1)}, f32[1,128,128]{2,1,0:T(8,128)S(1)}, u32[]{:S(2)}, u32[]{:S(2)}) collective-permute-start(f32[1,128,128]{2,1,0:T(8,128)S(1)} %get-tuple-element.61), channel_id=1, source_target_pairs={{0,8},{1,9},{2,10},{3,11},{4,12},{5,13},{6,14},{7,15},{8,0},{9,1},... | collective-permute-start | bytes 196616 | tf_op jit(solution)/shard_map/ppermute | solution.py:481
  17.0 9.1 %collective-permute-start.4 = (f32[1,128,128]{2,1,0:T(8,128)S(1)}, f32[1,128,128]{2,1,0:T(8,128)S(1)}, u32[]{:S(2)}, u32[]{:S(2)}) collective-permute-start(f32[1,128,128]{2,1,0:T(8,128)S(1)} %get-tuple-element.60.refs_0_), channel_id=1, source_target_pairs={{0,4},{1,5},{2,6},{3,7},{4,0},{5,1},{6,2},{7,3},{8,12},{9,13},{10,... | collective-permute-start | bytes 196616 | tf_op jit(solution)/shard_map/ppermute | solution.py:481
  19.6 8.5 %collective-permute-start.5 = (f32[1,128,128]{2,1,0:T(8,128)S(1)}, f32[1,128,128]{2,1,0:T(8,128)S(1)}, u32[]{:S(2)}, u32[]{:S(2)}) collective-permute-start(f32[1,128,128]{2,1,0:T(8,128)S(1)} %collective-permute-done.3.refs_1_), channel_id=1, source_target_pairs={{0,4},{1,5},{2,6},{3,7},{4,0},{5,1},{6,2},{7,3},{8,12},{9,13},{10,... | collective-permute-start | bytes 196616 | tf_op jit(solution)/shard_map/ppermute | solution.py:481
  20.8 9.5 %collective-permute-start.6 = (f32[1,128,128]{2,1,0:T(8,128)S(1)}, f32[1,128,128]{2,1,0:T(8,128)S(1)}, u32[]{:S(2)}, u32[]{:S(2)}) collective-permute-start(f32[1,128,128]{2,1,0:T(8,128)S(1)} %shard_map.89), channel_id=1, source_target_pairs={{0,20},{1,21},{2,22},{3,23},{4,16},{5,17},{6,18},{7,19},{8,28},{9,... | collective-permute-start | bytes 196616 | tf_op jit(solution)/shard_map/ppermute | solution.py:481
  23.6 6.8 %collective-permute-start.7 = (f32[1,128,128]{2,1,0:T(8,128)S(1)}, f32[1,128,128]{2,1,0:T(8,128)S(1)}, u32[]{:S(2)}, u32[]{:S(2)}) collective-permute-start(f32[1,128,128]{2,1,0:T(8,128)S(1)} %shard_map.89), channel_id=1, source_target_pairs={{0,16},{1,17},{2,18},{3,19},{4,20},{5,21},{6,22},{7,23},{8,24},{9,... | collective-permute-start | bytes 196616 | tf_op jit(solution)/shard_map/ppermute | solution.py:481
  30.4 1.3 %collective-permute-start.8 = (f32[1,128,128]{2,1,0:T(8,128)S(1)}, f32[1,128,128]{2,1,0:T(8,128)S(1)}, u32[]{:S(2)}, u32[]{:S(2)}) collective-permute-start(f32[1,128,128]{2,1,0:T(8,128)S(1)} %get-tuple-element.63), channel_id=1, source_target_pairs={{0,8},{1,9},{2,10},{3,11},{4,12},{5,13},{6,14},{7,15},{8,0},{9,1},... | collective-permute-start | bytes 196616 | tf_op jit(solution)/shard_map/ppermute | solution.py:481
  31.8 10.5 %collective-permute-start.9 = (f32[2,1,128,128]{3,2,1,0:T(8,128)S(1)}, f32[2,1,128,128]{3,2,1,0:T(8,128)S(1)}, u32[]{:S(2)}, u32[]{:S(2)}) collective-permute-start(f32[2,1,128,128]{3,2,1,0:T(8,128)S(1)} %get-tuple-element.64), channel_id=1, source_target_pairs={{0,1},{1,0},{2,3},{3,2},{4,5},{5,4},{6,7},{7,6},{8,9},{9,8},{10,11... | collective-permute-start | bytes 393224 | tf_op jit(solution)/shard_map/ppermute | solution.py:481
  32.4 9.9 %collective-permute-start.10 = (f32[2,1,128,128]{3,2,1,0:T(8,128)S(1)}, f32[2,1,128,128]{3,2,1,0:T(8,128)S(1)}, u32[]{:S(2)}, u32[]{:S(2)}) collective-permute-start(f32[2,1,128,128]{3,2,1,0:T(8,128)S(1)} %get-tuple-element.65), channel_id=1, source_target_pairs={{0,2},{1,3},{2,0},{3,1},{4,6},{5,7},{6,4},{7,5},{8,10},{9,11},{10,... | collective-permute-start | bytes 393224 | tf_op jit(solution)/shard_map/ppermute | solution.py:481
  32.4 7.0 %copy-start.5 = (bf16[1024,1024]{1,0:T(8,128)(2,1)S(1)}, bf16[1024,1024]{1,0:T(8,128)(2,1)}, u32[]{:S(2)}) copy-start(bf16[1024,1024]{1,0:T(8,128)(2,1)} %refs_6_.1) | copy-start | bytes 6291460
  32.4 7.0 %copy-start.6 = (f32[1024]{0:T(1024)S(1)}, f32[1024]{0:T(1024)}, u32[]{:S(2)}) copy-start(f32[1024]{0:T(1024)} %param.8) | copy-start | bytes 12292
  32.4 9.0 %collective-permute-start.11 = (f32[2,1,128,128]{3,2,1,0:T(8,128)S(1)}, f32[2,1,128,128]{3,2,1,0:T(8,128)S(1)}, u32[]{:S(2)}, u32[]{:S(2)}) collective-permute-start(f32[2,1,128,128]{3,2,1,0:T(8,128)S(1)} %get-tuple-element.68), channel_id=1, source_target_pairs={{0,3},{1,2},{2,1},{3,0},{4,7},{5,6},{6,5},{7,4},{8,11},{9,10},{10,... | collective-permute-start | bytes 393224 | tf_op jit(solution)/shard_map/ppermute | solution.py:481
  46.4 6.4 %collective-permute-start.12 = (f32[2,1,128,128]{3,2,1,0:T(8,128)S(1)}, f32[2,1,128,128]{3,2,1,0:T(8,128)S(1)}, u32[]{:S(2)}, u32[]{:S(2)}) collective-permute-start(f32[2,1,128,128]{3,2,1,0:T(8,128)S(1)} %get-tuple-element.89), channel_id=1, source_target_pairs={{0,1},{1,0},{2,3},{3,2},{4,5},{5,4},{6,7},{7,6},{8,9},{9,8},{10,11... | collective-permute-start | bytes 393224 | tf_op jit(solution)/shard_map/ppermute | solution.py:481
  47.0 5.8 %collective-permute-start.13 = (f32[2,1,128,128]{3,2,1,0:T(8,128)S(1)}, f32[2,1,128,128]{3,2,1,0:T(8,128)S(1)}, u32[]{:S(2)}, u32[]{:S(2)}) collective-permute-start(f32[2,1,128,128]{3,2,1,0:T(8,128)S(1)} %get-tuple-element.90), channel_id=1, source_target_pairs={{0,2},{1,3},{2,0},{3,1},{4,6},{5,7},{6,4},{7,5},{8,10},{9,11},{10,... | collective-permute-start | bytes 393224 | tf_op jit(solution)/shard_map/ppermute | solution.py:481
  47.3 7.6 %collective-permute-start.14 = (f32[2,1,128,128]{3,2,1,0:T(8,128)S(1)}, f32[2,1,128,128]{3,2,1,0:T(8,128)S(1)}, u32[]{:S(2)}, u32[]{:S(2)}) collective-permute-start(f32[2,1,128,128]{3,2,1,0:T(8,128)S(1)} %get-tuple-element.91), channel_id=1, source_target_pairs={{0,3},{1,2},{2,1},{3,0},{4,7},{5,6},{6,5},{7,4},{8,11},{9,10},{10,... | collective-permute-start | bytes 393224 | tf_op jit(solution)/shard_map/ppermute | solution.py:481
  54.9 2.1 %collective-permute-start.15 = (f32[1,128,128]{2,1,0:T(8,128)S(1)}, f32[1,128,128]{2,1,0:T(8,128)S(1)}, u32[]{:S(2)}, u32[]{:S(2)}) collective-permute-start(f32[1,128,128]{2,1,0:T(8,128)S(1)} %get-tuple-element.93), channel_id=1, source_target_pairs={{0,8},{1,9},{2,10},{3,11},{4,12},{5,13},{6,14},{7,15},{8,0},{9,1},... | collective-permute-start | bytes 196616 | tf_op jit(solution)/shard_map/ppermute | solution.py:481
  55.0 8.8 %collective-permute-start.16 = (f32[1,128,128]{2,1,0:T(8,128)S(1)}, f32[1,128,128]{2,1,0:T(8,128)S(1)}, u32[]{:S(2)}, u32[]{:S(2)}) collective-permute-start(f32[1,128,128]{2,1,0:T(8,128)S(1)} %get-tuple-element.92.refs_0_), channel_id=1, source_target_pairs={{0,4},{1,5},{2,6},{3,7},{4,0},{5,1},{6,2},{7,3},{8,12},{9,13},{10,... | collective-permute-start | bytes 196616 | tf_op jit(solution)/shard_map/ppermute | solution.py:481
  57.1 10.3 %collective-permute-start.18 = (f32[1,128,128]{2,1,0:T(8,128)S(1)}, f32[1,128,128]{2,1,0:T(8,128)S(1)}, u32[]{:S(2)}, u32[]{:S(2)}) collective-permute-start(f32[1,128,128]{2,1,0:T(8,128)S(1)} %shard_map.102), channel_id=1, source_target_pairs={{0,20},{1,21},{2,22},{3,23},{4,16},{5,17},{6,18},{7,19},{8,28},{9,... | collective-permute-start | bytes 196616 | tf_op jit(solution)/shard_map/ppermute | solution.py:481
  58.3 9.2 %collective-permute-start.19 = (f32[1,128,128]{2,1,0:T(8,128)S(1)}, f32[1,128,128]{2,1,0:T(8,128)S(1)}, u32[]{:S(2)}, u32[]{:S(2)}) collective-permute-start(f32[1,128,128]{2,1,0:T(8,128)S(1)} %shard_map.102), channel_id=1, source_target_pairs={{0,16},{1,17},{2,18},{3,19},{4,20},{5,21},{6,22},{7,23},{8,24},{9,... | collective-permute-start | bytes 196616 | tf_op jit(solution)/shard_map/ppermute | solution.py:481
  59.8 7.6 %collective-permute-start.17 = (f32[1,128,128]{2,1,0:T(8,128)S(1)}, f32[1,128,128]{2,1,0:T(8,128)S(1)}, u32[]{:S(2)}, u32[]{:S(2)}) collective-permute-start(f32[1,128,128]{2,1,0:T(8,128)S(1)} %collective-permute-done.15.refs_1_), channel_id=1, source_target_pairs={{0,4},{1,5},{2,6},{3,7},{4,0},{5,1},{6,2},{7,3},{8,12},{9,13},{10,... | collective-permute-start | bytes 196616 | tf_op jit(solution)/shard_map/ppermute | solution.py:481
  67.5 5.6 %collective-permute-start.20 = (f32[1,128,128]{2,1,0:T(8,128)S(1)}, f32[1,128,128]{2,1,0:T(8,128)S(1)}, u32[]{:S(2)}, u32[]{:S(2)}) collective-permute-start(f32[1,128,128]{2,1,0:T(8,128)S(1)} %get-tuple-element.95), channel_id=1, source_target_pairs={{0,8},{1,9},{2,10},{3,11},{4,12},{5,13},{6,14},{7,15},{8,0},{9,1},... | collective-permute-start | bytes 196616 | tf_op jit(solution)/shard_map/ppermute | solution.py:481
  73.3 11.2 %collective-permute-start.21 = (f32[2,1,128,128]{3,2,1,0:T(8,128)S(1)}, f32[2,1,128,128]{3,2,1,0:T(8,128)S(1)}, u32[]{:S(2)}, u32[]{:S(2)}) collective-permute-start(f32[2,1,128,128]{3,2,1,0:T(8,128)S(1)} %get-tuple-element.96), channel_id=1, source_target_pairs={{0,3},{1,2},{2,1},{3,0},{4,7},{5,6},{6,5},{7,4},{8,11},{9,10},{10,... | collective-permute-start | bytes 393224 | tf_op jit(solution)/shard_map/ppermute | solution.py:481
  73.6 10.8 %collective-permute-start.22 = (f32[2,1,128,128]{3,2,1,0:T(8,128)S(1)}, f32[2,1,128,128]{3,2,1,0:T(8,128)S(1)}, u32[]{:S(2)}, u32[]{:S(2)}) collective-permute-start(f32[2,1,128,128]{3,2,1,0:T(8,128)S(1)} %get-tuple-element.97), channel_id=1, source_target_pairs={{0,1},{1,0},{2,3},{3,2},{4,5},{5,4},{6,7},{7,6},{8,9},{9,8},{10,11... | collective-permute-start | bytes 393224 | tf_op jit(solution)/shard_map/ppermute | solution.py:481
  74.6 9.8 %collective-permute-start.23 = (f32[2,1,128,128]{3,2,1,0:T(8,128)S(1)}, f32[2,1,128,128]{3,2,1,0:T(8,128)S(1)}, u32[]{:S(2)}, u32[]{:S(2)}) collective-permute-start(f32[2,1,128,128]{3,2,1,0:T(8,128)S(1)} %get-tuple-element.98), channel_id=1, source_target_pairs={{0,2},{1,3},{2,0},{3,1},{4,6},{5,7},{6,4},{7,5},{8,10},{9,11},{10,... | collective-permute-start | bytes 393224 | tf_op jit(solution)/shard_map/ppermute | solution.py:481

commit v7 on v6

--- a/solution.py
+++ b/solution.py
@@ -21,6 +21,7 @@
 ORDER = (3, 1, 2, 0)
 EARLY = (0, 3)
 UNROLL = 8
+AHEAD = 2
 PAIR = 2
 F32 = jnp.float32
 BF16 = jnp.bfloat16
@@ -147,14 +148,17 @@
     return row <= col if upper else row >= col
 
 
-def over_units(count, step):
+def over_units(blocks, step, first=0, heads=H, most=UNROLL):
+    count = blocks * heads
+    unroll = max(u for u in range(1, most + 1) if count % u == 0)
+
     def several(i, _):
-        for j in range(UNROLL):
-            unit = i * UNROLL + j
-            step(unit // H, unit % H)
+        for j in range(unroll):
+            unit = i * unroll + j
+            step(unit // heads, first + unit % heads)
         return 0
 
-    lax.fori_loop(0, count // UNROLL, several, 0)
+    lax.fori_loop(0, count // unroll, several, 0)
 
 
 def block_part(block, first, count):
@@ -191,7 +195,7 @@
         for i, value in enumerate(sums):
             out_ref[block_part(block, i, 1), cols] = value
 
-    over_units(q_ref.shape[0] // BLOCK * H, step)
+    over_units(q_ref.shape[0] // BLOCK, step, most=4)
 
 
 def local_part(queries, keys, values):
@@ -217,7 +221,7 @@
             if j:
                 out_ref[block, head, pl.ds(0, j * CUT), to] = scores[: j * CUT].astype(BF16)
 
-    over_units(k_ref.shape[0] // BLOCK * H, step)
+    over_units(k_ref.shape[0] // BLOCK, step, most=4)
 
 
 def turned_scores(keys, queries):
@@ -248,7 +252,7 @@
         for i, value in enumerate(sums):
             out_ref[block_part(block, i, 1), cols] = value
 
-    over_units(g_ref.shape[0] // BLOCK * H, step)
+    over_units(g_ref.shape[0] // BLOCK, step)
     copy.wait()
 
 
@@ -403,9 +407,13 @@
     )[0]
 
 
-def turned_kernel(where, a_ref, b_ref, c_ref, ready_ref, out_ref, far_ref, sem):
-    copy = pltpu.make_async_copy(ready_ref, far_ref, sem)
-    copy.start()
+def turned_kernel(first, heads, ready, where, a_ref, b_ref, c_ref, *refs):
+    if ready:
+        ready_ref, out_ref, far_ref, sem = refs[-4:]
+        copy = pltpu.make_async_copy(ready_ref, far_ref, sem)
+        copy.start()
+    else:
+        out_ref = refs[-1]
     mask = triangle(CUT, True)
 
     def step(block, head):
@@ -414,19 +422,21 @@
         for i, value in enumerate(sums):
             out_ref[block_part(block, i, 1), cols] = value
 
-    over_units(a_ref.shape[0] // BLOCK * H, step)
-    copy.wait()
-
-
-def turned_part(a, b, c, ready):
+    over_units(a_ref.shape[0] // BLOCK, step, first, heads)
+    if ready:
+        copy.wait()
+
+
+def turned_part(first, heads, a, b, c, made=(), ready=()):
     tokens, features = a.shape
     return call(
-        turned_kernel,
-        [vmem(tokens, features), jax.ShapeDtypeStruct(ready.shape, ready.dtype)],
-        [a, b, c, ready],
-        4 * tokens * BLOCK * features,
-        scratch=[pltpu.SemaphoreType.DMA(())],
-        far_out=(1,),
+        functools.partial(turned_kernel, first, heads, len(ready)),
+        [vmem(tokens, features)] + [jax.ShapeDtypeStruct(r.shape, r.dtype) for r in ready],
+        [a, b, c, *made, *ready],
+        4 * tokens * BLOCK * heads * HD,
+        scratch=[pltpu.SemaphoreType.DMA(())] * len(ready),
+        far_out=(1,) if ready else (),
+        aliases={3: 0} if made else None,
     )
 
 
@@ -601,11 +611,12 @@
         priors[o] = prior
     carried, later = carry(first, (queries, grads), True)
     local_v, normed = value_part(scores, grads, normed)
+    local_k = turned_part(0, AHEAD, values, grads, queries)
     grad_q = query_part(grads, values, keys, priors)
-    local_k, grad_q = turned_part(values, grads, queries, grad_q)
+    local_k, grad_q = turned_part(AHEAD, H - AHEAD, values, grads, queries, local_k, [grad_q])
     args = local_k, local_v, keys, values, carried, later
-    made = final_part((0,), *args)
-    grad_k, grad_v = final_part(ORDER[:-1], *args, made)
+    made = final_part((0,) + ORDER[:1], *args)
+    grad_k, grad_v = final_part(ORDER[1:-1], *args, made)
     return normed, grad_q, grad_k, grad_v
 
 

time: 87.5 us -> 88.8 us (1.015)
  Pallas kernels: 31.7 us -> 32.8 us
    pallas_call x23 -> x24, Pallas kernels: 31.7 us -> 32.8 us  [call(): pl.pallas_call(lambda *refs: kernel(place(), *refs), out_shape=out_shape,...]
  transfers between devices with their start and end apart: 24 -> 24, of which waited for: 10 -> 11; matrix products, arithmetic and copies ran while one was open for 0% -> 0% of each run, Pallas kernels for 27% -> 29%
where the time goes in v7:
time: 88.8 us; the launch traced here: 88.6 us
  Pallas kernels  32.8 us (37%)
  starting transfers between devices  29.4 us (33%)
  waiting for transfers between devices  22.2 us (25%)
  local copies, waits for them, and re-layouts  3.2 us (4%)
  between operations  1.09 us (1%)
    pallas_call x24, Pallas kernels, call(): pl.pallas_call(lambda *refs: kernel(place(), *refs), out_shape=out_shape,...  32.8 us
    ppermute x24, starting transfers between devices, moved(): return lax.ppermute(value, AXES, pairs)  29.4 us
    ppermute x24, waiting for transfers between devices, moved(): return lax.ppermute(value, AXES, pairs)  22.2 us
    unnamed x14, local copies, waits for them, and re-layouts  3.2 us
  transfers between devices with their start and end apart: 24, of which 11 were waited for; matrix products, arithmetic and copies ran while one was open for 0% of the time, Pallas kernels for 29%

profile of v7, /device:TPU:0, one launch (start us, length us, event | category | flops | bytes accessed | tf_op | source)
XLA Modules:
  0.0 88.6 jit_solution(11950355090862239454)
XLA Ops:
  0.6 1.6 %copy-done = bf16[1024,1024]{1,0:T(8,128)(2,1)S(1)} copy-done((bf16[1024,1024]{1,0:T(8,128)(2,1)S(1)}, bf16[1024,1024]{1,0:T(8,128)(2,1)}, u32[]{:S(2)}) %copy-start) | copy-done | bytes 2097176
  2.2 1.6 %copy-done.3 = bf16[1024,1024]{1,0:T(8,128)(2,1)S(1)} copy-done((bf16[1024,1024]{1,0:T(8,128)(2,1)S(1)}, bf16[1024,1024]{1,0:T(8,128)(2,1)}, u32[]{:S(2)}) %copy-start.3) | copy-done | bytes 2097176
  3.8 0.8 shard_map.86
  4.7 3.0 %collective-permute-start = (f32[2,1,128,128]{3,2,1,0:T(8,128)S(1)}, f32[2,1,128,128]{3,2,1,0:T(8,128)S(1)}, u32[]{:S(2)}, u32[]{:S(2)}) collective-permute-start(f32[2,1,128,128]{3,2,1,0:T(8,128)S(1)} %get-tuple-element.57), channel_id=1, source_target_pairs={{0,1},{1,0},{2,3},{3,2},{4,5},{5,4},{6,7},{7,6},{8,9},{9,8},{10,11... | collective-permute-start | bytes 393224 | tf_op jit(solution)/shard_map/ppermute | solution.py:491
  7.7 1.6 %collective-permute-start.1 = (f32[2,1,128,128]{3,2,1,0:T(8,128)S(1)}, f32[2,1,128,128]{3,2,1,0:T(8,128)S(1)}, u32[]{:S(2)}, u32[]{:S(2)}) collective-permute-start(f32[2,1,128,128]{3,2,1,0:T(8,128)S(1)} %get-tuple-element.58), channel_id=1, source_target_pairs={{0,2},{1,3},{2,0},{3,1},{4,6},{5,7},{6,4},{7,5},{8,10},{9,11},{10,... | collective-permute-start | bytes 393224 | tf_op jit(solution)/shard_map/ppermute | solution.py:491
  9.3 1.6 %shard_map.87 = (f32[2,1,128,128]{3,2,1,0:T(8,128)S(1)}, f32[2,2,1,128,128]{4,3,2,1,0:T(8,128)S(1)}) custom-call(bf16[1024,1024]{1,0:T(8,128)(2,1)} %refs_2_.11, bf16[1024,1024]{1,0:T(8,128)(2,1)} %refs_3_.7), custom_call_target="tpu_custom_call" | custom-call | flops 67108864 | bytes 671088 | tf_op jit(solution)/shard_map/pallas_call | solution.py:54
  10.9 0.2 collective-permute-start.2
  11.1 0.5 shard_map.85
  11.6 1.1 %collective-permute-done.1.refs_2_.refs_4_ = f32[2,1,128,128]{3,2,1,0:T(8,128)S(1)} collective-permute-done((f32[2,1,128,128]{3,2,1,0:T(8,128)S(1)}, f32[2,1,128,128]{3,2,1,0:T(8,128)S(1)}, u32[]{:S(2)}, u32[]{:S(2)}) %collective-permute-start.1) | collective-permute-done | bytes 131104 | tf_op jit(solution)/shard_map/ppermute | solution.py:491
  12.7 4.1 %collective-permute-done.2.refs_3_.refs_5_ = f32[2,1,128,128]{3,2,1,0:T(8,128)S(1)} collective-permute-done((f32[2,1,128,128]{3,2,1,0:T(8,128)S(1)}, f32[2,1,128,128]{3,2,1,0:T(8,128)S(1)}, u32[]{:S(2)}, u32[]{:S(2)}) %collective-permute-start.2) | collective-permute-done | bytes 131104 | tf_op jit(solution)/shard_map/ppermute | solution.py:491
  17.0 2.7 %collective-permute-start.4 = (f32[1,128,128]{2,1,0:T(8,128)S(1)}, f32[1,128,128]{2,1,0:T(8,128)S(1)}, u32[]{:S(2)}, u32[]{:S(2)}) collective-permute-start(f32[1,128,128]{2,1,0:T(8,128)S(1)} %get-tuple-element.60.refs_0_), channel_id=1, source_target_pairs={{0,4},{1,5},{2,6},{3,7},{4,0},{5,1},{6,2},{7,3},{8,12},{9,13},{10,... | collective-permute-start | bytes 196616 | tf_op jit(solution)/shard_map/ppermute | solution.py:491
  19.6 1.2 %collective-permute-start.5 = (f32[1,128,128]{2,1,0:T(8,128)S(1)}, f32[1,128,128]{2,1,0:T(8,128)S(1)}, u32[]{:S(2)}, u32[]{:S(2)}) collective-permute-start(f32[1,128,128]{2,1,0:T(8,128)S(1)} %collective-permute-done.3.refs_1_), channel_id=1, source_target_pairs={{0,4},{1,5},{2,6},{3,7},{4,0},{5,1},{6,2},{7,3},{8,12},{9,13},{10,... | collective-permute-start | bytes 196616 | tf_op jit(solution)/shard_map/ppermute | solution.py:491
  20.8 2.8 %collective-permute-start.6 = (f32[1,128,128]{2,1,0:T(8,128)S(1)}, f32[1,128,128]{2,1,0:T(8,128)S(1)}, u32[]{:S(2)}, u32[]{:S(2)}) collective-permute-start(f32[1,128,128]{2,1,0:T(8,128)S(1)} %shard_map.89), channel_id=1, source_target_pairs={{0,20},{1,21},{2,22},{3,23},{4,16},{5,17},{6,18},{7,19},{8,28},{9,... | collective-permute-start | bytes 196616 | tf_op jit(solution)/shard_map/ppermute | solution.py:491
  23.6 0.5 collective-permute-start.7
  24.1 2.0 %collective-permute-done.4.refs_2_ = f32[1,128,128]{2,1,0:T(8,128)S(1)} collective-permute-done((f32[1,128,128]{2,1,0:T(8,128)S(1)}, f32[1,128,128]{2,1,0:T(8,128)S(1)}, u32[]{:S(2)}, u32[]{:S(2)}) %collective-permute-start.4) | collective-permute-done | bytes 65568 | tf_op jit(solution)/shard_map/ppermute | solution.py:491
  26.1 2.1 %collective-permute-done.5.refs_3_ = f32[1,128,128]{2,1,0:T(8,128)S(1)} collective-permute-done((f32[1,128,128]{2,1,0:T(8,128)S(1)}, f32[1,128,128]{2,1,0:T(8,128)S(1)}, u32[]{:S(2)}, u32[]{:S(2)}) %collective-permute-start.5) | collective-permute-done | bytes 65568 | tf_op jit(solution)/shard_map/ppermute | solution.py:491
  28.2 2.2 %collective-permute-done.6.refs_4_ = f32[1,128,128]{2,1,0:T(8,128)S(1)} collective-permute-done((f32[1,128,128]{2,1,0:T(8,128)S(1)}, f32[1,128,128]{2,1,0:T(8,128)S(1)}, u32[]{:S(2)}, u32[]{:S(2)}) %collective-permute-start.6) | collective-permute-done | bytes 65568 | tf_op jit(solution)/shard_map/ppermute | solution.py:491
  30.5 1.2 %collective-permute-done.8.refs_1_ = f32[1,128,128]{2,1,0:T(8,128)S(1)} collective-permute-done((f32[1,128,128]{2,1,0:T(8,128)S(1)}, f32[1,128,128]{2,1,0:T(8,128)S(1)}, u32[]{:S(2)}, u32[]{:S(2)}) %collective-permute-start.8) | collective-permute-done | bytes 65568 | tf_op jit(solution)/shard_map/ppermute | solution.py:491
  31.8 0.6 collective-permute-start.9
  32.4 3.0 %collective-permute-start.11 = (f32[2,1,128,128]{3,2,1,0:T(8,128)S(1)}, f32[2,1,128,128]{3,2,1,0:T(8,128)S(1)}, u32[]{:S(2)}, u32[]{:S(2)}) collective-permute-start(f32[2,1,128,128]{3,2,1,0:T(8,128)S(1)} %get-tuple-element.68), channel_id=1, source_target_pairs={{0,3},{1,2},{2,1},{3,0},{4,7},{5,6},{6,5},{7,4},{8,11},{9,10},{10,... | collective-permute-start | bytes 393224 | tf_op jit(solution)/shard_map/ppermute | solution.py:491
  35.4 4.6 %shard_map.92.refs_2_ = f32[1024,1024]{1,0:T(8,128)S(1)} custom-call(bf16[1024,1024]{1,0:T(8,128)(2,1)S(1)} %copy-done.2, bf16[1024,1024]{1,0:T(8,128)(2,1)S(1)} %copy-done.4, bf16[1024,1024]{1,0:T(8,128)(2,1)S(1)} %copy-done.1), custom_call_target="tpu_custom_call" | custom-call | flops 2147483648 | bytes 21474836 | tf_op jit(solution)/shard_map/pallas_call | solution.py:54
  40.0 0.8 shard_map.93
  40.8 0.6 collective-permute-done.11.refs_0_
  41.5 0.8 shard_map.94
  42.3 3.2 %shard_map.95 = (f32[1024,1024]{1,0:T(8,128)S(1)}, bf16[1024,1024]{1,0:T(8,128)(2,1)S(1)}, bf16[1024,1024]{1,0:T(8,128)(2,1)S(1)}, bf16[2,2,1,128,128]{4,3,2,1,0...) custom-call(f32[2,1,128,128]{3,2,1,0:T(8,128)S(1)} %collective-permu, ...), custom_call_target="tpu_custom_call", output_to_operand_aliasing={{0}: (4, {})} | custom-call | flops 20971520 | bytes 209715 | tf_op jit(solution)/shard_map/pallas_call | solution.py:54
  45.6 0.9 shard_map.101
  46.4 0.6 collective-permute-start.12
  47.0 0.3 collective-permute-start.13
  47.3 2.7 %collective-permute-start.14 = (f32[2,1,128,128]{3,2,1,0:T(8,128)S(1)}, f32[2,1,128,128]{3,2,1,0:T(8,128)S(1)}, u32[]{:S(2)}, u32[]{:S(2)}) collective-permute-start(f32[2,1,128,128]{3,2,1,0:T(8,128)S(1)} %get-tuple-element.91), channel_id=1, source_target_pairs={{0,3},{1,2},{2,1},{3,0},{4,7},{5,6},{6,5},{7,4},{8,11},{9,10},{10,... | collective-permute-start | bytes 393224 | tf_op jit(solution)/shard_map/ppermute | solution.py:491
  50.0 0.5 shard_map.100
  50.5 2.4 %collective-permute-done.12.refs_1_.refs_3_ = f32[2,1,128,128]{3,2,1,0:T(8,128)S(1)} collective-permute-done((f32[2,1,128,128]{3,2,1,0:T(8,128)S(1)}, f32[2,1,128,128]{3,2,1,0:T(8,128)S(1)}, u32[]{:S(2)}, u32[]{:S(2)}) %collective-permute-start.12) | collective-permute-done | bytes 131104 | tf_op jit(solution)/shard_map/ppermute | solution.py:491
  52.9 2.0 %collective-permute-done.14.refs_3_.refs_5_ = f32[2,1,128,128]{3,2,1,0:T(8,128)S(1)} collective-permute-done((f32[2,1,128,128]{3,2,1,0:T(8,128)S(1)}, f32[2,1,128,128]{3,2,1,0:T(8,128)S(1)}, u32[]{:S(2)}, u32[]{:S(2)}) %collective-permute-start.14) | collective-permute-done | bytes 131104 | tf_op jit(solution)/shard_map/ppermute | solution.py:491
  55.0 2.0 %collective-permute-start.16 = (f32[1,128,128]{2,1,0:T(8,128)S(1)}, f32[1,128,128]{2,1,0:T(8,128)S(1)}, u32[]{:S(2)}, u32[]{:S(2)}) collective-permute-start(f32[1,128,128]{2,1,0:T(8,128)S(1)} %get-tuple-element.92.refs_0_), channel_id=1, source_target_pairs={{0,4},{1,5},{2,6},{3,7},{4,0},{5,1},{6,2},{7,3},{8,12},{9,13},{10,... | collective-permute-start | bytes 196616 | tf_op jit(solution)/shard_map/ppermute | solution.py:491
  57.1 1.2 %collective-permute-start.18 = (f32[1,128,128]{2,1,0:T(8,128)S(1)}, f32[1,128,128]{2,1,0:T(8,128)S(1)}, u32[]{:S(2)}, u32[]{:S(2)}) collective-permute-start(f32[1,128,128]{2,1,0:T(8,128)S(1)} %shard_map.103), channel_id=1, source_target_pairs={{0,20},{1,21},{2,22},{3,23},{4,16},{5,17},{6,18},{7,19},{8,28},{9,... | collective-permute-start | bytes 196616 | tf_op jit(solution)/shard_map/ppermute | solution.py:491
  58.3 1.5 %collective-permute-start.19 = (f32[1,128,128]{2,1,0:T(8,128)S(1)}, f32[1,128,128]{2,1,0:T(8,128)S(1)}, u32[]{:S(2)}, u32[]{:S(2)}) collective-permute-start(f32[1,128,128]{2,1,0:T(8,128)S(1)} %shard_map.103), channel_id=1, source_target_pairs={{0,16},{1,17},{2,18},{3,19},{4,20},{5,21},{6,22},{7,23},{8,24},{9,... | collective-permute-start | bytes 196616 | tf_op jit(solution)/shard_map/ppermute | solution.py:491
  59.8 1.8 %collective-permute-start.17 = (f32[1,128,128]{2,1,0:T(8,128)S(1)}, f32[1,128,128]{2,1,0:T(8,128)S(1)}, u32[]{:S(2)}, u32[]{:S(2)}) collective-permute-start(f32[1,128,128]{2,1,0:T(8,128)S(1)} %collective-permute-done.15.refs_1_), channel_id=1, source_target_pairs={{0,4},{1,5},{2,6},{3,7},{4,0},{5,1},{6,2},{7,3},{8,12},{9,13},{10,... | collective-permute-start | bytes 196616 | tf_op jit(solution)/shard_map/ppermute | solution.py:491
  61.5 2.6 %shard_map.84.refs_0_ = bf16[2,8,512,512]{3,2,1,0:T(8,128)(2,1)S(1)} custom-call(bf16[1024,1024]{1,0:T(8,128)(2,1)S(1)} %copy-done.4, bf16[1024,1024]{1,0:T(8,128)(2,1)S(1)} %copy-done.2), custom_call_target="tpu_custom_call" | custom-call | flops 1073741824 | bytes 10737418 | tf_op jit(solution)/shard_map/pallas_call | solution.py:54
  64.2 3.2 %collective-permute-done.17.refs_3_ = f32[1,128,128]{2,1,0:T(8,128)S(1)} collective-permute-done((f32[1,128,128]{2,1,0:T(8,128)S(1)}, f32[1,128,128]{2,1,0:T(8,128)S(1)}, u32[]{:S(2)}, u32[]{:S(2)}) %collective-permute-start.17) | collective-permute-done | bytes 65568 | tf_op jit(solution)/shard_map/ppermute | solution.py:491
  67.6 5.5 %shard_map.98.refs_4_ = bf16[1024,1024]{1,0:T(8,128)(2,1)S(1)} custom-call(bf16[1024,1024]{1,0:T(8,128)(2,1)S(1)} %get-tuple-element.78.refs_1_.refs_0_, bf16[1024,1024]{1,0:T(8,128)(2,1)S(1)} %copy-done.1, bf16[1024,1024]{1,0:T(8,128)(2,1)S(1)} %copy-done.4, bf16[2,2,1,128,128]{4,3,2,1,0:T(8,128)(2,1)S(1)} %get-tuple-element.81.refs_3_, ...), custom_call_target="tpu_custom_call" | custom-call | flops 2147483648 | bytes 21474836 | tf_op jit(solution)/shard_map/pallas_call | solution.py:54
  73.1 1.1 %shard_map.97.refs_3_ = f32[1024,1024]{1,0:T(8,128)S(1)} custom-call(bf16[1024,1024]{1,0:T(8,128)(2,1)S(1)} %copy-done.1, bf16[1024,1024]{1,0:T(8,128)(2,1)S(1)} %get-tuple-element.78.refs_1_.refs_0_, bf16[1024,1024]{1,0:T(8,128)(2,1)S(1)} %copy-done.2), custom_call_target="tpu_custom_call" | custom-call | flops 536870912 | bytes 5368709 | tf_op jit(solution)/shard_map/pallas_call | solution.py:54
  74.3 0.6 collective-permute-start.21
  74.9 0.3 collective-permute-start.22
  75.3 2.6 %collective-permute-start.23 = (f32[2,1,128,128]{3,2,1,0:T(8,128)S(1)}, f32[2,1,128,128]{3,2,1,0:T(8,128)S(1)}, u32[]{:S(2)}, u32[]{:S(2)}) collective-permute-start(f32[2,1,128,128]{3,2,1,0:T(8,128)S(1)} %get-tuple-element.101), channel_id=1, source_target_pairs={{0,3},{1,2},{2,1},{3,0},{4,7},{5,6},{6,5},{7,4},{8,11},{9,10},{10,... | collective-permute-start | bytes 393224 | tf_op jit(solution)/shard_map/ppermute | solution.py:491
  77.9 3.1 %shard_map.99 = (f32[1024,1024]{1,0:T(8,128)S(1)}, bf16[1024,1024]{1,0:T(8,128)(2,1)}) custom-call(bf16[1024,1024]{1,0:T(8,128)(2,1)S(1)} %copy-done.1, bf16[1024,1024]{1,0:T(8,128)(2,1)S(1)} %get-tuple-element.78.refs_1_.refs_0_, bf16[1024,1024]{1,0:T(8,128)(2,1)S(1)} %copy-done.2, ...), custom_call_target="tpu_custom_call", output_to_operand_aliasing={{0}: (3, {})} | custom-call | flops 1610612736 | bytes 16106127 | tf_op jit(solution)/shard_map/pallas_call | solution.py:54
  81.0 2.1 %shard_map.96 = (f32[1024,1024]{1,0:T(8,128)S(1)}, bf16[1024,1024]{1,0:T(8,128)(2,1)}) custom-call(bf16[2,8,512,512]{3,2,1,0:T(8,128)(2,1)S(1)} %shard_map.84.refs_0_, bf16[1024,1024]{1,0:T(8,128)(2,1)S(1)} %get-tuple-element.78.refs_1_.refs_0_, bf16[1024,1024]{1,0:T(8,128)(2,1)S(1)} %get-tuple-element.79.refs_2_), custom_call_target="tpu_custom_call" | custom-call | flops 1073741824 | bytes 10737418 | tf_op jit(solution)/shard_map/pallas_call | solution.py:54
  83.2 1.1 %collective-permute-done.23.refs_5_ = f32[2,1,128,128]{3,2,1,0:T(8,128)S(1)} collective-permute-done((f32[2,1,128,128]{3,2,1,0:T(8,128)S(1)}, f32[2,1,128,128]{3,2,1,0:T(8,128)S(1)}, u32[]{:S(2)}, u32[]{:S(2)}) %collective-permute-start.23) | collective-permute-done | bytes 131104 | tf_op jit(solution)/shard_map/ppermute | solution.py:491
  84.3 2.0 %shard_map.106 = (bf16[1024,1024]{1,0:T(8,128)(2,1)}, bf16[1024,1024]{1,0:T(8,128)(2,1)}) custom-call(f32[1024,1024]{1,0:T(8,128)S(1)} %get-tuple-element.86.refs_0_, f32[1024,1024]{1,0:T(8,128)S(1)} %get-tuple-element.87.refs_1_, bf16[1024,1024]{1,0:T(8,128)(2,1)S(1)} %copy-done.4, bf16[1024,1024]{1,0:T(8,128)(2,1)S(1)} %copy-done.1, ...), custom_call_target="tpu_custom_call" | custom-call | flops 268435456 | bytes 2684354 | tf_op jit(solution)/shard_map/pallas_call | solution.py:54
  86.4 2.0 %shard_map.107 = (bf16[1024,1024]{1,0:T(8,128)(2,1)}, bf16[1024,1024]{1,0:T(8,128)(2,1)}) custom-call(f32[1024,1024]{1,0:T(8,128)S(1)} %get-tuple-element.86.refs_0_, f32[1024,1024]{1,0:T(8,128)S(1)} %get-tuple-element.87.refs_1_, bf16[1024,1024]{1,0:T(8,128)(2,1)S(1)} %copy-done.4, ...), custom_call_target="tpu_custom_call", output_to_operand_aliasing={{0}: (8, {}), {1}: (9, {})} | custom-call | flops 268435456 | bytes 2684354 | tf_op jit(solution)/shard_map/pallas_call | solution.py:54
  (38 shorter events, 0.8 us)
Async XLA Ops:
  0.6 1.6 %copy-start = (bf16[1024,1024]{1,0:T(8,128)(2,1)S(1)}, bf16[1024,1024]{1,0:T(8,128)(2,1)}, u32[]{:S(2)}) copy-start(bf16[1024,1024]{1,0:T(8,128)(2,1)} %refs_3_.7) | copy-start | bytes 6291460
  2.2 1.6 %copy-start.3 = (bf16[1024,1024]{1,0:T(8,128)(2,1)S(1)}, bf16[1024,1024]{1,0:T(8,128)(2,1)}, u32[]{:S(2)}) copy-start(bf16[1024,1024]{1,0:T(8,128)(2,1)} %refs_2_.11) | copy-start | bytes 6291460
  4.7 7.0 %collective-permute-start = (f32[2,1,128,128]{3,2,1,0:T(8,128)S(1)}, f32[2,1,128,128]{3,2,1,0:T(8,128)S(1)}, u32[]{:S(2)}, u32[]{:S(2)}) collective-permute-start(f32[2,1,128,128]{3,2,1,0:T(8,128)S(1)} %get-tuple-element.57), channel_id=1, source_target_pairs={{0,1},{1,0},{2,3},{3,2},{4,5},{5,4},{6,7},{7,6},{8,9},{9,8},{10,11... | collective-permute-start | bytes 393224 | tf_op jit(solution)/shard_map/ppermute | solution.py:491
  7.7 3.4 %copy-start.1 = (bf16[1024,1024]{1,0:T(8,128)(2,1)S(1)}, bf16[1024,1024]{1,0:T(8,128)(2,1)}, u32[]{:S(2)}) copy-start(bf16[1024,1024]{1,0:T(8,128)(2,1)} %refs_3_.7) | copy-start | bytes 6291460
  7.7 3.4 %copy-start.4 = (bf16[1024,1024]{1,0:T(8,128)(2,1)S(1)}, bf16[1024,1024]{1,0:T(8,128)(2,1)}, u32[]{:S(2)}) copy-start(bf16[1024,1024]{1,0:T(8,128)(2,1)} %refs_2_.11) | copy-start | bytes 6291460
  7.7 5.0 %collective-permute-start.1 = (f32[2,1,128,128]{3,2,1,0:T(8,128)S(1)}, f32[2,1,128,128]{3,2,1,0:T(8,128)S(1)}, u32[]{:S(2)}, u32[]{:S(2)}) collective-permute-start(f32[2,1,128,128]{3,2,1,0:T(8,128)S(1)} %get-tuple-element.58), channel_id=1, source_target_pairs={{0,2},{1,3},{2,0},{3,1},{4,6},{5,7},{6,4},{7,5},{8,10},{9,11},{10,... | collective-permute-start | bytes 393224 | tf_op jit(solution)/shard_map/ppermute | solution.py:491
  10.9 24.5 %copy-start.2 = (bf16[1024,1024]{1,0:T(8,128)(2,1)S(1)}, bf16[1024,1024]{1,0:T(8,128)(2,1)}, u32[]{:S(2)}) copy-start(bf16[1024,1024]{1,0:T(8,128)(2,1)} %refs_0_.17) | copy-start | bytes 6291460
  10.9 5.9 %collective-permute-start.2 = (f32[2,1,128,128]{3,2,1,0:T(8,128)S(1)}, f32[2,1,128,128]{3,2,1,0:T(8,128)S(1)}, u32[]{:S(2)}, u32[]{:S(2)}) collective-permute-start(f32[2,1,128,128]{3,2,1,0:T(8,128)S(1)} %get-tuple-element.59), channel_id=1, source_target_pairs={{0,3},{1,2},{2,1},{3,0},{4,7},{5,6},{6,5},{7,4},{8,11},{9,10},{10,... | collective-permute-start | bytes 393224 | tf_op jit(solution)/shard_map/ppermute | solution.py:491
  16.9 2.7 %collective-permute-start.3 = (f32[1,128,128]{2,1,0:T(8,128)S(1)}, f32[1,128,128]{2,1,0:T(8,128)S(1)}, u32[]{:S(2)}, u32[]{:S(2)}) collective-permute-start(f32[1,128,128]{2,1,0:T(8,128)S(1)} %get-tuple-element.61), channel_id=1, source_target_pairs={{0,8},{1,9},{2,10},{3,11},{4,12},{5,13},{6,14},{7,15},{8,0},{9,1},... | collective-permute-start | bytes 196616 | tf_op jit(solution)/shard_map/ppermute | solution.py:491
  17.0 9.1 %collective-permute-start.4 = (f32[1,128,128]{2,1,0:T(8,128)S(1)}, f32[1,128,128]{2,1,0:T(8,128)S(1)}, u32[]{:S(2)}, u32[]{:S(2)}) collective-permute-start(f32[1,128,128]{2,1,0:T(8,128)S(1)} %get-tuple-element.60.refs_0_), channel_id=1, source_target_pairs={{0,4},{1,5},{2,6},{3,7},{4,0},{5,1},{6,2},{7,3},{8,12},{9,13},{10,... | collective-permute-start | bytes 196616 | tf_op jit(solution)/shard_map/ppermute | solution.py:491
  19.6 8.5 %collective-permute-start.5 = (f32[1,128,128]{2,1,0:T(8,128)S(1)}, f32[1,128,128]{2,1,0:T(8,128)S(1)}, u32[]{:S(2)}, u32[]{:S(2)}) collective-permute-start(f32[1,128,128]{2,1,0:T(8,128)S(1)} %collective-permute-done.3.refs_1_), channel_id=1, source_target_pairs={{0,4},{1,5},{2,6},{3,7},{4,0},{5,1},{6,2},{7,3},{8,12},{9,13},{10,... | collective-permute-start | bytes 196616 | tf_op jit(solution)/shard_map/ppermute | solution.py:491
  20.8 9.5 %collective-permute-start.6 = (f32[1,128,128]{2,1,0:T(8,128)S(1)}, f32[1,128,128]{2,1,0:T(8,128)S(1)}, u32[]{:S(2)}, u32[]{:S(2)}) collective-permute-start(f32[1,128,128]{2,1,0:T(8,128)S(1)} %shard_map.89), channel_id=1, source_target_pairs={{0,20},{1,21},{2,22},{3,23},{4,16},{5,17},{6,18},{7,19},{8,28},{9,... | collective-permute-start | bytes 196616 | tf_op jit(solution)/shard_map/ppermute | solution.py:491
  23.6 6.8 %collective-permute-start.7 = (f32[1,128,128]{2,1,0:T(8,128)S(1)}, f32[1,128,128]{2,1,0:T(8,128)S(1)}, u32[]{:S(2)}, u32[]{:S(2)}) collective-permute-start(f32[1,128,128]{2,1,0:T(8,128)S(1)} %shard_map.89), channel_id=1, source_target_pairs={{0,16},{1,17},{2,18},{3,19},{4,20},{5,21},{6,22},{7,23},{8,24},{9,... | collective-permute-start | bytes 196616 | tf_op jit(solution)/shard_map/ppermute | solution.py:491
  30.4 1.3 %collective-permute-start.8 = (f32[1,128,128]{2,1,0:T(8,128)S(1)}, f32[1,128,128]{2,1,0:T(8,128)S(1)}, u32[]{:S(2)}, u32[]{:S(2)}) collective-permute-start(f32[1,128,128]{2,1,0:T(8,128)S(1)} %get-tuple-element.63), channel_id=1, source_target_pairs={{0,8},{1,9},{2,10},{3,11},{4,12},{5,13},{6,14},{7,15},{8,0},{9,1},... | collective-permute-start | bytes 196616 | tf_op jit(solution)/shard_map/ppermute | solution.py:491
  31.8 10.5 %collective-permute-start.9 = (f32[2,1,128,128]{3,2,1,0:T(8,128)S(1)}, f32[2,1,128,128]{3,2,1,0:T(8,128)S(1)}, u32[]{:S(2)}, u32[]{:S(2)}) collective-permute-start(f32[2,1,128,128]{3,2,1,0:T(8,128)S(1)} %get-tuple-element.64), channel_id=1, source_target_pairs={{0,1},{1,0},{2,3},{3,2},{4,5},{5,4},{6,7},{7,6},{8,9},{9,8},{10,11... | collective-permute-start | bytes 393224 | tf_op jit(solution)/shard_map/ppermute | solution.py:491
  32.4 9.9 %collective-permute-start.10 = (f32[2,1,128,128]{3,2,1,0:T(8,128)S(1)}, f32[2,1,128,128]{3,2,1,0:T(8,128)S(1)}, u32[]{:S(2)}, u32[]{:S(2)}) collective-permute-start(f32[2,1,128,128]{3,2,1,0:T(8,128)S(1)} %get-tuple-element.65), channel_id=1, source_target_pairs={{0,2},{1,3},{2,0},{3,1},{4,6},{5,7},{6,4},{7,5},{8,10},{9,11},{10,... | collective-permute-start | bytes 393224 | tf_op jit(solution)/shard_map/ppermute | solution.py:491
  32.4 7.6 %copy-start.5 = (bf16[1024,1024]{1,0:T(8,128)(2,1)S(1)}, bf16[1024,1024]{1,0:T(8,128)(2,1)}, u32[]{:S(2)}) copy-start(bf16[1024,1024]{1,0:T(8,128)(2,1)} %refs_6_.1) | copy-start | bytes 6291460
  32.4 7.6 %copy-start.6 = (f32[1024]{0:T(1024)S(1)}, f32[1024]{0:T(1024)}, u32[]{:S(2)}) copy-start(f32[1024]{0:T(1024)} %param.8) | copy-start | bytes 12292
  32.4 9.0 %collective-permute-start.11 = (f32[2,1,128,128]{3,2,1,0:T(8,128)S(1)}, f32[2,1,128,128]{3,2,1,0:T(8,128)S(1)}, u32[]{:S(2)}, u32[]{:S(2)}) collective-permute-start(f32[2,1,128,128]{3,2,1,0:T(8,128)S(1)} %get-tuple-element.68), channel_id=1, source_target_pairs={{0,3},{1,2},{2,1},{3,0},{4,7},{5,6},{6,5},{7,4},{8,11},{9,10},{10,... | collective-permute-start | bytes 393224 | tf_op jit(solution)/shard_map/ppermute | solution.py:491
  46.4 6.4 %collective-permute-start.12 = (f32[2,1,128,128]{3,2,1,0:T(8,128)S(1)}, f32[2,1,128,128]{3,2,1,0:T(8,128)S(1)}, u32[]{:S(2)}, u32[]{:S(2)}) collective-permute-start(f32[2,1,128,128]{3,2,1,0:T(8,128)S(1)} %get-tuple-element.89), channel_id=1, source_target_pairs={{0,1},{1,0},{2,3},{3,2},{4,5},{5,4},{6,7},{7,6},{8,9},{9,8},{10,11... | collective-permute-start | bytes 393224 | tf_op jit(solution)/shard_map/ppermute | solution.py:491
  47.0 5.8 %collective-permute-start.13 = (f32[2,1,128,128]{3,2,1,0:T(8,128)S(1)}, f32[2,1,128,128]{3,2,1,0:T(8,128)S(1)}, u32[]{:S(2)}, u32[]{:S(2)}) collective-permute-start(f32[2,1,128,128]{3,2,1,0:T(8,128)S(1)} %get-tuple-element.90), channel_id=1, source_target_pairs={{0,2},{1,3},{2,0},{3,1},{4,6},{5,7},{6,4},{7,5},{8,10},{9,11},{10,... | collective-permute-start | bytes 393224 | tf_op jit(solution)/shard_map/ppermute | solution.py:491
  47.3 7.6 %collective-permute-start.14 = (f32[2,1,128,128]{3,2,1,0:T(8,128)S(1)}, f32[2,1,128,128]{3,2,1,0:T(8,128)S(1)}, u32[]{:S(2)}, u32[]{:S(2)}) collective-permute-start(f32[2,1,128,128]{3,2,1,0:T(8,128)S(1)} %get-tuple-element.91), channel_id=1, source_target_pairs={{0,3},{1,2},{2,1},{3,0},{4,7},{5,6},{6,5},{7,4},{8,11},{9,10},{10,... | collective-permute-start | bytes 393224 | tf_op jit(solution)/shard_map/ppermute | solution.py:491
  54.9 2.1 %collective-permute-start.15 = (f32[1,128,128]{2,1,0:T(8,128)S(1)}, f32[1,128,128]{2,1,0:T(8,128)S(1)}, u32[]{:S(2)}, u32[]{:S(2)}) collective-permute-start(f32[1,128,128]{2,1,0:T(8,128)S(1)} %get-tuple-element.93), channel_id=1, source_target_pairs={{0,8},{1,9},{2,10},{3,11},{4,12},{5,13},{6,14},{7,15},{8,0},{9,1},... | collective-permute-start | bytes 196616 | tf_op jit(solution)/shard_map/ppermute | solution.py:491
  55.0 9.2 %collective-permute-start.16 = (f32[1,128,128]{2,1,0:T(8,128)S(1)}, f32[1,128,128]{2,1,0:T(8,128)S(1)}, u32[]{:S(2)}, u32[]{:S(2)}) collective-permute-start(f32[1,128,128]{2,1,0:T(8,128)S(1)} %get-tuple-element.92.refs_0_), channel_id=1, source_target_pairs={{0,4},{1,5},{2,6},{3,7},{4,0},{5,1},{6,2},{7,3},{8,12},{9,13},{10,... | collective-permute-start | bytes 196616 | tf_op jit(solution)/shard_map/ppermute | solution.py:491
  57.1 10.4 %collective-permute-start.18 = (f32[1,128,128]{2,1,0:T(8,128)S(1)}, f32[1,128,128]{2,1,0:T(8,128)S(1)}, u32[]{:S(2)}, u32[]{:S(2)}) collective-permute-start(f32[1,128,128]{2,1,0:T(8,128)S(1)} %shard_map.103), channel_id=1, source_target_pairs={{0,20},{1,21},{2,22},{3,23},{4,16},{5,17},{6,18},{7,19},{8,28},{9,... | collective-permute-start | bytes 196616 | tf_op jit(solution)/shard_map/ppermute | solution.py:491
  58.3 9.2 %collective-permute-start.19 = (f32[1,128,128]{2,1,0:T(8,128)S(1)}, f32[1,128,128]{2,1,0:T(8,128)S(1)}, u32[]{:S(2)}, u32[]{:S(2)}) collective-permute-start(f32[1,128,128]{2,1,0:T(8,128)S(1)} %shard_map.103), channel_id=1, source_target_pairs={{0,16},{1,17},{2,18},{3,19},{4,20},{5,21},{6,22},{7,23},{8,24},{9,... | collective-permute-start | bytes 196616 | tf_op jit(solution)/shard_map/ppermute | solution.py:491
  59.8 7.7 %collective-permute-start.17 = (f32[1,128,128]{2,1,0:T(8,128)S(1)}, f32[1,128,128]{2,1,0:T(8,128)S(1)}, u32[]{:S(2)}, u32[]{:S(2)}) collective-permute-start(f32[1,128,128]{2,1,0:T(8,128)S(1)} %collective-permute-done.15.refs_1_), channel_id=1, source_target_pairs={{0,4},{1,5},{2,6},{3,7},{4,0},{5,1},{6,2},{7,3},{8,12},{9,13},{10,... | collective-permute-start | bytes 196616 | tf_op jit(solution)/shard_map/ppermute | solution.py:491
  67.5 6.7 %collective-permute-start.20 = (f32[1,128,128]{2,1,0:T(8,128)S(1)}, f32[1,128,128]{2,1,0:T(8,128)S(1)}, u32[]{:S(2)}, u32[]{:S(2)}) collective-permute-start(f32[1,128,128]{2,1,0:T(8,128)S(1)} %get-tuple-element.95), channel_id=1, source_target_pairs={{0,8},{1,9},{2,10},{3,11},{4,12},{5,13},{6,14},{7,15},{8,0},{9,1},... | collective-permute-start | bytes 196616 | tf_op jit(solution)/shard_map/ppermute | solution.py:491
  74.3 12.0 %collective-permute-start.21 = (f32[2,1,128,128]{3,2,1,0:T(8,128)S(1)}, f32[2,1,128,128]{3,2,1,0:T(8,128)S(1)}, u32[]{:S(2)}, u32[]{:S(2)}) collective-permute-start(f32[2,1,128,128]{3,2,1,0:T(8,128)S(1)} %get-tuple-element.96), channel_id=1, source_target_pairs={{0,1},{1,0},{2,3},{3,2},{4,5},{5,4},{6,7},{7,6},{8,9},{9,8},{10,11... | collective-permute-start | bytes 393224 | tf_op jit(solution)/shard_map/ppermute | solution.py:491
  74.9 11.4 %collective-permute-start.22 = (f32[2,1,128,128]{3,2,1,0:T(8,128)S(1)}, f32[2,1,128,128]{3,2,1,0:T(8,128)S(1)}, u32[]{:S(2)}, u32[]{:S(2)}) collective-permute-start(f32[2,1,128,128]{3,2,1,0:T(8,128)S(1)} %get-tuple-element.97), channel_id=1, source_target_pairs={{0,2},{1,3},{2,0},{3,1},{4,6},{5,7},{6,4},{7,5},{8,10},{9,11},{10,... | collective-permute-start | bytes 393224 | tf_op jit(solution)/shard_map/ppermute | solution.py:491
  75.3 9.0 %collective-permute-start.23 = (f32[2,1,128,128]{3,2,1,0:T(8,128)S(1)}, f32[2,1,128,128]{3,2,1,0:T(8,128)S(1)}, u32[]{:S(2)}, u32[]{:S(2)}) collective-permute-start(f32[2,1,128,128]{3,2,1,0:T(8,128)S(1)} %get-tuple-element.101), channel_id=1, source_target_pairs={{0,3},{1,2},{2,1},{3,0},{4,7},{5,6},{6,5},{7,4},{8,11},{9,10},{10,... | collective-permute-start | bytes 393224 | tf_op jit(solution)/shard_map/ppermute | solution.py:491

commit v8 on v7

--- a/solution.py
+++ b/solution.py
@@ -594,7 +594,10 @@
 def body(queries, key_rows, value_rows, norm_gain, cotangent):
     gain = norm_gain[None, :]
     first = first_totals(ORDER[0], key_rows, value_rows)
-    keys, values, queries, cotangent = (near(a) for a in (key_rows, value_rows, queries, cotangent))
+    keys, values = near(key_rows), near(value_rows)
+    piece, *first = first
+    piece, queries, cotangent = lax.optimization_barrier((piece, queries, cotangent))
+    first, queries, cotangent = [piece, *first], near(queries), near(cotangent)
     carried, inside = carry(first, (keys, values), False)
     attended = local_part(queries, keys, values)
     scores = turned_scores(keys, queries)

time: 88.8 us -> 88.8 us (level)
  no operation moved by 1% of the time
where the time goes in v8:
time: 88.8 us; the launch traced here: 88.6 us
  Pallas kernels  32.8 us (37%)
  starting transfers between devices  29.4 us (33%)
  waiting for transfers between devices  22.2 us (25%)
  local copies, waits for them, and re-layouts  3.2 us (4%)
  between operations  1.09 us (1%)
    pallas_call x24, Pallas kernels, call(): pl.pallas_call(lambda *refs: kernel(place(), *refs), out_shape=out_shape,...  32.8 us
    ppermute x24, starting transfers between devices, moved(): return lax.ppermute(value, AXES, pairs)  29.4 us
    ppermute x24, waiting for transfers between devices, moved(): return lax.ppermute(value, AXES, pairs)  22.2 us
    unnamed x14, local copies, waits for them, and re-layouts  3.2 us
  transfers between devices with their start and end apart: 24, of which 11 were waited for; matrix products, arithmetic and copies ran while one was open for 0% of the time, Pallas kernels for 29%

profile of v8, /device:TPU:0, one launch (start us, length us, event | category | flops | bytes accessed | tf_op | source)
XLA Modules:
  0.0 88.6 jit_solution(11950355090862239454)
XLA Ops:
  0.6 1.6 %copy-done = bf16[1024,1024]{1,0:T(8,128)(2,1)S(1)} copy-done((bf16[1024,1024]{1,0:T(8,128)(2,1)S(1)}, bf16[1024,1024]{1,0:T(8,128)(2,1)}, u32[]{:S(2)}) %copy-start) | copy-done | bytes 2097176
  2.2 1.6 %copy-done.3 = bf16[1024,1024]{1,0:T(8,128)(2,1)S(1)} copy-done((bf16[1024,1024]{1,0:T(8,128)(2,1)S(1)}, bf16[1024,1024]{1,0:T(8,128)(2,1)}, u32[]{:S(2)}) %copy-start.3) | copy-done | bytes 2097176
  3.8 0.8 shard_map.87
  4.7 3.0 %collective-permute-start = (f32[2,1,128,128]{3,2,1,0:T(8,128)S(1)}, f32[2,1,128,128]{3,2,1,0:T(8,128)S(1)}, u32[]{:S(2)}, u32[]{:S(2)}) collective-permute-start(f32[2,1,128,128]{3,2,1,0:T(8,128)S(1)} %get-tuple-element.62), channel_id=1, source_target_pairs={{0,1},{1,0},{2,3},{3,2},{4,5},{5,4},{6,7},{7,6},{8,9},{9,8},{10,11... | collective-permute-start | bytes 393224 | tf_op jit(solution)/shard_map/ppermute | solution.py:491
  7.7 1.6 %collective-permute-start.1 = (f32[2,1,128,128]{3,2,1,0:T(8,128)S(1)}, f32[2,1,128,128]{3,2,1,0:T(8,128)S(1)}, u32[]{:S(2)}, u32[]{:S(2)}) collective-permute-start(f32[2,1,128,128]{3,2,1,0:T(8,128)S(1)} %get-tuple-element.63), channel_id=1, source_target_pairs={{0,2},{1,3},{2,0},{3,1},{4,6},{5,7},{6,4},{7,5},{8,10},{9,11},{10,... | collective-permute-start | bytes 393224 | tf_op jit(solution)/shard_map/ppermute | solution.py:491
  9.3 1.6 %shard_map.84 = (f32[2,1,128,128]{3,2,1,0:T(8,128)S(1)}, f32[2,2,1,128,128]{4,3,2,1,0:T(8,128)S(1)}) custom-call(bf16[1024,1024]{1,0:T(8,128)(2,1)} %refs_2_.9, bf16[1024,1024]{1,0:T(8,128)(2,1)} %refs_3_.5), custom_call_target="tpu_custom_call" | custom-call | flops 67108864 | bytes 671088 | tf_op jit(solution)/shard_map/pallas_call | solution.py:54
  10.9 0.2 collective-permute-start.2
  11.1 0.5 shard_map.86
  11.6 1.1 %collective-permute-done.1.refs_2_.refs_4_ = f32[2,1,128,128]{3,2,1,0:T(8,128)S(1)} collective-permute-done((f32[2,1,128,128]{3,2,1,0:T(8,128)S(1)}, f32[2,1,128,128]{3,2,1,0:T(8,128)S(1)}, u32[]{:S(2)}, u32[]{:S(2)}) %collective-permute-start.1) | collective-permute-done | bytes 131104 | tf_op jit(solution)/shard_map/ppermute | solution.py:491
  12.7 4.1 %collective-permute-done.2.refs_3_.refs_5_ = f32[2,1,128,128]{3,2,1,0:T(8,128)S(1)} collective-permute-done((f32[2,1,128,128]{3,2,1,0:T(8,128)S(1)}, f32[2,1,128,128]{3,2,1,0:T(8,128)S(1)}, u32[]{:S(2)}, u32[]{:S(2)}) %collective-permute-start.2) | collective-permute-done | bytes 131104 | tf_op jit(solution)/shard_map/ppermute | solution.py:491
  17.0 2.7 %collective-permute-start.4 = (f32[1,128,128]{2,1,0:T(8,128)S(1)}, f32[1,128,128]{2,1,0:T(8,128)S(1)}, u32[]{:S(2)}, u32[]{:S(2)}) collective-permute-start(f32[1,128,128]{2,1,0:T(8,128)S(1)} %get-tuple-element.65.refs_0_), channel_id=1, source_target_pairs={{0,4},{1,5},{2,6},{3,7},{4,0},{5,1},{6,2},{7,3},{8,12},{9,13},{10,... | collective-permute-start | bytes 196616 | tf_op jit(solution)/shard_map/ppermute | solution.py:491
  19.6 1.2 %collective-permute-start.5 = (f32[1,128,128]{2,1,0:T(8,128)S(1)}, f32[1,128,128]{2,1,0:T(8,128)S(1)}, u32[]{:S(2)}, u32[]{:S(2)}) collective-permute-start(f32[1,128,128]{2,1,0:T(8,128)S(1)} %collective-permute-done.3.refs_1_), channel_id=1, source_target_pairs={{0,4},{1,5},{2,6},{3,7},{4,0},{5,1},{6,2},{7,3},{8,12},{9,13},{10,... | collective-permute-start | bytes 196616 | tf_op jit(solution)/shard_map/ppermute | solution.py:491
  20.8 2.8 %collective-permute-start.6 = (f32[1,128,128]{2,1,0:T(8,128)S(1)}, f32[1,128,128]{2,1,0:T(8,128)S(1)}, u32[]{:S(2)}, u32[]{:S(2)}) collective-permute-start(f32[1,128,128]{2,1,0:T(8,128)S(1)} %shard_map.89), channel_id=1, source_target_pairs={{0,20},{1,21},{2,22},{3,23},{4,16},{5,17},{6,18},{7,19},{8,28},{9,... | collective-permute-start | bytes 196616 | tf_op jit(solution)/shard_map/ppermute | solution.py:491
  23.6 0.5 collective-permute-start.7
  24.1 2.0 %collective-permute-done.4.refs_2_ = f32[1,128,128]{2,1,0:T(8,128)S(1)} collective-permute-done((f32[1,128,128]{2,1,0:T(8,128)S(1)}, f32[1,128,128]{2,1,0:T(8,128)S(1)}, u32[]{:S(2)}, u32[]{:S(2)}) %collective-permute-start.4) | collective-permute-done | bytes 65568 | tf_op jit(solution)/shard_map/ppermute | solution.py:491
  26.1 2.1 %collective-permute-done.5.refs_3_ = f32[1,128,128]{2,1,0:T(8,128)S(1)} collective-permute-done((f32[1,128,128]{2,1,0:T(8,128)S(1)}, f32[1,128,128]{2,1,0:T(8,128)S(1)}, u32[]{:S(2)}, u32[]{:S(2)}) %collective-permute-start.5) | collective-permute-done | bytes 65568 | tf_op jit(solution)/shard_map/ppermute | solution.py:491
  28.2 2.2 %collective-permute-done.6.refs_4_ = f32[1,128,128]{2,1,0:T(8,128)S(1)} collective-permute-done((f32[1,128,128]{2,1,0:T(8,128)S(1)}, f32[1,128,128]{2,1,0:T(8,128)S(1)}, u32[]{:S(2)}, u32[]{:S(2)}) %collective-permute-start.6) | collective-permute-done | bytes 65568 | tf_op jit(solution)/shard_map/ppermute | solution.py:491
  30.5 1.2 %collective-permute-done.8.refs_1_ = f32[1,128,128]{2,1,0:T(8,128)S(1)} collective-permute-done((f32[1,128,128]{2,1,0:T(8,128)S(1)}, f32[1,128,128]{2,1,0:T(8,128)S(1)}, u32[]{:S(2)}, u32[]{:S(2)}) %collective-permute-start.8) | collective-permute-done | bytes 65568 | tf_op jit(solution)/shard_map/ppermute | solution.py:491
  31.8 0.6 collective-permute-start.9
  32.4 3.0 %collective-permute-start.11 = (f32[2,1,128,128]{3,2,1,0:T(8,128)S(1)}, f32[2,1,128,128]{3,2,1,0:T(8,128)S(1)}, u32[]{:S(2)}, u32[]{:S(2)}) collective-permute-start(f32[2,1,128,128]{3,2,1,0:T(8,128)S(1)} %get-tuple-element.73), channel_id=1, source_target_pairs={{0,3},{1,2},{2,1},{3,0},{4,7},{5,6},{6,5},{7,4},{8,11},{9,10},{10,... | collective-permute-start | bytes 393224 | tf_op jit(solution)/shard_map/ppermute | solution.py:491
  35.4 4.6 %shard_map.92.refs_2_ = f32[1024,1024]{1,0:T(8,128)S(1)} custom-call(bf16[1024,1024]{1,0:T(8,128)(2,1)S(1)} %copy-done.2, bf16[1024,1024]{1,0:T(8,128)(2,1)S(1)} %copy-done.4, bf16[1024,1024]{1,0:T(8,128)(2,1)S(1)} %copy-done.1), custom_call_target="tpu_custom_call" | custom-call | flops 2147483648 | bytes 21474836 | tf_op jit(solution)/shard_map/pallas_call | solution.py:54
  40.0 0.8 shard_map.93
  40.8 0.6 collective-permute-done.11.refs_0_
  41.5 0.8 shard_map.94
  42.3 3.2 %shard_map.95 = (f32[1024,1024]{1,0:T(8,128)S(1)}, bf16[1024,1024]{1,0:T(8,128)(2,1)S(1)}, bf16[1024,1024]{1,0:T(8,128)(2,1)S(1)}, bf16[2,2,1,128,128]{4,3,2,1,0...) custom-call(f32[2,1,128,128]{3,2,1,0:T(8,128)S(1)} %collective-permu, ...), custom_call_target="tpu_custom_call", output_to_operand_aliasing={{0}: (4, {})} | custom-call | flops 20971520 | bytes 209715 | tf_op jit(solution)/shard_map/pallas_call | solution.py:54
  45.6 0.9 shard_map.101
  46.4 0.6 collective-permute-start.12
  47.0 0.3 collective-permute-start.13
  47.3 2.7 %collective-permute-start.14 = (f32[2,1,128,128]{3,2,1,0:T(8,128)S(1)}, f32[2,1,128,128]{3,2,1,0:T(8,128)S(1)}, u32[]{:S(2)}, u32[]{:S(2)}) collective-permute-start(f32[2,1,128,128]{3,2,1,0:T(8,128)S(1)} %get-tuple-element.97), channel_id=1, source_target_pairs={{0,3},{1,2},{2,1},{3,0},{4,7},{5,6},{6,5},{7,4},{8,11},{9,10},{10,... | collective-permute-start | bytes 393224 | tf_op jit(solution)/shard_map/ppermute | solution.py:491
  50.0 0.5 shard_map.100
  50.5 2.4 %collective-permute-done.12.refs_1_.refs_3_ = f32[2,1,128,128]{3,2,1,0:T(8,128)S(1)} collective-permute-done((f32[2,1,128,128]{3,2,1,0:T(8,128)S(1)}, f32[2,1,128,128]{3,2,1,0:T(8,128)S(1)}, u32[]{:S(2)}, u32[]{:S(2)}) %collective-permute-start.12) | collective-permute-done | bytes 131104 | tf_op jit(solution)/shard_map/ppermute | solution.py:491
  52.9 2.0 %collective-permute-done.14.refs_3_.refs_5_ = f32[2,1,128,128]{3,2,1,0:T(8,128)S(1)} collective-permute-done((f32[2,1,128,128]{3,2,1,0:T(8,128)S(1)}, f32[2,1,128,128]{3,2,1,0:T(8,128)S(1)}, u32[]{:S(2)}, u32[]{:S(2)}) %collective-permute-start.14) | collective-permute-done | bytes 131104 | tf_op jit(solution)/shard_map/ppermute | solution.py:491
  55.0 2.0 %collective-permute-start.16 = (f32[1,128,128]{2,1,0:T(8,128)S(1)}, f32[1,128,128]{2,1,0:T(8,128)S(1)}, u32[]{:S(2)}, u32[]{:S(2)}) collective-permute-start(f32[1,128,128]{2,1,0:T(8,128)S(1)} %get-tuple-element.98.refs_0_), channel_id=1, source_target_pairs={{0,4},{1,5},{2,6},{3,7},{4,0},{5,1},{6,2},{7,3},{8,12},{9,13},{10,... | collective-permute-start | bytes 196616 | tf_op jit(solution)/shard_map/ppermute | solution.py:491
  57.1 1.2 %collective-permute-start.18 = (f32[1,128,128]{2,1,0:T(8,128)S(1)}, f32[1,128,128]{2,1,0:T(8,128)S(1)}, u32[]{:S(2)}, u32[]{:S(2)}) collective-permute-start(f32[1,128,128]{2,1,0:T(8,128)S(1)} %shard_map.103), channel_id=1, source_target_pairs={{0,20},{1,21},{2,22},{3,23},{4,16},{5,17},{6,18},{7,19},{8,28},{9,... | collective-permute-start | bytes 196616 | tf_op jit(solution)/shard_map/ppermute | solution.py:491
  58.3 1.5 %collective-permute-start.19 = (f32[1,128,128]{2,1,0:T(8,128)S(1)}, f32[1,128,128]{2,1,0:T(8,128)S(1)}, u32[]{:S(2)}, u32[]{:S(2)}) collective-permute-start(f32[1,128,128]{2,1,0:T(8,128)S(1)} %shard_map.103), channel_id=1, source_target_pairs={{0,16},{1,17},{2,18},{3,19},{4,20},{5,21},{6,22},{7,23},{8,24},{9,... | collective-permute-start | bytes 196616 | tf_op jit(solution)/shard_map/ppermute | solution.py:491
  59.8 1.8 %collective-permute-start.17 = (f32[1,128,128]{2,1,0:T(8,128)S(1)}, f32[1,128,128]{2,1,0:T(8,128)S(1)}, u32[]{:S(2)}, u32[]{:S(2)}) collective-permute-start(f32[1,128,128]{2,1,0:T(8,128)S(1)} %collective-permute-done.15.refs_1_), channel_id=1, source_target_pairs={{0,4},{1,5},{2,6},{3,7},{4,0},{5,1},{6,2},{7,3},{8,12},{9,13},{10,... | collective-permute-start | bytes 196616 | tf_op jit(solution)/shard_map/ppermute | solution.py:491
  61.5 2.6 %shard_map.85.refs_0_ = bf16[2,8,512,512]{3,2,1,0:T(8,128)(2,1)S(1)} custom-call(bf16[1024,1024]{1,0:T(8,128)(2,1)S(1)} %copy-done.4, bf16[1024,1024]{1,0:T(8,128)(2,1)S(1)} %copy-done.2), custom_call_target="tpu_custom_call" | custom-call | flops 1073741824 | bytes 10737418 | tf_op jit(solution)/shard_map/pallas_call | solution.py:54
  64.2 3.2 %collective-permute-done.17.refs_3_ = f32[1,128,128]{2,1,0:T(8,128)S(1)} collective-permute-done((f32[1,128,128]{2,1,0:T(8,128)S(1)}, f32[1,128,128]{2,1,0:T(8,128)S(1)}, u32[]{:S(2)}, u32[]{:S(2)}) %collective-permute-start.17) | collective-permute-done | bytes 65568 | tf_op jit(solution)/shard_map/ppermute | solution.py:491
  67.6 5.5 %shard_map.98.refs_4_ = bf16[1024,1024]{1,0:T(8,128)(2,1)S(1)} custom-call(bf16[1024,1024]{1,0:T(8,128)(2,1)S(1)} %get-tuple-element.84.refs_1_.refs_0_, bf16[1024,1024]{1,0:T(8,128)(2,1)S(1)} %copy-done.1, bf16[1024,1024]{1,0:T(8,128)(2,1)S(1)} %copy-done.4, bf16[2,2,1,128,128]{4,3,2,1,0:T(8,128)(2,1)S(1)} %get-tuple-element.87.refs_3_, ...), custom_call_target="tpu_custom_call" | custom-call | flops 2147483648 | bytes 21474836 | tf_op jit(solution)/shard_map/pallas_call | solution.py:54
  73.1 1.1 %shard_map.97.refs_3_ = f32[1024,1024]{1,0:T(8,128)S(1)} custom-call(bf16[1024,1024]{1,0:T(8,128)(2,1)S(1)} %copy-done.1, bf16[1024,1024]{1,0:T(8,128)(2,1)S(1)} %get-tuple-element.84.refs_1_.refs_0_, bf16[1024,1024]{1,0:T(8,128)(2,1)S(1)} %copy-done.2), custom_call_target="tpu_custom_call" | custom-call | flops 536870912 | bytes 5368709 | tf_op jit(solution)/shard_map/pallas_call | solution.py:54
  74.3 0.6 collective-permute-start.21
  74.9 0.3 collective-permute-start.22
  75.3 2.6 %collective-permute-start.23 = (f32[2,1,128,128]{3,2,1,0:T(8,128)S(1)}, f32[2,1,128,128]{3,2,1,0:T(8,128)S(1)}, u32[]{:S(2)}, u32[]{:S(2)}) collective-permute-start(f32[2,1,128,128]{3,2,1,0:T(8,128)S(1)} %get-tuple-element.107), channel_id=1, source_target_pairs={{0,3},{1,2},{2,1},{3,0},{4,7},{5,6},{6,5},{7,4},{8,11},{9,10},{10,... | collective-permute-start | bytes 393224 | tf_op jit(solution)/shard_map/ppermute | solution.py:491
  77.9 3.1 %shard_map.99 = (f32[1024,1024]{1,0:T(8,128)S(1)}, bf16[1024,1024]{1,0:T(8,128)(2,1)}) custom-call(bf16[1024,1024]{1,0:T(8,128)(2,1)S(1)} %copy-done.1, bf16[1024,1024]{1,0:T(8,128)(2,1)S(1)} %get-tuple-element.84.refs_1_.refs_0_, bf16[1024,1024]{1,0:T(8,128)(2,1)S(1)} %copy-done.2, ...), custom_call_target="tpu_custom_call", output_to_operand_aliasing={{0}: (3, {})} | custom-call | flops 1610612736 | bytes 16106127 | tf_op jit(solution)/shard_map/pallas_call | solution.py:54
  81.0 2.1 %shard_map.96 = (f32[1024,1024]{1,0:T(8,128)S(1)}, bf16[1024,1024]{1,0:T(8,128)(2,1)}) custom-call(bf16[2,8,512,512]{3,2,1,0:T(8,128)(2,1)S(1)} %shard_map.85.refs_0_, bf16[1024,1024]{1,0:T(8,128)(2,1)S(1)} %get-tuple-element.84.refs_1_.refs_0_, bf16[1024,1024]{1,0:T(8,128)(2,1)S(1)} %get-tuple-element.85.refs_2_), custom_call_target="tpu_custom_call" | custom-call | flops 1073741824 | bytes 10737418 | tf_op jit(solution)/shard_map/pallas_call | solution.py:54
  83.2 1.1 %collective-permute-done.23.refs_5_ = f32[2,1,128,128]{3,2,1,0:T(8,128)S(1)} collective-permute-done((f32[2,1,128,128]{3,2,1,0:T(8,128)S(1)}, f32[2,1,128,128]{3,2,1,0:T(8,128)S(1)}, u32[]{:S(2)}, u32[]{:S(2)}) %collective-permute-start.23) | collective-permute-done | bytes 131104 | tf_op jit(solution)/shard_map/ppermute | solution.py:491
  84.3 2.0 %shard_map.106 = (bf16[1024,1024]{1,0:T(8,128)(2,1)}, bf16[1024,1024]{1,0:T(8,128)(2,1)}) custom-call(f32[1024,1024]{1,0:T(8,128)S(1)} %get-tuple-element.92.refs_0_, f32[1024,1024]{1,0:T(8,128)S(1)} %get-tuple-element.93.refs_1_, bf16[1024,1024]{1,0:T(8,128)(2,1)S(1)} %copy-done.4, bf16[1024,1024]{1,0:T(8,128)(2,1)S(1)} %copy-done.1, ...), custom_call_target="tpu_custom_call" | custom-call | flops 268435456 | bytes 2684354 | tf_op jit(solution)/shard_map/pallas_call | solution.py:54
  86.4 2.0 %shard_map.107 = (bf16[1024,1024]{1,0:T(8,128)(2,1)}, bf16[1024,1024]{1,0:T(8,128)(2,1)}) custom-call(f32[1024,1024]{1,0:T(8,128)S(1)} %get-tuple-element.92.refs_0_, f32[1024,1024]{1,0:T(8,128)S(1)} %get-tuple-element.93.refs_1_, bf16[1024,1024]{1,0:T(8,128)(2,1)S(1)} %copy-done.4, ...), custom_call_target="tpu_custom_call", output_to_operand_aliasing={{0}: (8, {}), {1}: (9, {})} | custom-call | flops 268435456 | bytes 2684354 | tf_op jit(solution)/shard_map/pallas_call | solution.py:54
  (38 shorter events, 0.8 us)
Async XLA Ops:
  0.6 1.6 %copy-start = (bf16[1024,1024]{1,0:T(8,128)(2,1)S(1)}, bf16[1024,1024]{1,0:T(8,128)(2,1)}, u32[]{:S(2)}) copy-start(bf16[1024,1024]{1,0:T(8,128)(2,1)} %refs_3_.5) | copy-start | bytes 6291460
  2.2 1.6 %copy-start.3 = (bf16[1024,1024]{1,0:T(8,128)(2,1)S(1)}, bf16[1024,1024]{1,0:T(8,128)(2,1)}, u32[]{:S(2)}) copy-start(bf16[1024,1024]{1,0:T(8,128)(2,1)} %refs_2_.9) | copy-start | bytes 6291460
  4.7 7.0 %collective-permute-start = (f32[2,1,128,128]{3,2,1,0:T(8,128)S(1)}, f32[2,1,128,128]{3,2,1,0:T(8,128)S(1)}, u32[]{:S(2)}, u32[]{:S(2)}) collective-permute-start(f32[2,1,128,128]{3,2,1,0:T(8,128)S(1)} %get-tuple-element.62), channel_id=1, source_target_pairs={{0,1},{1,0},{2,3},{3,2},{4,5},{5,4},{6,7},{7,6},{8,9},{9,8},{10,11... | collective-permute-start | bytes 393224 | tf_op jit(solution)/shard_map/ppermute | solution.py:491
  7.7 3.4 %copy-start.1 = (bf16[1024,1024]{1,0:T(8,128)(2,1)S(1)}, bf16[1024,1024]{1,0:T(8,128)(2,1)}, u32[]{:S(2)}) copy-start(bf16[1024,1024]{1,0:T(8,128)(2,1)} %refs_3_.5) | copy-start | bytes 6291460
  7.7 3.4 %copy-start.4 = (bf16[1024,1024]{1,0:T(8,128)(2,1)S(1)}, bf16[1024,1024]{1,0:T(8,128)(2,1)}, u32[]{:S(2)}) copy-start(bf16[1024,1024]{1,0:T(8,128)(2,1)} %refs_2_.9) | copy-start | bytes 6291460
  7.7 5.0 %collective-permute-start.1 = (f32[2,1,128,128]{3,2,1,0:T(8,128)S(1)}, f32[2,1,128,128]{3,2,1,0:T(8,128)S(1)}, u32[]{:S(2)}, u32[]{:S(2)}) collective-permute-start(f32[2,1,128,128]{3,2,1,0:T(8,128)S(1)} %get-tuple-element.63), channel_id=1, source_target_pairs={{0,2},{1,3},{2,0},{3,1},{4,6},{5,7},{6,4},{7,5},{8,10},{9,11},{10,... | collective-permute-start | bytes 393224 | tf_op jit(solution)/shard_map/ppermute | solution.py:491
  10.9 24.5 %copy-start.2 = (bf16[1024,1024]{1,0:T(8,128)(2,1)S(1)}, bf16[1024,1024]{1,0:T(8,128)(2,1)}, u32[]{:S(2)}) copy-start(bf16[1024,1024]{1,0:T(8,128)(2,1)} %refs_0_.14) | copy-start | bytes 6291460
  10.9 5.9 %collective-permute-start.2 = (f32[2,1,128,128]{3,2,1,0:T(8,128)S(1)}, f32[2,1,128,128]{3,2,1,0:T(8,128)S(1)}, u32[]{:S(2)}, u32[]{:S(2)}) collective-permute-start(f32[2,1,128,128]{3,2,1,0:T(8,128)S(1)} %get-tuple-element.64), channel_id=1, source_target_pairs={{0,3},{1,2},{2,1},{3,0},{4,7},{5,6},{6,5},{7,4},{8,11},{9,10},{10,... | collective-permute-start | bytes 393224 | tf_op jit(solution)/shard_map/ppermute | solution.py:491
  16.9 2.7 %collective-permute-start.3 = (f32[1,128,128]{2,1,0:T(8,128)S(1)}, f32[1,128,128]{2,1,0:T(8,128)S(1)}, u32[]{:S(2)}, u32[]{:S(2)}) collective-permute-start(f32[1,128,128]{2,1,0:T(8,128)S(1)} %get-tuple-element.66), channel_id=1, source_target_pairs={{0,8},{1,9},{2,10},{3,11},{4,12},{5,13},{6,14},{7,15},{8,0},{9,1},... | collective-permute-start | bytes 196616 | tf_op jit(solution)/shard_map/ppermute | solution.py:491
  17.0 9.1 %collective-permute-start.4 = (f32[1,128,128]{2,1,0:T(8,128)S(1)}, f32[1,128,128]{2,1,0:T(8,128)S(1)}, u32[]{:S(2)}, u32[]{:S(2)}) collective-permute-start(f32[1,128,128]{2,1,0:T(8,128)S(1)} %get-tuple-element.65.refs_0_), channel_id=1, source_target_pairs={{0,4},{1,5},{2,6},{3,7},{4,0},{5,1},{6,2},{7,3},{8,12},{9,13},{10,... | collective-permute-start | bytes 196616 | tf_op jit(solution)/shard_map/ppermute | solution.py:491
  19.6 8.5 %collective-permute-start.5 = (f32[1,128,128]{2,1,0:T(8,128)S(1)}, f32[1,128,128]{2,1,0:T(8,128)S(1)}, u32[]{:S(2)}, u32[]{:S(2)}) collective-permute-start(f32[1,128,128]{2,1,0:T(8,128)S(1)} %collective-permute-done.3.refs_1_), channel_id=1, source_target_pairs={{0,4},{1,5},{2,6},{3,7},{4,0},{5,1},{6,2},{7,3},{8,12},{9,13},{10,... | collective-permute-start | bytes 196616 | tf_op jit(solution)/shard_map/ppermute | solution.py:491
  20.8 9.5 %collective-permute-start.6 = (f32[1,128,128]{2,1,0:T(8,128)S(1)}, f32[1,128,128]{2,1,0:T(8,128)S(1)}, u32[]{:S(2)}, u32[]{:S(2)}) collective-permute-start(f32[1,128,128]{2,1,0:T(8,128)S(1)} %shard_map.89), channel_id=1, source_target_pairs={{0,20},{1,21},{2,22},{3,23},{4,16},{5,17},{6,18},{7,19},{8,28},{9,... | collective-permute-start | bytes 196616 | tf_op jit(solution)/shard_map/ppermute | solution.py:491
  23.6 6.8 %collective-permute-start.7 = (f32[1,128,128]{2,1,0:T(8,128)S(1)}, f32[1,128,128]{2,1,0:T(8,128)S(1)}, u32[]{:S(2)}, u32[]{:S(2)}) collective-permute-start(f32[1,128,128]{2,1,0:T(8,128)S(1)} %shard_map.89), channel_id=1, source_target_pairs={{0,16},{1,17},{2,18},{3,19},{4,20},{5,21},{6,22},{7,23},{8,24},{9,... | collective-permute-start | bytes 196616 | tf_op jit(solution)/shard_map/ppermute | solution.py:491
  30.4 1.3 %collective-permute-start.8 = (f32[1,128,128]{2,1,0:T(8,128)S(1)}, f32[1,128,128]{2,1,0:T(8,128)S(1)}, u32[]{:S(2)}, u32[]{:S(2)}) collective-permute-start(f32[1,128,128]{2,1,0:T(8,128)S(1)} %get-tuple-element.68), channel_id=1, source_target_pairs={{0,8},{1,9},{2,10},{3,11},{4,12},{5,13},{6,14},{7,15},{8,0},{9,1},... | collective-permute-start | bytes 196616 | tf_op jit(solution)/shard_map/ppermute | solution.py:491
  31.8 10.5 %collective-permute-start.9 = (f32[2,1,128,128]{3,2,1,0:T(8,128)S(1)}, f32[2,1,128,128]{3,2,1,0:T(8,128)S(1)}, u32[]{:S(2)}, u32[]{:S(2)}) collective-permute-start(f32[2,1,128,128]{3,2,1,0:T(8,128)S(1)} %get-tuple-element.69), channel_id=1, source_target_pairs={{0,1},{1,0},{2,3},{3,2},{4,5},{5,4},{6,7},{7,6},{8,9},{9,8},{10,11... | collective-permute-start | bytes 393224 | tf_op jit(solution)/shard_map/ppermute | solution.py:491
  32.4 9.9 %collective-permute-start.10 = (f32[2,1,128,128]{3,2,1,0:T(8,128)S(1)}, f32[2,1,128,128]{3,2,1,0:T(8,128)S(1)}, u32[]{:S(2)}, u32[]{:S(2)}) collective-permute-start(f32[2,1,128,128]{3,2,1,0:T(8,128)S(1)} %get-tuple-element.70), channel_id=1, source_target_pairs={{0,2},{1,3},{2,0},{3,1},{4,6},{5,7},{6,4},{7,5},{8,10},{9,11},{10,... | collective-permute-start | bytes 393224 | tf_op jit(solution)/shard_map/ppermute | solution.py:491
  32.4 7.6 %copy-start.5 = (bf16[1024,1024]{1,0:T(8,128)(2,1)S(1)}, bf16[1024,1024]{1,0:T(8,128)(2,1)}, u32[]{:S(2)}) copy-start(bf16[1024,1024]{1,0:T(8,128)(2,1)} %refs_6_) | copy-start | bytes 6291460
  32.4 7.6 %copy-start.6 = (f32[1024]{0:T(1024)S(1)}, f32[1024]{0:T(1024)}, u32[]{:S(2)}) copy-start(f32[1024]{0:T(1024)} %param.8) | copy-start | bytes 12292
  32.4 9.0 %collective-permute-start.11 = (f32[2,1,128,128]{3,2,1,0:T(8,128)S(1)}, f32[2,1,128,128]{3,2,1,0:T(8,128)S(1)}, u32[]{:S(2)}, u32[]{:S(2)}) collective-permute-start(f32[2,1,128,128]{3,2,1,0:T(8,128)S(1)} %get-tuple-element.73), channel_id=1, source_target_pairs={{0,3},{1,2},{2,1},{3,0},{4,7},{5,6},{6,5},{7,4},{8,11},{9,10},{10,... | collective-permute-start | bytes 393224 | tf_op jit(solution)/shard_map/ppermute | solution.py:491
  46.4 6.4 %collective-permute-start.12 = (f32[2,1,128,128]{3,2,1,0:T(8,128)S(1)}, f32[2,1,128,128]{3,2,1,0:T(8,128)S(1)}, u32[]{:S(2)}, u32[]{:S(2)}) collective-permute-start(f32[2,1,128,128]{3,2,1,0:T(8,128)S(1)} %get-tuple-element.95), channel_id=1, source_target_pairs={{0,1},{1,0},{2,3},{3,2},{4,5},{5,4},{6,7},{7,6},{8,9},{9,8},{10,11... | collective-permute-start | bytes 393224 | tf_op jit(solution)/shard_map/ppermute | solution.py:491
  47.0 5.8 %collective-permute-start.13 = (f32[2,1,128,128]{3,2,1,0:T(8,128)S(1)}, f32[2,1,128,128]{3,2,1,0:T(8,128)S(1)}, u32[]{:S(2)}, u32[]{:S(2)}) collective-permute-start(f32[2,1,128,128]{3,2,1,0:T(8,128)S(1)} %get-tuple-element.96), channel_id=1, source_target_pairs={{0,2},{1,3},{2,0},{3,1},{4,6},{5,7},{6,4},{7,5},{8,10},{9,11},{10,... | collective-permute-start | bytes 393224 | tf_op jit(solution)/shard_map/ppermute | solution.py:491
  47.3 7.6 %collective-permute-start.14 = (f32[2,1,128,128]{3,2,1,0:T(8,128)S(1)}, f32[2,1,128,128]{3,2,1,0:T(8,128)S(1)}, u32[]{:S(2)}, u32[]{:S(2)}) collective-permute-start(f32[2,1,128,128]{3,2,1,0:T(8,128)S(1)} %get-tuple-element.97), channel_id=1, source_target_pairs={{0,3},{1,2},{2,1},{3,0},{4,7},{5,6},{6,5},{7,4},{8,11},{9,10},{10,... | collective-permute-start | bytes 393224 | tf_op jit(solution)/shard_map/ppermute | solution.py:491
  54.9 2.1 %collective-permute-start.15 = (f32[1,128,128]{2,1,0:T(8,128)S(1)}, f32[1,128,128]{2,1,0:T(8,128)S(1)}, u32[]{:S(2)}, u32[]{:S(2)}) collective-permute-start(f32[1,128,128]{2,1,0:T(8,128)S(1)} %get-tuple-element.99), channel_id=1, source_target_pairs={{0,8},{1,9},{2,10},{3,11},{4,12},{5,13},{6,14},{7,15},{8,0},{9,1},... | collective-permute-start | bytes 196616 | tf_op jit(solution)/shard_map/ppermute | solution.py:491
  55.0 9.2 %collective-permute-start.16 = (f32[1,128,128]{2,1,0:T(8,128)S(1)}, f32[1,128,128]{2,1,0:T(8,128)S(1)}, u32[]{:S(2)}, u32[]{:S(2)}) collective-permute-start(f32[1,128,128]{2,1,0:T(8,128)S(1)} %get-tuple-element.98.refs_0_), channel_id=1, source_target_pairs={{0,4},{1,5},{2,6},{3,7},{4,0},{5,1},{6,2},{7,3},{8,12},{9,13},{10,... | collective-permute-start | bytes 196616 | tf_op jit(solution)/shard_map/ppermute | solution.py:491
  57.1 10.4 %collective-permute-start.18 = (f32[1,128,128]{2,1,0:T(8,128)S(1)}, f32[1,128,128]{2,1,0:T(8,128)S(1)}, u32[]{:S(2)}, u32[]{:S(2)}) collective-permute-start(f32[1,128,128]{2,1,0:T(8,128)S(1)} %shard_map.103), channel_id=1, source_target_pairs={{0,20},{1,21},{2,22},{3,23},{4,16},{5,17},{6,18},{7,19},{8,28},{9,... | collective-permute-start | bytes 196616 | tf_op jit(solution)/shard_map/ppermute | solution.py:491
  58.3 9.2 %collective-permute-start.19 = (f32[1,128,128]{2,1,0:T(8,128)S(1)}, f32[1,128,128]{2,1,0:T(8,128)S(1)}, u32[]{:S(2)}, u32[]{:S(2)}) collective-permute-start(f32[1,128,128]{2,1,0:T(8,128)S(1)} %shard_map.103), channel_id=1, source_target_pairs={{0,16},{1,17},{2,18},{3,19},{4,20},{5,21},{6,22},{7,23},{8,24},{9,... | collective-permute-start | bytes 196616 | tf_op jit(solution)/shard_map/ppermute | solution.py:491
  59.8 7.7 %collective-permute-start.17 = (f32[1,128,128]{2,1,0:T(8,128)S(1)}, f32[1,128,128]{2,1,0:T(8,128)S(1)}, u32[]{:S(2)}, u32[]{:S(2)}) collective-permute-start(f32[1,128,128]{2,1,0:T(8,128)S(1)} %collective-permute-done.15.refs_1_), channel_id=1, source_target_pairs={{0,4},{1,5},{2,6},{3,7},{4,0},{5,1},{6,2},{7,3},{8,12},{9,13},{10,... | collective-permute-start | bytes 196616 | tf_op jit(solution)/shard_map/ppermute | solution.py:491
  67.5 6.7 %collective-permute-start.20 = (f32[1,128,128]{2,1,0:T(8,128)S(1)}, f32[1,128,128]{2,1,0:T(8,128)S(1)}, u32[]{:S(2)}, u32[]{:S(2)}) collective-permute-start(f32[1,128,128]{2,1,0:T(8,128)S(1)} %get-tuple-element.101), channel_id=1, source_target_pairs={{0,8},{1,9},{2,10},{3,11},{4,12},{5,13},{6,14},{7,15},{8,0},{9,1},... | collective-permute-start | bytes 196616 | tf_op jit(solution)/shard_map/ppermute | solution.py:491
  74.3 12.0 %collective-permute-start.21 = (f32[2,1,128,128]{3,2,1,0:T(8,128)S(1)}, f32[2,1,128,128]{3,2,1,0:T(8,128)S(1)}, u32[]{:S(2)}, u32[]{:S(2)}) collective-permute-start(f32[2,1,128,128]{3,2,1,0:T(8,128)S(1)} %get-tuple-element.102), channel_id=1, source_target_pairs={{0,1},{1,0},{2,3},{3,2},{4,5},{5,4},{6,7},{7,6},{8,9},{9,8},{10,11... | collective-permute-start | bytes 393224 | tf_op jit(solution)/shard_map/ppermute | solution.py:491
  74.9 11.4 %collective-permute-start.22 = (f32[2,1,128,128]{3,2,1,0:T(8,128)S(1)}, f32[2,1,128,128]{3,2,1,0:T(8,128)S(1)}, u32[]{:S(2)}, u32[]{:S(2)}) collective-permute-start(f32[2,1,128,128]{3,2,1,0:T(8,128)S(1)} %get-tuple-element.103), channel_id=1, source_target_pairs={{0,2},{1,3},{2,0},{3,1},{4,6},{5,7},{6,4},{7,5},{8,10},{9,11},{10,... | collective-permute-start | bytes 393224 | tf_op jit(solution)/shard_map/ppermute | solution.py:491
  75.3 9.0 %collective-permute-start.23 = (f32[2,1,128,128]{3,2,1,0:T(8,128)S(1)}, f32[2,1,128,128]{3,2,1,0:T(8,128)S(1)}, u32[]{:S(2)}, u32[]{:S(2)}) collective-permute-start(f32[2,1,128,128]{3,2,1,0:T(8,128)S(1)} %get-tuple-element.107), channel_id=1, source_target_pairs={{0,3},{1,2},{2,1},{3,0},{4,7},{5,6},{6,5},{7,4},{8,11},{9,10},{10,... | collective-permute-start | bytes 393224 | tf_op jit(solution)/shard_map/ppermute | solution.py:491
